TPU v7x, 128 devices: a whole 4x4x4 slice. The times are simulated.
128 devices in a mesh: depth: 8 (over y, z_hi), tan: 16 (over x, z_lo, core).
Axes of the slice: x: 4, y: 4, z: 4 (z_hi: 2, z_lo: 2; z = z_hi * 2 + z_lo), core: 2. Of those that a mesh axis runs over, the one named last changes fastest.
Arguments:
- displacement: float32 [3, 64, 512, 2048], P(None, 'depth', 'tan'), may hold values from -6 to 6
- stiffness: float32 [64, 512, 2048], P('depth', 'tan'), may hold values from 0.5 to 8
- node_list: int32 [512, 128], replicated, may hold values from 0 to 1048575, as said below
- active_count: int32 [512], replicated, may hold values from 1 to 128
- wear_class: int32 [512, 128], P('tan'), may hold values from 0 to 7
- pressure: float32 [512, 128], P('tan'), may hold values from 0.5 to 2
- slip_speed: float32 [512, 128], P('tan'), may hold values from 0.2 to 1.5
- rate_table: float32 [8], replicated, may hold values from 0.3 to 3
- tile_owner: int32 [512], replicated, may hold values from 0 to 15
- node_cell: int32 [1048576], replicated, may hold values from 0 to 65535, as said below
Outputs:
- new_displacement: float32 [3, 64, 512, 2048], P(None, 'depth', 'tan')
Inputs may be any that keep to these rules, and one draw needn't show every extreme that they name: `node_list`: row i lists 128 different surface nodes, all from i * 2048 to (i + 1) * 2048 - 1; only the first active_count[i] slots are in contact. `node_cell`: different nodes may share a cell.
All inputs are finite; a program needn't handle non-finite values.
Results may differ from a plain program's by a relative error of at most 0.00007.
Values sent between devices are 32-bit elements; how exact they have to be, the bound alone decides.
No kernel may reach another device: no remote copies, remote signals or barrier semaphores. Data moves between devices by JAX's collectives and lax.ppermute only.
A program may use at most 192 MiB of HBM per device.

v0:
```python
import jax
import jax.numpy as jnp
from jax import lax
from jax.sharding import PartitionSpec as P

wear_step = 0.6
hardness = 4.0


def padded_2(array, sides, width):
    for axis, dim in sides:
        size, length = (lax.axis_size(axis), array.shape[dim])
        up = [(i, (i + 1) % size) for i in range(size - 1)]
        down = [(j, i) for i, j in up]
        last = lax.slice_in_dim(array, length - width, length, axis=dim)
        first = lax.slice_in_dim(array, 0, width, axis=dim)
        before = lax.ppermute(last, axis, up)
        after = lax.ppermute(first, axis, down)
        array = jnp.concatenate([before, array, after], axis=dim)
    return array


def relax(values, stiff_ext):
    padded = jnp.pad(values, ((0, 0), (0, 0), (0, 0), (1, 1)))
    stiff_pad = jnp.pad(stiff_ext, ((0, 0), (0, 0), (1, 1)))
    center = stiff_pad[1:-1, 1:-1, 1:-1]
    selectors = [
        (slice(2, None), slice(1, -1), slice(1, -1)),
        (slice(None, -2), slice(1, -1), slice(1, -1)),
        (slice(1, -1), slice(2, None), slice(1, -1)),
        (slice(1, -1), slice(None, -2), slice(1, -1)),
        (slice(1, -1), slice(1, -1), slice(2, None)),
        (slice(1, -1), slice(1, -1), slice(None, -2)),
    ]
    numerator = jnp.zeros((values.shape[0],) + center.shape, jnp.float32)
    denominator = jnp.zeros(center.shape, jnp.float32)
    for chosen in selectors:
        weight = 0.5 * (center + stiff_pad[chosen])
        numerator = numerator + weight[None] * padded[(slice(None),) + chosen]
        denominator = denominator + weight
    return (numerator, denominator)


def archard(class_ids, contact, sliding, rates, counts):
    slot_pos = jnp.arange(class_ids.shape[1])[None, :]
    classes = jnp.arange(rates.shape[0])
    rate = jnp.sum(jnp.where(class_ids[:, :, None] == classes, rates, 0.0), axis=-1)
    product = contact * sliding
    wear_depth = wear_step * rate * product / (1.0 + product / hardness)
    return jnp.where(slot_pos < counts[:, None], wear_depth, 0.0)


def tile_cells(lists, table_rows, first_tile):
    tile_len = table_rows.shape[1]
    offsets = (first_tile + jnp.arange(lists.shape[0], dtype=jnp.int32)) * tile_len
    local_node = lists - offsets[:, None]
    matches = local_node[:, :, None] == jnp.arange(tile_len, dtype=jnp.int32)[None, None, :]
    return jnp.sum(jnp.where(matches, table_rows[:, None, :], 0), axis=-1)


def paint(row_ids, col_ids, wear, nrows, width):
    row_hot = jnp.where(
        jnp.arange(nrows, dtype=jnp.int32)[:, None] == row_ids.reshape(1, -1),
        wear.reshape(1, -1),
        0.0,
    )
    col_hot = jnp.where(
        col_ids.reshape(-1, 1) == jnp.arange(width, dtype=jnp.int32)[None, :], 1.0, 0.0
    )
    return jnp.dot(
        row_hot, col_hot, precision=lax.Precision.HIGHEST, preferred_element_type=jnp.float32
    )


def per_device(
    displacement,
    stiffness,
    node_list,
    active_count,
    wear_class,
    pressure,
    slip_speed,
    rate_table,
    tile_owner,
    node_cell,
):
    tan_pos = lax.axis_index("tan")
    depth_pos = lax.axis_index("depth")
    tiles_here = wear_class.shape[0]
    layers = displacement.shape[1]
    rows_tan = displacement.shape[2]
    width = displacement.shape[3]
    tan_count = lax.axis_size("tan")
    cell_table = node_cell.reshape(node_list.shape[0], -1)
    first_here = tan_pos * tiles_here
    own_count = lax.dynamic_slice_in_dim(active_count, first_here, tiles_here, 0)
    wear_depth = archard(wear_class, pressure, slip_speed, rate_table, own_count)
    own_list = lax.dynamic_slice_in_dim(node_list, first_here, tiles_here, 0)
    own_owner = lax.dynamic_slice_in_dim(tile_owner, first_here, tiles_here, 0)
    own_table = lax.dynamic_slice_in_dim(cell_table, first_here, tiles_here, 0)
    cells = tile_cells(own_list, own_table, first_here)
    row_ids = own_owner[:, None] * rows_tan + cells // width
    col_ids = cells % width
    buffer = paint(row_ids, col_ids, wear_depth, rows_tan * tan_count, width)
    surface_slab = lax.psum_scatter(buffer, "tan", scatter_dimension=0, tiled=True)
    on_top = depth_pos == 0
    field = displacement.at[0, 0].add(jnp.where(on_top, surface_slab, 0.0))
    pinned = field[0]
    top_layer = (jnp.arange(layers) + depth_pos * layers == 0)[:, None, None]
    stacked = jnp.concatenate([field, stiffness[None]], axis=0)
    extended = padded_2(stacked, (("depth", 1), ("tan", 2)), 1)
    stiff_ext = extended[3]
    numerator, denominator = relax(extended[:3], stiff_ext)
    first = numerator / denominator[None]
    first = first.at[0].set(jnp.where(top_layer, pinned, first[0]))
    second_ext = padded_2(first, (("depth", 1), ("tan", 2)), 1)
    numerator, denominator = relax(second_ext, stiff_ext)
    result = numerator / denominator[None]
    result = result.at[0].set(jnp.where(top_layer, pinned, result[0]))
    return result


def solution(mesh):
    in_specs = (
        P(None, "depth", "tan", None),
        P("depth", "tan", None),
        P(),
        P(),
        P("tan", None),
        P("tan", None),
        P("tan", None),
        P(),
        P(),
        P(),
    )
    out_specs = P(None, "depth", "tan", None)
    return jax.shard_map(
        per_device, mesh=mesh, in_specs=in_specs, out_specs=out_specs, check_vma=False
    )
```

profile of v0, /device:TPU:15, one launch (start us, length us, event | category | flops | bytes accessed | tf_op | source)
XLA Modules:
  0.0 395.0 jit_solution(6872935246526590972)
XLA Ops:
  6.5 6.3 %copy.43 = f32[3,8,32,2048]{3,2,1,0:T(8,128)} copy(f32[3,8,32,2048]{3,2,1,0:T(8,128)} %param.16) | data formatting | bytes 12582912
  12.9 0.8 dynamic_slice.15
  13.6 0.8 dynamic-slice_multiply_fusion
  14.4 4.9 %reshape.193 = s32[512,2048]{1,0:T(8,128)} reshape(s32[1048576]{0:T(1024)} %param.25) | data formatting | bytes 8388608 | tf_op jit(solution)/shard_map/reshape | solution.py:94
  19.3 1.0 constant_dynamic-slice_fusion
  20.2 0.8 dynamic-slice_subtract_fusion
  21.0 0.1 select_reduce_fusion.1
  21.1 4.9 %select_reduce_fusion = s32[32,128]{1,0:T(8,128)S(1)} fusion(s32[32,2048]{1,0:T(8,128)S(1)} %constant_dynamic-slice_fusion, s32[32,128]{1,0:T(8,128)S(1)} %dynamic-slice_subtract_fusion), kind=kLoop, calls=%fused_computation.3 | loop fusion | flops 25161728 | bytes 294912 | tf_op jit(solution)/shard_map/reduce_sum | solution.py:58
  26.1 0.1 fusion.41
  26.2 0.1 select_bitcast_fusion
  26.2 4.3 %fusion.60 = f32[512,4096]{1,0:T(8,128)} fusion(f32[4096]{0:T(1024)S(1)} %select_bitcast_fusion, s32[4096]{0:T(1024)S(1)} %get-tuple-element.56), kind=kLoop, calls=%fused_computation.20.clone.2 | loop fusion | flops 4194304 | bytes 8421376 | tf_op jit(solution)/shard_map/dot_general | solution.py:70
  30.5 100.1 %fusion = f32[512,2048]{1,0:T(8,128)} fusion(s32[4096]{0:T(1024)S(1)} %get-tuple-element.57, f32[512,4096]{1,0:T(8,128)} %fusion.60), kind=kOutput, calls=%fused_computation | convolution fusion | flops 51556384768 | bytes 12599296 | tf_op jit(solution)/shard_map/dot_general | solution.py:70
  130.7 65.1 %reduce-scatter.2.cloned.1.call-done = f32[32,2048]{1,0:T(8,128)} async-done(((f32[512,2048]{1,0:T(8,128)}), f32[32,2048]{1,0:T(8,128)}) %reduce-scatter.2.cloned.1.call-update) | async-done | bytes 262160 | tf_op jit(solution)/shard_map/reduce_scatter | solution.py:105
  195.8 1.7 fusion.40
  197.5 1.7 pad_maximum_fusion.21
  199.2 4.7 %collective-permute-start = (f32[4,1,32,2048]{3,2,1,0:T(8,128)S(1)}, f32[4,1,32,2048]{3,2,1,0:T(8,128)S(1)}, u32[]{:S(2)}, u32[]{:S(2)}) collective-permute-start(f32[4,1,32,2048]{3,2,1,0:T(8,128)S(1)} %get-tuple-element.50), channel_id=1, source_target_pairs={{0,16},{16,32},{32,48},{48,64},{64,80},{80,96},{96,112},{1,17},{17... | collective-permute-start | bytes 3145736 | tf_op jit(solution)/shard_map/ppermute | solution.py:17
  203.9 3.1 collective-permute-start.1
  207.0 42.0 %collective-permute-done = f32[4,1,32,2048]{3,2,1,0:T(8,128)S(1)} collective-permute-done((f32[4,1,32,2048]{3,2,1,0:T(8,128)S(1)}, f32[4,1,32,2048]{3,2,1,0:T(8,128)S(1)}, u32[]{:S(2)}, u32[]{:S(2)}) %collective-permute-start) | collective-permute-done | bytes 1048608 | tf_op jit(solution)/shard_map/ppermute | solution.py:17
  249.0 1.8 collective-permute-done.1
  250.8 0.6 pad_maximum_fusion.25
  251.4 0.9 copy.28
  252.3 2.3 collective-permute-start.3
  254.6 0.9 copy.27
  255.5 5.1 %collective-permute-start.2 = (f32[4,10,1,2048]{3,1,2,0:T(8,128)}, f32[4,10,1,2048]{3,1,2,0:T(8,128)}, u32[]{:S(2)}, u32[]{:S(2)}) collective-permute-start(f32[4,10,1,2048]{3,1,2,0:T(8,128)} %copy.27), channel_id=1, source_target_pairs={{0,1},{1,2},{2,3},{3,4},{4,5},{5,6},{6,7},{7,8},{8,9},{9,10},{10,1... | collective-permute-start | bytes 983048 | tf_op jit(solution)/shard_map/ppermute | solution.py:17
  260.7 9.9 %collective-permute-done.3 = f32[4,10,1,2048]{3,1,2,0:T(8,128)} collective-permute-done((f32[4,10,1,2048]{3,1,2,0:T(8,128)}, f32[4,10,1,2048]{3,1,2,0:T(8,128)}, u32[]{:S(2)}, u32[]{:S(2)}) %collective-permute-start.3) | collective-permute-done | bytes 327712 | tf_op jit(solution)/shard_map/ppermute | solution.py:18
  270.6 1.4 copy.30
  272.0 1.4 copy.29
  273.4 1.6 maximum_bitcast_fusion
  275.0 6.6 %add_add_fusion = (f32[8,32,2048]{2,1,0:T(8,128)}, f32[8,32,2048]{2,1,0:T(8,128)}, f32[8,32,2048]{2,1,0:T(8,128)}, f32[8,32,2048]{2,1,0:T(8,128)}, f32[8,32,2048...) fusion(f32[10,34,2048]{2,1,0:T(8,128)S(1)} %maximum_bitcast_fusion), kind=kLoop, calls=%fused_computation.88 | loop fusion | flops 8912896 | bytes 28442624 | tf_op jit(solution)/shard_map/add | solution.py:40
  281.6 13.4 %select_maximum_fusion.4 = f32[3,10,34,2050]{3,2,1,0:T(8,128)} fusion(f32[4,10,1,2048]{3,2,1,0:T(1,128)S(1)} %copy.30, f32[4,10,1,2048]{3,2,1,0:T(1,128)S(1)} %copy.29, f32[4,1,32,2048]{3,2,1,0:T(8,128)S(1)} %copy-done.6, f32[4,1,32,2048]{3,2,1,0:T(8,128)S(1)} %collective-permute-done, f32[1,8,32,2048]{3,2,1,0:T(8,128)S(1)} %bitcast.44, ...), kind=kLoop, calls=%fused_computation.14 | loop fusion | flops 29274000 | bytes 19505120 | tf_op jit(solution)/shard_map/concatenate | solution.py:19
  295.0 14.1 %fusion.18 = f32[3,8,32,2048]{3,2,1,0:T(8,128)S(1)} fusion(f32[3,10,34,2050]{3,2,1,0:T(8,128)} %select_maximum_fusion.4, f32[4,10,1,2048]{3,2,1,0:T(1,128)} %copy-done.9, f32[4,1,32,2048]{3,2,1,0:T(8,128)} %copy-done.5, f32[4,1,32,2048]{3,2,1,0:T(8,128)} %copy-done.4, f32[1,8,32,2048]{3,2,1,0:T(8,128)} %bitcast.40, f32[3,8,32,2048]{3,2,1,0:T(8,128)S(1)} %bitcast.39, ...), kind=kLoop, calls=%fused_computation.44 | loop fusion | flops 37748736 | bytes 44695552 | tf_op jit(solution)/shard_map/div | solution.py:114
  309.1 0.6 fusion.35
  309.7 0.1 fusion.53
  309.8 2.7 collective-permute-start.5
  312.4 5.0 %collective-permute-start.4 = (f32[3,1,32,2048]{3,2,1,0:T(8,128)S(1)}, f32[3,1,32,2048]{3,2,1,0:T(8,128)S(1)}, u32[]{:S(2)}, u32[]{:S(2)}) collective-permute-start(f32[3,1,32,2048]{3,2,1,0:T(8,128)S(1)} %get-tuple-element.55), channel_id=1, source_target_pairs={{16,0},{32,16},{48,32},{64,48},{80,64},{96,80},{112,96},{17,1},{33... | collective-permute-start | bytes 2359304 | tf_op jit(solution)/shard_map/ppermute | solution.py:18
  317.5 25.9 %collective-permute-done.5 = f32[3,1,32,2048]{3,2,1,0:T(8,128)S(1)} collective-permute-done((f32[3,1,32,2048]{3,2,1,0:T(8,128)S(1)}, f32[3,1,32,2048]{3,2,1,0:T(8,128)S(1)}, u32[]{:S(2)}, u32[]{:S(2)}) %collective-permute-start.5) | collective-permute-done | bytes 786464 | tf_op jit(solution)/shard_map/ppermute | solution.py:17
  343.3 2.9 collective-permute-done.4
  346.2 0.4 pad_maximum_fusion.26
  346.6 0.1 copy.33
  346.7 2.3 collective-permute-start.6
  349.0 0.1 copy.35
  349.1 3.3 collective-permute-start.7
  352.4 7.6 %collective-permute-done.6 = f32[3,10,1,2048]{3,1,2,0:T(8,128)S(1)} collective-permute-done((f32[3,10,1,2048]{3,1,2,0:T(8,128)S(1)}, f32[3,10,1,2048]{3,1,2,0:T(8,128)S(1)}, u32[]{:S(2)}, u32[]{:S(2)}) %collective-permute-start.6) | collective-permute-done | bytes 245792 | tf_op jit(solution)/shard_map/ppermute | solution.py:18
  360.0 0.3 copy.34
  360.3 0.3 copy.36
  360.6 8.5 %select_maximum_fusion = f32[3,10,34,2050]{3,2,1,0:T(8,128)} fusion(f32[3,10,1,2048]{3,2,1,0:T(1,128)S(1)} %copy.34, f32[3,10,1,2048]{3,2,1,0:T(1,128)S(1)} %copy.36, f32[3,1,32,2048]{3,2,1,0:T(8,128)S(1)} %collective-permute-done.4, f32[3,8,32,2048]{3,2,1,0:T(8,128)S(1)} %fusion.35, f32[3,1,32,2048]{3,2,1,0:T(8,128)S(1)} %collective-permute-done.5), kind=kLoop, calls=%fused_computation.10 | loop fusion | flops 25092000 | bytes 16719840 | tf_op jit(solution)/shard_map/concatenate | solution.py:19
  369.1 15.5 %fusion.8 = f32[3,8,32,2048]{3,2,1,0:T(8,128)} fusion(f32[3,10,34,2050]{3,2,1,0:T(8,128)} %select_maximum_fusion, f32[3,10,1,2048]{3,2,1,0:T(1,128)S(1)} %copy.36, f32[3,1,32,2048]{3,2,1,0:T(8,128)} %copy-done.8, f32[3,8,32,2048]{3,2,1,0:T(8,128)S(1)} %fusion.35, f32[3,1,32,2048]{3,2,1,0:T(8,128)} %copy-done.7, f32[3,10,1,2048]{3,2,1,0:T(1,128)S(1)} %copy.34, ...), kind=kLoop, calls=%fused_computation.24 | loop fusion | flops 31457280 | bytes 41910272 | tf_op jit(solution)/shard_map/div | solution.py:118
  384.6 3.3 fusion.34
  (39 shorter events, 0.1 us)
Async XLA Ops:
  6.5 189.3 %reduce-scatter.2.cloned.1.call-start = ((), (), s32[]{:S(2)}) async-start(), calls=%async_computation.1 | async-start | bytes 4456448 | tf_op jit(solution)/shard_map/reduce_scatter | solution.py:105
  12.8 8.2 %copy-start.10 = (s32[32,128]{1,0:T(8,128)S(1)}, s32[32,128]{1,0:T(8,128)}, u32[]{:S(2)}) copy-start(s32[32,128]{1,0:T(8,128)} %param.20) | copy-start | bytes 49156
  12.8 8.2 %copy-start.13 = (f32[8]{0:T(128)S(1)}, f32[8]{0:T(128)}, u32[]{:S(2)}) copy-start(f32[8]{0:T(128)} %param.23) | copy-start | bytes 100
  12.8 13.3 %copy-start.11 = (f32[32,128]{1,0:T(8,128)S(1)}, f32[32,128]{1,0:T(8,128)}, u32[]{:S(2)}) copy-start(f32[32,128]{1,0:T(8,128)} %param.21) | copy-start | bytes 49156
  12.8 13.3 %copy-start.12 = (f32[32,128]{1,0:T(8,128)S(1)}, f32[32,128]{1,0:T(8,128)}, u32[]{:S(2)}) copy-start(f32[32,128]{1,0:T(8,128)} %param.22) | copy-start | bytes 49156
  130.6 66.9 %copy-start.1 = (f32[8,32,2048]{2,1,0:T(8,128)S(1)}, f32[8,32,2048]{2,1,0:T(8,128)}, u32[]{:S(2)}) copy-start(f32[8,32,2048]{2,1,0:T(8,128)} %param.17) | copy-start | bytes 6291460
  197.5 53.3 %copy-start = (f32[3,8,32,2048]{3,2,1,0:T(8,128)S(1)}, f32[3,8,32,2048]{3,2,1,0:T(8,128)}, u32[]{:S(2)}) copy-start(f32[3,8,32,2048]{3,2,1,0:T(8,128)} %fusion.40) | copy-start | bytes 18874372
  199.2 49.9 %collective-permute-start = (f32[4,1,32,2048]{3,2,1,0:T(8,128)S(1)}, f32[4,1,32,2048]{3,2,1,0:T(8,128)S(1)}, u32[]{:S(2)}, u32[]{:S(2)}) collective-permute-start(f32[4,1,32,2048]{3,2,1,0:T(8,128)S(1)} %get-tuple-element.50), channel_id=1, source_target_pairs={{0,16},{16,32},{32,48},{48,64},{64,80},{80,96},{96,112},{1,17},{17... | collective-permute-start | bytes 3145736 | tf_op jit(solution)/shard_map/ppermute | solution.py:17
  203.9 46.9 %collective-permute-start.1 = (f32[4,1,32,2048]{3,2,1,0:T(8,128)S(1)}, f32[4,1,32,2048]{3,2,1,0:T(8,128)S(1)}, u32[]{:S(2)}, u32[]{:S(2)}) collective-permute-start(f32[4,1,32,2048]{3,2,1,0:T(8,128)S(1)} %get-tuple-element.51), channel_id=1, source_target_pairs={{16,0},{32,16},{48,32},{64,48},{80,64},{96,80},{112,96},{17,1},{33... | collective-permute-start | bytes 3145736 | tf_op jit(solution)/shard_map/ppermute | solution.py:18
  249.0 32.6 %copy-start.4 = (f32[4,1,32,2048]{3,2,1,0:T(8,128)}, f32[4,1,32,2048]{3,2,1,0:T(8,128)S(1)}, u32[]{:S(2)}) copy-start(f32[4,1,32,2048]{3,2,1,0:T(8,128)S(1)} %collective-permute-done) | copy-start | bytes 3145732
  250.8 4.7 %copy-start.5 = (f32[4,1,32,2048]{3,2,1,0:T(8,128)}, f32[4,1,32,2048]{3,2,1,0:T(8,128)S(1)}, u32[]{:S(2)}) copy-start(f32[4,1,32,2048]{3,2,1,0:T(8,128)S(1)} %collective-permute-done.1) | copy-start | bytes 3145732
  252.3 18.3 %collective-permute-start.3 = (f32[4,10,1,2048]{3,1,2,0:T(8,128)}, f32[4,10,1,2048]{3,1,2,0:T(8,128)}, u32[]{:S(2)}, u32[]{:S(2)}) collective-permute-start(f32[4,10,1,2048]{3,1,2,0:T(8,128)} %copy.28), channel_id=1, source_target_pairs={{1,0},{2,1},{3,2},{4,3},{5,4},{6,5},{7,6},{8,7},{9,8},{10,9},{11,1... | collective-permute-start | bytes 983048 | tf_op jit(solution)/shard_map/ppermute | solution.py:18
  255.5 16.5 %collective-permute-start.2 = (f32[4,10,1,2048]{3,1,2,0:T(8,128)}, f32[4,10,1,2048]{3,1,2,0:T(8,128)}, u32[]{:S(2)}, u32[]{:S(2)}) collective-permute-start(f32[4,10,1,2048]{3,1,2,0:T(8,128)} %copy.27), channel_id=1, source_target_pairs={{0,1},{1,2},{2,3},{3,4},{4,5},{5,6},{6,7},{7,8},{8,9},{9,10},{10,1... | collective-permute-start | bytes 983048 | tf_op jit(solution)/shard_map/ppermute | solution.py:17
  273.4 8.2 %copy-start.9 = (f32[4,10,1,2048]{3,2,1,0:T(1,128)}, f32[4,10,1,2048]{3,2,1,0:T(1,128)S(1)}, u32[]{:S(2)}) copy-start(f32[4,10,1,2048]{3,2,1,0:T(1,128)S(1)} %copy.29) | copy-start | bytes 983044
  273.4 8.2 %slice-start = ((s8[6291456]{0:T(1024)(128)(4,1)}), s8[4194304]{0:T(1024)(128)(4,1)S(1)}, s32[]{:S(2)}) async-start(s8[6291456]{0:T(1024)(128)(4,1)} %bitcast.38), calls=%async_computation.2 | async-start | bytes 8388608
  275.0 6.6 %slice-start.1 = ((s8[6291456]{0:T(1024)(128)(4,1)}), s8[2097152]{0:T(1024)(128)(4,1)S(1)}, s32[]{:S(2)}) async-start(s8[6291456]{0:T(1024)(128)(4,1)} %bitcast.38), calls=%async_computation.3 | async-start | bytes 4194304
  275.0 6.6 %copy-start.6 = (f32[4,1,32,2048]{3,2,1,0:T(8,128)S(1)}, f32[4,1,32,2048]{3,2,1,0:T(8,128)}, u32[]{:S(2)}) copy-start(f32[4,1,32,2048]{3,2,1,0:T(8,128)} %copy-done.5) | copy-start | bytes 3145732
  309.8 33.6 %collective-permute-start.5 = (f32[3,1,32,2048]{3,2,1,0:T(8,128)S(1)}, f32[3,1,32,2048]{3,2,1,0:T(8,128)S(1)}, u32[]{:S(2)}, u32[]{:S(2)}) collective-permute-start(f32[3,1,32,2048]{3,2,1,0:T(8,128)S(1)} %get-tuple-element.54), channel_id=1, source_target_pairs={{0,16},{16,32},{32,48},{48,64},{64,80},{80,96},{96,112},{1,17},{17... | collective-permute-start | bytes 2359304 | tf_op jit(solution)/shard_map/ppermute | solution.py:17
  312.4 33.8 %collective-permute-start.4 = (f32[3,1,32,2048]{3,2,1,0:T(8,128)S(1)}, f32[3,1,32,2048]{3,2,1,0:T(8,128)S(1)}, u32[]{:S(2)}, u32[]{:S(2)}) collective-permute-start(f32[3,1,32,2048]{3,2,1,0:T(8,128)S(1)} %get-tuple-element.55), channel_id=1, source_target_pairs={{16,0},{32,16},{48,32},{64,48},{80,64},{96,80},{112,96},{17,1},{33... | collective-permute-start | bytes 2359304 | tf_op jit(solution)/shard_map/ppermute | solution.py:18
  343.3 17.2 %copy-start.7 = (f32[3,1,32,2048]{3,2,1,0:T(8,128)}, f32[3,1,32,2048]{3,2,1,0:T(8,128)S(1)}, u32[]{:S(2)}) copy-start(f32[3,1,32,2048]{3,2,1,0:T(8,128)S(1)} %collective-permute-done.5) | copy-start | bytes 2359300
  346.2 14.4 %copy-start.8 = (f32[3,1,32,2048]{3,2,1,0:T(8,128)}, f32[3,1,32,2048]{3,2,1,0:T(8,128)S(1)}, u32[]{:S(2)}) copy-start(f32[3,1,32,2048]{3,2,1,0:T(8,128)S(1)} %collective-permute-done.4) | copy-start | bytes 2359300
  346.7 13.3 %collective-permute-start.6 = (f32[3,10,1,2048]{3,1,2,0:T(8,128)S(1)}, f32[3,10,1,2048]{3,1,2,0:T(8,128)S(1)}, u32[]{:S(2)}, u32[]{:S(2)}) collective-permute-start(f32[3,10,1,2048]{3,1,2,0:T(8,128)S(1)} %copy.33), channel_id=1, source_target_pairs={{1,0},{2,1},{3,2},{4,3},{5,4},{6,5},{7,6},{8,7},{9,8},{10,9},{11,1... | collective-permute-start | bytes 737288 | tf_op jit(solution)/shard_map/ppermute | solution.py:18
  349.1 11.2 %collective-permute-start.7 = (f32[3,10,1,2048]{3,1,2,0:T(8,128)S(1)}, f32[3,10,1,2048]{3,1,2,0:T(8,128)S(1)}, u32[]{:S(2)}, u32[]{:S(2)}) collective-permute-start(f32[3,10,1,2048]{3,1,2,0:T(8,128)S(1)} %copy.35), channel_id=1, source_target_pairs={{0,1},{1,2},{2,3},{3,4},{4,5},{5,6},{6,7},{7,8},{8,9},{9,10},{10,1... | collective-permute-start | bytes 737288 | tf_op jit(solution)/shard_map/ppermute | solution.py:17
  360.6 8.5 %copy-start.2 = (f32[8,32,2048]{2,1,0:T(8,128)S(1)}, f32[8,32,2048]{2,1,0:T(8,128)}, u32[]{:S(2)}) copy-start(f32[8,32,2048]{2,1,0:T(8,128)} %get-tuple-element.41) | copy-start | bytes 6291460
  360.6 8.5 %copy-start.3 = (f32[8,32,2048]{2,1,0:T(8,128)S(1)}, f32[8,32,2048]{2,1,0:T(8,128)}, u32[]{:S(2)}) copy-start(f32[8,32,2048]{2,1,0:T(8,128)} %get-tuple-element.42) | copy-start | bytes 6291460
Sparse Core Ops, SparseCore 0:
  130.8 64.9 reduce-scatter.1
where the time goes:
time: 401 us; the launch traced here: 395 us
  waiting for transfers between devices  155 us (39%)
  matrix products  100 us (25%)
  other arithmetic  78.9 us (20%)
  starting transfers between devices  28.5 us (7%)
  local copies, waits for them, and re-layouts  18.3 us (5%)
  between operations  14 us (3%)
    dot_general x1, matrix products, paint(): jnp.dot(row_hot, col_hot, precision=lax.Precision.HIGHEST, preferred_elem...  100 us
    ppermute x4, waiting for transfers between devices, padded_2(): before = lax.ppermute(last, axis, up)  67.9 us
    reduce_scatter x1, waiting for transfers between devices, per_device(): lax.psum_scatter(buffer, 'tan', scatter_dimension=0, tiled=True)  65.1 us
    concatenate x3, other arithmetic, padded_2(): array = jnp.concatenate([before, array, after], axis=dim)  22.3 us
    ppermute x4, waiting for transfers between devices, padded_2(): after = lax.ppermute(first, axis, down)  22.2 us
    ppermute x4, starting transfers between devices, padded_2(): before = lax.ppermute(last, axis, up)  15.7 us
    div x1, other arithmetic, per_device(): result = numerator / denominator[None]  15.5 us
    div x1, other arithmetic, per_device(): first = numerator / denominator[None]  14.1 us
  transfers between devices with their start and end apart: 9, of which 7 were waited for; matrix products, arithmetic and copies ran while one was open for 1% of the time, Pallas kernels for 0%

commit v1 on v0

v1 whole, which is shorter than its diff:
```python
import jax
import jax.numpy as jnp
from jax import lax
from jax.experimental import pallas as pl
from jax.experimental.pallas import tpu as pltpu
from jax.sharding import PartitionSpec as P

wear_step = 0.6
hardness = 4.0
GROUP = 8
VMEM_LIMIT = 48 * 1024 * 1024


def shift_both(last, first, axis):
    size = lax.axis_size(axis)
    up = [(i, i + 1) for i in range(size - 1)]
    down = [(j, i) for i, j in up]
    return lax.ppermute(last, axis, up), lax.ppermute(first, axis, down)


def archard(class_ids, contact, sliding, rates):
    classes = jnp.arange(rates.shape[0])
    rate = jnp.sum(jnp.where(class_ids[:, :, None] == classes, rates, 0.0), axis=-1)
    product = contact * sliding
    return wear_step * rate * product / (1.0 + product / hardness)


def three_parts(value):
    high = value.astype(jnp.bfloat16).astype(jnp.float32)
    rest = value - high
    middle = rest.astype(jnp.bfloat16).astype(jnp.float32)
    return high, middle, rest - middle


def paint_kernel(
    where_ref, owner_ref, count_ref, wear_ref, list_ref, table_ref, out_ref,
    own_ref, side_ref, acc_ref, edge_ref,
):
    slots = wear_ref.shape[1]
    ntile = wear_ref.shape[0]
    rows_table = table_ref.shape[0] // ntile
    tile_len = rows_table * 128
    width = out_ref.shape[1]
    rows = out_ref.shape[0] - 16
    me = where_ref[0]
    on_top = where_ref[1]
    out_ref[...] = jnp.zeros_like(out_ref)

    @pl.when(on_top == 1)
    def _():
        acc_ref[...] = jnp.zeros_like(acc_ref)
        edge_ref[...] = jnp.zeros_like(edge_ref)

        def collect(i, carry):
            n_own, n_side = carry
            offset = owner_ref[i] - me
            own_ref[n_own] = i
            side_ref[n_side] = i
            n_own = n_own + jnp.where(offset == 0, 1, 0)
            n_side = n_side + jnp.where(offset * offset == 1, 1, 0)
            return n_own, n_side

        n_own, n_side = lax.fori_loop(
            0, ntile, collect, (jnp.int32(0), jnp.int32(0)), unroll=8
        )

        lane = lax.broadcasted_iota(jnp.int32, (1, slots), 1)
        table_row = lax.broadcasted_iota(jnp.int32, (rows_table, slots), 0)
        block = width // 8
        fine = lax.broadcasted_iota(jnp.int32, (block, slots), 0)
        coarse = lax.broadcasted_iota(jnp.int32, (rows * 8, slots), 0)
        fine_edge = lax.broadcasted_iota(jnp.int32, (128, slots), 0)
        edge_blocks = width // 128
        coarse_edge = lax.broadcasted_iota(jnp.int32, (2 * edge_blocks, slots), 0)

        def entry(tiles_ref, position, total):
            i = tiles_ref[jnp.minimum(position, total - 1)]
            live = jnp.where(position < total, count_ref[i], 0)
            local = list_ref[pl.ds(i, 1), :] - i * tile_len
            table = table_ref[pl.ds(pl.multiple_of(i * rows_table, 8), rows_table), :]
            column = jnp.broadcast_to(local & 127, (rows_table, slots))
            picked = jnp.take_along_axis(table, column, axis=1)
            cell = jnp.sum(
                jnp.where(table_row == (local >> 7), picked, 0), axis=0, keepdims=True
            )
            wear = jnp.where(lane < live, wear_ref[pl.ds(i, 1), :], 0.0)
            return i, cell, wear

        def one_hot(mask, value):
            return jnp.where(mask, value, 0.0).astype(jnp.bfloat16)

        def add(into_ref, parts, hot):
            total = into_ref[...]
            for part in parts:
                total = total + lax.dot_general(
                    jnp.concatenate(part, axis=1), hot, (((1,), (1,)), ((), ())),
                    preferred_element_type=jnp.float32,
                )
            into_ref[...] = total

        def own_group(g, carry):
            parts = ([], [], [])
            hots = []
            for j in range(GROUP):
                _, cell, wear = entry(own_ref, g * GROUP + j, n_own)
                col = cell % width
                a_index = (col // block) * rows + cell // width
                hots.append(one_hot(fine == col % block, 1.0))
                mask = coarse == a_index
                for part, value in zip(parts, three_parts(wear)):
                    part.append(one_hot(mask, value))
            add(acc_ref, parts, jnp.concatenate(hots, axis=1))
            return carry

        def side_group(g, carry):
            parts = ([], [], [])
            hots = []
            for j in range(GROUP):
                i, cell, wear = entry(side_ref, g * GROUP + j, n_side)
                below = owner_ref[i] > me
                col = cell % width
                wanted = jnp.where(below, 0, rows - 1)
                shift = jnp.where(below, edge_blocks, 0)
                a_index = jnp.where(cell // width == wanted, col // 128 + shift, -1)
                hots.append(one_hot(fine_edge == col % 128, 1.0))
                mask = coarse_edge == a_index
                for part, value in zip(parts, three_parts(wear)):
                    part.append(one_hot(mask, value))
            add(edge_ref, parts, jnp.concatenate(hots, axis=1))
            return carry

        lax.fori_loop(0, (n_own + GROUP - 1) // GROUP, own_group, 0)
        lax.fori_loop(0, (n_side + GROUP - 1) // GROUP, side_group, 0)
        for j in range(8):
            out_ref[8 : 8 + rows, j * block : (j + 1) * block] = acc_ref[
                j * rows : (j + 1) * rows, :
            ]
        for j in range(edge_blocks):
            out_ref[7:8, j * 128 : (j + 1) * 128] = edge_ref[j : j + 1, :]
            out_ref[8 + rows : 9 + rows, j * 128 : (j + 1) * 128] = edge_ref[
                edge_blocks + j : edge_blocks + j + 1, :
            ]


def paint(position, owner, counts, wear, lists, table, rows, width):
    ntile, slots = lists.shape
    whole = lambda shape: pl.BlockSpec(shape, lambda i, *_: (0,) * len(shape))
    return pl.pallas_call(
        paint_kernel,
        name="paint_band",
        grid_spec=pltpu.PrefetchScalarGridSpec(
            num_scalar_prefetch=3,
            grid=(1,),
            in_specs=[whole(wear.shape), whole(lists.shape), whole(table.shape)],
            out_specs=whole((rows + 16, width)),
            scratch_shapes=[
                pltpu.SMEM((ntile + 1,), jnp.int32),
                pltpu.SMEM((ntile + 1,), jnp.int32),
                pltpu.VMEM((rows * 8, width // 8), jnp.float32),
                pltpu.VMEM((2 * width // 128, 128), jnp.float32),
            ],
        ),
        out_shape=jax.ShapeDtypeStruct((rows + 16, width), jnp.float32),
        compiler_params=pltpu.CompilerParams(vmem_limit_bytes=VMEM_LIMIT),
    )(position, owner, counts, wear, lists, table)


def relax_tile(load, edge_before, edge_after, t, ntiles):
    row = lax.broadcasted_iota(jnp.int32, (8, 1), 0)
    centers = {}

    def neighbours(c):
        here = load(c, 0, t)
        centers[c] = here
        width = here.shape[1]
        lane = lax.broadcasted_iota(jnp.int32, here.shape, 1)
        above = load(c, 0, t - 1)[7:8] if t > 0 else edge_before(c)
        below = load(c, 0, t + 1)[0:1] if t < ntiles - 1 else edge_after(c)
        yield load(c, 1, t)
        yield load(c, -1, t)
        yield jnp.where(row == 7, below, pltpu.roll(here, 7, 0))
        yield jnp.where(row == 0, above, pltpu.roll(here, 1, 0))
        yield jnp.where(lane == width - 1, 0.0, pltpu.roll(here, width - 1, 1))
        yield jnp.where(lane == 0, 0.0, pltpu.roll(here, 1, 1))

    around = list(neighbours(3))
    weights = [centers[3] + s for s in around]
    total = weights[0]
    for w in weights[1:]:
        total = total + w
    inverse = 1.0 / total
    outs = []
    for c in range(3):
        acc = None
        for w, f in zip(weights, neighbours(c)):
            acc = w * f if acc is None else acc + w * f
        outs.append(acc * inverse)
    return outs, centers


def inner_kernel(with_surface, with_rows, *refs):
    (low, mid, high, s_low, s_mid, s_high, before, after, s_before, s_after) = refs[:10]
    rest = list(refs[10:])
    surface = rest.pop(0) if with_surface else None
    out = rest.pop(0)
    layer = pl.program_id(0) + 1
    ntiles = mid.shape[2] // 8
    f_refs = {-1: low, 0: mid, 1: high}
    s_refs = {-1: s_low, 0: s_mid, 1: s_high}
    if with_rows:
        first_row, last_row = rest

        @pl.when(layer == 1)
        def _():
            first_row[...] = jnp.zeros_like(first_row)
            last_row[...] = jnp.zeros_like(last_row)

    scale = jnp.where(layer == 1, 1.0, 0.0)

    def load(c, side, t):
        if c == 3:
            return s_refs[side][0, 8 * t : 8 * t + 8, :]
        value = f_refs[side][c, 0, 8 * t : 8 * t + 8, :]
        if with_surface and c == 0 and side == -1:
            value = value + scale * surface[8 * t + 8 : 8 * t + 16, :]
        return value

    def edge(f_ref, s_ref):
        return lambda c: s_ref[3, pl.ds(layer, 1), :] if c == 3 else f_ref[c, pl.ds(layer, 1), :]

    for t in range(ntiles):
        outs, _ = relax_tile(load, edge(before, s_before), edge(after, s_after), t, ntiles)
        for c in range(3):
            out[c, 0, 8 * t : 8 * t + 8, :] = outs[c]
            if with_rows and t == 0:
                first_row[c, pl.ds(layer, 1), :] = outs[c][0:1]
            if with_rows and t == ntiles - 1:
                last_row[c, pl.ds(layer, 1), :] = outs[c][7:8]


def relax_inner(field, stiffness, before, after, s_before, s_after, surface):
    _, layers, rows, width = field.shape
    with_surface = surface is not None
    whole = lambda shape: pl.BlockSpec(shape, lambda i: (0,) * len(shape))
    f_spec = lambda k: pl.BlockSpec((3, 1, rows, width), lambda i: (0, i + k, 0, 0))
    s_spec = lambda k: pl.BlockSpec((1, rows, width), lambda i: (i + k, 0, 0))
    args = [field] * 3 + [stiffness] * 3 + [before, after, s_before, s_after]
    in_specs = [f_spec(k) for k in range(3)] + [s_spec(k) for k in range(3)]
    in_specs += [whole(a.shape) for a in args[6:]]
    out_shape = [jax.ShapeDtypeStruct(field.shape, jnp.float32)]
    out_specs = [f_spec(1)]
    if with_surface:
        args.append(surface)
        in_specs.append(whole(surface.shape))
        out_shape += [jax.ShapeDtypeStruct((3, layers, width), jnp.float32)] * 2
        out_specs += [whole((3, layers, width))] * 2
    return pl.pallas_call(
        lambda *refs: inner_kernel(with_surface, with_surface, *refs),
        name="relax_inner_first" if with_surface else "relax_inner_second",
        grid=(layers - 2,),
        in_specs=in_specs,
        out_specs=out_specs,
        out_shape=out_shape,
        compiler_params=pltpu.CompilerParams(vmem_limit_bytes=VMEM_LIMIT),
    )(*args)


def face_kernel(first_sweep, rows_at, *refs):
    (where_ref, here, inside, s_here, s_inside, low, high, s_low, s_high,
     before, after, s_before, s_after) = refs[:13]
    rest = list(refs[13:])
    surface = rest.pop(0) if first_sweep else None
    rest.pop(0)
    out = rest.pop(0)
    ntiles = here.shape[2] // 8
    on_top = where_ref[1] == 1

    def one(face, outer, s_outer, sends):
        layer = 0 if face == 0 else s_before.shape[1] - 1

        def load(c, side, t):
            at = slice(8 * t, 8 * t + 8)
            if side == 1:
                return s_outer[3, at, :] if c == 3 else outer[c, at, :]
            if side == -1:
                return s_inside[0, at, :] if c == 3 else inside[c, 0, at, :]
            value = s_here[0, at, :] if c == 3 else here[c, 0, at, :]
            if first_sweep and c == 0 and face == 0:
                value = value + surface[8 * t + 8 : 8 * t + 16, :]
            return value

        def edge(f_ref, s_ref, surface_row):
            def get(c):
                if c == 3:
                    return s_ref[3, layer : layer + 1, :]
                if not first_sweep:
                    return f_ref[2 * c + face : 2 * c + face + 1, :]
                value = f_ref[c, layer : layer + 1, :]
                if c == 0 and face == 0:
                    value = value + surface[surface_row : surface_row + 1, :]
                return value
            return get

        for t in range(ntiles):
            outs, centers = relax_tile(
                load, edge(before, s_before, 7), edge(after, s_after, 8 + 8 * ntiles), t, ntiles
            )
            if face == 0:
                outs[0] = jnp.where(on_top, centers[0], outs[0])
            for c in range(3):
                out[c, 0, 8 * t : 8 * t + 8, :] = outs[c]
                if first_sweep:
                    send, first_row, last_row = sends
                    send[c, 8 * t : 8 * t + 8, :] = outs[c]
                    k = 2 * c + face
                    if t == 0:
                        first_row[k : k + 1, :] = outs[c][0:1]
                    if t == ntiles - 1:
                        last_row[k : k + 1, :] = outs[c][7:8]

    step = pl.program_id(0)

    @pl.when(step == 0)
    def _():
        if first_sweep:
            rest[2][6:8, :] = jnp.zeros_like(rest[2][6:8, :])
            rest[3][6:8, :] = jnp.zeros_like(rest[3][6:8, :])
        one(0, low, s_low, (rest[0], rest[2], rest[3]) if first_sweep else None)

    @pl.when(step == 1)
    def _():
        one(1, high, s_high, (rest[1], rest[2], rest[3]) if first_sweep else None)


def relax_faces(position, field, stiffness, low, high, s_low, s_high,
                before, after, s_before, s_after, surface, partial):
    _, layers, rows, width = field.shape
    first_sweep = surface is not None
    whole = lambda shape: pl.BlockSpec(shape, lambda i, *_: (0,) * len(shape))
    f_spec = lambda at: pl.BlockSpec((3, 1, rows, width), lambda i, *_: (0, at(i), 0, 0))
    s_spec = lambda at: pl.BlockSpec((1, rows, width), lambda i, *_: (at(i), 0, 0))
    outermost = lambda i: i * (layers - 1)
    inner = lambda i: 1 + i * (layers - 3)
    args = [field, field, stiffness, stiffness, low, high, s_low, s_high,
            before, after, s_before, s_after]
    in_specs = [f_spec(outermost), f_spec(inner), s_spec(outermost), s_spec(inner)]
    in_specs += [whole(a.shape) for a in args[4:]]
    out_shape = [jax.ShapeDtypeStruct(field.shape, jnp.float32)]
    out_specs = [f_spec(outermost)]
    if first_sweep:
        args.append(surface)
        in_specs.append(whole(surface.shape))
        plane = (3, rows, width)
        out_shape += [jax.ShapeDtypeStruct(plane, jnp.float32)] * 2
        out_shape += [jax.ShapeDtypeStruct((8, width), jnp.float32)] * 2
        out_specs += [whole(plane)] * 2 + [whole((8, width))] * 2
    args.append(partial)
    in_specs.append(pl.BlockSpec(memory_space=pl.ANY))
    return pl.pallas_call(
        lambda *refs: face_kernel(first_sweep, None, *refs),
        name="relax_faces_first" if first_sweep else "relax_faces_second",
        grid_spec=pltpu.PrefetchScalarGridSpec(
            num_scalar_prefetch=1, grid=(2,), in_specs=in_specs, out_specs=out_specs
        ),
        out_shape=out_shape,
        input_output_aliases={len(args): 0},
        compiler_params=pltpu.CompilerParams(vmem_limit_bytes=VMEM_LIMIT),
    )(position, *args)


def per_device(
    displacement,
    stiffness,
    node_list,
    active_count,
    wear_class,
    pressure,
    slip_speed,
    rate_table,
    tile_owner,
    node_cell,
):
    rows, width = displacement.shape[2:]
    position = jnp.stack(
        [lax.axis_index("tan"), (lax.axis_index("depth") == 0).astype(jnp.int32)]
    ).astype(jnp.int32)

    def joined(cut):
        return jnp.concatenate([cut(displacement), cut(stiffness[None])], axis=0)

    low, high = shift_both(joined(lambda a: a[:, -1]), joined(lambda a: a[:, 0]), "depth")
    before, after = shift_both(
        joined(lambda a: a[:, :, -1]), joined(lambda a: a[:, :, 0]), "tan"
    )
    wear = archard(wear_class, pressure, slip_speed, rate_table)
    wear = lax.all_gather(wear, "tan", axis=0, tiled=True)
    surface = paint(position, tile_owner, active_count, wear, node_list,
                    node_cell.reshape(-1, 128), rows, width)

    first, row_first, row_last = relax_inner(
        displacement, stiffness, before, after, before, after, surface
    )
    before_mid, after_mid = shift_both(row_last, row_first, "tan")
    first, send_low, send_high, edge_first, edge_last = relax_faces(
        position, displacement, stiffness, low, high, low, high,
        before, after, before, after, surface, first,
    )
    low_2, high_2 = shift_both(send_high, send_low, "depth")
    before_face, after_face = shift_both(edge_last, edge_first, "tan")
    result = relax_inner(first, stiffness, before_mid, after_mid, before, after, None)[0]
    return relax_faces(
        position, first, stiffness, low_2, high_2, low, high,
        before_face, after_face, before, after, None, result,
    )[0]


def solution(mesh):
    in_specs = (
        P(None, "depth", "tan", None),
        P("depth", "tan", None),
        P(),
        P(),
        P("tan", None),
        P("tan", None),
        P("tan", None),
        P(),
        P(),
        P(),
    )
    out_specs = P(None, "depth", "tan", None)
    return jax.shard_map(
        per_device, mesh=mesh, in_specs=in_specs, out_specs=out_specs, check_vma=False
    )
```

time: 401 us -> 161 us (0.40)
  the two profiles are of different devices: /device:TPU:15 before, /device:TPU:33 now
where the time goes in v1:
time: 161 us
  starting transfers between devices  52.9 us (33%)
  blocking collectives  52.8 us (33%)
  Pallas kernels  43 us (27%)
  local copies, waits for them, and re-layouts  9.39 us (6%)
  other arithmetic  2.41 us (1%)
    ppermute x10, starting transfers between devices, shift_both(): return (lax.ppermute(last, axis, up), lax.ppermute(first, axis, down))  52.9 us
    all_gather x1, blocking collectives, per_device(): wear = lax.all_gather(wear, 'tan', axis=0, tiled=True)  52.8 us
    pallas_call x2, Pallas kernels, relax_inner(): pl.pallas_call(lambda *refs: inner_kernel(with_surface, with_surface, *re...  20.3 us
    pallas_call x2, Pallas kernels, relax_faces(): pl.pallas_call(lambda *refs: face_kernel(first_sweep, None, *refs), name=...  11.9 us
    pallas_call x1, Pallas kernels, paint(): pl.pallas_call(paint_kernel, name='paint_band', grid_spec=pltpu.PrefetchS...  10.9 us
    unnamed x23, local copies, waits for them, and re-layouts  5.22 us
  transfers between devices with their start and end apart: 10, of which 0 were waited for; matrix products, arithmetic and copies ran while one was open for 2% of the time, Pallas kernels for 19%

profile of v1, /device:TPU:33, one launch (start us, length us, event | category | flops | bytes accessed | tf_op | source)
XLA Modules:
  0.0 160.9 jit_solution(7523402200788549713)
XLA Ops:
  0.0 1.5 slice_bitcast_fusion
  1.5 0.0 copy-start.6
  1.5 0.0 copy-start.9
  1.5 0.0 copy-start.7
  1.5 0.0 copy-start.8
  1.5 0.0 copy-start.3
  1.5 0.0 copy-start.4
  1.6 0.0 copy-start.5
  1.6 2.9 %copy.34 = f32[8,32,2048]{2,0,1:T(8,128)S(1)} copy(f32[8,32,2048]{2,1,0:T(8,128)} %refs_4_.7) | data formatting | bytes 4194304 | tf_op args[1]
  4.4 0.3 slice_bitcast_fusion.2
  4.8 0.1 copy.22
  4.9 0.0 copy-start
  4.9 1.0 pad_maximum_fusion
  5.9 5.6 %collective-permute-start = (f32[4,32,2048]{2,1,0:T(8,128)}, f32[4,32,2048]{2,1,0:T(8,128)}, u32[]{:S(2)}, u32[]{:S(2)}) collective-permute-start(f32[4,32,2048]{2,1,0:T(8,128)} %pad_maximum_fusion), channel_id=1, source_target_pairs={{0,16},{16,32},{32,48},{48,64},{64,80},{80,96},{96,112},{1,17},{17... | collective-permute-start | bytes 3145736 | tf_op jit(solution)/shard_map/ppermute | solution.py:18
  11.5 0.1 copy.24
  11.6 1.1 pad_maximum_fusion.1
  12.7 1.3 collective-permute-start.1
  14.0 2.2 %fusion = (f32[3,8,1,2048]{3,2,1,0:T(1,128)S(1)}, f32[3,8,1,2048]{3,2,1,0:T(1,128)S(1)}) fusion(f32[3,8,32,2048]{3,2,1,0:T(8,128)} %refs_2_.3), kind=kLoop, calls=%fused_computation.17 | loop fusion | bytes 786432 | tf_op jit(solution)/shard_map/slice | solution.py:393
  16.2 0.1 copy.36
  16.3 4.4 %collective-permute-start.2 = (f32[4,8,2048]{2,1,0:T(8,128)S(1)}, f32[4,8,2048]{2,1,0:T(8,128)S(1)}, u32[]{:S(2)}, u32[]{:S(2)}) collective-permute-start(f32[4,8,2048]{2,1,0:T(8,128)S(1)} %pad_maximum_fusion.2), channel_id=1, source_target_pairs={{0,1},{1,2},{2,3},{3,4},{4,5},{5,6},{6,7},{7,8},{8,9},{9,10},{10,1... | collective-permute-start | bytes 786440 | tf_op jit(solution)/shard_map/ppermute | solution.py:18
  20.7 0.1 copy.35
  20.8 1.9 %collective-permute-start.3 = (f32[4,8,2048]{2,1,0:T(8,128)S(1)}, f32[4,8,2048]{2,1,0:T(8,128)S(1)}, u32[]{:S(2)}, u32[]{:S(2)}) collective-permute-start(f32[4,8,2048]{2,1,0:T(8,128)S(1)} %pad_maximum_fusion.3), channel_id=1, source_target_pairs={{1,0},{2,1},{3,2},{4,3},{5,4},{6,5},{7,6},{8,7},{9,8},{10,9},{11,1... | collective-permute-start | bytes 786440 | tf_op jit(solution)/shard_map/ppermute | solution.py:18
  22.7 0.1 select_reduce_fusion
  22.9 0.1 pad_add_fusion.where_ref.refs_0_
  23.0 52.8 %all_gather.3.wear_ref = f32[512,128]{1,0:T(8,128)S(1)} all-gather(f32[32,128]{1,0:T(8,128)S(1)} %add_divide_fusion), channel_id=1, replica_groups=mesh['depth'=8,'tan'=16] {'tan'}, dimensions={0}, use_global_device_ids=true | all-gather | bytes 278528 | tf_op jit(solution)/shard_map/all_gather | solution.py:396
  75.8 0.0 copy-start.2
  75.8 2.2 %copy-done.2 = s32[1048576]{0:T(1024)S(1)} copy-done((s32[1048576]{0:T(1024)S(1)}, s32[1048576]{0:T(1024)}, u32[]{:S(2)}) %copy-start.2) | copy-done | bytes 4194328
  77.9 10.9 %paint_band.1.refs_10_.refs_13_ = f32[48,2048]{1,0:T(8,128)S(1)} custom-call(s32[2]{0:T(128)S(1)} %pad_add_fusion.where_ref.refs_0_, s32[512]{0:T(512)S(1)} %copy-done.4, s32[512]{0:T(512)S(1)} %copy-done.5, f32[512,128]{1,0:T(8,128)S(1)} %all_gather.3.wear_ref, s32[512,128]{1,0:T(8,128)S(1)} %copy-done.3, s32[8192,128]{1,0:T(8,128)S(1)} %bitcast.28), custom_call_target="tpu_custom_call" | custom-call | tf_op jit(solution)/shard_map/paint_band/pallas_call | solution.py:148
  88.8 0.0 collective-permute-done.2.refs_6_.refs_8_.refs_9_.refs_11_
  88.8 0.0 collective-permute-done.3.refs_7_.refs_9_.refs_10_.refs_12_
  88.8 10.2 %relax_inner_first.1 = (f32[3,8,32,2048]{3,2,1,0:T(8,128)}, f32[3,8,2048]{2,1,0:T(8,128)S(1)}, f32[3,8,2048]{2,1,0:T(8,128)S(1)}) custom-call(f32[3,8,32,2048]{3,2,1,0:T(8,128)} %refs_2_.3, f32[3,8,32,2048]{3,2,1,0:T(8,128)} %refs_2_.3, f32[3,8,32,2048]{3,2,1,0:T(8,128)} %refs_2_.3, f32[8,32,2048]{2,1,0:T(8,128)S(1)} %copy-done, f32[8,32,2048]{2,1,0:T(8,128)S(1)} %copy-done, ...), custom_call_target="tpu_custom_call" | custom-call | tf_op jit(solution)/shard_map/relax_inner_first/pallas_call | solution.py:257
  99.0 0.0 collective-permute-done.refs_5_.refs_7_
  99.0 0.0 collective-permute-done.1.refs_6_.refs_8_
  99.1 0.0 copy-start.1
  99.1 6.6 %relax_faces_first.1 = (f32[3,8,32,2048]{3,2,1,0:T(8,128)}, f32[3,32,2048]{2,1,0:T(8,128)S(1)}, f32[3,32,2048]{2,1,0:T(8,128)S(1)}, f32[8,2048]{1,0:T(8,128)S(1)}, f32[8,2048]{1,0:T(8,128)S(1)}) custom-call(s32[2]{0:T(128)S(1)} %pad_add_fusion.where_ref.refs_0_, f32[3,8,32,2048]{3,2,1,0:T(8,128)} %refs_2_.3, ...), custom_call_target="tpu_custom_call", output_to_operand_aliasing={{0}: (14, {})} | custom-call | tf_op jit(solution)/shard_map/relax_faces_first/pallas_call | solution.py:359
  105.7 1.3 collective-permute-start.4
  107.0 1.3 collective-permute-start.5
  108.3 1.9 %collective-permute-start.8 = (f32[3,8,2048]{2,1,0:T(8,128)S(1)}, f32[3,8,2048]{2,1,0:T(8,128)S(1)}, u32[]{:S(2)}, u32[]{:S(2)}) collective-permute-start(f32[3,8,2048]{2,1,0:T(8,128)S(1)} %get-tuple-element.19), channel_id=1, source_target_pairs={{0,1},{1,2},{2,3},{3,4},{4,5},{5,6},{6,7},{7,8},{8,9},{9,10},{10,1... | collective-permute-start | bytes 589832 | tf_op jit(solution)/shard_map/ppermute | solution.py:18
  110.2 2.4 %collective-permute-start.9 = (f32[3,8,2048]{2,1,0:T(8,128)S(1)}, f32[3,8,2048]{2,1,0:T(8,128)S(1)}, u32[]{:S(2)}, u32[]{:S(2)}) collective-permute-start(f32[3,8,2048]{2,1,0:T(8,128)S(1)} %get-tuple-element.20), channel_id=1, source_target_pairs={{1,0},{2,1},{3,2},{4,3},{5,4},{6,5},{7,6},{8,7},{9,8},{10,9},{11,1... | collective-permute-start | bytes 589832 | tf_op jit(solution)/shard_map/ppermute | solution.py:18
  112.6 4.1 %collective-permute-start.6 = (f32[8,2048]{1,0:T(8,128)S(1)}, f32[8,2048]{1,0:T(8,128)S(1)}, u32[]{:S(2)}, u32[]{:S(2)}) collective-permute-start(f32[8,2048]{1,0:T(8,128)S(1)} %get-tuple-element.17), channel_id=1, source_target_pairs={{0,1},{1,2},{2,3},{3,4},{4,5},{5,6},{6,7},{7,8},{8,9},{9,10},{10,1... | collective-permute-start | bytes 196616 | tf_op jit(solution)/shard_map/ppermute | solution.py:18
  116.7 0.0 collective-permute-done.8.refs_6_
  116.7 28.7 %collective-permute-start.7 = (f32[8,2048]{1,0:T(8,128)S(1)}, f32[8,2048]{1,0:T(8,128)S(1)}, u32[]{:S(2)}, u32[]{:S(2)}) collective-permute-start(f32[8,2048]{1,0:T(8,128)S(1)} %get-tuple-element.18), channel_id=1, source_target_pairs={{1,0},{2,1},{3,2},{4,3},{5,4},{6,5},{7,6},{8,7},{9,8},{10,9},{11,1... | collective-permute-start | bytes 196616 | tf_op jit(solution)/shard_map/ppermute | solution.py:18
  145.5 0.0 collective-permute-done.9.refs_7_
  145.5 10.1 %relax_inner_second.1.refs_13_ = f32[3,8,32,2048]{3,2,1,0:T(8,128)} custom-call(f32[3,8,32,2048]{3,2,1,0:T(8,128)} %get-tuple-element.14.refs_0_.refs_1_.refs_2_, f32[3,8,32,2048]{3,2,1,0:T(8,128)} %get-tuple-element.14.refs_0_.refs_1_.refs_2_, f32[3,8,32,2048]{3,2,1,0:T(8,128)} %get-tuple-element.14.refs_0_.refs_1_.refs_2_, f32[8,32,2048]{2,1,0:T(8,128)S(1)} %copy-done.1, ...), custom_call_target="tpu_custom_call" | custom-call | tf_op jit(solution)/shard_map/relax_inner_second/pallas_call | solution.py:257
  155.6 0.0 collective-permute-done.6.refs_9_
  155.6 0.0 collective-permute-done.7.refs_10_
  155.6 0.0 collective-permute-done.4.refs_5_
  155.6 5.3 %relax_faces_second.1 = f32[3,8,32,2048]{3,2,1,0:T(8,128)} custom-call(s32[2]{0:T(128)S(1)} %pad_add_fusion.where_ref.refs_0_, f32[3,8,32,2048]{3,2,1,0:T(8,128)} %get-tuple-element.14.refs_0_.refs_1_.refs_2_, f32[3,8,32,2048]{3,2,1,0:T(8,128)} %get-tuple-element.14.refs_0_.refs_1_.refs_2_, f32[8,32,2048]{2,1,0:T(8,128)} %refs_4_.7, ...), custom_call_target="tpu_custom_call", output_to_operand_aliasing={{}: (13, {})} | custom-call | tf_op jit(solution)/shard_map/relax_faces_second/pallas_call | solution.py:359
  (14 shorter events, 0.1 us)
Async XLA Ops:
  1.5 21.2 %copy-start.6 = (s32[32,128]{1,0:T(8,128)S(1)}, s32[32,128]{1,0:T(8,128)}, u32[]{:S(2)}) copy-start(s32[32,128]{1,0:T(8,128)} %param.14) | copy-start | bytes 49156
  1.5 21.2 %copy-start.9 = (f32[8]{0:T(128)S(1)}, f32[8]{0:T(128)}, u32[]{:S(2)}) copy-start(f32[8]{0:T(128)} %param.17) | copy-start | bytes 100
  1.5 21.4 %copy-start.7 = (f32[32,128]{1,0:T(8,128)S(1)}, f32[32,128]{1,0:T(8,128)}, u32[]{:S(2)}) copy-start(f32[32,128]{1,0:T(8,128)} %param.15) | copy-start | bytes 49156
  1.5 21.4 %copy-start.8 = (f32[32,128]{1,0:T(8,128)S(1)}, f32[32,128]{1,0:T(8,128)}, u32[]{:S(2)}) copy-start(f32[32,128]{1,0:T(8,128)} %param.16) | copy-start | bytes 49156
  1.5 74.2 %copy-start.3 = (s32[512,128]{1,0:T(8,128)S(1)}, s32[512,128]{1,0:T(8,128)}, u32[]{:S(2)}) copy-start(s32[512,128]{1,0:T(8,128)} %list_ref.1) | copy-start | bytes 786436
  1.5 74.2 %copy-start.4 = (s32[512]{0:T(512)S(1)}, s32[512]{0:T(512)}, u32[]{:S(2)}) copy-start(s32[512]{0:T(512)} %owner_ref.1) | copy-start | bytes 6148
  1.6 74.2 %copy-start.5 = (s32[512]{0:T(512)S(1)}, s32[512]{0:T(512)}, u32[]{:S(2)}) copy-start(s32[512]{0:T(512)} %count_ref.1) | copy-start | bytes 6148
  4.9 84.0 %copy-start = (f32[8,32,2048]{2,1,0:T(8,128)S(1)}, f32[8,32,2048]{2,1,0:T(8,128)}, u32[]{:S(2)}) copy-start(f32[8,32,2048]{2,1,0:T(8,128)} %refs_4_.7) | copy-start | bytes 6291460
  5.9 93.1 %collective-permute-start = (f32[4,32,2048]{2,1,0:T(8,128)}, f32[4,32,2048]{2,1,0:T(8,128)}, u32[]{:S(2)}, u32[]{:S(2)}) collective-permute-start(f32[4,32,2048]{2,1,0:T(8,128)} %pad_maximum_fusion), channel_id=1, source_target_pairs={{0,16},{16,32},{32,48},{48,64},{64,80},{80,96},{96,112},{1,17},{17... | collective-permute-start | bytes 3145736 | tf_op jit(solution)/shard_map/ppermute | solution.py:18
  12.7 86.4 %collective-permute-start.1 = (f32[4,32,2048]{2,1,0:T(8,128)}, f32[4,32,2048]{2,1,0:T(8,128)}, u32[]{:S(2)}, u32[]{:S(2)}) collective-permute-start(f32[4,32,2048]{2,1,0:T(8,128)} %pad_maximum_fusion.1), channel_id=1, source_target_pairs={{16,0},{32,16},{48,32},{64,48},{80,64},{96,80},{112,96},{17,1},{33... | collective-permute-start | bytes 3145736 | tf_op jit(solution)/shard_map/ppermute | solution.py:18
  16.3 72.5 %collective-permute-start.2 = (f32[4,8,2048]{2,1,0:T(8,128)S(1)}, f32[4,8,2048]{2,1,0:T(8,128)S(1)}, u32[]{:S(2)}, u32[]{:S(2)}) collective-permute-start(f32[4,8,2048]{2,1,0:T(8,128)S(1)} %pad_maximum_fusion.2), channel_id=1, source_target_pairs={{0,1},{1,2},{2,3},{3,4},{4,5},{5,6},{6,7},{7,8},{8,9},{9,10},{10,1... | collective-permute-start | bytes 786440 | tf_op jit(solution)/shard_map/ppermute | solution.py:18
  20.8 68.0 %collective-permute-start.3 = (f32[4,8,2048]{2,1,0:T(8,128)S(1)}, f32[4,8,2048]{2,1,0:T(8,128)S(1)}, u32[]{:S(2)}, u32[]{:S(2)}) collective-permute-start(f32[4,8,2048]{2,1,0:T(8,128)S(1)} %pad_maximum_fusion.3), channel_id=1, source_target_pairs={{1,0},{2,1},{3,2},{4,3},{5,4},{6,5},{7,6},{8,7},{9,8},{10,9},{11,1... | collective-permute-start | bytes 786440 | tf_op jit(solution)/shard_map/ppermute | solution.py:18
  75.8 2.2 %copy-start.2 = (s32[1048576]{0:T(1024)S(1)}, s32[1048576]{0:T(1024)}, u32[]{:S(2)}) copy-start(s32[1048576]{0:T(1024)} %param.19) | copy-start | bytes 12582916
  99.1 46.4 %copy-start.1 = (f32[8,32,2048]{2,1,0:T(8,128)S(1)}, f32[8,32,2048]{2,1,0:T(8,128)}, u32[]{:S(2)}) copy-start(f32[8,32,2048]{2,1,0:T(8,128)} %refs_4_.7) | copy-start | bytes 6291460
  105.7 49.9 %collective-permute-start.4 = (f32[3,32,2048]{2,1,0:T(8,128)S(1)}, f32[3,32,2048]{2,1,0:T(8,128)S(1)}, u32[]{:S(2)}, u32[]{:S(2)}) collective-permute-start(f32[3,32,2048]{2,1,0:T(8,128)S(1)} %get-tuple-element.15), channel_id=1, source_target_pairs={{0,16},{16,32},{32,48},{48,64},{64,80},{80,96},{96,112},{1,17},{17... | collective-permute-start | bytes 2359304 | tf_op jit(solution)/shard_map/ppermute | solution.py:18
  107.0 48.6 %collective-permute-start.5 = (f32[3,32,2048]{2,1,0:T(8,128)S(1)}, f32[3,32,2048]{2,1,0:T(8,128)S(1)}, u32[]{:S(2)}, u32[]{:S(2)}) collective-permute-start(f32[3,32,2048]{2,1,0:T(8,128)S(1)} %get-tuple-element.16), channel_id=1, source_target_pairs={{16,0},{32,16},{48,32},{64,48},{80,64},{96,80},{112,96},{17,1},{33... | collective-permute-start | bytes 2359304 | tf_op jit(solution)/shard_map/ppermute | solution.py:18
  108.3 8.4 %collective-permute-start.8 = (f32[3,8,2048]{2,1,0:T(8,128)S(1)}, f32[3,8,2048]{2,1,0:T(8,128)S(1)}, u32[]{:S(2)}, u32[]{:S(2)}) collective-permute-start(f32[3,8,2048]{2,1,0:T(8,128)S(1)} %get-tuple-element.19), channel_id=1, source_target_pairs={{0,1},{1,2},{2,3},{3,4},{4,5},{5,6},{6,7},{7,8},{8,9},{9,10},{10,1... | collective-permute-start | bytes 589832 | tf_op jit(solution)/shard_map/ppermute | solution.py:18
  110.2 35.2 %collective-permute-start.9 = (f32[3,8,2048]{2,1,0:T(8,128)S(1)}, f32[3,8,2048]{2,1,0:T(8,128)S(1)}, u32[]{:S(2)}, u32[]{:S(2)}) collective-permute-start(f32[3,8,2048]{2,1,0:T(8,128)S(1)} %get-tuple-element.20), channel_id=1, source_target_pairs={{1,0},{2,1},{3,2},{4,3},{5,4},{6,5},{7,6},{8,7},{9,8},{10,9},{11,1... | collective-permute-start | bytes 589832 | tf_op jit(solution)/shard_map/ppermute | solution.py:18
  112.6 42.9 %collective-permute-start.6 = (f32[8,2048]{1,0:T(8,128)S(1)}, f32[8,2048]{1,0:T(8,128)S(1)}, u32[]{:S(2)}, u32[]{:S(2)}) collective-permute-start(f32[8,2048]{1,0:T(8,128)S(1)} %get-tuple-element.17), channel_id=1, source_target_pairs={{0,1},{1,2},{2,3},{3,4},{4,5},{5,6},{6,7},{7,8},{8,9},{9,10},{10,1... | collective-permute-start | bytes 196616 | tf_op jit(solution)/shard_map/ppermute | solution.py:18
  116.7 38.9 %collective-permute-start.7 = (f32[8,2048]{1,0:T(8,128)S(1)}, f32[8,2048]{1,0:T(8,128)S(1)}, u32[]{:S(2)}, u32[]{:S(2)}) collective-permute-start(f32[8,2048]{1,0:T(8,128)S(1)} %get-tuple-element.18), channel_id=1, source_target_pairs={{1,0},{2,1},{3,2},{4,3},{5,4},{6,5},{7,6},{8,7},{9,8},{10,9},{11,1... | collective-permute-start | bytes 196616 | tf_op jit(solution)/shard_map/ppermute | solution.py:18

commit v2 on v1

v2 whole, which is shorter than its diff:
```python
import functools

import jax
import jax.numpy as jnp
from jax import lax
from jax.experimental import pallas as pl
from jax.experimental.pallas import tpu as pltpu
from jax.sharding import PartitionSpec as P

wear_step = 0.6
hardness = 4.0
GROUP = 8
VMEM_LIMIT = 48 * 1024 * 1024


def shift_both(last, first, axis):
    size = lax.axis_size(axis)
    up = [(i, i + 1) for i in range(size - 1)]
    down = [(j, i) for i, j in up]
    return lax.ppermute(last, axis, up), lax.ppermute(first, axis, down)


def wear_kernel(rates_ref, class_ref, contact_ref, sliding_ref, wear_ref):
    ids = class_ref[...]
    rate = jnp.zeros(ids.shape, jnp.float32)
    for k in range(rates_ref.shape[0]):
        rate = jnp.where(ids == k, rates_ref[k], rate)
    product = contact_ref[...] * sliding_ref[...]
    wear_ref[...] = wear_step * rate * product / (1.0 + product / hardness)


def archard(class_ids, contact, sliding, rates):
    near = pl.BlockSpec(memory_space=pltpu.VMEM)
    return pl.pallas_call(
        wear_kernel,
        name="archard",
        in_specs=[pl.BlockSpec(memory_space=pltpu.SMEM), near, near, near],
        out_specs=near,
        out_shape=jax.ShapeDtypeStruct(contact.shape, jnp.float32),
    )(rates, class_ids, contact, sliding)


def pack_kernel(field_ref, stiff_ref, wear_ref, first_ref, last_ref, sems):
    layers = field_ref.shape[1]
    copies = []
    for k, (to, layer) in enumerate(((last_ref, layers - 1), (first_ref, 0))):
        copies.append(pltpu.make_async_copy(
            field_ref.at[:, layer], to.at[pl.ds(0, 3)], sems.at[2 * k]))
        copies.append(pltpu.make_async_copy(
            stiff_ref.at[pl.ds(layer, 1)], to.at[pl.ds(3, 1)], sems.at[2 * k + 1]))
    for copy in copies:
        copy.start()
    for copy in copies:
        copy.wait()


def pack_faces(field, stiffness, wear):
    _, _, rows, width = field.shape
    face = jax.ShapeDtypeStruct((4, rows, width), jnp.float32)
    far = pl.BlockSpec(memory_space=pl.ANY)
    return pl.pallas_call(
        pack_kernel,
        name="pack_faces",
        in_specs=[far, far, far],
        out_specs=[far, far],
        out_shape=[face, face],
        scratch_shapes=[pltpu.SemaphoreType.DMA((4,))],
    )(field, stiffness, wear)


def rows_kernel(f_top, s_top, f_bottom, s_bottom, first_ref, last_ref):
    for l in range(f_top.shape[1]):
        first_ref[3, l : l + 1, :] = s_top[l, 0:1, :]
        last_ref[3, l : l + 1, :] = s_bottom[l, 7:8, :]
        for c in range(3):
            first_ref[c, l : l + 1, :] = f_top[c, l, 0:1, :]
            last_ref[c, l : l + 1, :] = f_bottom[c, l, 7:8, :]


def pack_rows(field, stiffness):
    _, layers, rows, width = field.shape
    bottom = rows // 8 - 1
    f_spec = lambda at: pl.BlockSpec((3, layers, 8, width), lambda i: (0, 0, at, 0))
    s_spec = lambda at: pl.BlockSpec((layers, 8, width), lambda i: (0, at, 0))
    out = jax.ShapeDtypeStruct((4, layers, width), jnp.float32)
    out_spec = pl.BlockSpec((4, layers, width), lambda i: (0, 0, 0))
    return pl.pallas_call(
        rows_kernel,
        name="pack_rows",
        grid=(1,),
        in_specs=[f_spec(0), s_spec(0), f_spec(bottom), s_spec(bottom)],
        out_specs=[out_spec, out_spec],
        out_shape=[out, out],
        compiler_params=pltpu.CompilerParams(vmem_limit_bytes=VMEM_LIMIT),
    )(field, stiffness, field, stiffness)


def swap_halves(wear):
    size = lax.axis_size("tan")
    return lax.ppermute(wear, "tan", [(i, i ^ 2) for i in range(size)])


def gather_wear(wear, other):
    size = lax.axis_size("tan")
    both = jnp.concatenate([wear, other], axis=0)
    groups = [[i for i in range(size) if (i // 2) % 2 == half] for half in range(2)]
    return lax.all_gather(both, "tan", axis=0, axis_index_groups=groups, tiled=True)


def three_parts(value):
    high = value.astype(jnp.bfloat16).astype(jnp.float32)
    rest = value - high
    middle = rest.astype(jnp.bfloat16).astype(jnp.float32)
    return high, middle, rest - middle


def paint_kernel(
    shard_tiles, where_ref, owner_ref, count_ref, wear_ref, list_ref, table_ref, out_ref,
    own_ref, side_ref, acc_ref, edge_ref,
):
    slots = wear_ref.shape[1]
    ntile = wear_ref.shape[0]
    rows_table = table_ref.shape[0] // ntile
    tile_len = rows_table * 128
    width = out_ref.shape[1]
    rows = out_ref.shape[0] - 16
    me = where_ref[0]
    on_top = where_ref[1]
    out_ref[...] = jnp.zeros_like(out_ref)

    @pl.when(on_top == 1)
    def _():
        acc_ref[...] = jnp.zeros_like(acc_ref)
        edge_ref[...] = jnp.zeros_like(edge_ref)

        def collect(i, carry):
            n_own, n_side = carry
            offset = owner_ref[i] - me
            own_ref[n_own] = i
            side_ref[n_side] = i
            n_own = n_own + jnp.where(offset == 0, 1, 0)
            n_side = n_side + jnp.where(offset * offset == 1, 1, 0)
            return n_own, n_side

        n_own, n_side = lax.fori_loop(
            0, ntile, collect, (jnp.int32(0), jnp.int32(0)), unroll=8
        )

        lane = lax.broadcasted_iota(jnp.int32, (1, slots), 1)
        table_row = lax.broadcasted_iota(jnp.int32, (rows_table, slots), 0)
        block = width // 8
        fine = lax.broadcasted_iota(jnp.int32, (block, slots), 0)
        coarse = lax.broadcasted_iota(jnp.int32, (rows * 8, slots), 0)
        fine_edge = lax.broadcasted_iota(jnp.int32, (128, slots), 0)
        edge_blocks = width // 128
        coarse_edge = lax.broadcasted_iota(jnp.int32, (2 * edge_blocks, slots), 0)

        def entry(tiles_ref, position, total):
            i = tiles_ref[jnp.minimum(position, total - 1)]
            live = jnp.where(position < total, count_ref[i], 0)
            local = list_ref[pl.ds(i, 1), :] - i * tile_len
            table = table_ref[pl.ds(pl.multiple_of(i * rows_table, 8), rows_table), :]
            column = jnp.broadcast_to(local & 127, (rows_table, slots))
            picked = jnp.take_along_axis(table, column, axis=1)
            cell = jnp.sum(
                jnp.where(table_row == (local >> 7), picked, 0), axis=0, keepdims=True
            )
            shard = i // shard_tiles
            half = jnp.where((shard // 2) % 2 == (me // 2) % 2, 0, 1)
            place = (shard // 4) * 4 + (shard % 2) * 2 + half
            at = place * shard_tiles + i % shard_tiles
            wear = jnp.where(lane < live, wear_ref[pl.ds(at, 1), :], 0.0)
            return i, cell, wear

        def one_hot(mask, value):
            return jnp.where(mask, value, 0.0).astype(jnp.bfloat16)

        def add(into_ref, parts, hot):
            total = into_ref[...]
            for part in parts:
                total = total + lax.dot_general(
                    jnp.concatenate(part, axis=1), hot, (((1,), (1,)), ((), ())),
                    preferred_element_type=jnp.float32,
                )
            into_ref[...] = total

        def own_group(g, carry):
            parts = ([], [], [])
            hots = []
            for j in range(GROUP):
                _, cell, wear = entry(own_ref, g * GROUP + j, n_own)
                col = cell % width
                a_index = (col // block) * rows + cell // width
                hots.append(one_hot(fine == col % block, 1.0))
                mask = coarse == a_index
                for part, value in zip(parts, three_parts(wear)):
                    part.append(one_hot(mask, value))
            add(acc_ref, parts, jnp.concatenate(hots, axis=1))
            return carry

        def side_group(g, carry):
            parts = ([], [], [])
            hots = []
            for j in range(GROUP):
                i, cell, wear = entry(side_ref, g * GROUP + j, n_side)
                below = owner_ref[i] > me
                col = cell % width
                wanted = jnp.where(below, 0, rows - 1)
                shift = jnp.where(below, edge_blocks, 0)
                a_index = jnp.where(cell // width == wanted, col // 128 + shift, -1)
                hots.append(one_hot(fine_edge == col % 128, 1.0))
                mask = coarse_edge == a_index
                for part, value in zip(parts, three_parts(wear)):
                    part.append(one_hot(mask, value))
            add(edge_ref, parts, jnp.concatenate(hots, axis=1))
            return carry

        lax.fori_loop(0, (n_own + GROUP - 1) // GROUP, own_group, 0)
        lax.fori_loop(0, (n_side + GROUP - 1) // GROUP, side_group, 0)
        for j in range(8):
            out_ref[8 : 8 + rows, j * block : (j + 1) * block] = acc_ref[
                j * rows : (j + 1) * rows, :
            ]
        for j in range(edge_blocks):
            out_ref[7:8, j * 128 : (j + 1) * 128] = edge_ref[j : j + 1, :]
            out_ref[8 + rows : 9 + rows, j * 128 : (j + 1) * 128] = edge_ref[
                edge_blocks + j : edge_blocks + j + 1, :
            ]


def paint(position, owner, counts, wear, lists, table, rows, width, shard_tiles):
    ntile, slots = lists.shape
    whole = lambda shape: pl.BlockSpec(shape, lambda i, *_: (0,) * len(shape))
    return pl.pallas_call(
        functools.partial(paint_kernel, shard_tiles),
        name="paint_band",
        grid_spec=pltpu.PrefetchScalarGridSpec(
            num_scalar_prefetch=3,
            grid=(1,),
            in_specs=[whole(wear.shape), whole(lists.shape), whole(table.shape)],
            out_specs=whole((rows + 16, width)),
            scratch_shapes=[
                pltpu.SMEM((ntile + 1,), jnp.int32),
                pltpu.SMEM((ntile + 1,), jnp.int32),
                pltpu.VMEM((rows * 8, width // 8), jnp.float32),
                pltpu.VMEM((2 * width // 128, 128), jnp.float32),
            ],
        ),
        out_shape=jax.ShapeDtypeStruct((rows + 16, width), jnp.float32),
        compiler_params=pltpu.CompilerParams(vmem_limit_bytes=VMEM_LIMIT),
    )(position, owner, counts, wear, lists, table)


def relax_tile(load, row_above, row_below):
    row = lax.broadcasted_iota(jnp.int32, (8, 1), 0)
    centers = {}

    def neighbours(c):
        here = load(c, 0)
        centers[c] = here
        width = here.shape[1]
        lane = lax.broadcasted_iota(jnp.int32, here.shape, 1)
        yield load(c, 1)
        yield load(c, -1)
        yield jnp.where(row == 7, row_below(c), pltpu.roll(here, 7, 0))
        yield jnp.where(row == 0, row_above(c), pltpu.roll(here, 1, 0))
        yield jnp.where(lane == width - 1, 0.0, pltpu.roll(here, width - 1, 1))
        yield jnp.where(lane == 0, 0.0, pltpu.roll(here, 1, 1))

    around = list(neighbours(3))
    weights = [centers[3] + s for s in around]
    total = weights[0]
    for w in weights[1:]:
        total = total + w
    inverse = 1.0 / total
    outs = []
    for c in range(3):
        acc = None
        for w, f in zip(weights, neighbours(c)):
            acc = w * f if acc is None else acc + w * f
        outs.append(acc * inverse)
    return outs, centers


def inner_kernel(first_sweep, *refs):
    (low, mid, high, s_low, s_mid, s_high, before, after, s_before, s_after) = refs[:10]
    rest = list(refs[10:])
    surface = rest.pop(0) if first_sweep else None
    out = rest.pop(0)
    layer = pl.program_id(0) + 1
    ntiles = mid.shape[2] // 8
    f_refs = {-1: low, 0: mid, 1: high}
    s_refs = {-1: s_low, 0: s_mid, 1: s_high}
    if first_sweep:
        first_row, last_row = rest

        @pl.when(layer == 1)
        def _():
            first_row[...] = jnp.zeros_like(first_row)
            last_row[...] = jnp.zeros_like(last_row)

    scale = jnp.where(layer == 1, 1.0, 0.0)

    for t in range(ntiles):

        def load(c, side):
            if c == 3:
                return s_refs[side][0, 8 * t : 8 * t + 8, :]
            value = f_refs[side][c, 0, 8 * t : 8 * t + 8, :]
            if first_sweep and c == 0 and side == -1:
                value = value + scale * surface[8 * t + 8 : 8 * t + 16, :]
            return value

        def beside(inside, at, f_edge, s_edge):
            def get(c):
                if inside:
                    return s_mid[0, at : at + 1, :] if c == 3 else mid[c, 0, at : at + 1, :]
                edge = s_edge.at[0] if c == 3 else f_edge.at[c]
                return edge[pl.ds(layer, 1), :]
            return get

        outs, _ = relax_tile(
            load,
            beside(t > 0, 8 * t - 1, before, s_before),
            beside(t < ntiles - 1, 8 * t + 8, after, s_after),
        )
        for c in range(3):
            out[c, 0, 8 * t : 8 * t + 8, :] = outs[c]
            if first_sweep and t == 0:
                first_row[c, pl.ds(layer, 1), :] = outs[c][0:1]
            if first_sweep and t == ntiles - 1:
                last_row[c, pl.ds(layer, 1), :] = outs[c][7:8]


def relax_inner(field, stiffness, before, after, s_before, s_after, surface):
    _, layers, rows, width = field.shape
    first_sweep = surface is not None
    whole = lambda shape: pl.BlockSpec(shape, lambda i: (0,) * len(shape))
    f_spec = lambda k: pl.BlockSpec((3, 1, rows, width), lambda i: (0, i + k, 0, 0))
    s_spec = lambda k: pl.BlockSpec((1, rows, width), lambda i: (i + k, 0, 0))
    f_edge = whole((3, layers, width))
    s_edge = pl.BlockSpec((1, layers, width), lambda i: (3, 0, 0))
    args = [field] * 3 + [stiffness] * 3 + [before, after, s_before, s_after]
    in_specs = [f_spec(k) for k in range(3)] + [s_spec(k) for k in range(3)]
    in_specs += [f_edge, f_edge, s_edge, s_edge]
    out_shape = [jax.ShapeDtypeStruct(field.shape, jnp.float32)]
    out_specs = [f_spec(1)]
    if first_sweep:
        args.append(surface)
        in_specs.append(whole(surface.shape))
        out_shape += [jax.ShapeDtypeStruct((3, layers, width), jnp.float32)] * 2
        out_specs += [f_edge] * 2
    return pl.pallas_call(
        functools.partial(inner_kernel, first_sweep),
        name="relax_inner_first" if first_sweep else "relax_inner_second",
        grid=(layers - 2,),
        in_specs=in_specs,
        out_specs=out_specs,
        out_shape=out_shape,
        compiler_params=pltpu.CompilerParams(vmem_limit_bytes=VMEM_LIMIT),
    )(*args)


def face_kernel(first_sweep, *refs):
    (where_ref, here, inside, s_here, s_inside, low, high, s_low, s_high,
     before, after, s_before, s_after) = refs[:13]
    rest = list(refs[13:])
    if first_sweep:
        surface, _, rows_in_first, rows_in_last, out = rest[:5]
        first_row, last_row, send_low, send_high = rest[5:]
    else:
        _, out = rest
    face = pl.program_id(0)
    t = pl.program_id(1)
    ntiles = here.shape[2] // 8
    layer = face * (before.shape[1] - 1)
    start = pl.multiple_of(8 * t, 8)
    pinned = jnp.logical_and(where_ref[1] == 1, face == 0)
    scale = jnp.where(face == 0, 1.0, 0.0)

    if first_sweep:
        @pl.when(jnp.logical_and(face == 0, t == 0))
        def _():
            first_row[...] = rows_in_first[...]
            last_row[...] = rows_in_last[...]

    def one(outer, s_outer, send):
        def load(c, side):
            if side == 1:
                return s_outer[0] if c == 3 else outer[c]
            if side == -1:
                return s_inside[0] if c == 3 else inside[c, 0]
            if c == 3:
                return s_here[0, pl.ds(start, 8), :]
            value = here[c, 0, pl.ds(start, 8), :]
            if first_sweep and c == 0:
                value = value + scale * surface[pl.ds(start + 8, 8), :]
            return value

        def beside(is_inside, at, f_edge, s_edge, surface_at):
            kept = jnp.clip(at, 0, 8 * ntiles - 1)

            def get(c):
                if c == 3:
                    near = s_here[0, pl.ds(kept, 1), :]
                    edge = s_edge[0, pl.ds(layer, 1), :]
                else:
                    near = here[c, 0, pl.ds(kept, 1), :]
                    edge = f_edge[c, pl.ds(layer, 1), :]
                value = jnp.where(is_inside, near, edge)
                if first_sweep and c == 0:
                    value = value + scale * surface[pl.ds(surface_at, 1), :]
                return value

            return get

        outs, centers = relax_tile(
            load,
            beside(t > 0, 8 * t - 1, before, s_before, 8 * t + 7),
            beside(t < ntiles - 1, 8 * t + 8, after, s_after, 8 * t + 16),
        )
        outs[0] = jnp.where(pinned, centers[0], outs[0])
        for c in range(3):
            out[c, 0] = outs[c]
            if first_sweep:
                send[c] = outs[c]
        if first_sweep:
            @pl.when(t == 0)
            def _():
                for c in range(3):
                    first_row[c, pl.ds(layer, 1), :] = outs[c][0:1]

            @pl.when(t == ntiles - 1)
            def _():
                for c in range(3):
                    last_row[c, pl.ds(layer, 1), :] = outs[c][7:8]

    @pl.when(face == 0)
    def _():
        one(low, s_low, send_low if first_sweep else None)

    @pl.when(face == 1)
    def _():
        one(high, s_high, send_high if first_sweep else None)


def relax_faces(position, field, stiffness, low, high, s_low, s_high,
                before, after, s_before, s_after, surface, partial):
    _, layers, rows, width = field.shape
    ntiles = rows // 8
    first_sweep = surface is not None
    whole = lambda shape: pl.BlockSpec(shape, lambda i, t, *_: (0,) * len(shape))
    outermost = lambda i: i * (layers - 1)
    inner = lambda i: 1 + i * (layers - 3)
    low_at = lambda i, t: jnp.where(i == 0, t, ntiles - 1)
    high_at = lambda i, t: jnp.where(i == 0, 0, t)
    plane = lambda at: pl.BlockSpec((3, 8, width), lambda i, t, *_: (0, at(i, t), 0))
    s_plane = lambda at: pl.BlockSpec((1, 8, width), lambda i, t, *_: (3, at(i, t), 0))
    f_edge = whole((3, layers, width))
    s_edge = pl.BlockSpec((1, layers, width), lambda i, t, *_: (3, 0, 0))
    f_out = pl.BlockSpec((3, 1, 8, width), lambda i, t, *_: (0, outermost(i), t, 0))
    args = [field, field, stiffness, stiffness, low, high, s_low, s_high,
            before, after, s_before, s_after]
    in_specs = [
        pl.BlockSpec((3, 1, rows, width), lambda i, t, *_: (0, outermost(i), 0, 0)),
        pl.BlockSpec((3, 1, 8, width), lambda i, t, *_: (0, inner(i), t, 0)),
        pl.BlockSpec((1, rows, width), lambda i, t, *_: (outermost(i), 0, 0)),
        pl.BlockSpec((1, 8, width), lambda i, t, *_: (inner(i), t, 0)),
        plane(low_at), plane(high_at), s_plane(low_at), s_plane(high_at),
        f_edge, f_edge, s_edge, s_edge,
    ]
    out_shape = [jax.ShapeDtypeStruct(field.shape, jnp.float32)]
    out_specs = [f_out]
    if first_sweep:
        args.append(surface)
        in_specs.append(whole(surface.shape))
    aliases = {len(args) + 1: 0}
    args.append(partial[0])
    in_specs.append(pl.BlockSpec(memory_space=pl.ANY))
    if first_sweep:
        aliases.update({len(args) + 1: 1, len(args) + 2: 2})
        args += partial[1:]
        in_specs += [f_edge, f_edge]
        out_shape += [jax.ShapeDtypeStruct((3, layers, width), jnp.float32)] * 2
        out_shape += [jax.ShapeDtypeStruct((3, rows, width), jnp.float32)] * 2
        out_specs += [f_edge, f_edge, plane(low_at), plane(high_at)]
    return pl.pallas_call(
        functools.partial(face_kernel, first_sweep),
        name="relax_faces_first" if first_sweep else "relax_faces_second",
        grid_spec=pltpu.PrefetchScalarGridSpec(
            num_scalar_prefetch=1, grid=(2, ntiles), in_specs=in_specs, out_specs=out_specs
        ),
        out_shape=out_shape,
        input_output_aliases=aliases,
        compiler_params=pltpu.CompilerParams(vmem_limit_bytes=VMEM_LIMIT),
    )(position, *args)


def per_device(
    displacement,
    stiffness,
    node_list,
    active_count,
    wear_class,
    pressure,
    slip_speed,
    rate_table,
    tile_owner,
    node_cell,
):
    rows, width = displacement.shape[2:]
    position = jnp.stack(
        [lax.axis_index("tan"), (lax.axis_index("depth") == 0).astype(jnp.int32)]
    ).astype(jnp.int32)

    wear = archard(wear_class, pressure, slip_speed, rate_table)
    other = swap_halves(wear)
    face_first, face_last = pack_faces(displacement, stiffness, wear)
    face_first, face_last, other = lax.optimization_barrier((face_first, face_last, other))
    wear = gather_wear(wear, other)
    low, high = shift_both(face_last, face_first, "depth")
    row_first, row_last = pack_rows(displacement, stiffness)
    before, after = shift_both(row_last, row_first, "tan")
    surface = paint(position, tile_owner, active_count, wear, node_list,
                    node_cell.reshape(-1, 128), rows, width, wear_class.shape[0])

    first, row_first, row_last = relax_inner(
        displacement, stiffness, before, after, before, after, surface
    )
    first, row_first, row_last, send_low, send_high = relax_faces(
        position, displacement, stiffness, low, high, low, high,
        before, after, before, after, surface, (first, row_first, row_last),
    )
    low_2, high_2 = shift_both(send_high, send_low, "depth")
    before_2, after_2 = shift_both(row_last, row_first, "tan")
    result = relax_inner(first, stiffness, before_2, after_2, before, after, None)[0]
    return relax_faces(
        position, first, stiffness, low_2, high_2, low, high,
        before_2, after_2, before, after, None, (result,),
    )[0]


def solution(mesh):
    in_specs = (
        P(None, "depth", "tan", None),
        P("depth", "tan", None),
        P(),
        P(),
        P("tan", None),
        P("tan", None),
        P("tan", None),
        P(),
        P(),
        P(),
    )
    out_specs = P(None, "depth", "tan", None)
    return jax.shard_map(
        per_device, mesh=mesh, in_specs=in_specs, out_specs=out_specs, check_vma=False
    )
```

time: 161 us -> 196 us (1.22)
  the two profiles are of different devices: /device:TPU:33 before, /device:TPU:1 now
where the time goes in v2:
time: 196 us; the launch traced here: 195 us
  Pallas kernels  115 us (59%)
  waiting for transfers between devices  35.6 us (18%)
  starting transfers between devices  23.5 us (12%)
  blocking collectives  18.3 us (9%)
  local copies, waits for them, and re-layouts  2.22 us (1%)
    pallas_call x1, Pallas kernels, pack_faces(): pl.pallas_call(pack_kernel, name='pack_faces', in_specs=[far, far, far],...  64.7 us
    ppermute x8, waiting for transfers between devices, shift_both(): return (lax.ppermute(last, axis, up), lax.ppermute(first, axis, down))  35.6 us
    ppermute x8, starting transfers between devices, shift_both(): return (lax.ppermute(last, axis, up), lax.ppermute(first, axis, down))  21 us
    pallas_call x2, Pallas kernels, relax_inner(): pl.pallas_call(functools.partial(inner_kernel, first_sweep), name='relax_...  20.4 us
    all_gather x1, blocking collectives, gather_wear(): lax.all_gather(both, 'tan', axis=0, axis_index_groups=groups, tiled=True)  18.3 us
    pallas_call x2, Pallas kernels, relax_faces(): pl.pallas_call(functools.partial(face_kernel, first_sweep), name='relax_f...  15.6 us
    pallas_call x1, Pallas kernels, paint(): pl.pallas_call(functools.partial(paint_kernel, shard_tiles), name='paint_...  10.8 us
  transfers between devices with their start and end apart: 9, of which 2 were waited for; matrix products, arithmetic and copies ran while one was open for 0% of the time, Pallas kernels for 50%

profile of v2, /device:TPU:1, one launch (start us, length us, event | category | flops | bytes accessed | tf_op | source)
XLA Modules:
  0.0 194.8 jit_solution(17052211243179883572)
XLA Ops:
  0.0 0.0 copy-start
  0.0 1.5 archard.1.wear_ref
  1.5 2.5 %collective-permute-start = (f32[32,128]{1,0:T(8,128)}, f32[32,128]{1,0:T(8,128)S(1)}, u32[]{:S(2)}, u32[]{:S(2)}) collective-permute-start(f32[32,128]{1,0:T(8,128)} %archard.1.wear_ref), channel_id=1, source_target_pairs={{0,2},{1,3},{2,0},{3,1},{4,6},{5,7},{6,4},{7,5},{8,10},{9,11},{10,... | collective-permute-start | bytes 49160 | tf_op jit(solution)/shard_map/ppermute | solution.py:100
  4.0 64.7 %pack_faces.1 = (f32[4,32,2048]{2,1,0:T(8,128)}, f32[4,32,2048]{2,1,0:T(8,128)}) custom-call(f32[3,8,32,2048]{3,2,1,0:T(8,128)} %refs_2_.3, f32[8,32,2048]{2,1,0:T(8,128)} %refs_4_.7, f32[32,128]{1,0:T(8,128)} %archard.1.wear_ref), custom_call_target="tpu_custom_call" | custom-call | tf_op jit(solution)/shard_map/pack_faces/pallas_call | solution.py:61
  68.7 0.0 collective-permute-done
  68.7 0.0 copy-start.6
  68.7 0.0 copy-start.3
  68.7 0.0 copy-start.4
  68.7 0.0 copy-start.5
  68.7 6.3 %collective-permute-start.1 = (f32[4,32,2048]{2,1,0:T(8,128)}, f32[4,32,2048]{2,1,0:T(8,128)}, u32[]{:S(2)}, u32[]{:S(2)}) collective-permute-start(f32[4,32,2048]{2,1,0:T(8,128)} %get-tuple-element.22), channel_id=1, source_target_pairs={{0,16},{16,32},{32,48},{48,64},{64,80},{80,96},{96,112},{1,17},{17... | collective-permute-start | bytes 3145736 | tf_op jit(solution)/shard_map/ppermute | solution.py:20
  75.1 1.3 collective-permute-start.2
  76.3 0.0 copy-done
  76.3 2.0 %pack_rows.1 = (f32[4,8,2048]{2,1,0:T(8,128)S(1)}, f32[4,8,2048]{2,1,0:T(8,128)S(1)}) custom-call(f32[3,8,32,2048]{3,2,1,0:T(8,128)} %refs_2_.3, f32[8,32,2048]{2,1,0:T(8,128)S(1)} %copy-done, f32[3,8,32,2048]{3,2,1,0:T(8,128)} %refs_2_.3, f32[8,32,2048]{2,1,0:T(8,128)S(1)} %copy-done), custom_call_target="tpu_custom_call" | custom-call | tf_op jit(solution)/shard_map/pack_rows/pallas_call | solution.py:87
  78.4 2.5 %collective-permute-start.3 = (f32[4,8,2048]{2,1,0:T(8,128)S(1)}, f32[4,8,2048]{2,1,0:T(8,128)S(1)}, u32[]{:S(2)}, u32[]{:S(2)}) collective-permute-start(f32[4,8,2048]{2,1,0:T(8,128)S(1)} %get-tuple-element.24), channel_id=1, source_target_pairs={{0,1},{1,2},{2,3},{3,4},{4,5},{5,6},{6,7},{7,8},{8,9},{9,10},{10,1... | collective-permute-start | bytes 786440 | tf_op jit(solution)/shard_map/ppermute | solution.py:20
  80.9 1.9 collective-permute-start.4
  82.9 0.1 pad_add_fusion.where_ref.refs_0_
  82.9 0.0 copy-done.6
  83.0 18.3 %all_gather.3.wear_ref = f32[512,128]{1,0:T(8,128)S(1)} all-gather(f32[64,128]{1,0:T(8,128)S(1)} %pad_maximum_fusion), channel_id=1, replica_groups={{0,1,4,5,8,9,12,13},{2,3,6,7,10,11,14,15},{16,17,20,21,24,25,28,29},{18..., dimensions={0}, use_global_device_ids=true | all-gather | bytes 294912 | tf_op jit(solution)/shard_map/all_gather | solution.py:107
  101.2 0.0 copy-done.3
  101.2 0.0 copy-done.4
  101.2 0.0 copy-done.5
  101.2 0.0 copy-start.2
  101.2 2.2 %copy-done.2 = s32[1048576]{0:T(1024)S(1)} copy-done((s32[1048576]{0:T(1024)S(1)}, s32[1048576]{0:T(1024)}, u32[]{:S(2)}) %copy-start.2) | copy-done | bytes 4194328
  103.4 10.8 %paint_band.1.refs_10_.refs_13_ = f32[48,2048]{1,0:T(8,128)S(1)} custom-call(s32[2]{0:T(128)S(1)} %pad_add_fusion.where_ref.refs_0_, s32[512]{0:T(512)S(1)} %copy-done.4, s32[512]{0:T(512)S(1)} %copy-done.5, f32[512,128]{1,0:T(8,128)S(1)} %all_gather.3.wear_ref, s32[512,128]{1,0:T(8,128)S(1)} %copy-done.3, s32[8192,128]{1,0:T(8,128)S(1)} %bitcast.3), custom_call_target="tpu_custom_call" | custom-call | tf_op jit(solution)/shard_map/paint_band/pallas_call | solution.py:234
  114.2 11.1 %collective-permute-done.3.refs_6_.refs_8_.refs_9_.refs_11_ = f32[4,8,2048]{2,1,0:T(8,128)S(1)} collective-permute-done((f32[4,8,2048]{2,1,0:T(8,128)S(1)}, f32[4,8,2048]{2,1,0:T(8,128)S(1)}, u32[]{:S(2)}, u32[]{:S(2)}) %collective-permute-start.3) | collective-permute-done | bytes 262176 | tf_op jit(solution)/shard_map/ppermute | solution.py:20
  125.3 0.0 collective-permute-done.4.refs_7_.refs_9_.refs_10_.refs_12_
  125.3 10.2 %relax_inner_first.1 = (f32[3,8,32,2048]{3,2,1,0:T(8,128)}, f32[3,8,2048]{2,1,0:T(8,128)S(1)}, f32[3,8,2048]{2,1,0:T(8,128)S(1)}) custom-call(f32[3,8,32,2048]{3,2,1,0:T(8,128)} %refs_2_.3, f32[3,8,32,2048]{3,2,1,0:T(8,128)} %refs_2_.3, f32[3,8,32,2048]{3,2,1,0:T(8,128)} %refs_2_.3, f32[8,32,2048]{2,1,0:T(8,128)S(1)} %copy-done, f32[8,32,2048]{2,1,0:T(8,128)S(1)} %copy-done, ...), custom_call_target="tpu_custom_call" | custom-call | tf_op jit(solution)/shard_map/relax_inner_first/pallas_call | solution.py:353
  135.5 0.0 collective-permute-done.1.refs_5_.refs_7_
  135.5 0.0 collective-permute-done.2.refs_6_.refs_8_
  135.5 0.0 copy-start.1
  135.6 8.1 %relax_faces_first.1 = (f32[3,8,32,2048]{3,2,1,0:T(8,128)}, f32[3,8,2048]{2,1,0:T(8,128)S(1)}, f32[3,8,2048]{2,1,0:T(8,128)S(1)}, f32[3,32,2048]{2,1,0:T(8,128)S(1)}, f32[3,32,2048]{2,1,0:T(8,128)S(1)}) custom-call(s32[2]{0:T(128)S(1)} %pad_add_fusion.where_ref.refs_0_, ...), custom_call_target="tpu_custom_call", output_to_operand_aliasing={{0}: (14, {}), {1}: (15, {}), {2}: (16, {})} | custom-call | tf_op jit(solution)/shard_map/relax_faces_first/pallas_call | solution.py:487
  143.6 1.3 collective-permute-start.5
  145.0 1.3 collective-permute-start.6
  146.3 4.4 %collective-permute-start.7 = (f32[3,8,2048]{2,1,0:T(8,128)S(1)}, f32[3,8,2048]{2,1,0:T(8,128)S(1)}, u32[]{:S(2)}, u32[]{:S(2)}) collective-permute-start(f32[3,8,2048]{2,1,0:T(8,128)S(1)} %get-tuple-element.33), channel_id=1, source_target_pairs={{0,1},{1,2},{2,3},{3,4},{4,5},{5,6},{6,7},{7,8},{8,9},{9,10},{10,1... | collective-permute-start | bytes 589832 | tf_op jit(solution)/shard_map/ppermute | solution.py:20
  150.7 1.9 collective-permute-start.8
  152.6 24.4 %collective-permute-done.7.refs_6_.refs_9_ = f32[3,8,2048]{2,1,0:T(8,128)S(1)} collective-permute-done((f32[3,8,2048]{2,1,0:T(8,128)S(1)}, f32[3,8,2048]{2,1,0:T(8,128)S(1)}, u32[]{:S(2)}, u32[]{:S(2)}) %collective-permute-start.7) | collective-permute-done | bytes 196640 | tf_op jit(solution)/shard_map/ppermute | solution.py:20
  177.0 0.0 collective-permute-done.8.refs_7_.refs_10_
  177.0 0.0 copy-done.1
  177.0 10.2 %relax_inner_second.1.refs_13_ = f32[3,8,32,2048]{3,2,1,0:T(8,128)} custom-call(f32[3,8,32,2048]{3,2,1,0:T(8,128)} %get-tuple-element.30.refs_0_.refs_1_.refs_2_, f32[3,8,32,2048]{3,2,1,0:T(8,128)} %get-tuple-element.30.refs_0_.refs_1_.refs_2_, f32[3,8,32,2048]{3,2,1,0:T(8,128)} %get-tuple-element.30.refs_0_.refs_1_.refs_2_, f32[8,32,2048]{2,1,0:T(8,128)S(1)} %copy-done.1, ...), custom_call_target="tpu_custom_call" | custom-call | tf_op jit(solution)/shard_map/relax_inner_second/pallas_call | solution.py:353
  187.3 0.0 collective-permute-done.5.refs_5_
  187.3 0.0 collective-permute-done.6.refs_6_
  187.3 7.5 %relax_faces_second.1 = f32[3,8,32,2048]{3,2,1,0:T(8,128)} custom-call(s32[2]{0:T(128)S(1)} %pad_add_fusion.where_ref.refs_0_, f32[3,8,32,2048]{3,2,1,0:T(8,128)} %get-tuple-element.30.refs_0_.refs_1_.refs_2_, f32[3,8,32,2048]{3,2,1,0:T(8,128)} %get-tuple-element.30.refs_0_.refs_1_.refs_2_, f32[8,32,2048]{2,1,0:T(8,128)} %refs_4_.7, ...), custom_call_target="tpu_custom_call", output_to_operand_aliasing={{}: (13, {})} | custom-call | tf_op jit(solution)/shard_map/relax_faces_second/pallas_call | solution.py:487
  (1 shorter events, 0.0 us)
Async XLA Ops:
  0.0 76.3 %copy-start = (f32[8,32,2048]{2,1,0:T(8,128)S(1)}, f32[8,32,2048]{2,1,0:T(8,128)}, u32[]{:S(2)}) copy-start(f32[8,32,2048]{2,1,0:T(8,128)} %refs_4_.7) | copy-start | bytes 6291460
  1.5 67.1 %collective-permute-start = (f32[32,128]{1,0:T(8,128)}, f32[32,128]{1,0:T(8,128)S(1)}, u32[]{:S(2)}, u32[]{:S(2)}) collective-permute-start(f32[32,128]{1,0:T(8,128)} %archard.1.wear_ref), channel_id=1, source_target_pairs={{0,2},{1,3},{2,0},{3,1},{4,6},{5,7},{6,4},{7,5},{8,10},{9,11},{10,... | collective-permute-start | bytes 49160 | tf_op jit(solution)/shard_map/ppermute | solution.py:100
  68.7 14.3 %copy-start.6 = (f32[32,128]{1,0:T(8,128)S(1)}, f32[32,128]{1,0:T(8,128)}, u32[]{:S(2)}) copy-start(f32[32,128]{1,0:T(8,128)} %archard.1.wear_ref) | copy-start | bytes 49156
  68.7 32.5 %copy-start.3 = (s32[512,128]{1,0:T(8,128)S(1)}, s32[512,128]{1,0:T(8,128)}, u32[]{:S(2)}) copy-start(s32[512,128]{1,0:T(8,128)} %list_ref.1) | copy-start | bytes 786436
  68.7 32.5 %copy-start.4 = (s32[512]{0:T(512)S(1)}, s32[512]{0:T(512)}, u32[]{:S(2)}) copy-start(s32[512]{0:T(512)} %owner_ref.1) | copy-start | bytes 6148
  68.7 32.5 %copy-start.5 = (s32[512]{0:T(512)S(1)}, s32[512]{0:T(512)}, u32[]{:S(2)}) copy-start(s32[512]{0:T(512)} %count_ref.1) | copy-start | bytes 6148
  68.7 66.8 %collective-permute-start.1 = (f32[4,32,2048]{2,1,0:T(8,128)}, f32[4,32,2048]{2,1,0:T(8,128)}, u32[]{:S(2)}, u32[]{:S(2)}) collective-permute-start(f32[4,32,2048]{2,1,0:T(8,128)} %get-tuple-element.22), channel_id=1, source_target_pairs={{0,16},{16,32},{32,48},{48,64},{64,80},{80,96},{96,112},{1,17},{17... | collective-permute-start | bytes 3145736 | tf_op jit(solution)/shard_map/ppermute | solution.py:20
  75.1 60.5 %collective-permute-start.2 = (f32[4,32,2048]{2,1,0:T(8,128)}, f32[4,32,2048]{2,1,0:T(8,128)}, u32[]{:S(2)}, u32[]{:S(2)}) collective-permute-start(f32[4,32,2048]{2,1,0:T(8,128)} %get-tuple-element.23), channel_id=1, source_target_pairs={{16,0},{32,16},{48,32},{64,48},{80,64},{96,80},{112,96},{17,1},{33... | collective-permute-start | bytes 3145736 | tf_op jit(solution)/shard_map/ppermute | solution.py:20
  78.4 46.9 %collective-permute-start.3 = (f32[4,8,2048]{2,1,0:T(8,128)S(1)}, f32[4,8,2048]{2,1,0:T(8,128)S(1)}, u32[]{:S(2)}, u32[]{:S(2)}) collective-permute-start(f32[4,8,2048]{2,1,0:T(8,128)S(1)} %get-tuple-element.24), channel_id=1, source_target_pairs={{0,1},{1,2},{2,3},{3,4},{4,5},{5,6},{6,7},{7,8},{8,9},{9,10},{10,1... | collective-permute-start | bytes 786440 | tf_op jit(solution)/shard_map/ppermute | solution.py:20
  80.9 44.4 %collective-permute-start.4 = (f32[4,8,2048]{2,1,0:T(8,128)S(1)}, f32[4,8,2048]{2,1,0:T(8,128)S(1)}, u32[]{:S(2)}, u32[]{:S(2)}) collective-permute-start(f32[4,8,2048]{2,1,0:T(8,128)S(1)} %get-tuple-element.25), channel_id=1, source_target_pairs={{1,0},{2,1},{3,2},{4,3},{5,4},{6,5},{7,6},{8,7},{9,8},{10,9},{11,1... | collective-permute-start | bytes 786440 | tf_op jit(solution)/shard_map/ppermute | solution.py:20
  101.2 2.2 %copy-start.2 = (s32[1048576]{0:T(1024)S(1)}, s32[1048576]{0:T(1024)}, u32[]{:S(2)}) copy-start(s32[1048576]{0:T(1024)} %param.19) | copy-start | bytes 12582916
  135.5 41.5 %copy-start.1 = (f32[8,32,2048]{2,1,0:T(8,128)S(1)}, f32[8,32,2048]{2,1,0:T(8,128)}, u32[]{:S(2)}) copy-start(f32[8,32,2048]{2,1,0:T(8,128)} %refs_4_.7) | copy-start | bytes 6291460
  143.6 43.6 %collective-permute-start.5 = (f32[3,32,2048]{2,1,0:T(8,128)S(1)}, f32[3,32,2048]{2,1,0:T(8,128)S(1)}, u32[]{:S(2)}, u32[]{:S(2)}) collective-permute-start(f32[3,32,2048]{2,1,0:T(8,128)S(1)} %get-tuple-element.31), channel_id=1, source_target_pairs={{0,16},{16,32},{32,48},{48,64},{64,80},{80,96},{96,112},{1,17},{17... | collective-permute-start | bytes 2359304 | tf_op jit(solution)/shard_map/ppermute | solution.py:20
  145.0 42.3 %collective-permute-start.6 = (f32[3,32,2048]{2,1,0:T(8,128)S(1)}, f32[3,32,2048]{2,1,0:T(8,128)S(1)}, u32[]{:S(2)}, u32[]{:S(2)}) collective-permute-start(f32[3,32,2048]{2,1,0:T(8,128)S(1)} %get-tuple-element.32), channel_id=1, source_target_pairs={{16,0},{32,16},{48,32},{64,48},{80,64},{96,80},{112,96},{17,1},{33... | collective-permute-start | bytes 2359304 | tf_op jit(solution)/shard_map/ppermute | solution.py:20
  146.3 30.8 %collective-permute-start.7 = (f32[3,8,2048]{2,1,0:T(8,128)S(1)}, f32[3,8,2048]{2,1,0:T(8,128)S(1)}, u32[]{:S(2)}, u32[]{:S(2)}) collective-permute-start(f32[3,8,2048]{2,1,0:T(8,128)S(1)} %get-tuple-element.33), channel_id=1, source_target_pairs={{0,1},{1,2},{2,3},{3,4},{4,5},{5,6},{6,7},{7,8},{8,9},{9,10},{10,1... | collective-permute-start | bytes 589832 | tf_op jit(solution)/shard_map/ppermute | solution.py:20
  150.7 26.4 %collective-permute-start.8 = (f32[3,8,2048]{2,1,0:T(8,128)S(1)}, f32[3,8,2048]{2,1,0:T(8,128)S(1)}, u32[]{:S(2)}, u32[]{:S(2)}) collective-permute-start(f32[3,8,2048]{2,1,0:T(8,128)S(1)} %get-tuple-element.34), channel_id=1, source_target_pairs={{1,0},{2,1},{3,2},{4,3},{5,4},{6,5},{7,6},{8,7},{9,8},{10,9},{11,1... | collective-permute-start | bytes 589832 | tf_op jit(solution)/shard_map/ppermute | solution.py:20

commit v3 on v2

v3 whole, which is shorter than its diff:
```python
import functools

import jax
import jax.numpy as jnp
from jax import lax
from jax.experimental import pallas as pl
from jax.experimental.pallas import tpu as pltpu
from jax.sharding import PartitionSpec as P

wear_step = 0.6
hardness = 4.0
GROUP = 8
VMEM_LIMIT = 48 * 1024 * 1024


def shift_both(last, first, axis):
    size = lax.axis_size(axis)
    up = [(i, i + 1) for i in range(size - 1)]
    down = [(j, i) for i, j in up]
    return lax.ppermute(last, axis, up), lax.ppermute(first, axis, down)


def rows_kernel(rates_ref, class_ref, contact_ref, sliding_ref, f_top, s_top, f_bottom,
                s_bottom, wear_ref, first_ref, last_ref):
    ids = class_ref[...]
    rate = jnp.zeros(ids.shape, jnp.float32)
    for k in range(rates_ref.shape[0]):
        rate = jnp.where(ids == k, rates_ref[k], rate)
    product = contact_ref[...] * sliding_ref[...]
    wear_ref[...] = wear_step * rate * product / (1.0 + product / hardness)
    for l in range(f_top.shape[1]):
        first_ref[3, l : l + 1, :] = s_top[l, 0:1, :]
        last_ref[3, l : l + 1, :] = s_bottom[l, 7:8, :]
        for c in range(3):
            first_ref[c, l : l + 1, :] = f_top[c, l, 0:1, :]
            last_ref[c, l : l + 1, :] = f_bottom[c, l, 7:8, :]


def pack_rows(field, stiffness, class_ids, contact, sliding, rates):
    _, layers, rows, width = field.shape
    bottom = rows // 8 - 1
    f_spec = lambda at: pl.BlockSpec((3, layers, 8, width), lambda i: (0, 0, at, 0))
    s_spec = lambda at: pl.BlockSpec((layers, 8, width), lambda i: (0, at, 0))
    out = jax.ShapeDtypeStruct((4, layers, width), jnp.float32)
    out_spec = pl.BlockSpec((4, layers, width), lambda i: (0, 0, 0))
    slot_spec = pl.BlockSpec(contact.shape, lambda i: (0, 0))
    return pl.pallas_call(
        rows_kernel,
        name="pack_rows",
        grid=(1,),
        in_specs=[pl.BlockSpec(memory_space=pltpu.SMEM), slot_spec, slot_spec, slot_spec,
                  f_spec(0), s_spec(0), f_spec(bottom), s_spec(bottom)],
        out_specs=[slot_spec, out_spec, out_spec],
        out_shape=[jax.ShapeDtypeStruct(contact.shape, jnp.float32), out, out],
        compiler_params=pltpu.CompilerParams(vmem_limit_bytes=VMEM_LIMIT),
    )(rates, class_ids, contact, sliding, field, stiffness, field, stiffness)


def faces_kernel(field_ref, stiff_ref, after_ref, first_ref, last_ref):
    step = pl.program_id(0)

    def put(to):
        to[0:3] = field_ref[:, 0]
        to[3:4] = stiff_ref[...]

    pl.when(step == 0)(lambda: put(last_ref))
    pl.when(step == 1)(lambda: put(first_ref))


def pack_faces(field, stiffness, earlier):
    _, layers, rows, width = field.shape
    face = jax.ShapeDtypeStruct((4, rows, width), jnp.float32)
    layer = lambda i: (1 - i) * (layers - 1)
    whole = pl.BlockSpec((4, rows, width), lambda i: (0, 0, 0))
    return pl.pallas_call(
        faces_kernel,
        name="pack_faces",
        grid=(2,),
        in_specs=[
            pl.BlockSpec((3, 1, rows, width), lambda i: (0, layer(i), 0, 0)),
            pl.BlockSpec((1, rows, width), lambda i: (layer(i), 0, 0)),
            pl.BlockSpec(memory_space=pl.ANY),
        ],
        out_specs=[whole, whole],
        out_shape=[face, face],
        compiler_params=pltpu.CompilerParams(vmem_limit_bytes=VMEM_LIMIT),
    )(field, stiffness, earlier)


def swap_halves(wear):
    size = lax.axis_size("tan")
    return lax.ppermute(wear, "tan", [(i, i ^ 2) for i in range(size)])


def gather_wear(wear, other):
    size = lax.axis_size("tan")
    both = jnp.concatenate([wear, other], axis=0)
    groups = [[i for i in range(size) if (i // 2) % 2 == half] for half in range(2)]
    return lax.all_gather(both, "tan", axis=0, axis_index_groups=groups, tiled=True)


def three_parts(value):
    high = value.astype(jnp.bfloat16).astype(jnp.float32)
    rest = value - high
    middle = rest.astype(jnp.bfloat16).astype(jnp.float32)
    return high, middle, rest - middle


def paint_kernel(
    shard_tiles, where_ref, owner_ref, count_ref, wear_ref, list_ref, table_ref, out_ref,
    own_ref, side_ref, acc_ref, edge_ref,
):
    slots = wear_ref.shape[1]
    ntile = wear_ref.shape[0]
    rows_table = table_ref.shape[0] // ntile
    tile_len = rows_table * 128
    width = out_ref.shape[1]
    rows = out_ref.shape[0] - 16
    me = where_ref[0]
    on_top = where_ref[1]
    out_ref[...] = jnp.zeros_like(out_ref)

    @pl.when(on_top == 1)
    def _():
        acc_ref[...] = jnp.zeros_like(acc_ref)
        edge_ref[...] = jnp.zeros_like(edge_ref)

        def collect(i, carry):
            n_own, n_side = carry
            offset = owner_ref[i] - me
            own_ref[n_own] = i
            side_ref[n_side] = i
            n_own = n_own + jnp.where(offset == 0, 1, 0)
            n_side = n_side + jnp.where(offset * offset == 1, 1, 0)
            return n_own, n_side

        n_own, n_side = lax.fori_loop(
            0, ntile, collect, (jnp.int32(0), jnp.int32(0)), unroll=8
        )

        lane = lax.broadcasted_iota(jnp.int32, (1, slots), 1)
        table_row = lax.broadcasted_iota(jnp.int32, (rows_table, slots), 0)
        block = width // 8
        fine = lax.broadcasted_iota(jnp.int32, (block, slots), 0)
        coarse = lax.broadcasted_iota(jnp.int32, (rows * 8, slots), 0)
        fine_edge = lax.broadcasted_iota(jnp.int32, (128, slots), 0)
        edge_blocks = width // 128
        coarse_edge = lax.broadcasted_iota(jnp.int32, (2 * edge_blocks, slots), 0)

        def entry(tiles_ref, position, total):
            i = tiles_ref[jnp.minimum(position, total - 1)]
            live = jnp.where(position < total, count_ref[i], 0)
            local = list_ref[pl.ds(i, 1), :] - i * tile_len
            table = table_ref[pl.ds(pl.multiple_of(i * rows_table, 8), rows_table), :]
            column = jnp.broadcast_to(local & 127, (rows_table, slots))
            picked = jnp.take_along_axis(table, column, axis=1)
            cell = jnp.sum(
                jnp.where(table_row == (local >> 7), picked, 0), axis=0, keepdims=True
            )
            shard = i // shard_tiles
            half = jnp.where((shard // 2) % 2 == (me // 2) % 2, 0, 1)
            place = (shard // 4) * 4 + (shard % 2) * 2 + half
            at = place * shard_tiles + i % shard_tiles
            wear = jnp.where(lane < live, wear_ref[pl.ds(at, 1), :], 0.0)
            return i, cell, wear

        def one_hot(mask, value):
            return jnp.where(mask, value, 0.0).astype(jnp.bfloat16)

        def add(into_ref, parts, hot):
            total = into_ref[...]
            for part in parts:
                total = total + lax.dot_general(
                    jnp.concatenate(part, axis=1), hot, (((1,), (1,)), ((), ())),
                    preferred_element_type=jnp.float32,
                )
            into_ref[...] = total

        def own_group(g, carry):
            parts = ([], [], [])
            hots = []
            for j in range(GROUP):
                _, cell, wear = entry(own_ref, g * GROUP + j, n_own)
                col = cell % width
                a_index = (col // block) * rows + cell // width
                hots.append(one_hot(fine == col % block, 1.0))
                mask = coarse == a_index
                for part, value in zip(parts, three_parts(wear)):
                    part.append(one_hot(mask, value))
            add(acc_ref, parts, jnp.concatenate(hots, axis=1))
            return carry

        def side_group(g, carry):
            parts = ([], [], [])
            hots = []
            for j in range(GROUP):
                i, cell, wear = entry(side_ref, g * GROUP + j, n_side)
                below = owner_ref[i] > me
                col = cell % width
                wanted = jnp.where(below, 0, rows - 1)
                shift = jnp.where(below, edge_blocks, 0)
                a_index = jnp.where(cell // width == wanted, col // 128 + shift, -1)
                hots.append(one_hot(fine_edge == col % 128, 1.0))
                mask = coarse_edge == a_index
                for part, value in zip(parts, three_parts(wear)):
                    part.append(one_hot(mask, value))
            add(edge_ref, parts, jnp.concatenate(hots, axis=1))
            return carry

        lax.fori_loop(0, (n_own + GROUP - 1) // GROUP, own_group, 0)
        lax.fori_loop(0, (n_side + GROUP - 1) // GROUP, side_group, 0)
        for j in range(8):
            out_ref[8 : 8 + rows, j * block : (j + 1) * block] = acc_ref[
                j * rows : (j + 1) * rows, :
            ]
        for j in range(edge_blocks):
            out_ref[7:8, j * 128 : (j + 1) * 128] = edge_ref[j : j + 1, :]
            out_ref[8 + rows : 9 + rows, j * 128 : (j + 1) * 128] = edge_ref[
                edge_blocks + j : edge_blocks + j + 1, :
            ]


def paint(position, owner, counts, wear, lists, table, rows, width, shard_tiles):
    ntile, slots = lists.shape
    whole = lambda shape: pl.BlockSpec(shape, lambda i, *_: (0,) * len(shape))
    return pl.pallas_call(
        functools.partial(paint_kernel, shard_tiles),
        name="paint_band",
        grid_spec=pltpu.PrefetchScalarGridSpec(
            num_scalar_prefetch=3,
            grid=(1,),
            in_specs=[whole(wear.shape), whole(lists.shape), whole(table.shape)],
            out_specs=whole((rows + 16, width)),
            scratch_shapes=[
                pltpu.SMEM((ntile + 1,), jnp.int32),
                pltpu.SMEM((ntile + 1,), jnp.int32),
                pltpu.VMEM((rows * 8, width // 8), jnp.float32),
                pltpu.VMEM((2 * width // 128, 128), jnp.float32),
            ],
        ),
        out_shape=jax.ShapeDtypeStruct((rows + 16, width), jnp.float32),
        compiler_params=pltpu.CompilerParams(vmem_limit_bytes=VMEM_LIMIT),
    )(position, owner, counts, wear, lists, table)


def relax_tile(load, row_above, row_below, has_high, has_low):
    row = lax.broadcasted_iota(jnp.int32, (8, 1), 0)
    centers = {}

    def neighbours(c):
        here = load(c, 0)
        centers[c] = here
        width = here.shape[1]
        lane = lax.broadcasted_iota(jnp.int32, here.shape, 1)
        yield load(c, 1)
        yield load(c, -1)
        yield jnp.where(row == 7, row_below(c), pltpu.roll(here, 7, 0))
        yield jnp.where(row == 0, row_above(c), pltpu.roll(here, 1, 0))
        yield jnp.where(lane == width - 1, 0.0, pltpu.roll(here, width - 1, 1))
        yield jnp.where(lane == 0, 0.0, pltpu.roll(here, 1, 1))

    around = list(neighbours(3))
    weights = [centers[3] + s for s in around]
    weights[0] = weights[0] * has_high
    weights[1] = weights[1] * has_low
    total = weights[0]
    for w in weights[1:]:
        total = total + w
    sums = []
    for c in range(3):
        acc = None
        for w, f in zip(weights, neighbours(c)):
            acc = w * f if acc is None else acc + w * f
        sums.append(acc)
    return sums, total, centers


def layer_kernel(first_sweep, *refs):
    (where_ref, low, mid, high, s_low, s_mid, s_high, before, after, s_before,
     s_after) = refs[:11]
    rest = list(refs[11:])
    surface = rest.pop(0) if first_sweep else None
    out, totals = rest[:2]
    layer = pl.program_id(0)
    last = pl.num_programs(0) - 1
    ntiles = mid.shape[2] // 8
    f_refs = {-1: low, 0: mid, 1: high}
    s_refs = {-1: s_low, 0: s_mid, 1: s_high}
    outermost = jnp.logical_or(layer == 0, layer == last)
    if first_sweep:
        first_row, last_row = rest[2:]

        @pl.when(layer == 0)
        def _():
            first_row[...] = jnp.zeros_like(first_row)
            last_row[...] = jnp.zeros_like(last_row)

    has_low = jnp.where(layer == 0, 0.0, 1.0)
    has_high = jnp.where(layer == last, 0.0, 1.0)
    scales = {0: jnp.where(layer == 0, 1.0, 0.0), -1: jnp.where(layer == 1, 1.0, 0.0)}
    pinned = jnp.logical_and(layer == 0, where_ref[1] == 1)

    for t in range(ntiles):
        at = slice(8 * t, 8 * t + 8)

        def load(c, side):
            if c == 3:
                return s_refs[side][0, at, :]
            value = f_refs[side][c, 0, at, :]
            if first_sweep and c == 0 and side <= 0:
                value = value + scales[side] * surface[8 * t + 8 : 8 * t + 16, :]
            return value

        def beside(inside, row, f_edge, s_edge):
            def get(c):
                if c == 3:
                    if inside:
                        return s_mid[0, row : row + 1, :]
                    return s_edge[0, pl.ds(layer, 1), :]
                value = mid[c, 0, row : row + 1, :] if inside else f_edge[c, pl.ds(layer, 1), :]
                if first_sweep and c == 0:
                    value = value + scales[0] * surface[row + 8 : row + 9, :]
                return value
            return get

        sums, total, centers = relax_tile(
            load,
            beside(t > 0, 8 * t - 1, before, s_before),
            beside(t < ntiles - 1, 8 * t + 8, after, s_after),
            has_high,
            has_low,
        )
        inverse = jnp.where(outermost, 1.0, 1.0 / total)
        outs = [part * inverse for part in sums]
        outs[0] = jnp.where(pinned, centers[0], outs[0])
        for c in range(3):
            out[c, 0, at, :] = outs[c]

        @pl.when(outermost)
        def _():
            totals[0, at, :] = total

        if first_sweep and t in (0, ntiles - 1):
            @pl.when(jnp.logical_not(outermost))
            def _():
                for c in range(3):
                    if t == 0:
                        first_row[c, pl.ds(layer, 1), :] = outs[c][0:1]
                    if t == ntiles - 1:
                        last_row[c, pl.ds(layer, 1), :] = outs[c][7:8]


def relax_layers(position, field, stiffness, before, after, s_before, s_after, surface):
    _, layers, rows, width = field.shape
    first_sweep = surface is not None
    whole = lambda shape: pl.BlockSpec(shape, lambda i, *_: (0,) * len(shape))
    at = lambda i, k: jnp.clip(i + k, 0, layers - 1)
    f_spec = lambda k: pl.BlockSpec((3, 1, rows, width), lambda i, *_: (0, at(i, k), 0, 0))
    s_spec = lambda k: pl.BlockSpec((1, rows, width), lambda i, *_: (at(i, k), 0, 0))
    f_edge = whole((3, layers, width))
    s_edge = pl.BlockSpec((1, layers, width), lambda i, *_: (3, 0, 0))
    sides = (-1, 0, 1)
    args = [field] * 3 + [stiffness] * 3 + [before, after, s_before, s_after]
    in_specs = [f_spec(k) for k in sides] + [s_spec(k) for k in sides]
    in_specs += [f_edge, f_edge, s_edge, s_edge]
    out_shape = [jax.ShapeDtypeStruct(field.shape, jnp.float32),
                 jax.ShapeDtypeStruct((2, rows, width), jnp.float32)]
    out_specs = [f_spec(0),
                 pl.BlockSpec((1, rows, width), lambda i, *_: (i // (layers // 2), 0, 0))]
    if first_sweep:
        args.append(surface)
        in_specs.append(whole(surface.shape))
        out_shape += [jax.ShapeDtypeStruct((3, layers, width), jnp.float32)] * 2
        out_specs += [f_edge] * 2
    return pl.pallas_call(
        functools.partial(layer_kernel, first_sweep),
        name="relax_layers_first" if first_sweep else "relax_layers_second",
        grid_spec=pltpu.PrefetchScalarGridSpec(
            num_scalar_prefetch=1, grid=(layers,), in_specs=in_specs, out_specs=out_specs
        ),
        out_shape=out_shape,
        compiler_params=pltpu.CompilerParams(vmem_limit_bytes=VMEM_LIMIT),
    )(position, *args)


def finish_first_kernel(face, *refs):
    where_ref, sums, s_here, totals, outer, s_outer = refs[:6]
    out, send, first_row, last_row = refs[-4:]
    ntiles = sums.shape[2] // 8
    pinned = where_ref[1] == 1
    if len(refs) > 10:
        first_row[...] = refs[6][...]
        last_row[...] = refs[7][...]
    else:
        first_row[...] = jnp.zeros_like(first_row)
        last_row[...] = jnp.zeros_like(last_row)
    for t in range(ntiles):
        at = slice(8 * t, 8 * t + 8)
        weight = s_here[0, at, :] + s_outer[0, at, :]
        inverse = 1.0 / (totals[0, at, :] + weight)
        for c in range(3):
            so_far = sums[c, 0, at, :]
            value = (so_far + weight * outer[c, at, :]) * inverse
            if face == 0 and c == 0:
                value = jnp.where(pinned, so_far, value)
            out[c, 0, at, :] = value
            send[c, at, :] = value
            k = 2 * c + face
            if t == 0:
                first_row[k : k + 1, :] = value[0:1]
            if t == ntiles - 1:
                last_row[k : k + 1, :] = value[7:8]


def finish_first(position, face, field, stiffness, totals, outer, edges):
    _, layers, rows, width = field.shape
    layer = face * (layers - 1)
    block = lambda shape, *at: pl.BlockSpec(shape, lambda i, *_: at)
    plane = block((3, rows, width), 0, 0, 0)
    own = block((3, 1, rows, width), 0, layer, 0, 0)
    edge = block((8, width), 0, 0)
    args = [field, stiffness, totals, outer, outer]
    in_specs = [own, block((1, rows, width), layer, 0, 0), block((1, rows, width), face, 0, 0),
                plane, block((1, rows, width), 3, 0, 0)]
    if edges is not None:
        args += edges
        in_specs += [edge, edge]
    edge_shape = jax.ShapeDtypeStruct((8, width), jnp.float32)
    return pl.pallas_call(
        functools.partial(finish_first_kernel, face),
        name="finish_first",
        grid_spec=pltpu.PrefetchScalarGridSpec(
            num_scalar_prefetch=1, grid=(1,), in_specs=in_specs,
            out_specs=[own, plane, edge, edge],
        ),
        out_shape=[jax.ShapeDtypeStruct(field.shape, jnp.float32),
                   jax.ShapeDtypeStruct((3, rows, width), jnp.float32),
                   edge_shape, edge_shape],
        input_output_aliases={1: 0},
        compiler_params=pltpu.CompilerParams(vmem_limit_bytes=VMEM_LIMIT),
    )(position, *args)


def finish_second_kernel(where_ref, sums, s_here, totals, low, high, s_low, s_high,
                         before, after, s_before, s_after, out):
    ntiles = sums.shape[2] // 8
    pinned = where_ref[1] == 1
    row = lax.broadcasted_iota(jnp.int32, (8, 1), 0)

    def one(face, outer, s_outer):
        layer = face * (s_before.shape[1] - 1)
        for t in range(ntiles):
            at = slice(8 * t, 8 * t + 8)
            here = s_here[0, at, :]
            weight = here + s_outer[0, at, :]
            inverse = 1.0 / (totals[0, at, :] + weight)
            for c in range(3):
                so_far = sums[c, 0, at, :]
                value = so_far + weight * outer[c, at, :]
                k = 2 * c + face
                if t == 0:
                    side = here + s_before[0, layer : layer + 1, :]
                    value = value + jnp.where(row == 0, side * before[k : k + 1, :], 0.0)
                if t == ntiles - 1:
                    side = here + s_after[0, layer : layer + 1, :]
                    value = value + jnp.where(row == 7, side * after[k : k + 1, :], 0.0)
                value = value * inverse
                if face == 0 and c == 0:
                    value = jnp.where(pinned, so_far, value)
                out[c, 0, at, :] = value

    step = pl.program_id(0)
    pl.when(step == 0)(lambda: one(0, low, s_low))
    pl.when(step == 1)(lambda: one(1, high, s_high))


def finish_second(position, field, stiffness, totals, low, high, s_low, s_high,
                  before, after, s_before, s_after):
    _, layers, rows, width = field.shape
    block = lambda shape, at: pl.BlockSpec(shape, lambda i, *_: at(i))
    layer = lambda i: i * (layers - 1)
    plane = block((3, rows, width), lambda i: (0, 0, 0))
    s_plane = block((1, rows, width), lambda i: (3, 0, 0))
    own = block((3, 1, rows, width), lambda i: (0, layer(i), 0, 0))
    edge = block((8, width), lambda i: (0, 0))
    s_edge = block((1, layers, width), lambda i: (3, 0, 0))
    return pl.pallas_call(
        finish_second_kernel,
        name="finish_second",
        grid_spec=pltpu.PrefetchScalarGridSpec(
            num_scalar_prefetch=1, grid=(2,),
            in_specs=[own, block((1, rows, width), lambda i: (layer(i), 0, 0)),
                      block((1, rows, width), lambda i: (i, 0, 0)),
                      plane, plane, s_plane, s_plane, edge, edge, s_edge, s_edge],
            out_specs=own,
        ),
        out_shape=jax.ShapeDtypeStruct(field.shape, jnp.float32),
        input_output_aliases={1: 0},
        compiler_params=pltpu.CompilerParams(vmem_limit_bytes=VMEM_LIMIT),
    )(position, field, stiffness, totals, low, high, s_low, s_high,
      before, after, s_before, s_after)


def per_device(
    displacement,
    stiffness,
    node_list,
    active_count,
    wear_class,
    pressure,
    slip_speed,
    rate_table,
    tile_owner,
    node_cell,
):
    rows, width = displacement.shape[2:]
    position = jnp.stack(
        [lax.axis_index("tan"), (lax.axis_index("depth") == 0).astype(jnp.int32)]
    ).astype(jnp.int32)

    wear, row_first, row_last = pack_rows(
        displacement, stiffness, wear_class, pressure, slip_speed, rate_table
    )
    other = swap_halves(wear)
    before, after = shift_both(row_last, row_first, "tan")
    face_first, face_last = pack_faces(displacement, stiffness, wear)
    face_first, face_last, other, before, after = lax.optimization_barrier(
        (face_first, face_last, other, before, after)
    )
    low, high = shift_both(face_last, face_first, "depth")
    wear = gather_wear(wear, other)
    surface = paint(position, tile_owner, active_count, wear, node_list,
                    node_cell.reshape(-1, 128), rows, width, wear_class.shape[0])

    first, totals, row_first, row_last = relax_layers(
        position, displacement, stiffness, before, after, before, after, surface
    )
    before_2, after_2 = shift_both(row_last, row_first, "tan")
    first, send_last, edge_first, edge_last = finish_first(
        position, 1, first, stiffness, totals, high, None
    )
    first, send_first, edge_first, edge_last = finish_first(
        position, 0, first, stiffness, totals, low, (edge_first, edge_last)
    )
    low_2, high_2 = shift_both(send_last, send_first, "depth")
    edge_before, edge_after = shift_both(edge_last, edge_first, "tan")
    result, totals = relax_layers(
        position, first, stiffness, before_2, after_2, before, after, None
    )
    return finish_second(position, result, stiffness, totals, low_2, high_2, low, high,
                         edge_before, edge_after, before, after)


def solution(mesh):
    in_specs = (
        P(None, "depth", "tan", None),
        P("depth", "tan", None),
        P(),
        P(),
        P("tan", None),
        P("tan", None),
        P("tan", None),
        P(),
        P(),
        P(),
    )
    out_specs = P(None, "depth", "tan", None)
    return jax.shard_map(
        per_device, mesh=mesh, in_specs=in_specs, out_specs=out_specs, check_vma=False
    )
```

time: 196 us -> 140 us (0.71)
  the two profiles are of different devices: /device:TPU:1 before, /device:TPU:37 now
where the time goes in v3:
time: 140 us; the launch traced here: 139 us
  starting transfers between devices  62.3 us (44%)
  Pallas kernels  52 us (37%)
  blocking collectives  12.7 us (9%)
  local copies, waits for them, and re-layouts  9.22 us (7%)
  waiting for transfers between devices  2.83 us (2%)
    ppermute x10, starting transfers between devices, shift_both(): return (lax.ppermute(last, axis, up), lax.ppermute(first, axis, down))  61.3 us
    pallas_call x2, Pallas kernels, relax_layers(): pl.pallas_call(functools.partial(layer_kernel, first_sweep), name='relax_...  27.3 us
    all_gather x1, blocking collectives, gather_wear(): lax.all_gather(both, 'tan', axis=0, axis_index_groups=groups, tiled=True)  12.7 us
    pallas_call x1, Pallas kernels, paint(): pl.pallas_call(functools.partial(paint_kernel, shard_tiles), name='paint_...  10.6 us
    unnamed x26, local copies, waits for them, and re-layouts  9.22 us
    pallas_call x2, Pallas kernels, finish_first(): pl.pallas_call(functools.partial(finish_first_kernel, face), name='finish...  5.77 us
    pallas_call x1, Pallas kernels, finish_second(): pl.pallas_call(finish_second_kernel, name='finish_second', grid_spec=pltp...  3.25 us
    pallas_call x1, Pallas kernels, pack_faces(): pl.pallas_call(faces_kernel, name='pack_faces', grid=(2,), in_specs=[pl.B...  2.87 us
  transfers between devices with their start and end apart: 11, of which 1 were waited for; matrix products, arithmetic and copies ran while one was open for 0% of the time, Pallas kernels for 31%

profile of v3, /device:TPU:37, one launch (start us, length us, event | category | flops | bytes accessed | tf_op | source)
XLA Modules:
  0.0 139.4 jit_solution(7415800946725840522)
XLA Ops:
  0.0 1.6 %copy-done = f32[8,32,2048]{2,1,0:T(8,128)S(1)} copy-done((f32[8,32,2048]{2,1,0:T(8,128)S(1)}, f32[8,32,2048]{2,1,0:T(8,128)}, u32[]{:S(2)}) %copy-start) | copy-done | bytes 2097176
  1.6 0.7 copy-done.7
  2.3 0.7 copy-done.8
  3.0 0.7 copy-done.9
  3.7 0.7 copy-done.12
  4.4 2.2 %pack_rows.1 = (f32[32,128]{1,0:T(8,128)S(1)}, f32[4,8,2048]{2,1,0:T(8,128)S(1)}, f32[4,8,2048]{2,1,0:T(8,128)S(1)}) custom-call(f32[8]{0:T(128)S(1)} %copy-done.12, s32[32,128]{1,0:T(8,128)S(1)} %copy-done.7, f32[32,128]{1,0:T(8,128)S(1)} %copy-done.8, f32[32,128]{1,0:T(8,128)S(1)} %copy-done.9, f32[3,8,32,2048]{3,2,1,0:T(8,128)} %refs_3_.1, ...), custom_call_target="tpu_custom_call" | custom-call | tf_op jit(solution)/shard_map/pack_rows/pallas_call | solution.py:47
  6.6 0.0 copy-start.10
  6.6 0.0 copy-start.11
  6.6 2.9 %collective-permute-start.1 = (f32[4,8,2048]{2,1,0:T(8,128)S(1)}, f32[4,8,2048]{2,1,0:T(8,128)S(1)}, u32[]{:S(2)}, u32[]{:S(2)}) collective-permute-start(f32[4,8,2048]{2,1,0:T(8,128)S(1)} %get-tuple-element.32), channel_id=1, source_target_pairs={{0,1},{1,2},{2,3},{3,4},{4,5},{5,6},{6,7},{7,8},{8,9},{9,10},{10,1... | collective-permute-start | bytes 786440 | tf_op jit(solution)/shard_map/ppermute | solution.py:20
  9.6 1.9 %collective-permute-start.2 = (f32[4,8,2048]{2,1,0:T(8,128)S(1)}, f32[4,8,2048]{2,1,0:T(8,128)S(1)}, u32[]{:S(2)}, u32[]{:S(2)}) collective-permute-start(f32[4,8,2048]{2,1,0:T(8,128)S(1)} %get-tuple-element.33), channel_id=1, source_target_pairs={{1,0},{2,1},{3,2},{4,3},{5,4},{6,5},{7,6},{8,7},{9,8},{10,9},{11,1... | collective-permute-start | bytes 786440 | tf_op jit(solution)/shard_map/ppermute | solution.py:20
  11.5 1.1 collective-permute-start
  12.6 0.0 copy-done.1
  12.6 2.9 %pack_faces.1 = (f32[4,32,2048]{2,1,0:T(8,128)}, f32[4,32,2048]{2,1,0:T(8,128)}) custom-call(f32[3,8,32,2048]{3,2,1,0:T(8,128)} %refs_3_.1, f32[8,32,2048]{2,1,0:T(8,128)S(1)} %copy-done.1, f32[32,128]{1,0:T(8,128)S(1)} %get-tuple-element.29.after_ref), custom_call_target="tpu_custom_call" | custom-call | tf_op jit(solution)/shard_map/pack_faces/pallas_call | solution.py:75
  15.5 0.0 collective-permute-done
  15.5 0.0 collective-permute-done.1.refs_7_.refs_9_.s_before
  15.5 2.8 %collective-permute-done.2.refs_8_.refs_10_.s_after = f32[4,8,2048]{2,1,0:T(8,128)S(1)} collective-permute-done((f32[4,8,2048]{2,1,0:T(8,128)S(1)}, f32[4,8,2048]{2,1,0:T(8,128)S(1)}, u32[]{:S(2)}, u32[]{:S(2)}) %collective-permute-start.2) | collective-permute-done | bytes 262176 | tf_op jit(solution)/shard_map/ppermute | solution.py:20
  18.3 0.7 copy-done.2
  19.0 1.3 collective-permute-start.3
  20.3 6.5 %collective-permute-start.4 = (f32[4,32,2048]{2,1,0:T(8,128)}, f32[4,32,2048]{2,1,0:T(8,128)}, u32[]{:S(2)}, u32[]{:S(2)}) collective-permute-start(f32[4,32,2048]{2,1,0:T(8,128)} %get-tuple-element.41), channel_id=1, source_target_pairs={{0,16},{16,32},{32,48},{48,64},{64,80},{80,96},{96,112},{1,17},{17... | collective-permute-start | bytes 3145736 | tf_op jit(solution)/shard_map/ppermute | solution.py:20
  26.8 0.1 pad_add_fusion.where_ref.refs_0_
  26.8 12.7 %all_gather.3.wear_ref = f32[512,128]{1,0:T(8,128)S(1)} all-gather(f32[64,128]{1,0:T(8,128)S(1)} %pad_maximum_fusion), channel_id=1, replica_groups={{0,1,4,5,8,9,12,13},{2,3,6,7,10,11,14,15},{16,17,20,21,24,25,28,29},{18..., dimensions={0}, use_global_device_ids=true | all-gather | bytes 294912 | tf_op jit(solution)/shard_map/all_gather | solution.py:99
  39.6 0.0 copy-done.10
  39.6 0.0 copy-done.11
  39.6 2.2 %copy-done.5 = s32[1048576]{0:T(1024)S(1)} copy-done((s32[1048576]{0:T(1024)S(1)}, s32[1048576]{0:T(1024)}, u32[]{:S(2)}) %copy-start.5) | copy-done | bytes 4194328
  41.8 0.9 copy-done.6
  42.7 10.6 %paint_band.1.refs_11_ = f32[48,2048]{1,0:T(8,128)S(1)} custom-call(s32[2]{0:T(128)S(1)} %pad_add_fusion.where_ref.refs_0_, s32[512]{0:T(512)S(1)} %copy-done.10, s32[512]{0:T(512)S(1)} %copy-done.11, f32[512,128]{1,0:T(8,128)S(1)} %all_gather.3.wear_ref, s32[512,128]{1,0:T(8,128)S(1)} %copy-done.6, s32[8192,128]{1,0:T(8,128)S(1)} %bitcast.3), custom_call_target="tpu_custom_call" | custom-call | tf_op jit(solution)/shard_map/paint_band/pallas_call | solution.py:226
  53.3 0.0 copy-start.3
  53.3 0.9 copy-done.3
  54.3 13.7 %relax_layers_first.1 = (f32[3,8,32,2048]{3,2,1,0:T(8,128)}, f32[2,32,2048]{2,1,0:T(8,128)S(1)}, f32[3,8,2048]{2,1,0:T(8,128)S(1)}, f32[3,8,2048]{2,1,0:T(8,128)S(1)}) custom-call(s32[2]{0:T(128)S(1)} %pad_add_fusion.where_ref.refs_0_, f32[3,8,32,2048]{3,2,1,0:T(8,128)} %refs_3_.1, f32[3,8,32,2048]{3,2,1,0:T(8,128)} %refs_3_.1, f32[3,8,32,2048]{3,2,1,0:T(8,128)} %refs_3_.1, ...), custom_call_target="tpu_custom_call" | custom-call | tf_op jit(solution)/shard_map/relax_layers_first/pallas_call | solution.py:375
  68.0 0.0 collective-permute-done.3.refs_4_.refs_5_.s_high
  68.0 2.7 %finish_first.2 = (f32[3,8,32,2048]{3,2,1,0:T(8,128)}, f32[3,32,2048]{2,1,0:T(8,128)S(1)}, f32[8,2048]{1,0:T(8,128)S(1)}, f32[8,2048]{1,0:T(8,128)S(1)}) custom-call(s32[2]{0:T(128)S(1)} %pad_add_fusion.where_ref.refs_0_, f32[3,8,32,2048]{3,2,1,0:T(8,128)} %get-tuple-element.37.refs_1_, ...), custom_call_target="tpu_custom_call", output_to_operand_aliasing={{0}: (1, {})} | custom-call | tf_op jit(solution)/shard_map/finish_first/pallas_call | solution.py:429
  70.7 0.0 collective-permute-done.4.refs_4_.refs_5_.s_low
  70.7 3.0 %finish_first.3 = (f32[3,8,32,2048]{3,2,1,0:T(8,128)}, f32[3,32,2048]{2,1,0:T(8,128)S(1)}, f32[8,2048]{1,0:T(8,128)S(1)}, f32[8,2048]{1,0:T(8,128)S(1)}) custom-call(s32[2]{0:T(128)S(1)} %pad_add_fusion.where_ref.refs_0_, f32[3,8,32,2048]{3,2,1,0:T(8,128)} %get-tuple-element.40.refs_1_, ...), custom_call_target="tpu_custom_call", output_to_operand_aliasing={{0}: (1, {})} | custom-call | tf_op jit(solution)/shard_map/finish_first/pallas_call | solution.py:429
  73.8 1.3 collective-permute-start.8
  75.1 6.0 %collective-permute-start.7 = (f32[3,32,2048]{2,1,0:T(8,128)S(1)}, f32[3,32,2048]{2,1,0:T(8,128)S(1)}, u32[]{:S(2)}, u32[]{:S(2)}) collective-permute-start(f32[3,32,2048]{2,1,0:T(8,128)S(1)} %get-tuple-element.49), channel_id=1, source_target_pairs={{0,16},{16,32},{32,48},{48,64},{64,80},{80,96},{96,112},{1,17},{17... | collective-permute-start | bytes 2359304 | tf_op jit(solution)/shard_map/ppermute | solution.py:20
  81.0 5.2 %collective-permute-start.5 = (f32[3,8,2048]{2,1,0:T(8,128)S(1)}, f32[3,8,2048]{2,1,0:T(8,128)S(1)}, u32[]{:S(2)}, u32[]{:S(2)}) collective-permute-start(f32[3,8,2048]{2,1,0:T(8,128)S(1)} %get-tuple-element.45), channel_id=1, source_target_pairs={{0,1},{1,2},{2,3},{3,4},{4,5},{5,6},{6,7},{7,8},{8,9},{9,10},{10,1... | collective-permute-start | bytes 589832 | tf_op jit(solution)/shard_map/ppermute | solution.py:20
  86.2 1.9 %collective-permute-start.6 = (f32[3,8,2048]{2,1,0:T(8,128)S(1)}, f32[3,8,2048]{2,1,0:T(8,128)S(1)}, u32[]{:S(2)}, u32[]{:S(2)}) collective-permute-start(f32[3,8,2048]{2,1,0:T(8,128)S(1)} %get-tuple-element.46), channel_id=1, source_target_pairs={{1,0},{2,1},{3,2},{4,3},{5,4},{6,5},{7,6},{8,7},{9,8},{10,9},{11,1... | collective-permute-start | bytes 589832 | tf_op jit(solution)/shard_map/ppermute | solution.py:20
  88.1 4.5 %collective-permute-start.9 = (f32[8,2048]{1,0:T(8,128)S(1)}, f32[8,2048]{1,0:T(8,128)S(1)}, u32[]{:S(2)}, u32[]{:S(2)}) collective-permute-start(f32[8,2048]{1,0:T(8,128)S(1)} %get-tuple-element.51), channel_id=1, source_target_pairs={{0,1},{1,2},{2,3},{3,4},{4,5},{5,6},{6,7},{7,8},{8,9},{9,10},{10,1... | collective-permute-start | bytes 196616 | tf_op jit(solution)/shard_map/ppermute | solution.py:20
  92.7 0.0 collective-permute-done.5.refs_7_
  92.7 29.8 %collective-permute-start.10 = (f32[8,2048]{1,0:T(8,128)S(1)}, f32[8,2048]{1,0:T(8,128)S(1)}, u32[]{:S(2)}, u32[]{:S(2)}) collective-permute-start(f32[8,2048]{1,0:T(8,128)S(1)} %get-tuple-element.52), channel_id=1, source_target_pairs={{1,0},{2,1},{3,2},{4,3},{5,4},{6,5},{7,6},{8,7},{9,8},{10,9},{11,1... | collective-permute-start | bytes 196616 | tf_op jit(solution)/shard_map/ppermute | solution.py:20
  122.5 0.0 collective-permute-done.6.refs_8_
  122.5 0.0 copy-done.4
  122.5 13.6 %relax_layers_second.1 = (f32[3,8,32,2048]{3,2,1,0:T(8,128)}, f32[2,32,2048]{2,1,0:T(8,128)S(1)}) custom-call(s32[2]{0:T(128)S(1)} %pad_add_fusion.where_ref.refs_0_, f32[3,8,32,2048]{3,2,1,0:T(8,128)} %get-tuple-element.44.refs_1_.refs_2_.refs_3_, f32[3,8,32,2048]{3,2,1,0:T(8,128)} %get-tuple-element.44.refs_1_.refs_2_.refs_3_, ...), custom_call_target="tpu_custom_call" | custom-call | tf_op jit(solution)/shard_map/relax_layers_second/pallas_call | solution.py:375
  136.1 0.0 collective-permute-done.9.before
  136.1 0.0 collective-permute-done.10.after
  136.1 0.0 collective-permute-done.8.high
  136.1 0.0 collective-permute-done.7.low
  136.1 3.2 %finish_second.1 = f32[3,8,32,2048]{3,2,1,0:T(8,128)} custom-call(s32[2]{0:T(128)S(1)} %pad_add_fusion.where_ref.refs_0_, f32[3,8,32,2048]{3,2,1,0:T(8,128)} %get-tuple-element.47.sums, f32[8,32,2048]{2,1,0:T(8,128)} %s_here.1, f32[2,32,2048]{2,1,0:T(8,128)S(1)} %get-tuple-element.48.totals, ...), custom_call_target="tpu_custom_call", output_to_operand_aliasing={{}: (1, {})} | custom-call | tf_op jit(solution)/shard_map/finish_second/pallas_call | solution.py:487
  (11 shorter events, 0.0 us)
Async XLA Ops:
  0.0 1.6 %copy-start = (f32[8,32,2048]{2,1,0:T(8,128)S(1)}, f32[8,32,2048]{2,1,0:T(8,128)}, u32[]{:S(2)}) copy-start(f32[8,32,2048]{2,1,0:T(8,128)} %s_here.1) | copy-start | bytes 6291460
  1.6 0.7 copy-start.7
  2.3 0.7 copy-start.8
  3.0 0.7 copy-start.9
  3.7 0.7 copy-start.12
  4.4 8.2 %copy-start.1 = (f32[8,32,2048]{2,1,0:T(8,128)S(1)}, f32[8,32,2048]{2,1,0:T(8,128)}, u32[]{:S(2)}) copy-start(f32[8,32,2048]{2,1,0:T(8,128)} %s_here.1) | copy-start | bytes 6291460
  6.6 33.0 %copy-start.10 = (s32[512]{0:T(512)S(1)}, s32[512]{0:T(512)}, u32[]{:S(2)}) copy-start(s32[512]{0:T(512)} %owner_ref.1) | copy-start | bytes 6148
  6.6 33.0 %copy-start.11 = (s32[512]{0:T(512)S(1)}, s32[512]{0:T(512)}, u32[]{:S(2)}) copy-start(s32[512]{0:T(512)} %count_ref.1) | copy-start | bytes 6148
  6.6 8.8 %collective-permute-start.1 = (f32[4,8,2048]{2,1,0:T(8,128)S(1)}, f32[4,8,2048]{2,1,0:T(8,128)S(1)}, u32[]{:S(2)}, u32[]{:S(2)}) collective-permute-start(f32[4,8,2048]{2,1,0:T(8,128)S(1)} %get-tuple-element.32), channel_id=1, source_target_pairs={{0,1},{1,2},{2,3},{3,4},{4,5},{5,6},{6,7},{7,8},{8,9},{9,10},{10,1... | collective-permute-start | bytes 786440 | tf_op jit(solution)/shard_map/ppermute | solution.py:20
  9.6 8.7 %collective-permute-start.2 = (f32[4,8,2048]{2,1,0:T(8,128)S(1)}, f32[4,8,2048]{2,1,0:T(8,128)S(1)}, u32[]{:S(2)}, u32[]{:S(2)}) collective-permute-start(f32[4,8,2048]{2,1,0:T(8,128)S(1)} %get-tuple-element.33), channel_id=1, source_target_pairs={{1,0},{2,1},{3,2},{4,3},{5,4},{6,5},{7,6},{8,7},{9,8},{10,9},{11,1... | collective-permute-start | bytes 786440 | tf_op jit(solution)/shard_map/ppermute | solution.py:20
  11.5 4.0 %collective-permute-start = (f32[32,128]{1,0:T(8,128)S(1)}, f32[32,128]{1,0:T(8,128)S(1)}, u32[]{:S(2)}, u32[]{:S(2)}) collective-permute-start(f32[32,128]{1,0:T(8,128)S(1)} %get-tuple-element.29.after_ref), channel_id=1, source_target_pairs={{0,2},{1,3},{2,0},{3,1},{4,6},{5,7},{6,4},{7,5},{8,10},{9,11},{10,... | collective-permute-start | bytes 49160 | tf_op jit(solution)/shard_map/ppermute | solution.py:92
  18.3 0.7 copy-start.2
  19.0 49.0 %collective-permute-start.3 = (f32[4,32,2048]{2,1,0:T(8,128)}, f32[4,32,2048]{2,1,0:T(8,128)S(1)}, u32[]{:S(2)}, u32[]{:S(2)}) collective-permute-start(f32[4,32,2048]{2,1,0:T(8,128)} %get-tuple-element.39), channel_id=1, source_target_pairs={{16,0},{32,16},{48,32},{64,48},{80,64},{96,80},{112,96},{17,1},{33... | collective-permute-start | bytes 3145736 | tf_op jit(solution)/shard_map/ppermute | solution.py:20
  20.3 50.5 %collective-permute-start.4 = (f32[4,32,2048]{2,1,0:T(8,128)}, f32[4,32,2048]{2,1,0:T(8,128)}, u32[]{:S(2)}, u32[]{:S(2)}) collective-permute-start(f32[4,32,2048]{2,1,0:T(8,128)} %get-tuple-element.41), channel_id=1, source_target_pairs={{0,16},{16,32},{32,48},{48,64},{64,80},{80,96},{96,112},{1,17},{17... | collective-permute-start | bytes 3145736 | tf_op jit(solution)/shard_map/ppermute | solution.py:20
  39.6 2.2 %copy-start.5 = (s32[1048576]{0:T(1024)S(1)}, s32[1048576]{0:T(1024)}, u32[]{:S(2)}) copy-start(s32[1048576]{0:T(1024)} %param.19) | copy-start | bytes 12582916
  41.8 0.9 copy-start.6
  53.3 1.0 copy-start.3
  70.7 51.7 %copy-start.4 = (f32[4,8,2048]{2,1,0:T(8,128)S(1)}, f32[4,8,2048]{2,1,0:T(8,128)}, u32[]{:S(2)}) copy-start(f32[4,8,2048]{2,1,0:T(8,128)} %copy-done.2) | copy-start | bytes 786436
  73.8 62.3 %collective-permute-start.8 = (f32[3,32,2048]{2,1,0:T(8,128)S(1)}, f32[3,32,2048]{2,1,0:T(8,128)S(1)}, u32[]{:S(2)}, u32[]{:S(2)}) collective-permute-start(f32[3,32,2048]{2,1,0:T(8,128)S(1)} %get-tuple-element.50), channel_id=1, source_target_pairs={{16,0},{32,16},{48,32},{64,48},{80,64},{96,80},{112,96},{17,1},{33... | collective-permute-start | bytes 2359304 | tf_op jit(solution)/shard_map/ppermute | solution.py:20
  75.1 61.0 %collective-permute-start.7 = (f32[3,32,2048]{2,1,0:T(8,128)S(1)}, f32[3,32,2048]{2,1,0:T(8,128)S(1)}, u32[]{:S(2)}, u32[]{:S(2)}) collective-permute-start(f32[3,32,2048]{2,1,0:T(8,128)S(1)} %get-tuple-element.49), channel_id=1, source_target_pairs={{0,16},{16,32},{32,48},{48,64},{64,80},{80,96},{96,112},{1,17},{17... | collective-permute-start | bytes 2359304 | tf_op jit(solution)/shard_map/ppermute | solution.py:20
  81.0 11.6 %collective-permute-start.5 = (f32[3,8,2048]{2,1,0:T(8,128)S(1)}, f32[3,8,2048]{2,1,0:T(8,128)S(1)}, u32[]{:S(2)}, u32[]{:S(2)}) collective-permute-start(f32[3,8,2048]{2,1,0:T(8,128)S(1)} %get-tuple-element.45), channel_id=1, source_target_pairs={{0,1},{1,2},{2,3},{3,4},{4,5},{5,6},{6,7},{7,8},{8,9},{9,10},{10,1... | collective-permute-start | bytes 589832 | tf_op jit(solution)/shard_map/ppermute | solution.py:20
  86.2 36.3 %collective-permute-start.6 = (f32[3,8,2048]{2,1,0:T(8,128)S(1)}, f32[3,8,2048]{2,1,0:T(8,128)S(1)}, u32[]{:S(2)}, u32[]{:S(2)}) collective-permute-start(f32[3,8,2048]{2,1,0:T(8,128)S(1)} %get-tuple-element.46), channel_id=1, source_target_pairs={{1,0},{2,1},{3,2},{4,3},{5,4},{6,5},{7,6},{8,7},{9,8},{10,9},{11,1... | collective-permute-start | bytes 589832 | tf_op jit(solution)/shard_map/ppermute | solution.py:20
  88.1 47.9 %collective-permute-start.9 = (f32[8,2048]{1,0:T(8,128)S(1)}, f32[8,2048]{1,0:T(8,128)S(1)}, u32[]{:S(2)}, u32[]{:S(2)}) collective-permute-start(f32[8,2048]{1,0:T(8,128)S(1)} %get-tuple-element.51), channel_id=1, source_target_pairs={{0,1},{1,2},{2,3},{3,4},{4,5},{5,6},{6,7},{7,8},{8,9},{9,10},{10,1... | collective-permute-start | bytes 196616 | tf_op jit(solution)/shard_map/ppermute | solution.py:20
  92.7 43.4 %collective-permute-start.10 = (f32[8,2048]{1,0:T(8,128)S(1)}, f32[8,2048]{1,0:T(8,128)S(1)}, u32[]{:S(2)}, u32[]{:S(2)}) collective-permute-start(f32[8,2048]{1,0:T(8,128)S(1)} %get-tuple-element.52), channel_id=1, source_target_pairs={{1,0},{2,1},{3,2},{4,3},{5,4},{6,5},{7,6},{8,7},{9,8},{10,9},{11,1... | collective-permute-start | bytes 196616 | tf_op jit(solution)/shard_map/ppermute | solution.py:20

commit v4 on v3

--- a/solution.py
+++ b/solution.py
@@ -20,40 +20,52 @@
     return lax.ppermute(last, axis, up), lax.ppermute(first, axis, down)
 
 
-def rows_kernel(rates_ref, class_ref, contact_ref, sliding_ref, f_top, s_top, f_bottom,
-                s_bottom, wear_ref, first_ref, last_ref):
+def wear_kernel(rates_ref, class_ref, contact_ref, sliding_ref, wear_ref):
     ids = class_ref[...]
     rate = jnp.zeros(ids.shape, jnp.float32)
     for k in range(rates_ref.shape[0]):
         rate = jnp.where(ids == k, rates_ref[k], rate)
     product = contact_ref[...] * sliding_ref[...]
     wear_ref[...] = wear_step * rate * product / (1.0 + product / hardness)
+
+
+def archard(class_ids, contact, sliding, rates):
+    near = pl.BlockSpec(memory_space=pltpu.VMEM)
+    return pl.pallas_call(
+        wear_kernel,
+        name="archard",
+        in_specs=[pl.BlockSpec(memory_space=pltpu.SMEM), near, near, near],
+        out_specs=near,
+        out_shape=jax.ShapeDtypeStruct(contact.shape, jnp.float32),
+    )(rates, class_ids, contact, sliding)
+
+
+def rows_kernel(f_top, s_top, f_bottom, s_bottom, first_ref, last_ref):
     for l in range(f_top.shape[1]):
-        first_ref[3, l : l + 1, :] = s_top[l, 0:1, :]
-        last_ref[3, l : l + 1, :] = s_bottom[l, 7:8, :]
-        for c in range(3):
-            first_ref[c, l : l + 1, :] = f_top[c, l, 0:1, :]
-            last_ref[c, l : l + 1, :] = f_bottom[c, l, 7:8, :]
-
-
-def pack_rows(field, stiffness, class_ids, contact, sliding, rates):
+        for k in range(2):
+            first_ref[4 * k + 3, l : l + 1, :] = s_top[l, k : k + 1, :]
+            last_ref[4 * k + 3, l : l + 1, :] = s_bottom[l, 7 - k : 8 - k, :]
+            for c in range(3):
+                first_ref[4 * k + c, l : l + 1, :] = f_top[c, l, k : k + 1, :]
+                last_ref[4 * k + c, l : l + 1, :] = f_bottom[c, l, 7 - k : 8 - k, :]
+
+
+def pack_rows(field, stiffness):
     _, layers, rows, width = field.shape
     bottom = rows // 8 - 1
     f_spec = lambda at: pl.BlockSpec((3, layers, 8, width), lambda i: (0, 0, at, 0))
     s_spec = lambda at: pl.BlockSpec((layers, 8, width), lambda i: (0, at, 0))
-    out = jax.ShapeDtypeStruct((4, layers, width), jnp.float32)
-    out_spec = pl.BlockSpec((4, layers, width), lambda i: (0, 0, 0))
-    slot_spec = pl.BlockSpec(contact.shape, lambda i: (0, 0))
+    out = jax.ShapeDtypeStruct((8, layers, width), jnp.float32)
+    out_spec = pl.BlockSpec((8, layers, width), lambda i: (0, 0, 0))
     return pl.pallas_call(
         rows_kernel,
         name="pack_rows",
         grid=(1,),
-        in_specs=[pl.BlockSpec(memory_space=pltpu.SMEM), slot_spec, slot_spec, slot_spec,
-                  f_spec(0), s_spec(0), f_spec(bottom), s_spec(bottom)],
-        out_specs=[slot_spec, out_spec, out_spec],
-        out_shape=[jax.ShapeDtypeStruct(contact.shape, jnp.float32), out, out],
+        in_specs=[f_spec(0), s_spec(0), f_spec(bottom), s_spec(bottom)],
+        out_specs=[out_spec, out_spec],
+        out_shape=[out, out],
         compiler_params=pltpu.CompilerParams(vmem_limit_bytes=VMEM_LIMIT),
-    )(rates, class_ids, contact, sliding, field, stiffness, field, stiffness)
+    )(field, stiffness, field, stiffness)
 
 
 def faces_kernel(field_ref, stiff_ref, after_ref, first_ref, last_ref):
@@ -243,8 +255,7 @@
     )(position, owner, counts, wear, lists, table)
 
 
-def relax_tile(load, row_above, row_below, has_high, has_low):
-    row = lax.broadcasted_iota(jnp.int32, (8, 1), 0)
+def relax_tile(load, beside, has_high, has_low):
     centers = {}
 
     def neighbours(c):
@@ -254,8 +265,7 @@
         lane = lax.broadcasted_iota(jnp.int32, here.shape, 1)
         yield load(c, 1)
         yield load(c, -1)
-        yield jnp.where(row == 7, row_below(c), pltpu.roll(here, 7, 0))
-        yield jnp.where(row == 0, row_above(c), pltpu.roll(here, 1, 0))
+        yield from beside(c, here)
         yield jnp.where(lane == width - 1, 0.0, pltpu.roll(here, width - 1, 1))
         yield jnp.where(lane == 0, 0.0, pltpu.roll(here, 1, 1))
 
@@ -275,25 +285,43 @@
     return sums, total, centers
 
 
+def relax_outside(out, near, s_near, far, inside, surface, at, layer):
+    def load(c, side):
+        here = s_near[0] if c == 3 else near[c]
+        if c == 0:
+            here = here + jnp.where(layer == 0, surface[at : at + 1, :], 0.0)
+        return here if side == 0 else pltpu.roll(here, 7 if side == 1 else 1, 0)
+
+    sums, total, _ = relax_tile(load, lambda c, here: (far[c], inside[c]), 1.0, 1.0)
+    inverse = 1.0 / total
+    between = jnp.logical_and(layer > 0, layer < out.shape[1] - 1)
+    kept = jnp.logical_and(between, s_near[0] > 0.0)
+    for c in range(3):
+        out[c] = jnp.where(kept, sums[c] * inverse, 0.0)
+
+
 def layer_kernel(first_sweep, *refs):
     (where_ref, low, mid, high, s_low, s_mid, s_high, before, after, s_before,
      s_after) = refs[:11]
     rest = list(refs[11:])
     surface = rest.pop(0) if first_sweep else None
-    out, totals = rest[:2]
+    extra = rest[:4] + rest[6:]
+    out, totals = rest[4:6] if first_sweep else rest
     layer = pl.program_id(0)
     last = pl.num_programs(0) - 1
     ntiles = mid.shape[2] // 8
     f_refs = {-1: low, 0: mid, 1: high}
     s_refs = {-1: s_low, 0: s_mid, 1: s_high}
     outermost = jnp.logical_or(layer == 0, layer == last)
+    row = lax.broadcasted_iota(jnp.int32, (8, 1), 0)
     if first_sweep:
-        first_row, last_row = rest[2:]
 
         @pl.when(layer == 0)
         def _():
-            first_row[...] = jnp.zeros_like(first_row)
-            last_row[...] = jnp.zeros_like(last_row)
+            far_before, far_after, own_first, own_last, out_before, out_after = extra
+            relax_outside(out_before, before, s_before, far_before, own_first, surface, 7, row)
+            relax_outside(out_after, after, s_after, far_after, own_last, surface,
+                          8 + 8 * ntiles, row)
 
     has_low = jnp.where(layer == 0, 0.0, 1.0)
     has_high = jnp.where(layer == last, 0.0, 1.0)
@@ -323,13 +351,14 @@
                 return value
             return get
 
-        sums, total, centers = relax_tile(
-            load,
-            beside(t > 0, 8 * t - 1, before, s_before),
-            beside(t < ntiles - 1, 8 * t + 8, after, s_after),
-            has_high,
-            has_low,
-        )
+        above = beside(t > 0, 8 * t - 1, before, s_before)
+        below = beside(t < ntiles - 1, 8 * t + 8, after, s_after)
+
+        def rolled(c, here):
+            yield jnp.where(row == 7, below(c), pltpu.roll(here, 7, 0))
+            yield jnp.where(row == 0, above(c), pltpu.roll(here, 1, 0))
+
+        sums, total, centers = relax_tile(load, rolled, has_high, has_low)
         inverse = jnp.where(outermost, 1.0, 1.0 / total)
         outs = [part * inverse for part in sums]
         outs[0] = jnp.where(pinned, centers[0], outs[0])
@@ -340,17 +369,9 @@
         def _():
             totals[0, at, :] = total
 
-        if first_sweep and t in (0, ntiles - 1):
-            @pl.when(jnp.logical_not(outermost))
-            def _():
-                for c in range(3):
-                    if t == 0:
-                        first_row[c, pl.ds(layer, 1), :] = outs[c][0:1]
-                    if t == ntiles - 1:
-                        last_row[c, pl.ds(layer, 1), :] = outs[c][7:8]
-
-
-def relax_layers(position, field, stiffness, before, after, s_before, s_after, surface):
+
+def relax_layers(position, field, stiffness, before, after, s_before, s_after, surface,
+                 own=()):
     _, layers, rows, width = field.shape
     first_sweep = surface is not None
     whole = lambda shape: pl.BlockSpec(shape, lambda i, *_: (0,) * len(shape))
@@ -370,6 +391,10 @@
     if first_sweep:
         args.append(surface)
         in_specs.append(whole(surface.shape))
+        args += [before, after, *own]
+        near = pl.BlockSpec((4, layers, width), lambda i, *_: (0, 0, 0))
+        far = pl.BlockSpec((4, layers, width), lambda i, *_: (1, 0, 0))
+        in_specs += [far, far, near, near]
         out_shape += [jax.ShapeDtypeStruct((3, layers, width), jnp.float32)] * 2
         out_specs += [f_edge] * 2
     return pl.pallas_call(
@@ -518,12 +543,11 @@
         [lax.axis_index("tan"), (lax.axis_index("depth") == 0).astype(jnp.int32)]
     ).astype(jnp.int32)
 
-    wear, row_first, row_last = pack_rows(
-        displacement, stiffness, wear_class, pressure, slip_speed, rate_table
-    )
+    row_first, row_last = pack_rows(displacement, stiffness)
+    wear = archard(wear_class, pressure, slip_speed, rate_table)
     other = swap_halves(wear)
     before, after = shift_both(row_last, row_first, "tan")
-    face_first, face_last = pack_faces(displacement, stiffness, wear)
+    face_first, face_last = pack_faces(displacement, stiffness, row_first)
     face_first, face_last, other, before, after = lax.optimization_barrier(
         (face_first, face_last, other, before, after)
     )
@@ -532,10 +556,10 @@
     surface = paint(position, tile_owner, active_count, wear, node_list,
                     node_cell.reshape(-1, 128), rows, width, wear_class.shape[0])
 
-    first, totals, row_first, row_last = relax_layers(
-        position, displacement, stiffness, before, after, before, after, surface
-    )
-    before_2, after_2 = shift_both(row_last, row_first, "tan")
+    first, totals, before_2, after_2 = relax_layers(
+        position, displacement, stiffness, before, after, before, after, surface,
+        (row_first, row_last),
+    )
     first, send_last, edge_first, edge_last = finish_first(
         position, 1, first, stiffness, totals, high, None
     )

time: 140 us -> 125 us (0.89)
  the two profiles are of different devices: /device:TPU:37 before, /device:TPU:22 now
where the time goes in v4:
time: 125 us; the launch traced here: 124 us
  Pallas kernels  45.3 us (36%)
  waiting for transfers between devices  31.4 us (25%)
  starting transfers between devices  30.7 us (25%)
  blocking collectives  12.8 us (10%)
  local copies, waits for them, and re-layouts  3.79 us (3%)
    ppermute x8, starting transfers between devices, shift_both(): return (lax.ppermute(last, axis, up), lax.ppermute(first, axis, down))  29.7 us
    pallas_call x2, Pallas kernels, relax_layers(): pl.pallas_call(functools.partial(layer_kernel, first_sweep), name='relax_...  27.7 us
    ppermute x8, waiting for transfers between devices, shift_both(): return (lax.ppermute(last, axis, up), lax.ppermute(first, axis, down))  25.6 us
    all_gather x1, blocking collectives, gather_wear(): lax.all_gather(both, 'tan', axis=0, axis_index_groups=groups, tiled=True)  12.8 us
    pallas_call x2, Pallas kernels, finish_first(): pl.pallas_call(functools.partial(finish_first_kernel, face), name='finish...  6.05 us
    ppermute x1, waiting for transfers between devices, swap_halves(): return lax.ppermute(wear, 'tan', [(i, i ^ 2) for i in range(size)])  5.79 us
    unnamed x14, local copies, waits for them, and re-layouts  3.79 us
    pallas_call x1, Pallas kernels, finish_second(): pl.pallas_call(finish_second_kernel, name='finish_second', grid_spec=pltp...  3.32 us
  transfers between devices with their start and end apart: 9, of which 3 were waited for; matrix products, arithmetic and copies ran while one was open for 0% of the time, Pallas kernels for 29%

profile of v4, /device:TPU:22, one launch (start us, length us, event | category | flops | bytes accessed | tf_op | source)
XLA Modules:
  0.0 124.2 jit_solution(17727656875392005124)
XLA Ops:
  0.0 0.0 copy-start
  0.0 1.6 %copy-done = f32[8,32,2048]{2,1,0:T(8,128)S(1)} copy-done((f32[8,32,2048]{2,1,0:T(8,128)S(1)}, f32[8,32,2048]{2,1,0:T(8,128)}, u32[]{:S(2)}) %copy-start) | copy-done | bytes 2097176
  1.6 0.0 copy-start.1
  1.6 3.3 %pack_rows.1 = (f32[8,8,2048]{2,1,0:T(8,128)}, f32[8,8,2048]{2,1,0:T(8,128)}) custom-call(f32[3,8,32,2048]{3,2,1,0:T(8,128)} %refs_3_.1, f32[8,32,2048]{2,1,0:T(8,128)S(1)} %copy-done, f32[3,8,32,2048]{3,2,1,0:T(8,128)} %refs_3_.1, f32[8,32,2048]{2,1,0:T(8,128)S(1)} %copy-done), custom_call_target="tpu_custom_call" | custom-call | tf_op jit(solution)/shard_map/pack_rows/pallas_call | solution.py:60
  4.9 0.0 copy-start.3
  4.9 0.0 copy-start.4
  4.9 0.0 copy-start.5
  4.9 2.0 %collective-permute-start.1 = (f32[8,8,2048]{2,1,0:T(8,128)}, f32[8,8,2048]{2,1,0:T(8,128)S(1)}, u32[]{:S(2)}, u32[]{:S(2)}) collective-permute-start(f32[8,8,2048]{2,1,0:T(8,128)} %get-tuple-element.31.refs_15_), channel_id=1, source_target_pairs={{0,1},{1,2},{2,3},{3,4},{4,5},{5,6},{6,7},{7,8},{8,9},{9,10},{10,1... | collective-permute-start | bytes 1572872 | tf_op jit(solution)/shard_map/ppermute | solution.py:20
  7.0 4.5 %collective-permute-start.2 = (f32[8,8,2048]{2,1,0:T(8,128)}, f32[8,8,2048]{2,1,0:T(8,128)S(1)}, u32[]{:S(2)}, u32[]{:S(2)}) collective-permute-start(f32[8,8,2048]{2,1,0:T(8,128)} %get-tuple-element.28.after_ref.refs_14_), channel_id=1, source_target_pairs={{1,0},{2,1},{3,2},{4,3},{5,4},{6,5},{7,6},{8,7},{9,8},{10,9},{11,1... | collective-permute-start | bytes 1572872 | tf_op jit(solution)/shard_map/ppermute | solution.py:20
  11.5 1.4 %archard.1 = f32[32,128]{1,0:T(8,128)} custom-call(f32[8]{0:T(128)} %rates_ref.1, s32[32,128]{1,0:T(8,128)} %class_ref.1, f32[32,128]{1,0:T(8,128)} %contact_ref.1, f32[32,128]{1,0:T(8,128)} %sliding_ref.1), custom_call_target="tpu_custom_call" | custom-call | tf_op jit(solution)/shard_map/archard/pallas_call | solution.py:34
  12.9 0.0 copy-start.6
  12.9 1.0 collective-permute-start
  13.9 0.0 copy-done.1
  14.0 2.9 %pack_faces.1 = (f32[4,32,2048]{2,1,0:T(8,128)}, f32[4,32,2048]{2,1,0:T(8,128)}) custom-call(f32[3,8,32,2048]{3,2,1,0:T(8,128)} %refs_3_.1, f32[8,32,2048]{2,1,0:T(8,128)S(1)} %copy-done.1, f32[8,8,2048]{2,1,0:T(8,128)} %get-tuple-element.28.after_ref.refs_14_), custom_call_target="tpu_custom_call" | custom-call | tf_op jit(solution)/shard_map/pack_faces/pallas_call | solution.py:87
  16.8 5.8 %collective-permute-done = f32[32,128]{1,0:T(8,128)S(1)} collective-permute-done((f32[32,128]{1,0:T(8,128)}, f32[32,128]{1,0:T(8,128)S(1)}, u32[]{:S(2)}, u32[]{:S(2)}) %collective-permute-start) | collective-permute-done | bytes 16416 | tf_op jit(solution)/shard_map/ppermute | solution.py:104
  22.6 0.0 collective-permute-done.1.refs_7_.refs_9_.refs_12_.s_before
  22.6 0.0 collective-permute-done.2.refs_8_.refs_10_.refs_13_.s_after
  22.6 7.3 %collective-permute-start.3 = (f32[4,32,2048]{2,1,0:T(8,128)}, f32[4,32,2048]{2,1,0:T(8,128)}, u32[]{:S(2)}, u32[]{:S(2)}) collective-permute-start(f32[4,32,2048]{2,1,0:T(8,128)} %get-tuple-element.37), channel_id=1, source_target_pairs={{16,0},{32,16},{48,32},{64,48},{80,64},{96,80},{112,96},{17,1},{33... | collective-permute-start | bytes 3145736 | tf_op jit(solution)/shard_map/ppermute | solution.py:20
  29.9 2.0 %collective-permute-start.4 = (f32[4,32,2048]{2,1,0:T(8,128)}, f32[4,32,2048]{2,1,0:T(8,128)}, u32[]{:S(2)}, u32[]{:S(2)}) collective-permute-start(f32[4,32,2048]{2,1,0:T(8,128)} %get-tuple-element.39), channel_id=1, source_target_pairs={{0,16},{16,32},{32,48},{48,64},{64,80},{80,96},{96,112},{1,17},{17... | collective-permute-start | bytes 3145736 | tf_op jit(solution)/shard_map/ppermute | solution.py:20
  32.0 0.1 pad_add_fusion.where_ref.refs_0_
  32.0 0.0 copy-done.6
  32.0 12.8 %all_gather.3.wear_ref = f32[512,128]{1,0:T(8,128)S(1)} all-gather(f32[64,128]{1,0:T(8,128)S(1)} %pad_maximum_fusion), channel_id=1, replica_groups={{0,1,4,5,8,9,12,13},{2,3,6,7,10,11,14,15},{16,17,20,21,24,25,28,29},{18..., dimensions={0}, use_global_device_ids=true | all-gather | bytes 294912 | tf_op jit(solution)/shard_map/all_gather | solution.py:111
  44.9 0.0 copy-done.3
  44.9 0.0 copy-done.4
  44.9 0.0 copy-done.5
  44.9 0.0 copy-start.2
  44.9 2.2 %copy-done.2 = s32[1048576]{0:T(1024)S(1)} copy-done((s32[1048576]{0:T(1024)S(1)}, s32[1048576]{0:T(1024)}, u32[]{:S(2)}) %copy-start.2) | copy-done | bytes 4194328
  47.1 0.6 paint_band.1.refs_11_
  47.7 14.2 %relax_layers_first.1 = (f32[3,8,32,2048]{3,2,1,0:T(8,128)}, f32[2,32,2048]{2,1,0:T(8,128)S(1)}, f32[3,8,2048]{2,1,0:T(8,128)S(1)}, f32[3,8,2048]{2,1,0:T(8,128)S(1)}) custom-call(s32[2]{0:T(128)S(1)} %pad_add_fusion.where_ref.refs_0_, f32[3,8,32,2048]{3,2,1,0:T(8,128)} %refs_3_.1, f32[3,8,32,2048]{3,2,1,0:T(8,128)} %refs_3_.1, f32[3,8,32,2048]{3,2,1,0:T(8,128)} %refs_3_.1, ...), custom_call_target="tpu_custom_call" | custom-call | tf_op jit(solution)/shard_map/relax_layers_first/pallas_call | solution.py:400
  61.8 13.7 %collective-permute-done.3.refs_4_.refs_5_.s_high = f32[4,32,2048]{2,1,0:T(8,128)} collective-permute-done((f32[4,32,2048]{2,1,0:T(8,128)}, f32[4,32,2048]{2,1,0:T(8,128)}, u32[]{:S(2)}, u32[]{:S(2)}) %collective-permute-start.3) | collective-permute-done | bytes 1048608 | tf_op jit(solution)/shard_map/ppermute | solution.py:20
  75.6 3.0 %finish_first.2 = (f32[3,8,32,2048]{3,2,1,0:T(8,128)}, f32[3,32,2048]{2,1,0:T(8,128)S(1)}, f32[8,2048]{1,0:T(8,128)S(1)}, f32[8,2048]{1,0:T(8,128)S(1)}) custom-call(s32[2]{0:T(128)S(1)} %pad_add_fusion.where_ref.refs_0_, f32[3,8,32,2048]{3,2,1,0:T(8,128)} %get-tuple-element.35.refs_1_, ...), custom_call_target="tpu_custom_call", output_to_operand_aliasing={{0}: (1, {})} | custom-call | tf_op jit(solution)/shard_map/finish_first/pallas_call | solution.py:454
  78.6 0.0 collective-permute-done.4.refs_4_.refs_5_.s_low
  78.6 3.0 %finish_first.3 = (f32[3,8,32,2048]{3,2,1,0:T(8,128)}, f32[3,32,2048]{2,1,0:T(8,128)S(1)}, f32[8,2048]{1,0:T(8,128)S(1)}, f32[8,2048]{1,0:T(8,128)S(1)}) custom-call(s32[2]{0:T(128)S(1)} %pad_add_fusion.where_ref.refs_0_, f32[3,8,32,2048]{3,2,1,0:T(8,128)} %get-tuple-element.38.refs_1_, ...), custom_call_target="tpu_custom_call", output_to_operand_aliasing={{0}: (1, {})} | custom-call | tf_op jit(solution)/shard_map/finish_first/pallas_call | solution.py:454
  81.6 2.9 %collective-permute-start.6 = (f32[3,32,2048]{2,1,0:T(8,128)S(1)}, f32[3,32,2048]{2,1,0:T(8,128)S(1)}, u32[]{:S(2)}, u32[]{:S(2)}) collective-permute-start(f32[3,32,2048]{2,1,0:T(8,128)S(1)} %get-tuple-element.48), channel_id=1, source_target_pairs={{16,0},{32,16},{48,32},{64,48},{80,64},{96,80},{112,96},{17,1},{33... | collective-permute-start | bytes 2359304 | tf_op jit(solution)/shard_map/ppermute | solution.py:20
  84.5 4.4 %collective-permute-start.5 = (f32[3,32,2048]{2,1,0:T(8,128)S(1)}, f32[3,32,2048]{2,1,0:T(8,128)S(1)}, u32[]{:S(2)}, u32[]{:S(2)}) collective-permute-start(f32[3,32,2048]{2,1,0:T(8,128)S(1)} %get-tuple-element.47), channel_id=1, source_target_pairs={{0,16},{16,32},{32,48},{48,64},{64,80},{80,96},{96,112},{1,17},{17... | collective-permute-start | bytes 2359304 | tf_op jit(solution)/shard_map/ppermute | solution.py:20
  89.0 1.9 %collective-permute-start.7 = (f32[8,2048]{1,0:T(8,128)S(1)}, f32[8,2048]{1,0:T(8,128)S(1)}, u32[]{:S(2)}, u32[]{:S(2)}) collective-permute-start(f32[8,2048]{1,0:T(8,128)S(1)} %get-tuple-element.49), channel_id=1, source_target_pairs={{0,1},{1,2},{2,3},{3,4},{4,5},{5,6},{6,7},{7,8},{8,9},{9,10},{10,1... | collective-permute-start | bytes 196616 | tf_op jit(solution)/shard_map/ppermute | solution.py:20
  90.9 4.5 %collective-permute-start.8 = (f32[8,2048]{1,0:T(8,128)S(1)}, f32[8,2048]{1,0:T(8,128)S(1)}, u32[]{:S(2)}, u32[]{:S(2)}) collective-permute-start(f32[8,2048]{1,0:T(8,128)S(1)} %get-tuple-element.50), channel_id=1, source_target_pairs={{1,0},{2,1},{3,2},{4,3},{5,4},{6,5},{7,6},{8,7},{9,8},{10,9},{11,1... | collective-permute-start | bytes 196616 | tf_op jit(solution)/shard_map/ppermute | solution.py:20
  95.5 13.6 %relax_layers_second.1 = (f32[3,8,32,2048]{3,2,1,0:T(8,128)}, f32[2,32,2048]{2,1,0:T(8,128)S(1)}) custom-call(s32[2]{0:T(128)S(1)} %pad_add_fusion.where_ref.refs_0_, f32[3,8,32,2048]{3,2,1,0:T(8,128)} %get-tuple-element.42.refs_1_.refs_2_.refs_3_, f32[3,8,32,2048]{3,2,1,0:T(8,128)} %get-tuple-element.42.refs_1_.refs_2_.refs_3_, ...), custom_call_target="tpu_custom_call" | custom-call | tf_op jit(solution)/shard_map/relax_layers_second/pallas_call | solution.py:400
  109.0 0.0 collective-permute-done.7.before
  109.0 0.0 collective-permute-done.8.after
  109.0 11.8 %collective-permute-done.6.high = f32[3,32,2048]{2,1,0:T(8,128)S(1)} collective-permute-done((f32[3,32,2048]{2,1,0:T(8,128)S(1)}, f32[3,32,2048]{2,1,0:T(8,128)S(1)}, u32[]{:S(2)}, u32[]{:S(2)}) %collective-permute-start.6) | collective-permute-done | bytes 786464 | tf_op jit(solution)/shard_map/ppermute | solution.py:20
  120.9 0.0 collective-permute-done.5.low
  120.9 3.3 %finish_second.1 = f32[3,8,32,2048]{3,2,1,0:T(8,128)} custom-call(s32[2]{0:T(128)S(1)} %pad_add_fusion.where_ref.refs_0_, f32[3,8,32,2048]{3,2,1,0:T(8,128)} %get-tuple-element.45.sums, f32[8,32,2048]{2,1,0:T(8,128)} %s_here.1, f32[2,32,2048]{2,1,0:T(8,128)S(1)} %get-tuple-element.46.totals, ...), custom_call_target="tpu_custom_call", output_to_operand_aliasing={{}: (1, {})} | custom-call | tf_op jit(solution)/shard_map/finish_second/pallas_call | solution.py:512
  (1 shorter events, 0.0 us)
Async XLA Ops:
  0.0 1.6 %copy-start = (f32[8,32,2048]{2,1,0:T(8,128)S(1)}, f32[8,32,2048]{2,1,0:T(8,128)}, u32[]{:S(2)}) copy-start(f32[8,32,2048]{2,1,0:T(8,128)} %s_here.1) | copy-start | bytes 6291460
  1.6 12.4 %copy-start.1 = (f32[8,32,2048]{2,1,0:T(8,128)S(1)}, f32[8,32,2048]{2,1,0:T(8,128)}, u32[]{:S(2)}) copy-start(f32[8,32,2048]{2,1,0:T(8,128)} %s_here.1) | copy-start | bytes 6291460
  4.9 40.0 %copy-start.3 = (s32[512,128]{1,0:T(8,128)S(1)}, s32[512,128]{1,0:T(8,128)}, u32[]{:S(2)}) copy-start(s32[512,128]{1,0:T(8,128)} %list_ref.1) | copy-start | bytes 786436
  4.9 40.0 %copy-start.4 = (s32[512]{0:T(512)S(1)}, s32[512]{0:T(512)}, u32[]{:S(2)}) copy-start(s32[512]{0:T(512)} %owner_ref.1) | copy-start | bytes 6148
  4.9 40.0 %copy-start.5 = (s32[512]{0:T(512)S(1)}, s32[512]{0:T(512)}, u32[]{:S(2)}) copy-start(s32[512]{0:T(512)} %count_ref.1) | copy-start | bytes 6148
  4.9 17.7 %collective-permute-start.1 = (f32[8,8,2048]{2,1,0:T(8,128)}, f32[8,8,2048]{2,1,0:T(8,128)S(1)}, u32[]{:S(2)}, u32[]{:S(2)}) collective-permute-start(f32[8,8,2048]{2,1,0:T(8,128)} %get-tuple-element.31.refs_15_), channel_id=1, source_target_pairs={{0,1},{1,2},{2,3},{3,4},{4,5},{5,6},{6,7},{7,8},{8,9},{9,10},{10,1... | collective-permute-start | bytes 1572872 | tf_op jit(solution)/shard_map/ppermute | solution.py:20
  7.0 15.7 %collective-permute-start.2 = (f32[8,8,2048]{2,1,0:T(8,128)}, f32[8,8,2048]{2,1,0:T(8,128)S(1)}, u32[]{:S(2)}, u32[]{:S(2)}) collective-permute-start(f32[8,8,2048]{2,1,0:T(8,128)} %get-tuple-element.28.after_ref.refs_14_), channel_id=1, source_target_pairs={{1,0},{2,1},{3,2},{4,3},{5,4},{6,5},{7,6},{8,7},{9,8},{10,9},{11,1... | collective-permute-start | bytes 1572872 | tf_op jit(solution)/shard_map/ppermute | solution.py:20
  12.9 19.1 %copy-start.6 = (f32[32,128]{1,0:T(8,128)S(1)}, f32[32,128]{1,0:T(8,128)}, u32[]{:S(2)}) copy-start(f32[32,128]{1,0:T(8,128)} %archard.1) | copy-start | bytes 49156
  12.9 9.7 %collective-permute-start = (f32[32,128]{1,0:T(8,128)}, f32[32,128]{1,0:T(8,128)S(1)}, u32[]{:S(2)}, u32[]{:S(2)}) collective-permute-start(f32[32,128]{1,0:T(8,128)} %archard.1), channel_id=1, source_target_pairs={{0,2},{1,3},{2,0},{3,1},{4,6},{5,7},{6,4},{7,5},{8,10},{9,11},{10,... | collective-permute-start | bytes 49160 | tf_op jit(solution)/shard_map/ppermute | solution.py:104
  22.6 53.0 %collective-permute-start.3 = (f32[4,32,2048]{2,1,0:T(8,128)}, f32[4,32,2048]{2,1,0:T(8,128)}, u32[]{:S(2)}, u32[]{:S(2)}) collective-permute-start(f32[4,32,2048]{2,1,0:T(8,128)} %get-tuple-element.37), channel_id=1, source_target_pairs={{16,0},{32,16},{48,32},{64,48},{80,64},{96,80},{112,96},{17,1},{33... | collective-permute-start | bytes 3145736 | tf_op jit(solution)/shard_map/ppermute | solution.py:20
  29.9 48.7 %collective-permute-start.4 = (f32[4,32,2048]{2,1,0:T(8,128)}, f32[4,32,2048]{2,1,0:T(8,128)}, u32[]{:S(2)}, u32[]{:S(2)}) collective-permute-start(f32[4,32,2048]{2,1,0:T(8,128)} %get-tuple-element.39), channel_id=1, source_target_pairs={{0,16},{16,32},{32,48},{48,64},{64,80},{80,96},{96,112},{1,17},{17... | collective-permute-start | bytes 3145736 | tf_op jit(solution)/shard_map/ppermute | solution.py:20
  44.9 2.2 %copy-start.2 = (s32[1048576]{0:T(1024)S(1)}, s32[1048576]{0:T(1024)}, u32[]{:S(2)}) copy-start(s32[1048576]{0:T(1024)} %param.19) | copy-start | bytes 12582916
  81.6 39.2 %collective-permute-start.6 = (f32[3,32,2048]{2,1,0:T(8,128)S(1)}, f32[3,32,2048]{2,1,0:T(8,128)S(1)}, u32[]{:S(2)}, u32[]{:S(2)}) collective-permute-start(f32[3,32,2048]{2,1,0:T(8,128)S(1)} %get-tuple-element.48), channel_id=1, source_target_pairs={{16,0},{32,16},{48,32},{64,48},{80,64},{96,80},{112,96},{17,1},{33... | collective-permute-start | bytes 2359304 | tf_op jit(solution)/shard_map/ppermute | solution.py:20
  84.5 36.3 %collective-permute-start.5 = (f32[3,32,2048]{2,1,0:T(8,128)S(1)}, f32[3,32,2048]{2,1,0:T(8,128)S(1)}, u32[]{:S(2)}, u32[]{:S(2)}) collective-permute-start(f32[3,32,2048]{2,1,0:T(8,128)S(1)} %get-tuple-element.47), channel_id=1, source_target_pairs={{0,16},{16,32},{32,48},{48,64},{64,80},{80,96},{96,112},{1,17},{17... | collective-permute-start | bytes 2359304 | tf_op jit(solution)/shard_map/ppermute | solution.py:20
  89.0 20.1 %collective-permute-start.7 = (f32[8,2048]{1,0:T(8,128)S(1)}, f32[8,2048]{1,0:T(8,128)S(1)}, u32[]{:S(2)}, u32[]{:S(2)}) collective-permute-start(f32[8,2048]{1,0:T(8,128)S(1)} %get-tuple-element.49), channel_id=1, source_target_pairs={{0,1},{1,2},{2,3},{3,4},{4,5},{5,6},{6,7},{7,8},{8,9},{9,10},{10,1... | collective-permute-start | bytes 196616 | tf_op jit(solution)/shard_map/ppermute | solution.py:20
  90.9 18.1 %collective-permute-start.8 = (f32[8,2048]{1,0:T(8,128)S(1)}, f32[8,2048]{1,0:T(8,128)S(1)}, u32[]{:S(2)}, u32[]{:S(2)}) collective-permute-start(f32[8,2048]{1,0:T(8,128)S(1)} %get-tuple-element.50), channel_id=1, source_target_pairs={{1,0},{2,1},{3,2},{4,3},{5,4},{6,5},{7,6},{8,7},{9,8},{10,9},{11,1... | collective-permute-start | bytes 196616 | tf_op jit(solution)/shard_map/ppermute | solution.py:20

commit v5 on v4

--- a/solution.py
+++ b/solution.py
@@ -68,7 +68,7 @@
     )(field, stiffness, field, stiffness)
 
 
-def faces_kernel(field_ref, stiff_ref, after_ref, first_ref, last_ref):
+def faces_kernel(field_ref, stiff_ref, first_ref, last_ref):
     step = pl.program_id(0)
 
     def put(to):
@@ -79,7 +79,7 @@
     pl.when(step == 1)(lambda: put(first_ref))
 
 
-def pack_faces(field, stiffness, earlier):
+def pack_faces(field, stiffness):
     _, layers, rows, width = field.shape
     face = jax.ShapeDtypeStruct((4, rows, width), jnp.float32)
     layer = lambda i: (1 - i) * (layers - 1)
@@ -91,12 +91,11 @@
         in_specs=[
             pl.BlockSpec((3, 1, rows, width), lambda i: (0, layer(i), 0, 0)),
             pl.BlockSpec((1, rows, width), lambda i: (layer(i), 0, 0)),
-            pl.BlockSpec(memory_space=pl.ANY),
         ],
         out_specs=[whole, whole],
         out_shape=[face, face],
         compiler_params=pltpu.CompilerParams(vmem_limit_bytes=VMEM_LIMIT),
-    )(field, stiffness, earlier)
+    )(field, stiffness)
 
 
 def swap_halves(wear):
@@ -305,8 +304,12 @@
      s_after) = refs[:11]
     rest = list(refs[11:])
     surface = rest.pop(0) if first_sweep else None
-    extra = rest[:4] + rest[6:]
-    out, totals = rest[4:6] if first_sweep else rest
+    if first_sweep:
+        face_first, face_last = rest[:2]
+        out = rest[6]
+        extra = rest[2:6] + rest[7:]
+    else:
+        out, totals = rest
     layer = pl.program_id(0)
     last = pl.num_programs(0) - 1
     ntiles = mid.shape[2] // 8
@@ -325,53 +328,68 @@
 
     has_low = jnp.where(layer == 0, 0.0, 1.0)
     has_high = jnp.where(layer == last, 0.0, 1.0)
-    scales = {0: jnp.where(layer == 0, 1.0, 0.0), -1: jnp.where(layer == 1, 1.0, 0.0)}
+    scale = jnp.where(layer == 1, 1.0, 0.0)
     pinned = jnp.logical_and(layer == 0, where_ref[1] == 1)
 
-    for t in range(ntiles):
-        at = slice(8 * t, 8 * t + 8)
-
-        def load(c, side):
-            if c == 3:
-                return s_refs[side][0, at, :]
-            value = f_refs[side][c, 0, at, :]
-            if first_sweep and c == 0 and side <= 0:
-                value = value + scales[side] * surface[8 * t + 8 : 8 * t + 16, :]
-            return value
-
-        def beside(inside, row, f_edge, s_edge):
-            def get(c):
+    def sweep():
+        for t in range(ntiles):
+            at = slice(8 * t, 8 * t + 8)
+
+            def load(c, side):
                 if c == 3:
+                    return s_refs[side][0, at, :]
+                value = f_refs[side][c, 0, at, :]
+                if first_sweep and c == 0 and side < 0:
+                    value = value + scale * surface[8 * t + 8 : 8 * t + 16, :]
+                return value
+
+            def beside(inside, row, f_edge, s_edge):
+                def get(c):
+                    if c == 3:
+                        if inside:
+                            return s_mid[0, row : row + 1, :]
+                        return s_edge[0, pl.ds(layer, 1), :]
                     if inside:
-                        return s_mid[0, row : row + 1, :]
-                    return s_edge[0, pl.ds(layer, 1), :]
-                value = mid[c, 0, row : row + 1, :] if inside else f_edge[c, pl.ds(layer, 1), :]
-                if first_sweep and c == 0:
-                    value = value + scales[0] * surface[row + 8 : row + 9, :]
-                return value
-            return get
-
-        above = beside(t > 0, 8 * t - 1, before, s_before)
-        below = beside(t < ntiles - 1, 8 * t + 8, after, s_after)
-
-        def rolled(c, here):
-            yield jnp.where(row == 7, below(c), pltpu.roll(here, 7, 0))
-            yield jnp.where(row == 0, above(c), pltpu.roll(here, 1, 0))
-
-        sums, total, centers = relax_tile(load, rolled, has_high, has_low)
-        inverse = jnp.where(outermost, 1.0, 1.0 / total)
-        outs = [part * inverse for part in sums]
-        outs[0] = jnp.where(pinned, centers[0], outs[0])
-        for c in range(3):
-            out[c, 0, at, :] = outs[c]
-
-        @pl.when(outermost)
-        def _():
-            totals[0, at, :] = total
-
-
-def relax_layers(position, field, stiffness, before, after, s_before, s_after, surface,
-                 own=()):
+                        return mid[c, 0, row : row + 1, :]
+                    return f_edge[c, pl.ds(layer, 1), :]
+                return get
+
+            above = beside(t > 0, 8 * t - 1, before, s_before)
+            below = beside(t < ntiles - 1, 8 * t + 8, after, s_after)
+
+            def rolled(c, here):
+                yield jnp.where(row == 7, below(c), pltpu.roll(here, 7, 0))
+                yield jnp.where(row == 0, above(c), pltpu.roll(here, 1, 0))
+
+            sums, total, centers = relax_tile(load, rolled, has_high, has_low)
+            inverse = 1.0 / total
+            if not first_sweep:
+                inverse = jnp.where(outermost, 1.0, inverse)
+            outs = [part * inverse for part in sums]
+            if not first_sweep:
+                outs[0] = jnp.where(pinned, centers[0], outs[0])
+                totals[0, at, :] = total
+            for c in range(3):
+                out[c, 0, at, :] = outs[c]
+
+    if not first_sweep:
+        sweep()
+        return
+    pl.when(jnp.logical_not(outermost))(sweep)
+
+    @pl.when(layer == last)
+    def _():
+        out[:, 0] = face_last[...]
+
+    @pl.when(layer == 0)
+    def _():
+        out[1:3, 0] = face_first[1:3]
+        held = mid[0, 0] + surface[8 : 8 + 8 * ntiles, :]
+        out[0, 0] = jnp.where(where_ref[1] == 1, held, face_first[0])
+
+
+def relax_layers(position, field, stiffness, before, after, s_before, s_after, surface=None,
+                 faces=(), own=()):
     _, layers, rows, width = field.shape
     first_sweep = surface is not None
     whole = lambda shape: pl.BlockSpec(shape, lambda i, *_: (0,) * len(shape))
@@ -384,14 +402,15 @@
     args = [field] * 3 + [stiffness] * 3 + [before, after, s_before, s_after]
     in_specs = [f_spec(k) for k in sides] + [s_spec(k) for k in sides]
     in_specs += [f_edge, f_edge, s_edge, s_edge]
-    out_shape = [jax.ShapeDtypeStruct(field.shape, jnp.float32),
-                 jax.ShapeDtypeStruct((2, rows, width), jnp.float32)]
-    out_specs = [f_spec(0),
-                 pl.BlockSpec((1, rows, width), lambda i, *_: (i // (layers // 2), 0, 0))]
-    if first_sweep:
-        args.append(surface)
-        in_specs.append(whole(surface.shape))
-        args += [before, after, *own]
+    out_shape = [jax.ShapeDtypeStruct(field.shape, jnp.float32)]
+    out_specs = [f_spec(0)]
+    if not first_sweep:
+        out_shape.append(jax.ShapeDtypeStruct((2, rows, width), jnp.float32))
+        out_specs.append(
+            pl.BlockSpec((1, rows, width), lambda i, *_: (jnp.minimum(i, 1), 0, 0)))
+    else:
+        args += [surface, *faces, before, after, *own]
+        in_specs += [whole(surface.shape)] + [whole((3, rows, width))] * 2
         near = pl.BlockSpec((4, layers, width), lambda i, *_: (0, 0, 0))
         far = pl.BlockSpec((4, layers, width), lambda i, *_: (1, 0, 0))
         in_specs += [far, far, near, near]
@@ -408,62 +427,117 @@
     )(position, *args)
 
 
-def finish_first_kernel(face, *refs):
-    where_ref, sums, s_here, totals, outer, s_outer = refs[:6]
-    out, send, first_row, last_row = refs[-4:]
+def face_sums_kernel(here, inside, s_here, s_inside, sums, totals):
+    ntiles = here.shape[2] // 8
+    row = lax.broadcasted_iota(jnp.int32, (8, 1), 0)
+    for t in range(ntiles):
+        at = slice(8 * t, 8 * t + 8)
+
+        def load(c, side):
+            if side == 0:
+                return s_here[0, at, :] if c == 3 else here[c, 0, at, :]
+            return s_inside[0, at, :] if c == 3 else inside[c, 0, at, :]
+
+        def beside(c, tile):
+            def take(k, missing, own):
+                if missing:
+                    return -s_here[0, own : own + 1, :] if c == 3 else 0.0
+                return s_here[0, k : k + 1, :] if c == 3 else here[c, 0, k : k + 1, :]
+
+            below = take(8 * t + 8, t == ntiles - 1, 8 * t + 7)
+            above = take(8 * t - 1, t == 0, 8 * t)
+            yield jnp.where(row == 7, below, pltpu.roll(tile, 7, 0))
+            yield jnp.where(row == 0, above, pltpu.roll(tile, 1, 0))
+
+        parts, total, _ = relax_tile(load, beside, 1.0, 0.0)
+        for c in range(3):
+            sums[c, 0, at, :] = parts[c]
+        totals[0, at, :] = total
+
+
+def face_sums(field, stiffness):
+    _, layers, rows, width = field.shape
+    outer = lambda i: i * (layers - 1)
+    inner = lambda i: 1 + i * (layers - 3)
+    f_spec = lambda at: pl.BlockSpec((3, 1, rows, width), lambda i: (0, at(i), 0, 0))
+    s_spec = lambda at: pl.BlockSpec((1, rows, width), lambda i: (at(i), 0, 0))
+    itself = lambda i: i
+    return pl.pallas_call(
+        face_sums_kernel,
+        name="face_sums",
+        grid=(2,),
+        in_specs=[f_spec(outer), f_spec(inner), s_spec(outer), s_spec(inner)],
+        out_specs=[f_spec(itself), s_spec(itself)],
+        out_shape=[jax.ShapeDtypeStruct((3, 2, rows, width), jnp.float32),
+                   jax.ShapeDtypeStruct((2, rows, width), jnp.float32)],
+        compiler_params=pltpu.CompilerParams(vmem_limit_bytes=VMEM_LIMIT),
+    )(field, field, stiffness, stiffness)
+
+
+def finish_first_kernel(sums, s_here, totals, low, high, s_low, s_high, before, after,
+                        s_before, s_after, send_first, send_last, first_row, last_row):
     ntiles = sums.shape[2] // 8
-    pinned = where_ref[1] == 1
-    if len(refs) > 10:
-        first_row[...] = refs[6][...]
-        last_row[...] = refs[7][...]
-    else:
+    row = lax.broadcasted_iota(jnp.int32, (8, 1), 0)
+
+    def one(face, outer, s_outer, send):
+        layer = face * (s_before.shape[1] - 1)
+        for t in range(ntiles):
+            at = slice(8 * t, 8 * t + 8)
+            here = s_here[0, at, :]
+            weight = here + s_outer[0, at, :]
+            total = totals[0, at, :] + weight
+            values = [sums[c, 0, at, :] + weight * outer[c, at, :] for c in range(3)]
+            for wanted, k, f_edge, s_edge in ((0, 0, before, s_before),
+                                              (ntiles - 1, 7, after, s_after)):
+                if t == wanted:
+                    side = jnp.where(row == k, here + s_edge[0, layer : layer + 1, :], 0.0)
+                    total = total + side
+                    for c in range(3):
+                        values[c] = values[c] + side * f_edge[c, layer : layer + 1, :]
+            inverse = 1.0 / total
+            for c in range(3):
+                value = values[c] * inverse
+                send[c, at, :] = value
+                k = 2 * c + face
+                if t == 0:
+                    first_row[k : k + 1, :] = value[0:1]
+                if t == ntiles - 1:
+                    last_row[k : k + 1, :] = value[7:8]
+
+    step = pl.program_id(0)
+
+    @pl.when(step == 0)
+    def _():
         first_row[...] = jnp.zeros_like(first_row)
         last_row[...] = jnp.zeros_like(last_row)
-    for t in range(ntiles):
-        at = slice(8 * t, 8 * t + 8)
-        weight = s_here[0, at, :] + s_outer[0, at, :]
-        inverse = 1.0 / (totals[0, at, :] + weight)
-        for c in range(3):
-            so_far = sums[c, 0, at, :]
-            value = (so_far + weight * outer[c, at, :]) * inverse
-            if face == 0 and c == 0:
-                value = jnp.where(pinned, so_far, value)
-            out[c, 0, at, :] = value
-            send[c, at, :] = value
-            k = 2 * c + face
-            if t == 0:
-                first_row[k : k + 1, :] = value[0:1]
-            if t == ntiles - 1:
-                last_row[k : k + 1, :] = value[7:8]
-
-
-def finish_first(position, face, field, stiffness, totals, outer, edges):
-    _, layers, rows, width = field.shape
-    layer = face * (layers - 1)
-    block = lambda shape, *at: pl.BlockSpec(shape, lambda i, *_: at)
-    plane = block((3, rows, width), 0, 0, 0)
-    own = block((3, 1, rows, width), 0, layer, 0, 0)
-    edge = block((8, width), 0, 0)
-    args = [field, stiffness, totals, outer, outer]
-    in_specs = [own, block((1, rows, width), layer, 0, 0), block((1, rows, width), face, 0, 0),
-                plane, block((1, rows, width), 3, 0, 0)]
-    if edges is not None:
-        args += edges
-        in_specs += [edge, edge]
+        one(0, low, s_low, send_first)
+
+    pl.when(step == 1)(lambda: one(1, high, s_high, send_last))
+
+
+def finish_first(sums, stiffness, totals, low, high, before, after):
+    layers = stiffness.shape[0]
+    rows, width = sums.shape[2:]
+    block = lambda shape, at: pl.BlockSpec(shape, lambda i: at(i))
+    plane = block((3, rows, width), lambda i: (0, 0, 0))
+    s_plane = block((1, rows, width), lambda i: (3, 0, 0))
+    edge = block((8, width), lambda i: (0, 0))
+    f_edge = block((3, layers, width), lambda i: (0, 0, 0))
+    s_edge = block((1, layers, width), lambda i: (3, 0, 0))
+    face_shape = jax.ShapeDtypeStruct((3, rows, width), jnp.float32)
     edge_shape = jax.ShapeDtypeStruct((8, width), jnp.float32)
     return pl.pallas_call(
-        functools.partial(finish_first_kernel, face),
+        finish_first_kernel,
         name="finish_first",
-        grid_spec=pltpu.PrefetchScalarGridSpec(
-            num_scalar_prefetch=1, grid=(1,), in_specs=in_specs,
-            out_specs=[own, plane, edge, edge],
-        ),
-        out_shape=[jax.ShapeDtypeStruct(field.shape, jnp.float32),
-                   jax.ShapeDtypeStruct((3, rows, width), jnp.float32),
-                   edge_shape, edge_shape],
-        input_output_aliases={1: 0},
+        grid=(2,),
+        in_specs=[block((3, 1, rows, width), lambda i: (0, i, 0, 0)),
+                  block((1, rows, width), lambda i: (i * (layers - 1), 0, 0)),
+                  block((1, rows, width), lambda i: (i, 0, 0)),
+                  plane, plane, s_plane, s_plane, f_edge, f_edge, s_edge, s_edge],
+        out_specs=[plane, plane, edge, edge],
+        out_shape=[face_shape, face_shape, edge_shape, edge_shape],
         compiler_params=pltpu.CompilerParams(vmem_limit_bytes=VMEM_LIMIT),
-    )(position, *args)
+    )(sums, stiffness, totals, low, high, low, high, before, after, before, after)
 
 
 def finish_second_kernel(where_ref, sums, s_here, totals, low, high, s_low, s_high,
@@ -543,33 +617,28 @@
         [lax.axis_index("tan"), (lax.axis_index("depth") == 0).astype(jnp.int32)]
     ).astype(jnp.int32)
 
+    face_first, face_last = pack_faces(displacement, stiffness)
+    low, high = shift_both(face_last, face_first, "depth")
     row_first, row_last = pack_rows(displacement, stiffness)
+    before, after = shift_both(row_last, row_first, "tan")
     wear = archard(wear_class, pressure, slip_speed, rate_table)
-    other = swap_halves(wear)
-    before, after = shift_both(row_last, row_first, "tan")
-    face_first, face_last = pack_faces(displacement, stiffness, row_first)
-    face_first, face_last, other, before, after = lax.optimization_barrier(
-        (face_first, face_last, other, before, after)
-    )
-    low, high = shift_both(face_last, face_first, "depth")
-    wear = gather_wear(wear, other)
+    wear = gather_wear(wear, swap_halves(wear))
     surface = paint(position, tile_owner, active_count, wear, node_list,
                     node_cell.reshape(-1, 128), rows, width, wear_class.shape[0])
-
-    first, totals, before_2, after_2 = relax_layers(
+    sums, totals = face_sums(displacement, stiffness)
+
+    low, high, surface = lax.optimization_barrier((low, high, surface))
+    face_first, face_last, edge_first, edge_last = finish_first(
+        sums, stiffness, totals, low, high, before, after
+    )
+    low_2, high_2 = shift_both(face_last, face_first, "depth")
+    edge_before, edge_after = shift_both(edge_last, edge_first, "tan")
+    first, before_2, after_2 = relax_layers(
         position, displacement, stiffness, before, after, before, after, surface,
-        (row_first, row_last),
+        (face_first, face_last), (row_first, row_last),
     )
-    first, send_last, edge_first, edge_last = finish_first(
-        position, 1, first, stiffness, totals, high, None
-    )
-    first, send_first, edge_first, edge_last = finish_first(
-        position, 0, first, stiffness, totals, low, (edge_first, edge_last)
-    )
-    low_2, high_2 = shift_both(send_last, send_first, "depth")
-    edge_before, edge_after = shift_both(edge_last, edge_first, "tan")
     result, totals = relax_layers(
-        position, first, stiffness, before_2, after_2, before, after, None
+        position, first, stiffness, before_2, after_2, before, after
     )
     return finish_second(position, result, stiffness, totals, low_2, high_2, low, high,
                          edge_before, edge_after, before, after)

time: 125 us -> 141 us (1.13)
  the two profiles are of different devices: /device:TPU:22 before, /device:TPU:4 now
where the time goes in v5:
time: 141 us; the launch traced here: 139 us
  Pallas kernels  55.5 us (39%)
  waiting for transfers between devices  40.1 us (28%)
  starting transfers between devices  28.7 us (20%)
  blocking collectives  11.6 us (8%)
  local copies, waits for them, and re-layouts  2.76 us (2%)
    ppermute x1, waiting for transfers between devices, swap_halves(): return lax.ppermute(wear, 'tan', [(i, i ^ 2) for i in range(size)])  40 us
    ppermute x8, starting transfers between devices, shift_both(): return (lax.ppermute(last, axis, up), lax.ppermute(first, axis, down))  28.6 us
    pallas_call x2, Pallas kernels, relax_layers(): pl.pallas_call(functools.partial(layer_kernel, first_sweep), name='relax_...  28.3 us
    all_gather x1, blocking collectives, gather_wear(): lax.all_gather(both, 'tan', axis=0, axis_index_groups=groups, tiled=True)  11.6 us
    pallas_call x1, Pallas kernels, paint(): pl.pallas_call(functools.partial(paint_kernel, shard_tiles), name='paint_...  10.8 us
    pallas_call x1, Pallas kernels, finish_second(): pl.pallas_call(finish_second_kernel, name='finish_second', grid_spec=pltp...  3.34 us
    pallas_call x1, Pallas kernels, face_sums(): pl.pallas_call(face_sums_kernel, name='face_sums', grid=(2,), in_specs=[f...  3.22 us
    pallas_call x1, Pallas kernels, pack_rows(): pl.pallas_call(rows_kernel, name='pack_rows', grid=(1,), in_specs=[f_spec...  3.22 us
  transfers between devices with their start and end apart: 9, of which 1 were waited for; matrix products, arithmetic and copies ran while one was open for 0% of the time, Pallas kernels for 34%

profile of v5, /device:TPU:4, one launch (start us, length us, event | category | flops | bytes accessed | tf_op | source)
XLA Modules:
  0.0 138.9 jit_solution(6770802767884545330)
XLA Ops:
  0.0 0.0 copy-start
  0.0 1.6 %copy-done = f32[8,32,2048]{2,1,0:T(8,128)S(1)} copy-done((f32[8,32,2048]{2,1,0:T(8,128)S(1)}, f32[8,32,2048]{2,1,0:T(8,128)}, u32[]{:S(2)}) %copy-start) | copy-done | bytes 2097176
  1.6 2.8 %pack_faces.1 = (f32[4,32,2048]{2,1,0:T(8,128)}, f32[4,32,2048]{2,1,0:T(8,128)}) custom-call(f32[3,8,32,2048]{3,2,1,0:T(8,128)} %refs_3_.1, f32[8,32,2048]{2,1,0:T(8,128)S(1)} %copy-done), custom_call_target="tpu_custom_call" | custom-call | tf_op jit(solution)/shard_map/pack_faces/pallas_call | solution.py:87
  4.4 6.7 %collective-permute-start.2 = (f32[4,32,2048]{2,1,0:T(8,128)}, f32[4,32,2048]{2,1,0:T(8,128)}, u32[]{:S(2)}, u32[]{:S(2)}) collective-permute-start(f32[4,32,2048]{2,1,0:T(8,128)} %get-tuple-element.25), channel_id=1, source_target_pairs={{0,16},{16,32},{32,48},{48,64},{64,80},{80,96},{96,112},{1,17},{17... | collective-permute-start | bytes 3145736 | tf_op jit(solution)/shard_map/ppermute | solution.py:20
  11.1 0.0 copy-start.1
  11.1 1.4 %collective-permute-start.3 = (f32[4,32,2048]{2,1,0:T(8,128)}, f32[4,32,2048]{2,1,0:T(8,128)}, u32[]{:S(2)}, u32[]{:S(2)}) collective-permute-start(f32[4,32,2048]{2,1,0:T(8,128)} %get-tuple-element.26), channel_id=1, source_target_pairs={{16,0},{32,16},{48,32},{64,48},{80,64},{96,80},{112,96},{17,1},{33... | collective-permute-start | bytes 3145736 | tf_op jit(solution)/shard_map/ppermute | solution.py:20
  12.5 3.2 %pack_rows.1 = (f32[8,8,2048]{2,1,0:T(8,128)}, f32[8,8,2048]{2,1,0:T(8,128)}) custom-call(f32[3,8,32,2048]{3,2,1,0:T(8,128)} %refs_3_.1, f32[8,32,2048]{2,1,0:T(8,128)S(1)} %copy-done, f32[3,8,32,2048]{3,2,1,0:T(8,128)} %refs_3_.1, f32[8,32,2048]{2,1,0:T(8,128)S(1)} %copy-done), custom_call_target="tpu_custom_call" | custom-call | tf_op jit(solution)/shard_map/pack_rows/pallas_call | solution.py:60
  15.7 1.9 %collective-permute-start = (f32[8,8,2048]{2,1,0:T(8,128)}, f32[8,8,2048]{2,1,0:T(8,128)S(1)}, u32[]{:S(2)}, u32[]{:S(2)}) collective-permute-start(f32[8,8,2048]{2,1,0:T(8,128)} %get-tuple-element.23.refs_17_), channel_id=1, source_target_pairs={{0,1},{1,2},{2,3},{3,4},{4,5},{5,6},{6,7},{7,8},{8,9},{9,10},{10,1... | collective-permute-start | bytes 1572872 | tf_op jit(solution)/shard_map/ppermute | solution.py:20
  17.7 4.5 %collective-permute-start.1 = (f32[8,8,2048]{2,1,0:T(8,128)}, f32[8,8,2048]{2,1,0:T(8,128)S(1)}, u32[]{:S(2)}, u32[]{:S(2)}) collective-permute-start(f32[8,8,2048]{2,1,0:T(8,128)} %get-tuple-element.24.refs_16_), channel_id=1, source_target_pairs={{1,0},{2,1},{3,2},{4,3},{5,4},{6,5},{7,6},{8,7},{9,8},{10,9},{11,1... | collective-permute-start | bytes 1572872 | tf_op jit(solution)/shard_map/ppermute | solution.py:20
  22.2 1.4 %archard.1 = f32[32,128]{1,0:T(8,128)} custom-call(f32[8]{0:T(128)} %rates_ref.1, s32[32,128]{1,0:T(8,128)} %class_ref.1, f32[32,128]{1,0:T(8,128)} %contact_ref.1, f32[32,128]{1,0:T(8,128)} %sliding_ref.1), custom_call_target="tpu_custom_call" | custom-call | tf_op jit(solution)/shard_map/archard/pallas_call | solution.py:34
  23.6 0.1 collective-permute-start.4
  23.8 0.1 pad_add_fusion.where_ref.refs_0_
  23.8 0.0 copy-done.1
  23.8 0.0 copy-start.8
  23.8 0.0 copy-start.3
  23.8 0.0 copy-start.5
  23.8 0.0 copy-start.6
  23.9 0.0 copy-start.7
  23.9 3.2 %face_sums.1 = (f32[3,2,32,2048]{3,2,1,0:T(8,128)S(1)}, f32[2,32,2048]{2,1,0:T(8,128)S(1)}) custom-call(f32[3,8,32,2048]{3,2,1,0:T(8,128)} %refs_3_.1, f32[3,8,32,2048]{3,2,1,0:T(8,128)} %refs_3_.1, f32[8,32,2048]{2,1,0:T(8,128)S(1)} %copy-done.1, f32[8,32,2048]{2,1,0:T(8,128)S(1)} %copy-done.1), custom_call_target="tpu_custom_call" | custom-call | tf_op jit(solution)/shard_map/face_sums/pallas_call | solution.py:465
  27.1 0.0 copy-start.4
  27.1 1.1 copy-done.4
  28.2 40.0 %collective-permute-done.4 = f32[32,128]{1,0:T(8,128)S(1)} collective-permute-done((f32[32,128]{1,0:T(8,128)}, f32[32,128]{1,0:T(8,128)S(1)}, u32[]{:S(2)}, u32[]{:S(2)}) %collective-permute-start.4) | collective-permute-done | bytes 16416 | tf_op jit(solution)/shard_map/ppermute | solution.py:103
  68.3 0.0 copy-done.8
  68.3 11.6 %all_gather.3.wear_ref = f32[512,128]{1,0:T(8,128)S(1)} all-gather(f32[64,128]{1,0:T(8,128)S(1)} %pad_maximum_fusion), channel_id=1, replica_groups={{0,1,4,5,8,9,12,13},{2,3,6,7,10,11,14,15},{16,17,20,21,24,25,28,29},{18..., dimensions={0}, use_global_device_ids=true | all-gather | bytes 294912 | tf_op jit(solution)/shard_map/all_gather | solution.py:110
  79.9 0.0 copy-done.3
  79.9 0.0 copy-done.5
  79.9 0.0 copy-done.6
  79.9 0.0 copy-done.7
  79.9 10.8 %paint_band.1.refs_11_ = f32[48,2048]{1,0:T(8,128)S(1)} custom-call(s32[2]{0:T(128)S(1)} %pad_add_fusion.where_ref.refs_0_, s32[512]{0:T(512)S(1)} %copy-done.6, s32[512]{0:T(512)S(1)} %copy-done.7, f32[512,128]{1,0:T(8,128)S(1)} %all_gather.3.wear_ref, s32[512,128]{1,0:T(8,128)S(1)} %copy-done.5, s32[8192,128]{1,0:T(8,128)S(1)} %bitcast.3), custom_call_target="tpu_custom_call" | custom-call | tf_op jit(solution)/shard_map/paint_band/pallas_call | solution.py:237
  90.7 0.0 collective-permute-done.2.low.s_low
  90.7 0.0 collective-permute-done.3.high.s_high
  90.7 0.0 collective-permute-done.before.s_before.refs_7_.refs_9_.refs_14_
  90.7 0.0 collective-permute-done.1.after.s_after.refs_8_.refs_10_.refs_15_
  90.8 2.4 %finish_first.1 = (f32[3,32,2048]{2,1,0:T(8,128)S(1)}, f32[3,32,2048]{2,1,0:T(8,128)S(1)}, f32[8,2048]{1,0:T(8,128)S(1)}, f32[8,2048]{1,0:T(8,128)S(1)}) custom-call(f32[3,2,32,2048]{3,2,1,0:T(8,128)} %copy-done.4, f32[8,32,2048]{2,1,0:T(8,128)} %s_here.5, f32[2,32,2048]{2,1,0:T(8,128)S(1)} %get-tuple-element.29.totals, ...), custom_call_target="tpu_custom_call" | custom-call | tf_op jit(solution)/shard_map/finish_first/pallas_call | solution.py:529
  93.2 1.3 collective-permute-start.6
  94.5 6.1 %collective-permute-start.5 = (f32[3,32,2048]{2,1,0:T(8,128)S(1)}, f32[3,32,2048]{2,1,0:T(8,128)S(1)}, u32[]{:S(2)}, u32[]{:S(2)}) collective-permute-start(f32[3,32,2048]{2,1,0:T(8,128)S(1)} %get-tuple-element.33.refs_13_), channel_id=1, source_target_pairs={{0,16},{16,32},{32,48},{48,64},{64,80},{80,96},{96,112},{1,17},{17... | collective-permute-start | bytes 2359304 | tf_op jit(solution)/shard_map/ppermute | solution.py:20
  100.6 2.8 %collective-permute-start.7 = (f32[8,2048]{1,0:T(8,128)S(1)}, f32[8,2048]{1,0:T(8,128)S(1)}, u32[]{:S(2)}, u32[]{:S(2)}) collective-permute-start(f32[8,2048]{1,0:T(8,128)S(1)} %get-tuple-element.39), channel_id=1, source_target_pairs={{0,1},{1,2},{2,3},{3,4},{4,5},{5,6},{6,7},{7,8},{8,9},{9,10},{10,1... | collective-permute-start | bytes 196616 | tf_op jit(solution)/shard_map/ppermute | solution.py:20
  103.4 0.0 copy-start.2
  103.4 3.8 %collective-permute-start.8 = (f32[8,2048]{1,0:T(8,128)S(1)}, f32[8,2048]{1,0:T(8,128)S(1)}, u32[]{:S(2)}, u32[]{:S(2)}) collective-permute-start(f32[8,2048]{1,0:T(8,128)S(1)} %get-tuple-element.40), channel_id=1, source_target_pairs={{1,0},{2,1},{3,2},{4,3},{5,4},{6,5},{7,6},{8,7},{9,8},{10,9},{11,1... | collective-permute-start | bytes 196616 | tf_op jit(solution)/shard_map/ppermute | solution.py:20
  107.2 14.8 %relax_layers_first.1 = (f32[3,8,32,2048]{3,2,1,0:T(8,128)}, f32[3,8,2048]{2,1,0:T(8,128)S(1)}, f32[3,8,2048]{2,1,0:T(8,128)S(1)}) custom-call(s32[2]{0:T(128)S(1)} %pad_add_fusion.where_ref.refs_0_, f32[3,8,32,2048]{3,2,1,0:T(8,128)} %refs_3_.1, f32[3,8,32,2048]{3,2,1,0:T(8,128)} %refs_3_.1, f32[3,8,32,2048]{3,2,1,0:T(8,128)} %refs_3_.1, ...), custom_call_target="tpu_custom_call" | custom-call | tf_op jit(solution)/shard_map/relax_layers_first/pallas_call | solution.py:419
  122.0 0.0 copy-done.2
  122.0 13.5 %relax_layers_second.1 = (f32[3,8,32,2048]{3,2,1,0:T(8,128)}, f32[2,32,2048]{2,1,0:T(8,128)S(1)}) custom-call(s32[2]{0:T(128)S(1)} %pad_add_fusion.where_ref.refs_0_, f32[3,8,32,2048]{3,2,1,0:T(8,128)} %get-tuple-element.34.refs_1_.refs_2_.refs_3_, f32[3,8,32,2048]{3,2,1,0:T(8,128)} %get-tuple-element.34.refs_1_.refs_2_.refs_3_, ...), custom_call_target="tpu_custom_call" | custom-call | tf_op jit(solution)/shard_map/relax_layers_second/pallas_call | solution.py:419
  135.5 0.0 collective-permute-done.7.before
  135.6 0.0 collective-permute-done.8.after
  135.6 0.0 collective-permute-done.6.high
  135.6 0.0 collective-permute-done.5.low
  135.6 3.3 %finish_second.1 = f32[3,8,32,2048]{3,2,1,0:T(8,128)} custom-call(s32[2]{0:T(128)S(1)} %pad_add_fusion.where_ref.refs_0_, f32[3,8,32,2048]{3,2,1,0:T(8,128)} %get-tuple-element.37.sums, f32[8,32,2048]{2,1,0:T(8,128)} %s_here.5, f32[2,32,2048]{2,1,0:T(8,128)S(1)} %get-tuple-element.38.totals, ...), custom_call_target="tpu_custom_call", output_to_operand_aliasing={{}: (1, {})} | custom-call | tf_op jit(solution)/shard_map/finish_second/pallas_call | solution.py:586
  (1 shorter events, 0.0 us)
Async XLA Ops:
  0.0 1.6 %copy-start = (f32[8,32,2048]{2,1,0:T(8,128)S(1)}, f32[8,32,2048]{2,1,0:T(8,128)}, u32[]{:S(2)}) copy-start(f32[8,32,2048]{2,1,0:T(8,128)} %s_here.5) | copy-start | bytes 6291460
  4.4 86.4 %collective-permute-start.2 = (f32[4,32,2048]{2,1,0:T(8,128)}, f32[4,32,2048]{2,1,0:T(8,128)}, u32[]{:S(2)}, u32[]{:S(2)}) collective-permute-start(f32[4,32,2048]{2,1,0:T(8,128)} %get-tuple-element.25), channel_id=1, source_target_pairs={{0,16},{16,32},{32,48},{48,64},{64,80},{80,96},{96,112},{1,17},{17... | collective-permute-start | bytes 3145736 | tf_op jit(solution)/shard_map/ppermute | solution.py:20
  11.1 12.7 %copy-start.1 = (f32[8,32,2048]{2,1,0:T(8,128)S(1)}, f32[8,32,2048]{2,1,0:T(8,128)}, u32[]{:S(2)}) copy-start(f32[8,32,2048]{2,1,0:T(8,128)} %s_here.5) | copy-start | bytes 6291460
  11.1 79.6 %collective-permute-start.3 = (f32[4,32,2048]{2,1,0:T(8,128)}, f32[4,32,2048]{2,1,0:T(8,128)}, u32[]{:S(2)}, u32[]{:S(2)}) collective-permute-start(f32[4,32,2048]{2,1,0:T(8,128)} %get-tuple-element.26), channel_id=1, source_target_pairs={{16,0},{32,16},{48,32},{64,48},{80,64},{96,80},{112,96},{17,1},{33... | collective-permute-start | bytes 3145736 | tf_op jit(solution)/shard_map/ppermute | solution.py:20
  15.7 75.0 %collective-permute-start = (f32[8,8,2048]{2,1,0:T(8,128)}, f32[8,8,2048]{2,1,0:T(8,128)S(1)}, u32[]{:S(2)}, u32[]{:S(2)}) collective-permute-start(f32[8,8,2048]{2,1,0:T(8,128)} %get-tuple-element.23.refs_17_), channel_id=1, source_target_pairs={{0,1},{1,2},{2,3},{3,4},{4,5},{5,6},{6,7},{7,8},{8,9},{9,10},{10,1... | collective-permute-start | bytes 1572872 | tf_op jit(solution)/shard_map/ppermute | solution.py:20
  17.7 73.1 %collective-permute-start.1 = (f32[8,8,2048]{2,1,0:T(8,128)}, f32[8,8,2048]{2,1,0:T(8,128)S(1)}, u32[]{:S(2)}, u32[]{:S(2)}) collective-permute-start(f32[8,8,2048]{2,1,0:T(8,128)} %get-tuple-element.24.refs_16_), channel_id=1, source_target_pairs={{1,0},{2,1},{3,2},{4,3},{5,4},{6,5},{7,6},{8,7},{9,8},{10,9},{11,1... | collective-permute-start | bytes 1572872 | tf_op jit(solution)/shard_map/ppermute | solution.py:20
  23.6 44.6 %collective-permute-start.4 = (f32[32,128]{1,0:T(8,128)}, f32[32,128]{1,0:T(8,128)S(1)}, u32[]{:S(2)}, u32[]{:S(2)}) collective-permute-start(f32[32,128]{1,0:T(8,128)} %archard.1), channel_id=1, source_target_pairs={{0,2},{1,3},{2,0},{3,1},{4,6},{5,7},{6,4},{7,5},{8,10},{9,11},{10,... | collective-permute-start | bytes 49160 | tf_op jit(solution)/shard_map/ppermute | solution.py:103
  23.8 44.4 %copy-start.8 = (f32[32,128]{1,0:T(8,128)S(1)}, f32[32,128]{1,0:T(8,128)}, u32[]{:S(2)}) copy-start(f32[32,128]{1,0:T(8,128)} %archard.1) | copy-start | bytes 49156
  23.8 56.1 %copy-start.3 = (s32[1048576]{0:T(1024)S(1)}, s32[1048576]{0:T(1024)}, u32[]{:S(2)}) copy-start(s32[1048576]{0:T(1024)} %param.19) | copy-start | bytes 12582916
  23.8 56.1 %copy-start.5 = (s32[512,128]{1,0:T(8,128)S(1)}, s32[512,128]{1,0:T(8,128)}, u32[]{:S(2)}) copy-start(s32[512,128]{1,0:T(8,128)} %list_ref.1) | copy-start | bytes 786436
  23.8 56.1 %copy-start.6 = (s32[512]{0:T(512)S(1)}, s32[512]{0:T(512)}, u32[]{:S(2)}) copy-start(s32[512]{0:T(512)} %owner_ref.1) | copy-start | bytes 6148
  23.9 56.1 %copy-start.7 = (s32[512]{0:T(512)S(1)}, s32[512]{0:T(512)}, u32[]{:S(2)}) copy-start(s32[512]{0:T(512)} %count_ref.1) | copy-start | bytes 6148
  27.1 1.1 copy-start.4
  93.2 42.4 %collective-permute-start.6 = (f32[3,32,2048]{2,1,0:T(8,128)S(1)}, f32[3,32,2048]{2,1,0:T(8,128)S(1)}, u32[]{:S(2)}, u32[]{:S(2)}) collective-permute-start(f32[3,32,2048]{2,1,0:T(8,128)S(1)} %get-tuple-element.32.refs_12_), channel_id=1, source_target_pairs={{16,0},{32,16},{48,32},{64,48},{80,64},{96,80},{112,96},{17,1},{33... | collective-permute-start | bytes 2359304 | tf_op jit(solution)/shard_map/ppermute | solution.py:20
  94.5 41.1 %collective-permute-start.5 = (f32[3,32,2048]{2,1,0:T(8,128)S(1)}, f32[3,32,2048]{2,1,0:T(8,128)S(1)}, u32[]{:S(2)}, u32[]{:S(2)}) collective-permute-start(f32[3,32,2048]{2,1,0:T(8,128)S(1)} %get-tuple-element.33.refs_13_), channel_id=1, source_target_pairs={{0,16},{16,32},{32,48},{48,64},{64,80},{80,96},{96,112},{1,17},{17... | collective-permute-start | bytes 2359304 | tf_op jit(solution)/shard_map/ppermute | solution.py:20
  100.6 35.0 %collective-permute-start.7 = (f32[8,2048]{1,0:T(8,128)S(1)}, f32[8,2048]{1,0:T(8,128)S(1)}, u32[]{:S(2)}, u32[]{:S(2)}) collective-permute-start(f32[8,2048]{1,0:T(8,128)S(1)} %get-tuple-element.39), channel_id=1, source_target_pairs={{0,1},{1,2},{2,3},{3,4},{4,5},{5,6},{6,7},{7,8},{8,9},{9,10},{10,1... | collective-permute-start | bytes 196616 | tf_op jit(solution)/shard_map/ppermute | solution.py:20
  103.4 18.6 %copy-start.2 = (f32[8,32,2048]{2,1,0:T(8,128)S(1)}, f32[8,32,2048]{2,1,0:T(8,128)}, u32[]{:S(2)}) copy-start(f32[8,32,2048]{2,1,0:T(8,128)} %s_here.5) | copy-start | bytes 6291460
  103.4 32.2 %collective-permute-start.8 = (f32[8,2048]{1,0:T(8,128)S(1)}, f32[8,2048]{1,0:T(8,128)S(1)}, u32[]{:S(2)}, u32[]{:S(2)}) collective-permute-start(f32[8,2048]{1,0:T(8,128)S(1)} %get-tuple-element.40), channel_id=1, source_target_pairs={{1,0},{2,1},{3,2},{4,3},{5,4},{6,5},{7,6},{8,7},{9,8},{10,9},{11,1... | collective-permute-start | bytes 196616 | tf_op jit(solution)/shard_map/ppermute | solution.py:20

commit v6 on v5

--- a/solution.py
+++ b/solution.py
@@ -98,16 +98,11 @@
     )(field, stiffness)
 
 
-def swap_halves(wear):
+def gather_wear(wear):
     size = lax.axis_size("tan")
-    return lax.ppermute(wear, "tan", [(i, i ^ 2) for i in range(size)])
-
-
-def gather_wear(wear, other):
-    size = lax.axis_size("tan")
-    both = jnp.concatenate([wear, other], axis=0)
     groups = [[i for i in range(size) if (i // 2) % 2 == half] for half in range(2)]
-    return lax.all_gather(both, "tan", axis=0, axis_index_groups=groups, tiled=True)
+    own = lax.all_gather(wear, "tan", axis=0, axis_index_groups=groups, tiled=True)
+    return own, lax.ppermute(own, "tan", [(i, i ^ 2) for i in range(size)])
 
 
 def three_parts(value):
@@ -170,7 +165,7 @@
             )
             shard = i // shard_tiles
             half = jnp.where((shard // 2) % 2 == (me // 2) % 2, 0, 1)
-            place = (shard // 4) * 4 + (shard % 2) * 2 + half
+            place = half * (ntile // shard_tiles // 2) + (shard // 4) * 2 + shard % 2
             at = place * shard_tiles + i % shard_tiles
             wear = jnp.where(lane < live, wear_ref[pl.ds(at, 1), :], 0.0)
             return i, cell, wear
@@ -300,9 +295,9 @@
 
 
 def layer_kernel(first_sweep, *refs):
-    (where_ref, low, mid, high, s_low, s_mid, s_high, before, after, s_before,
-     s_after) = refs[:11]
-    rest = list(refs[11:])
+    where_ref, f_in, s_in, before, after, s_before, s_after = refs[:7]
+    rest = list(refs[7:-2])
+    f_kept, s_kept = refs[-2:]
     surface = rest.pop(0) if first_sweep else None
     if first_sweep:
         face_first, face_last = rest[:2]
@@ -310,17 +305,22 @@
         extra = rest[2:6] + rest[7:]
     else:
         out, totals = rest
-    layer = pl.program_id(0)
-    last = pl.num_programs(0) - 1
-    ntiles = mid.shape[2] // 8
-    f_refs = {-1: low, 0: mid, 1: high}
-    s_refs = {-1: s_low, 0: s_mid, 1: s_high}
+    step = pl.program_id(0)
+    layer = step - 1
+    last = pl.num_programs(0) - 2
+    slot = step % 2
+    ntiles = f_in.shape[2] // 8
+    mid, s_mid = f_kept.at[1 - slot], s_kept.at[1 - slot]
+    f_refs = {-1: f_kept.at[slot], 0: mid, 1: f_in.at[:, 0]}
+    s_refs = {-1: s_kept.at[slot], 0: s_mid, 1: s_in.at[0]}
     outermost = jnp.logical_or(layer == 0, layer == last)
     row = lax.broadcasted_iota(jnp.int32, (8, 1), 0)
-    if first_sweep:
-
-        @pl.when(layer == 0)
-        def _():
+
+    @pl.when(step == 0)
+    def _():
+        f_kept[1] = f_in[:, 0]
+        s_kept[1] = s_in[0]
+        if first_sweep:
             far_before, far_after, own_first, own_last, out_before, out_after = extra
             relax_outside(out_before, before, s_before, far_before, own_first, surface, 7, row)
             relax_outside(out_after, after, s_after, far_after, own_last, surface,
@@ -337,8 +337,8 @@
 
             def load(c, side):
                 if c == 3:
-                    return s_refs[side][0, at, :]
-                value = f_refs[side][c, 0, at, :]
+                    return s_refs[side][at, :]
+                value = f_refs[side][c, at, :]
                 if first_sweep and c == 0 and side < 0:
                     value = value + scale * surface[8 * t + 8 : 8 * t + 16, :]
                 return value
@@ -347,10 +347,10 @@
                 def get(c):
                     if c == 3:
                         if inside:
-                            return s_mid[0, row : row + 1, :]
+                            return s_mid[row : row + 1, :]
                         return s_edge[0, pl.ds(layer, 1), :]
                     if inside:
-                        return mid[c, 0, row : row + 1, :]
+                        return mid[c, row : row + 1, :]
                     return f_edge[c, pl.ds(layer, 1), :]
                 return get
 
@@ -372,20 +372,24 @@
             for c in range(3):
                 out[c, 0, at, :] = outs[c]
 
-    if not first_sweep:
-        sweep()
-        return
-    pl.when(jnp.logical_not(outermost))(sweep)
-
-    @pl.when(layer == last)
-    def _():
-        out[:, 0] = face_last[...]
-
-    @pl.when(layer == 0)
-    def _():
-        out[1:3, 0] = face_first[1:3]
-        held = mid[0, 0] + surface[8 : 8 + 8 * ntiles, :]
-        out[0, 0] = jnp.where(where_ref[1] == 1, held, face_first[0])
+    if first_sweep:
+        inner = jnp.logical_and(layer > 0, layer < last)
+        pl.when(inner)(sweep)
+
+        @pl.when(layer == last)
+        def _():
+            out[:, 0] = face_last[...]
+
+        @pl.when(layer == 0)
+        def _():
+            out[1:3, 0] = face_first[1:3]
+            held = mid[0] + surface[8 : 8 + 8 * ntiles, :]
+            out[0, 0] = jnp.where(where_ref[1] == 1, held, face_first[0])
+    else:
+        pl.when(layer >= 0)(sweep)
+
+    f_kept[slot] = f_in[:, 0]
+    s_kept[slot] = s_in[0]
 
 
 def relax_layers(position, field, stiffness, before, after, s_before, s_after, surface=None,
@@ -393,21 +397,20 @@
     _, layers, rows, width = field.shape
     first_sweep = surface is not None
     whole = lambda shape: pl.BlockSpec(shape, lambda i, *_: (0,) * len(shape))
-    at = lambda i, k: jnp.clip(i + k, 0, layers - 1)
-    f_spec = lambda k: pl.BlockSpec((3, 1, rows, width), lambda i, *_: (0, at(i, k), 0, 0))
-    s_spec = lambda k: pl.BlockSpec((1, rows, width), lambda i, *_: (at(i, k), 0, 0))
+    came = lambda k: jnp.minimum(k, layers - 1)
+    swept = lambda k: jnp.maximum(k - 1, 0)
+    f_spec = lambda at: pl.BlockSpec((3, 1, rows, width), lambda k, *_: (0, at(k), 0, 0))
     f_edge = whole((3, layers, width))
-    s_edge = pl.BlockSpec((1, layers, width), lambda i, *_: (3, 0, 0))
-    sides = (-1, 0, 1)
-    args = [field] * 3 + [stiffness] * 3 + [before, after, s_before, s_after]
-    in_specs = [f_spec(k) for k in sides] + [s_spec(k) for k in sides]
+    s_edge = pl.BlockSpec((1, layers, width), lambda k, *_: (3, 0, 0))
+    args = [field, stiffness, before, after, s_before, s_after]
+    in_specs = [f_spec(came), pl.BlockSpec((1, rows, width), lambda k, *_: (came(k), 0, 0))]
     in_specs += [f_edge, f_edge, s_edge, s_edge]
     out_shape = [jax.ShapeDtypeStruct(field.shape, jnp.float32)]
-    out_specs = [f_spec(0)]
+    out_specs = [f_spec(swept)]
     if not first_sweep:
         out_shape.append(jax.ShapeDtypeStruct((2, rows, width), jnp.float32))
         out_specs.append(
-            pl.BlockSpec((1, rows, width), lambda i, *_: (jnp.minimum(i, 1), 0, 0)))
+            pl.BlockSpec((1, rows, width), lambda k, *_: (jnp.minimum(swept(k), 1), 0, 0)))
     else:
         args += [surface, *faces, before, after, *own]
         in_specs += [whole(surface.shape)] + [whole((3, rows, width))] * 2
@@ -420,7 +423,9 @@
         functools.partial(layer_kernel, first_sweep),
         name="relax_layers_first" if first_sweep else "relax_layers_second",
         grid_spec=pltpu.PrefetchScalarGridSpec(
-            num_scalar_prefetch=1, grid=(layers,), in_specs=in_specs, out_specs=out_specs
+            num_scalar_prefetch=1, grid=(layers + 1,), in_specs=in_specs, out_specs=out_specs,
+            scratch_shapes=[pltpu.VMEM((2, 3, rows, width), jnp.float32),
+                            pltpu.VMEM((2, rows, width), jnp.float32)],
         ),
         out_shape=out_shape,
         compiler_params=pltpu.CompilerParams(vmem_limit_bytes=VMEM_LIMIT),
@@ -622,17 +627,16 @@
     row_first, row_last = pack_rows(displacement, stiffness)
     before, after = shift_both(row_last, row_first, "tan")
     wear = archard(wear_class, pressure, slip_speed, rate_table)
-    wear = gather_wear(wear, swap_halves(wear))
-    surface = paint(position, tile_owner, active_count, wear, node_list,
-                    node_cell.reshape(-1, 128), rows, width, wear_class.shape[0])
+    wear = gather_wear(wear)
     sums, totals = face_sums(displacement, stiffness)
-
-    low, high, surface = lax.optimization_barrier((low, high, surface))
+    low, high, wear = lax.optimization_barrier((low, high, wear))
     face_first, face_last, edge_first, edge_last = finish_first(
         sums, stiffness, totals, low, high, before, after
     )
     low_2, high_2 = shift_both(face_last, face_first, "depth")
     edge_before, edge_after = shift_both(edge_last, edge_first, "tan")
+    surface = paint(position, tile_owner, active_count, jnp.concatenate(wear), node_list,
+                    node_cell.reshape(-1, 128), rows, width, wear_class.shape[0])
     first, before_2, after_2 = relax_layers(
         position, displacement, stiffness, before, after, before, after, surface,
         (face_first, face_last), (row_first, row_last),

time: 141 us -> 131 us (0.929); the launches traced: 139 us -> 131 us
  waiting for transfers between devices: 40.1 us -> 25.1 us
  blocking collectives: 11.6 us -> 17.9 us
  local copies, waits for them, and re-layouts: 2.76 us -> 4.93 us
  Pallas kernels: 55.5 us -> 54 us
    ppermute x1, waiting for transfers between devices: 40 us -> 25.1 us  [gather_wear(): return (own, lax.ppermute(own, 'tan', [(i, i ^ 2) for i in range(size)]))]
    all_gather x1, blocking collectives: 11.6 us -> 17.9 us  [gather_wear(): lax.all_gather(wear, 'tan', axis=0, axis_index_groups=groups, tiled=True)]
    pallas_call x2, Pallas kernels: 28.3 us -> 24.4 us  [relax_layers(): pl.pallas_call(functools.partial(layer_kernel, first_sweep), name='relax_...]
    unnamed x18 -> x16, local copies, waits for them, and re-layouts: 2.76 us -> 4.93 us
    pallas_call x1, Pallas kernels: 10.8 us -> 12.4 us  [paint(): pl.pallas_call(functools.partial(paint_kernel, shard_tiles), name='paint_...]
where the time goes in v6:
time: 131 us
  Pallas kernels  54 us (41%)
  starting transfers between devices  28.4 us (22%)
  waiting for transfers between devices  25.1 us (19%)
  blocking collectives  17.9 us (14%)
  local copies, waits for them, and re-layouts  4.93 us (4%)
    ppermute x8, starting transfers between devices, shift_both(): return (lax.ppermute(last, axis, up), lax.ppermute(first, axis, down))  28.4 us
    ppermute x1, waiting for transfers between devices, gather_wear(): return (own, lax.ppermute(own, 'tan', [(i, i ^ 2) for i in range(size)]))  25.1 us
    pallas_call x2, Pallas kernels, relax_layers(): pl.pallas_call(functools.partial(layer_kernel, first_sweep), name='relax_...  24.4 us
    all_gather x1, blocking collectives, gather_wear(): lax.all_gather(wear, 'tan', axis=0, axis_index_groups=groups, tiled=True)  17.9 us
    pallas_call x1, Pallas kernels, paint(): pl.pallas_call(functools.partial(paint_kernel, shard_tiles), name='paint_...  12.4 us
    unnamed x16, local copies, waits for them, and re-layouts  4.93 us
    pallas_call x1, Pallas kernels, finish_first(): pl.pallas_call(finish_first_kernel, name='finish_first', grid=(2,), in_sp...  3.58 us
    pallas_call x1, Pallas kernels, finish_second(): pl.pallas_call(finish_second_kernel, name='finish_second', grid_spec=pltp...  3.29 us
  transfers between devices with their start and end apart: 9, of which 1 were waited for; matrix products, arithmetic and copies ran while one was open for 0% of the time, Pallas kernels for 34%

profile of v6, /device:TPU:4, one launch (start us, length us, event | category | flops | bytes accessed | tf_op | source)
XLA Modules:
  0.0 130.7 jit_solution(5045579493822543404)
XLA Ops:
  0.0 0.0 copy-start
  0.0 1.6 %copy-done = f32[8,32,2048]{2,1,0:T(8,128)S(1)} copy-done((f32[8,32,2048]{2,1,0:T(8,128)S(1)}, f32[8,32,2048]{2,1,0:T(8,128)}, u32[]{:S(2)}) %copy-start) | copy-done | bytes 2097176
  1.6 2.8 %pack_faces.1 = (f32[4,32,2048]{2,1,0:T(8,128)}, f32[4,32,2048]{2,1,0:T(8,128)}) custom-call(f32[3,8,32,2048]{3,2,1,0:T(8,128)} %refs_1_.1, f32[8,32,2048]{2,1,0:T(8,128)S(1)} %copy-done), custom_call_target="tpu_custom_call" | custom-call | tf_op jit(solution)/shard_map/pack_faces/pallas_call | solution.py:87
  4.4 6.8 %collective-permute-start.2 = (f32[4,32,2048]{2,1,0:T(8,128)}, f32[4,32,2048]{2,1,0:T(8,128)}, u32[]{:S(2)}, u32[]{:S(2)}) collective-permute-start(f32[4,32,2048]{2,1,0:T(8,128)} %get-tuple-element.26), channel_id=1, source_target_pairs={{0,16},{16,32},{32,48},{48,64},{64,80},{80,96},{96,112},{1,17},{17... | collective-permute-start | bytes 3145736 | tf_op jit(solution)/shard_map/ppermute | solution.py:20
  11.1 0.0 copy-start.1
  11.1 1.4 %collective-permute-start.3 = (f32[4,32,2048]{2,1,0:T(8,128)}, f32[4,32,2048]{2,1,0:T(8,128)}, u32[]{:S(2)}, u32[]{:S(2)}) collective-permute-start(f32[4,32,2048]{2,1,0:T(8,128)} %get-tuple-element.27), channel_id=1, source_target_pairs={{16,0},{32,16},{48,32},{64,48},{80,64},{96,80},{112,96},{17,1},{33... | collective-permute-start | bytes 3145736 | tf_op jit(solution)/shard_map/ppermute | solution.py:20
  12.5 3.1 %pack_rows.1 = (f32[8,8,2048]{2,1,0:T(8,128)}, f32[8,8,2048]{2,1,0:T(8,128)}) custom-call(f32[3,8,32,2048]{3,2,1,0:T(8,128)} %refs_1_.1, f32[8,32,2048]{2,1,0:T(8,128)S(1)} %copy-done, f32[3,8,32,2048]{3,2,1,0:T(8,128)} %refs_1_.1, f32[8,32,2048]{2,1,0:T(8,128)S(1)} %copy-done), custom_call_target="tpu_custom_call" | custom-call | tf_op jit(solution)/shard_map/pack_rows/pallas_call | solution.py:60
  15.7 1.9 %collective-permute-start = (f32[8,8,2048]{2,1,0:T(8,128)}, f32[8,8,2048]{2,1,0:T(8,128)S(1)}, u32[]{:S(2)}, u32[]{:S(2)}) collective-permute-start(f32[8,8,2048]{2,1,0:T(8,128)} %get-tuple-element.24.refs_13_), channel_id=1, source_target_pairs={{0,1},{1,2},{2,3},{3,4},{4,5},{5,6},{6,7},{7,8},{8,9},{9,10},{10,1... | collective-permute-start | bytes 1572872 | tf_op jit(solution)/shard_map/ppermute | solution.py:20
  17.6 4.5 %collective-permute-start.1 = (f32[8,8,2048]{2,1,0:T(8,128)}, f32[8,8,2048]{2,1,0:T(8,128)S(1)}, u32[]{:S(2)}, u32[]{:S(2)}) collective-permute-start(f32[8,8,2048]{2,1,0:T(8,128)} %get-tuple-element.25.refs_12_), channel_id=1, source_target_pairs={{1,0},{2,1},{3,2},{4,3},{5,4},{6,5},{7,6},{8,7},{9,8},{10,9},{11,1... | collective-permute-start | bytes 1572872 | tf_op jit(solution)/shard_map/ppermute | solution.py:20
  22.1 1.4 %archard.1 = f32[32,128]{1,0:T(8,128)} custom-call(f32[8]{0:T(128)} %rates_ref.1, s32[32,128]{1,0:T(8,128)} %class_ref.1, f32[32,128]{1,0:T(8,128)} %contact_ref.1, f32[32,128]{1,0:T(8,128)} %sliding_ref.1), custom_call_target="tpu_custom_call" | custom-call | tf_op jit(solution)/shard_map/archard/pallas_call | solution.py:34
  23.6 17.9 %all_gather.3 = f32[256,128]{1,0:T(8,128)S(1)} all-gather(f32[32,128]{1,0:T(8,128)} %archard.1), channel_id=1, replica_groups={{0,1,4,5,8,9,12,13},{2,3,6,7,10,11,14,15},{16,17,20,21,24,25,28,29},{18..., dimensions={0}, use_global_device_ids=true | all-gather | bytes 147456 | tf_op jit(solution)/shard_map/all_gather | solution.py:104
  41.5 0.0 collective-permute-start.4
  41.5 0.0 copy-done.1
  41.5 3.0 %face_sums.1 = (f32[3,2,32,2048]{3,2,1,0:T(8,128)S(1)}, f32[2,32,2048]{2,1,0:T(8,128)S(1)}) custom-call(f32[3,8,32,2048]{3,2,1,0:T(8,128)} %refs_1_.1, f32[3,8,32,2048]{3,2,1,0:T(8,128)} %refs_1_.1, f32[8,32,2048]{2,1,0:T(8,128)S(1)} %copy-done.1, f32[8,32,2048]{2,1,0:T(8,128)S(1)} %copy-done.1), custom_call_target="tpu_custom_call" | custom-call | tf_op jit(solution)/shard_map/face_sums/pallas_call | solution.py:470
  44.5 0.0 copy-start.4
  44.5 1.1 copy-done.4
  45.6 0.0 copy-start.5
  45.6 0.0 copy-start.6
  45.6 0.0 copy-start.7
  45.6 25.1 %collective-permute-done.4 = f32[256,128]{1,0:T(8,128)S(1)} collective-permute-done((f32[256,128]{1,0:T(8,128)S(1)}, f32[256,128]{1,0:T(8,128)S(1)}, u32[]{:S(2)}, u32[]{:S(2)}) %collective-permute-start.4) | collective-permute-done | bytes 131104 | tf_op jit(solution)/shard_map/ppermute | solution.py:105
  70.7 0.0 collective-permute-done.2.low.s_low
  70.7 0.0 collective-permute-done.3.high.s_high
  70.7 0.0 collective-permute-done.before.s_before.refs_3_.refs_5_.refs_10_
  70.7 0.0 collective-permute-done.1.after.s_after.refs_4_.refs_6_.refs_11_
  70.8 3.6 %finish_first.1 = (f32[3,32,2048]{2,1,0:T(8,128)}, f32[3,32,2048]{2,1,0:T(8,128)}, f32[8,2048]{1,0:T(8,128)S(1)}, f32[8,2048]{1,0:T(8,128)S(1)}) custom-call(f32[3,2,32,2048]{3,2,1,0:T(8,128)} %copy-done.4, f32[8,32,2048]{2,1,0:T(8,128)} %s_here.5, f32[2,32,2048]{2,1,0:T(8,128)S(1)} %get-tuple-element.31.totals, ...), custom_call_target="tpu_custom_call" | custom-call | tf_op jit(solution)/shard_map/finish_first/pallas_call | solution.py:534
  74.3 1.3 collective-permute-start.6
  75.6 6.1 %collective-permute-start.5 = (f32[3,32,2048]{2,1,0:T(8,128)}, f32[3,32,2048]{2,1,0:T(8,128)S(1)}, u32[]{:S(2)}, u32[]{:S(2)}) collective-permute-start(f32[3,32,2048]{2,1,0:T(8,128)} %get-tuple-element.35.refs_9_), channel_id=1, source_target_pairs={{0,16},{16,32},{32,48},{48,64},{64,80},{80,96},{96,112},{1,17},{17... | collective-permute-start | bytes 2359304 | tf_op jit(solution)/shard_map/ppermute | solution.py:20
  81.7 0.1 pad_add_fusion.where_ref.refs_0_
  81.8 1.9 %collective-permute-start.7 = (f32[8,2048]{1,0:T(8,128)S(1)}, f32[8,2048]{1,0:T(8,128)S(1)}, u32[]{:S(2)}, u32[]{:S(2)}) collective-permute-start(f32[8,2048]{1,0:T(8,128)S(1)} %get-tuple-element.41), channel_id=1, source_target_pairs={{0,1},{1,2},{2,3},{3,4},{4,5},{5,6},{6,7},{7,8},{8,9},{9,10},{10,1... | collective-permute-start | bytes 196616 | tf_op jit(solution)/shard_map/ppermute | solution.py:20
  83.7 4.5 %collective-permute-start.8 = (f32[8,2048]{1,0:T(8,128)S(1)}, f32[8,2048]{1,0:T(8,128)S(1)}, u32[]{:S(2)}, u32[]{:S(2)}) collective-permute-start(f32[8,2048]{1,0:T(8,128)S(1)} %get-tuple-element.42), channel_id=1, source_target_pairs={{1,0},{2,1},{3,2},{4,3},{5,4},{6,5},{7,6},{8,7},{9,8},{10,9},{11,1... | collective-permute-start | bytes 196616 | tf_op jit(solution)/shard_map/ppermute | solution.py:20
  88.3 0.0 copy-done.5
  88.3 0.0 copy-done.6
  88.3 0.0 copy-done.7
  88.3 0.0 copy-start.3
  88.4 2.2 %copy-done.3 = s32[1048576]{0:T(1024)S(1)} copy-done((s32[1048576]{0:T(1024)S(1)}, s32[1048576]{0:T(1024)}, u32[]{:S(2)}) %copy-start.3) | copy-done | bytes 4194328
  90.5 12.4 %paint_band.1.refs_7_ = f32[48,2048]{1,0:T(8,128)S(1)} custom-call(s32[2]{0:T(128)S(1)} %pad_add_fusion.where_ref.refs_0_, s32[512]{0:T(512)S(1)} %copy-done.6, s32[512]{0:T(512)S(1)} %copy-done.7, f32[512,128]{1,0:T(8,128)S(1)} %pad_maximum_fusion.wear_ref, s32[512,128]{1,0:T(8,128)S(1)} %copy-done.5, s32[8192,128]{1,0:T(8,128)S(1)} %bitcast.3), custom_call_target="tpu_custom_call" | custom-call | tf_op jit(solution)/shard_map/paint_band/pallas_call | solution.py:232
  103.0 0.0 copy-start.2
  103.0 12.5 %relax_layers_first.1 = (f32[3,8,32,2048]{3,2,1,0:T(8,128)}, f32[3,8,2048]{2,1,0:T(8,128)S(1)}, f32[3,8,2048]{2,1,0:T(8,128)S(1)}) custom-call(s32[2]{0:T(128)S(1)} %pad_add_fusion.where_ref.refs_0_, f32[3,8,32,2048]{3,2,1,0:T(8,128)} %refs_1_.1, f32[8,32,2048]{2,1,0:T(8,128)} %s_here.5, ...), custom_call_target="tpu_custom_call" | custom-call | tf_op jit(solution)/shard_map/relax_layers_first/pallas_call | solution.py:422
  115.5 0.0 copy-done.2
  115.5 11.9 %relax_layers_second.1 = (f32[3,8,32,2048]{3,2,1,0:T(8,128)}, f32[2,32,2048]{2,1,0:T(8,128)S(1)}) custom-call(s32[2]{0:T(128)S(1)} %pad_add_fusion.where_ref.refs_0_, f32[3,8,32,2048]{3,2,1,0:T(8,128)} %get-tuple-element.36.refs_1_, f32[8,32,2048]{2,1,0:T(8,128)S(1)} %copy-done.2, f32[3,8,2048]{2,1,0:T(8,128)S(1)} %get-tuple-element.37.refs_3_, ...), custom_call_target="tpu_custom_call" | custom-call | tf_op jit(solution)/shard_map/relax_layers_second/pallas_call | solution.py:422
  127.4 0.0 collective-permute-done.7.before
  127.4 0.0 collective-permute-done.8.after
  127.4 0.0 collective-permute-done.6.high
  127.4 0.0 collective-permute-done.5.low
  127.4 3.3 %finish_second.1 = f32[3,8,32,2048]{3,2,1,0:T(8,128)} custom-call(s32[2]{0:T(128)S(1)} %pad_add_fusion.where_ref.refs_0_, f32[3,8,32,2048]{3,2,1,0:T(8,128)} %get-tuple-element.39.sums, f32[8,32,2048]{2,1,0:T(8,128)} %s_here.5, f32[2,32,2048]{2,1,0:T(8,128)S(1)} %get-tuple-element.40.totals, ...), custom_call_target="tpu_custom_call", output_to_operand_aliasing={{}: (1, {})} | custom-call | tf_op jit(solution)/shard_map/finish_second/pallas_call | solution.py:591
  (1 shorter events, 0.0 us)
Async XLA Ops:
  0.0 1.6 %copy-start = (f32[8,32,2048]{2,1,0:T(8,128)S(1)}, f32[8,32,2048]{2,1,0:T(8,128)}, u32[]{:S(2)}) copy-start(f32[8,32,2048]{2,1,0:T(8,128)} %s_here.5) | copy-start | bytes 6291460
  4.4 66.4 %collective-permute-start.2 = (f32[4,32,2048]{2,1,0:T(8,128)}, f32[4,32,2048]{2,1,0:T(8,128)}, u32[]{:S(2)}, u32[]{:S(2)}) collective-permute-start(f32[4,32,2048]{2,1,0:T(8,128)} %get-tuple-element.26), channel_id=1, source_target_pairs={{0,16},{16,32},{32,48},{48,64},{64,80},{80,96},{96,112},{1,17},{17... | collective-permute-start | bytes 3145736 | tf_op jit(solution)/shard_map/ppermute | solution.py:20
  11.1 30.3 %copy-start.1 = (f32[8,32,2048]{2,1,0:T(8,128)S(1)}, f32[8,32,2048]{2,1,0:T(8,128)}, u32[]{:S(2)}) copy-start(f32[8,32,2048]{2,1,0:T(8,128)} %s_here.5) | copy-start | bytes 6291460
  11.1 59.6 %collective-permute-start.3 = (f32[4,32,2048]{2,1,0:T(8,128)}, f32[4,32,2048]{2,1,0:T(8,128)}, u32[]{:S(2)}, u32[]{:S(2)}) collective-permute-start(f32[4,32,2048]{2,1,0:T(8,128)} %get-tuple-element.27), channel_id=1, source_target_pairs={{16,0},{32,16},{48,32},{64,48},{80,64},{96,80},{112,96},{17,1},{33... | collective-permute-start | bytes 3145736 | tf_op jit(solution)/shard_map/ppermute | solution.py:20
  15.7 55.1 %collective-permute-start = (f32[8,8,2048]{2,1,0:T(8,128)}, f32[8,8,2048]{2,1,0:T(8,128)S(1)}, u32[]{:S(2)}, u32[]{:S(2)}) collective-permute-start(f32[8,8,2048]{2,1,0:T(8,128)} %get-tuple-element.24.refs_13_), channel_id=1, source_target_pairs={{0,1},{1,2},{2,3},{3,4},{4,5},{5,6},{6,7},{7,8},{8,9},{9,10},{10,1... | collective-permute-start | bytes 1572872 | tf_op jit(solution)/shard_map/ppermute | solution.py:20
  17.6 53.2 %collective-permute-start.1 = (f32[8,8,2048]{2,1,0:T(8,128)}, f32[8,8,2048]{2,1,0:T(8,128)S(1)}, u32[]{:S(2)}, u32[]{:S(2)}) collective-permute-start(f32[8,8,2048]{2,1,0:T(8,128)} %get-tuple-element.25.refs_12_), channel_id=1, source_target_pairs={{1,0},{2,1},{3,2},{4,3},{5,4},{6,5},{7,6},{8,7},{9,8},{10,9},{11,1... | collective-permute-start | bytes 1572872 | tf_op jit(solution)/shard_map/ppermute | solution.py:20
  41.5 29.3 %collective-permute-start.4 = (f32[256,128]{1,0:T(8,128)S(1)}, f32[256,128]{1,0:T(8,128)S(1)}, u32[]{:S(2)}, u32[]{:S(2)}) collective-permute-start(f32[256,128]{1,0:T(8,128)S(1)} %all_gather.3), channel_id=1, source_target_pairs={{0,2},{1,3},{2,0},{3,1},{4,6},{5,7},{6,4},{7,5},{8,10},{9,11},{10,... | collective-permute-start | bytes 393224 | tf_op jit(solution)/shard_map/ppermute | solution.py:105
  44.5 1.1 copy-start.4
  45.6 42.7 %copy-start.5 = (s32[512,128]{1,0:T(8,128)S(1)}, s32[512,128]{1,0:T(8,128)}, u32[]{:S(2)}) copy-start(s32[512,128]{1,0:T(8,128)} %list_ref.1) | copy-start | bytes 786436
  45.6 42.7 %copy-start.6 = (s32[512]{0:T(512)S(1)}, s32[512]{0:T(512)}, u32[]{:S(2)}) copy-start(s32[512]{0:T(512)} %owner_ref.1) | copy-start | bytes 6148
  45.6 42.7 %copy-start.7 = (s32[512]{0:T(512)S(1)}, s32[512]{0:T(512)}, u32[]{:S(2)}) copy-start(s32[512]{0:T(512)} %count_ref.1) | copy-start | bytes 6148
  74.3 53.0 %collective-permute-start.6 = (f32[3,32,2048]{2,1,0:T(8,128)}, f32[3,32,2048]{2,1,0:T(8,128)S(1)}, u32[]{:S(2)}, u32[]{:S(2)}) collective-permute-start(f32[3,32,2048]{2,1,0:T(8,128)} %get-tuple-element.34.refs_8_), channel_id=1, source_target_pairs={{16,0},{32,16},{48,32},{64,48},{80,64},{96,80},{112,96},{17,1},{33... | collective-permute-start | bytes 2359304 | tf_op jit(solution)/shard_map/ppermute | solution.py:20
  75.6 51.8 %collective-permute-start.5 = (f32[3,32,2048]{2,1,0:T(8,128)}, f32[3,32,2048]{2,1,0:T(8,128)S(1)}, u32[]{:S(2)}, u32[]{:S(2)}) collective-permute-start(f32[3,32,2048]{2,1,0:T(8,128)} %get-tuple-element.35.refs_9_), channel_id=1, source_target_pairs={{0,16},{16,32},{32,48},{48,64},{64,80},{80,96},{96,112},{1,17},{17... | collective-permute-start | bytes 2359304 | tf_op jit(solution)/shard_map/ppermute | solution.py:20
  81.8 45.6 %collective-permute-start.7 = (f32[8,2048]{1,0:T(8,128)S(1)}, f32[8,2048]{1,0:T(8,128)S(1)}, u32[]{:S(2)}, u32[]{:S(2)}) collective-permute-start(f32[8,2048]{1,0:T(8,128)S(1)} %get-tuple-element.41), channel_id=1, source_target_pairs={{0,1},{1,2},{2,3},{3,4},{4,5},{5,6},{6,7},{7,8},{8,9},{9,10},{10,1... | collective-permute-start | bytes 196616 | tf_op jit(solution)/shard_map/ppermute | solution.py:20
  83.7 43.6 %collective-permute-start.8 = (f32[8,2048]{1,0:T(8,128)S(1)}, f32[8,2048]{1,0:T(8,128)S(1)}, u32[]{:S(2)}, u32[]{:S(2)}) collective-permute-start(f32[8,2048]{1,0:T(8,128)S(1)} %get-tuple-element.42), channel_id=1, source_target_pairs={{1,0},{2,1},{3,2},{4,3},{5,4},{6,5},{7,6},{8,7},{9,8},{10,9},{11,1... | collective-permute-start | bytes 196616 | tf_op jit(solution)/shard_map/ppermute | solution.py:20
  88.3 2.2 %copy-start.3 = (s32[1048576]{0:T(1024)S(1)}, s32[1048576]{0:T(1024)}, u32[]{:S(2)}) copy-start(s32[1048576]{0:T(1024)} %param.19) | copy-start | bytes 12582916
  103.0 12.5 %copy-start.2 = (f32[8,32,2048]{2,1,0:T(8,128)S(1)}, f32[8,32,2048]{2,1,0:T(8,128)}, u32[]{:S(2)}) copy-start(f32[8,32,2048]{2,1,0:T(8,128)} %s_here.5) | copy-start | bytes 6291460

commit v7 on v4

--- a/solution.py
+++ b/solution.py
@@ -301,23 +301,28 @@
 
 
 def layer_kernel(first_sweep, *refs):
-    (where_ref, low, mid, high, s_low, s_mid, s_high, before, after, s_before,
-     s_after) = refs[:11]
-    rest = list(refs[11:])
+    where_ref, f_in, s_in, before, after, s_before, s_after = refs[:7]
+    rest = list(refs[7:-2])
+    f_kept, s_kept = refs[-2:]
     surface = rest.pop(0) if first_sweep else None
     extra = rest[:4] + rest[6:]
     out, totals = rest[4:6] if first_sweep else rest
-    layer = pl.program_id(0)
-    last = pl.num_programs(0) - 1
-    ntiles = mid.shape[2] // 8
-    f_refs = {-1: low, 0: mid, 1: high}
-    s_refs = {-1: s_low, 0: s_mid, 1: s_high}
+    step = pl.program_id(0)
+    layer = step - 1
+    last = pl.num_programs(0) - 2
+    slot = step % 2
+    ntiles = f_in.shape[2] // 8
+    mid, s_mid = f_kept.at[1 - slot], s_kept.at[1 - slot]
+    f_refs = {-1: f_kept.at[slot], 0: mid, 1: f_in.at[:, 0]}
+    s_refs = {-1: s_kept.at[slot], 0: s_mid, 1: s_in.at[0]}
     outermost = jnp.logical_or(layer == 0, layer == last)
     row = lax.broadcasted_iota(jnp.int32, (8, 1), 0)
-    if first_sweep:
-
-        @pl.when(layer == 0)
-        def _():
+
+    @pl.when(step == 0)
+    def _():
+        f_kept[1] = f_in[:, 0]
+        s_kept[1] = s_in[0]
+        if first_sweep:
             far_before, far_after, own_first, own_last, out_before, out_after = extra
             relax_outside(out_before, before, s_before, far_before, own_first, surface, 7, row)
             relax_outside(out_after, after, s_after, far_after, own_last, surface,
@@ -328,46 +333,49 @@
     scales = {0: jnp.where(layer == 0, 1.0, 0.0), -1: jnp.where(layer == 1, 1.0, 0.0)}
     pinned = jnp.logical_and(layer == 0, where_ref[1] == 1)
 
-    for t in range(ntiles):
-        at = slice(8 * t, 8 * t + 8)
-
-        def load(c, side):
-            if c == 3:
-                return s_refs[side][0, at, :]
-            value = f_refs[side][c, 0, at, :]
-            if first_sweep and c == 0 and side <= 0:
-                value = value + scales[side] * surface[8 * t + 8 : 8 * t + 16, :]
-            return value
-
-        def beside(inside, row, f_edge, s_edge):
-            def get(c):
+    @pl.when(layer >= 0)
+    def _():
+        for t in range(ntiles):
+            at = slice(8 * t, 8 * t + 8)
+
+            def load(c, side):
                 if c == 3:
-                    if inside:
-                        return s_mid[0, row : row + 1, :]
-                    return s_edge[0, pl.ds(layer, 1), :]
-                value = mid[c, 0, row : row + 1, :] if inside else f_edge[c, pl.ds(layer, 1), :]
-                if first_sweep and c == 0:
-                    value = value + scales[0] * surface[row + 8 : row + 9, :]
+                    return s_refs[side][at, :]
+                value = f_refs[side][c, at, :]
+                if first_sweep and c == 0 and side <= 0:
+                    value = value + scales[side] * surface[8 * t + 8 : 8 * t + 16, :]
                 return value
-            return get
-
-        above = beside(t > 0, 8 * t - 1, before, s_before)
-        below = beside(t < ntiles - 1, 8 * t + 8, after, s_after)
-
-        def rolled(c, here):
-            yield jnp.where(row == 7, below(c), pltpu.roll(here, 7, 0))
-            yield jnp.where(row == 0, above(c), pltpu.roll(here, 1, 0))
-
-        sums, total, centers = relax_tile(load, rolled, has_high, has_low)
-        inverse = jnp.where(outermost, 1.0, 1.0 / total)
-        outs = [part * inverse for part in sums]
-        outs[0] = jnp.where(pinned, centers[0], outs[0])
-        for c in range(3):
-            out[c, 0, at, :] = outs[c]
-
-        @pl.when(outermost)
-        def _():
+
+            def beside(inside, row, f_edge, s_edge):
+                def get(c):
+                    if c == 3:
+                        if inside:
+                            return s_mid[row : row + 1, :]
+                        return s_edge[0, pl.ds(layer, 1), :]
+                    value = mid[c, row : row + 1, :] if inside else f_edge[c, pl.ds(layer, 1), :]
+                    if first_sweep and c == 0:
+                        value = value + scales[0] * surface[row + 8 : row + 9, :]
+                    return value
+                return get
+
+            above = beside(t > 0, 8 * t - 1, before, s_before)
+            below = beside(t < ntiles - 1, 8 * t + 8, after, s_after)
+
+            def rolled(c, here):
+                yield jnp.where(row == 7, below(c), pltpu.roll(here, 7, 0))
+                yield jnp.where(row == 0, above(c), pltpu.roll(here, 1, 0))
+
+            sums, total, centers = relax_tile(load, rolled, has_high, has_low)
+            inverse = jnp.where(outermost, 1.0, 1.0 / total)
+            outs = [part * inverse for part in sums]
+            outs[0] = jnp.where(pinned, centers[0], outs[0])
+            for c in range(3):
+                out[c, 0, at, :] = outs[c]
+
             totals[0, at, :] = total
+
+    f_kept[slot] = f_in[:, 0]
+    s_kept[slot] = s_in[0]
 
 
 def relax_layers(position, field, stiffness, before, after, s_before, s_after, surface,
@@ -375,19 +383,18 @@
     _, layers, rows, width = field.shape
     first_sweep = surface is not None
     whole = lambda shape: pl.BlockSpec(shape, lambda i, *_: (0,) * len(shape))
-    at = lambda i, k: jnp.clip(i + k, 0, layers - 1)
-    f_spec = lambda k: pl.BlockSpec((3, 1, rows, width), lambda i, *_: (0, at(i, k), 0, 0))
-    s_spec = lambda k: pl.BlockSpec((1, rows, width), lambda i, *_: (at(i, k), 0, 0))
+    came = lambda k: jnp.minimum(k, layers - 1)
+    swept = lambda k: jnp.maximum(k - 1, 0)
+    f_spec = lambda at: pl.BlockSpec((3, 1, rows, width), lambda k, *_: (0, at(k), 0, 0))
     f_edge = whole((3, layers, width))
-    s_edge = pl.BlockSpec((1, layers, width), lambda i, *_: (3, 0, 0))
-    sides = (-1, 0, 1)
-    args = [field] * 3 + [stiffness] * 3 + [before, after, s_before, s_after]
-    in_specs = [f_spec(k) for k in sides] + [s_spec(k) for k in sides]
+    s_edge = pl.BlockSpec((1, layers, width), lambda k, *_: (3, 0, 0))
+    args = [field, stiffness, before, after, s_before, s_after]
+    in_specs = [f_spec(came), pl.BlockSpec((1, rows, width), lambda k, *_: (came(k), 0, 0))]
     in_specs += [f_edge, f_edge, s_edge, s_edge]
     out_shape = [jax.ShapeDtypeStruct(field.shape, jnp.float32),
                  jax.ShapeDtypeStruct((2, rows, width), jnp.float32)]
-    out_specs = [f_spec(0),
-                 pl.BlockSpec((1, rows, width), lambda i, *_: (i // (layers // 2), 0, 0))]
+    out_specs = [f_spec(swept),
+                 pl.BlockSpec((1, rows, width), lambda k, *_: (jnp.minimum(swept(k), 1), 0, 0))]
     if first_sweep:
         args.append(surface)
         in_specs.append(whole(surface.shape))
@@ -401,69 +408,74 @@
         functools.partial(layer_kernel, first_sweep),
         name="relax_layers_first" if first_sweep else "relax_layers_second",
         grid_spec=pltpu.PrefetchScalarGridSpec(
-            num_scalar_prefetch=1, grid=(layers,), in_specs=in_specs, out_specs=out_specs
+            num_scalar_prefetch=1, grid=(layers + 1,), in_specs=in_specs, out_specs=out_specs,
+            scratch_shapes=[pltpu.VMEM((2, 3, rows, width), jnp.float32),
+                            pltpu.VMEM((2, rows, width), jnp.float32)],
         ),
         out_shape=out_shape,
         compiler_params=pltpu.CompilerParams(vmem_limit_bytes=VMEM_LIMIT),
     )(position, *args)
 
 
-def finish_first_kernel(face, *refs):
-    where_ref, sums, s_here, totals, outer, s_outer = refs[:6]
-    out, send, first_row, last_row = refs[-4:]
+def finish_first_kernel(where_ref, sums, s_here, totals, low, high, s_low, s_high,
+                        out, send_first, send_last, first_row, last_row):
     ntiles = sums.shape[2] // 8
     pinned = where_ref[1] == 1
-    if len(refs) > 10:
-        first_row[...] = refs[6][...]
-        last_row[...] = refs[7][...]
-    else:
+
+    def one(face, outer, s_outer, send):
+        for t in range(ntiles):
+            at = slice(8 * t, 8 * t + 8)
+            weight = s_here[0, at, :] + s_outer[0, at, :]
+            inverse = 1.0 / (totals[0, at, :] + weight)
+            for c in range(3):
+                so_far = sums[c, 0, at, :]
+                value = (so_far + weight * outer[c, at, :]) * inverse
+                if face == 0 and c == 0:
+                    value = jnp.where(pinned, so_far, value)
+                out[c, 0, at, :] = value
+                send[c, at, :] = value
+                k = 2 * c + face
+                if t == 0:
+                    first_row[k : k + 1, :] = value[0:1]
+                if t == ntiles - 1:
+                    last_row[k : k + 1, :] = value[7:8]
+
+    step = pl.program_id(0)
+
+    @pl.when(step == 0)
+    def _():
         first_row[...] = jnp.zeros_like(first_row)
         last_row[...] = jnp.zeros_like(last_row)
-    for t in range(ntiles):
-        at = slice(8 * t, 8 * t + 8)
-        weight = s_here[0, at, :] + s_outer[0, at, :]
-        inverse = 1.0 / (totals[0, at, :] + weight)
-        for c in range(3):
-            so_far = sums[c, 0, at, :]
-            value = (so_far + weight * outer[c, at, :]) * inverse
-            if face == 0 and c == 0:
-                value = jnp.where(pinned, so_far, value)
-            out[c, 0, at, :] = value
-            send[c, at, :] = value
-            k = 2 * c + face
-            if t == 0:
-                first_row[k : k + 1, :] = value[0:1]
-            if t == ntiles - 1:
-                last_row[k : k + 1, :] = value[7:8]
-
-
-def finish_first(position, face, field, stiffness, totals, outer, edges):
+        one(0, low, s_low, send_first)
+
+    pl.when(step == 1)(lambda: one(1, high, s_high, send_last))
+
+
+def finish_first(position, field, stiffness, totals, low, high):
     _, layers, rows, width = field.shape
-    layer = face * (layers - 1)
-    block = lambda shape, *at: pl.BlockSpec(shape, lambda i, *_: at)
-    plane = block((3, rows, width), 0, 0, 0)
-    own = block((3, 1, rows, width), 0, layer, 0, 0)
-    edge = block((8, width), 0, 0)
-    args = [field, stiffness, totals, outer, outer]
-    in_specs = [own, block((1, rows, width), layer, 0, 0), block((1, rows, width), face, 0, 0),
-                plane, block((1, rows, width), 3, 0, 0)]
-    if edges is not None:
-        args += edges
-        in_specs += [edge, edge]
+    block = lambda shape, at: pl.BlockSpec(shape, lambda i, *_: at(i))
+    layer = lambda i: i * (layers - 1)
+    plane = block((3, rows, width), lambda i: (0, 0, 0))
+    s_plane = block((1, rows, width), lambda i: (3, 0, 0))
+    own = block((3, 1, rows, width), lambda i: (0, layer(i), 0, 0))
+    edge = block((8, width), lambda i: (0, 0))
+    face_shape = jax.ShapeDtypeStruct((3, rows, width), jnp.float32)
     edge_shape = jax.ShapeDtypeStruct((8, width), jnp.float32)
     return pl.pallas_call(
-        functools.partial(finish_first_kernel, face),
+        finish_first_kernel,
         name="finish_first",
         grid_spec=pltpu.PrefetchScalarGridSpec(
-            num_scalar_prefetch=1, grid=(1,), in_specs=in_specs,
-            out_specs=[own, plane, edge, edge],
+            num_scalar_prefetch=1, grid=(2,),
+            in_specs=[own, block((1, rows, width), lambda i: (layer(i), 0, 0)),
+                      block((1, rows, width), lambda i: (i, 0, 0)),
+                      plane, plane, s_plane, s_plane],
+            out_specs=[own, plane, plane, edge, edge],
         ),
         out_shape=[jax.ShapeDtypeStruct(field.shape, jnp.float32),
-                   jax.ShapeDtypeStruct((3, rows, width), jnp.float32),
-                   edge_shape, edge_shape],
+                   face_shape, face_shape, edge_shape, edge_shape],
         input_output_aliases={1: 0},
         compiler_params=pltpu.CompilerParams(vmem_limit_bytes=VMEM_LIMIT),
-    )(position, *args)
+    )(position, field, stiffness, totals, low, high, low, high)
 
 
 def finish_second_kernel(where_ref, sums, s_here, totals, low, high, s_low, s_high,
@@ -560,11 +572,8 @@
         position, displacement, stiffness, before, after, before, after, surface,
         (row_first, row_last),
     )
-    first, send_last, edge_first, edge_last = finish_first(
-        position, 1, first, stiffness, totals, high, None
-    )
-    first, send_first, edge_first, edge_last = finish_first(
-        position, 0, first, stiffness, totals, low, (edge_first, edge_last)
+    first, send_first, send_last, edge_first, edge_last = finish_first(
+        position, first, stiffness, totals, low, high
     )
     low_2, high_2 = shift_both(send_last, send_first, "depth")
     edge_before, edge_after = shift_both(edge_last, edge_first, "tan")

time: 125 us -> 144 us (1.15)
  the two profiles are of different devices: /device:TPU:22 before, /device:TPU:15 now
where the time goes in v7:
time: 144 us; the launch traced here: 143 us
  starting transfers between devices  50.7 us (35%)
  Pallas kernels  39.7 us (28%)
  waiting for transfers between devices  34.4 us (24%)
  blocking collectives  14 us (10%)
  local copies, waits for them, and re-layouts  3.8 us (3%)
    ppermute x8, starting transfers between devices, shift_both(): return (lax.ppermute(last, axis, up), lax.ppermute(first, axis, down))  50.5 us
    ppermute x8, waiting for transfers between devices, shift_both(): return (lax.ppermute(last, axis, up), lax.ppermute(first, axis, down))  32.8 us
    pallas_call x2, Pallas kernels, relax_layers(): pl.pallas_call(functools.partial(layer_kernel, first_sweep), name='relax_...  24.4 us
    all_gather x1, blocking collectives, gather_wear(): lax.all_gather(both, 'tan', axis=0, axis_index_groups=groups, tiled=True)  14 us
    pallas_call x1, Pallas kernels, finish_first(): pl.pallas_call(finish_first_kernel, name='finish_first', grid_spec=pltpu....  3.8 us
    unnamed x16, local copies, waits for them, and re-layouts  3.8 us
    pallas_call x1, Pallas kernels, finish_second(): pl.pallas_call(finish_second_kernel, name='finish_second', grid_spec=pltp...  3.32 us
    pallas_call x1, Pallas kernels, pack_rows(): pl.pallas_call(rows_kernel, name='pack_rows', grid=(1,), in_specs=[f_spec...  3.29 us
  transfers between devices with their start and end apart: 9, of which 5 were waited for; matrix products, arithmetic and copies ran while one was open for 0% of the time, Pallas kernels for 21%

profile of v7, /device:TPU:15, one launch (start us, length us, event | category | flops | bytes accessed | tf_op | source)
XLA Modules:
  0.0 142.7 jit_solution(8660553976218381874)
XLA Ops:
  0.0 0.0 copy-start
  0.0 1.6 %copy-done = f32[8,32,2048]{2,1,0:T(8,128)S(1)} copy-done((f32[8,32,2048]{2,1,0:T(8,128)S(1)}, f32[8,32,2048]{2,1,0:T(8,128)}, u32[]{:S(2)}) %copy-start) | copy-done | bytes 2097176
  1.6 0.0 copy-start.1
  1.6 3.3 %pack_rows.1 = (f32[8,8,2048]{2,1,0:T(8,128)}, f32[8,8,2048]{2,1,0:T(8,128)}) custom-call(f32[3,8,32,2048]{3,2,1,0:T(8,128)} %refs_1_.1, f32[8,32,2048]{2,1,0:T(8,128)S(1)} %copy-done, f32[3,8,32,2048]{3,2,1,0:T(8,128)} %refs_1_.1, f32[8,32,2048]{2,1,0:T(8,128)S(1)} %copy-done), custom_call_target="tpu_custom_call" | custom-call | tf_op jit(solution)/shard_map/pack_rows/pallas_call | solution.py:60
  4.9 0.0 copy-start.4
  4.9 0.0 copy-start.5
  4.9 0.0 copy-start.6
  4.9 4.2 %collective-permute-start.1 = (f32[8,8,2048]{2,1,0:T(8,128)}, f32[8,8,2048]{2,1,0:T(8,128)S(1)}, u32[]{:S(2)}, u32[]{:S(2)}) collective-permute-start(f32[8,8,2048]{2,1,0:T(8,128)} %get-tuple-element.28.refs_11_), channel_id=1, source_target_pairs={{0,1},{1,2},{2,3},{3,4},{4,5},{5,6},{6,7},{7,8},{8,9},{9,10},{10,1... | collective-permute-start | bytes 1572872 | tf_op jit(solution)/shard_map/ppermute | solution.py:20
  9.1 1.9 %collective-permute-start.2 = (f32[8,8,2048]{2,1,0:T(8,128)}, f32[8,8,2048]{2,1,0:T(8,128)S(1)}, u32[]{:S(2)}, u32[]{:S(2)}) collective-permute-start(f32[8,8,2048]{2,1,0:T(8,128)} %get-tuple-element.25.after_ref.refs_10_), channel_id=1, source_target_pairs={{1,0},{2,1},{3,2},{4,3},{5,4},{6,5},{7,6},{8,7},{9,8},{10,9},{11,1... | collective-permute-start | bytes 1572872 | tf_op jit(solution)/shard_map/ppermute | solution.py:20
  11.1 1.4 %archard.1 = f32[32,128]{1,0:T(8,128)} custom-call(f32[8]{0:T(128)} %rates_ref.1, s32[32,128]{1,0:T(8,128)} %class_ref.1, f32[32,128]{1,0:T(8,128)} %contact_ref.1, f32[32,128]{1,0:T(8,128)} %sliding_ref.1), custom_call_target="tpu_custom_call" | custom-call | tf_op jit(solution)/shard_map/archard/pallas_call | solution.py:34
  12.5 0.0 copy-start.7
  12.5 0.1 collective-permute-start
  12.6 0.0 copy-done.1
  12.6 2.9 %pack_faces.1 = (f32[4,32,2048]{2,1,0:T(8,128)}, f32[4,32,2048]{2,1,0:T(8,128)}) custom-call(f32[3,8,32,2048]{3,2,1,0:T(8,128)} %refs_1_.1, f32[8,32,2048]{2,1,0:T(8,128)S(1)} %copy-done.1, f32[8,8,2048]{2,1,0:T(8,128)} %get-tuple-element.25.after_ref.refs_10_), custom_call_target="tpu_custom_call" | custom-call | tf_op jit(solution)/shard_map/pack_faces/pallas_call | solution.py:87
  15.5 1.6 %collective-permute-done = f32[32,128]{1,0:T(8,128)S(1)} collective-permute-done((f32[32,128]{1,0:T(8,128)}, f32[32,128]{1,0:T(8,128)S(1)}, u32[]{:S(2)}, u32[]{:S(2)}) %collective-permute-start) | collective-permute-done | bytes 16416 | tf_op jit(solution)/shard_map/ppermute | solution.py:104
  17.1 0.0 collective-permute-done.1.refs_3_.refs_5_.refs_8_.s_before
  17.1 5.4 %collective-permute-done.2.refs_4_.refs_6_.refs_9_.s_after = f32[8,8,2048]{2,1,0:T(8,128)S(1)} collective-permute-done((f32[8,8,2048]{2,1,0:T(8,128)}, f32[8,8,2048]{2,1,0:T(8,128)S(1)}, u32[]{:S(2)}, u32[]{:S(2)}) %collective-permute-start.2) | collective-permute-done | bytes 524320 | tf_op jit(solution)/shard_map/ppermute | solution.py:20
  22.4 28.4 %collective-permute-start.3 = (f32[4,32,2048]{2,1,0:T(8,128)}, f32[4,32,2048]{2,1,0:T(8,128)}, u32[]{:S(2)}, u32[]{:S(2)}) collective-permute-start(f32[4,32,2048]{2,1,0:T(8,128)} %get-tuple-element.34), channel_id=1, source_target_pairs={{0,16},{16,32},{32,48},{48,64},{64,80},{80,96},{96,112},{1,17},{17... | collective-permute-start | bytes 3145736 | tf_op jit(solution)/shard_map/ppermute | solution.py:20
  50.8 1.9 %collective-permute-start.4 = (f32[4,32,2048]{2,1,0:T(8,128)}, f32[4,32,2048]{2,1,0:T(8,128)}, u32[]{:S(2)}, u32[]{:S(2)}) collective-permute-start(f32[4,32,2048]{2,1,0:T(8,128)} %get-tuple-element.35), channel_id=1, source_target_pairs={{16,0},{32,16},{48,32},{64,48},{80,64},{96,80},{112,96},{17,1},{33... | collective-permute-start | bytes 3145736 | tf_op jit(solution)/shard_map/ppermute | solution.py:20
  52.8 0.1 pad_add_fusion.where_ref.refs_0_
  52.9 0.0 copy-done.7
  52.9 14.0 %all_gather.3.wear_ref = f32[512,128]{1,0:T(8,128)S(1)} all-gather(f32[64,128]{1,0:T(8,128)S(1)} %pad_maximum_fusion), channel_id=1, replica_groups={{0,1,4,5,8,9,12,13},{2,3,6,7,10,11,14,15},{16,17,20,21,24,25,28,29},{18..., dimensions={0}, use_global_device_ids=true | all-gather | bytes 294912 | tf_op jit(solution)/shard_map/all_gather | solution.py:111
  66.8 0.0 copy-done.4
  66.8 0.0 copy-done.5
  66.8 0.0 copy-done.6
  66.8 0.0 copy-start.3
  66.9 2.2 %copy-done.3 = s32[1048576]{0:T(1024)S(1)} copy-done((s32[1048576]{0:T(1024)S(1)}, s32[1048576]{0:T(1024)}, u32[]{:S(2)}) %copy-start.3) | copy-done | bytes 4194328
  69.0 0.6 paint_band.1.refs_7_
  69.7 12.5 %relax_layers_first.1 = (f32[3,8,32,2048]{3,2,1,0:T(8,128)}, f32[2,32,2048]{2,1,0:T(8,128)S(1)}, f32[3,8,2048]{2,1,0:T(8,128)S(1)}, f32[3,8,2048]{2,1,0:T(8,128)S(1)}) custom-call(s32[2]{0:T(128)S(1)} %pad_add_fusion.where_ref.refs_0_, f32[3,8,32,2048]{3,2,1,0:T(8,128)} %refs_1_.1, f32[8,32,2048]{2,1,0:T(8,128)S(1)} %copy-done.1, ...), custom_call_target="tpu_custom_call" | custom-call | tf_op jit(solution)/shard_map/relax_layers_first/pallas_call | solution.py:407
  82.2 12.8 %collective-permute-done.3.low.s_low = f32[4,32,2048]{2,1,0:T(8,128)} collective-permute-done((f32[4,32,2048]{2,1,0:T(8,128)}, f32[4,32,2048]{2,1,0:T(8,128)}, u32[]{:S(2)}, u32[]{:S(2)}) %collective-permute-start.3) | collective-permute-done | bytes 1048608 | tf_op jit(solution)/shard_map/ppermute | solution.py:20
  95.0 0.0 collective-permute-done.4.high.s_high
  95.0 0.0 copy-start.2
  95.0 3.8 %finish_first.1 = (f32[3,8,32,2048]{3,2,1,0:T(8,128)}, f32[3,32,2048]{2,1,0:T(8,128)S(1)}, f32[3,32,2048]{2,1,0:T(8,128)S(1)}, f32[8,2048]{1,0:T(8,128)S(1)}, f32[8,2048]{1,0:T(8,128)S(1)}) custom-call(s32[2]{0:T(128)S(1)} %pad_add_fusion.where_ref.refs_0_, f32[3,8,32,2048]{3,2,1,0:T(8,128)} %get-tuple-element.32.sums, ...), custom_call_target="tpu_custom_call", output_to_operand_aliasing={{0}: (1, {})} | custom-call | tf_op jit(solution)/shard_map/finish_first/pallas_call | solution.py:464
  98.8 5.6 %collective-permute-start.5 = (f32[3,32,2048]{2,1,0:T(8,128)S(1)}, f32[3,32,2048]{2,1,0:T(8,128)S(1)}, u32[]{:S(2)}, u32[]{:S(2)}) collective-permute-start(f32[3,32,2048]{2,1,0:T(8,128)S(1)} %get-tuple-element.41), channel_id=1, source_target_pairs={{0,16},{16,32},{32,48},{48,64},{64,80},{80,96},{96,112},{1,17},{17... | collective-permute-start | bytes 2359304 | tf_op jit(solution)/shard_map/ppermute | solution.py:20
  104.4 2.1 %collective-permute-start.6 = (f32[3,32,2048]{2,1,0:T(8,128)S(1)}, f32[3,32,2048]{2,1,0:T(8,128)S(1)}, u32[]{:S(2)}, u32[]{:S(2)}) collective-permute-start(f32[3,32,2048]{2,1,0:T(8,128)S(1)} %get-tuple-element.42), channel_id=1, source_target_pairs={{16,0},{32,16},{48,32},{64,48},{80,64},{96,80},{112,96},{17,1},{33... | collective-permute-start | bytes 2359304 | tf_op jit(solution)/shard_map/ppermute | solution.py:20
  106.5 1.9 %collective-permute-start.7 = (f32[8,2048]{1,0:T(8,128)S(1)}, f32[8,2048]{1,0:T(8,128)S(1)}, u32[]{:S(2)}, u32[]{:S(2)}) collective-permute-start(f32[8,2048]{1,0:T(8,128)S(1)} %get-tuple-element.43), channel_id=1, source_target_pairs={{0,1},{1,2},{2,3},{3,4},{4,5},{5,6},{6,7},{7,8},{8,9},{9,10},{10,1... | collective-permute-start | bytes 196616 | tf_op jit(solution)/shard_map/ppermute | solution.py:20
  108.4 4.4 %collective-permute-start.8 = (f32[8,2048]{1,0:T(8,128)S(1)}, f32[8,2048]{1,0:T(8,128)S(1)}, u32[]{:S(2)}, u32[]{:S(2)}) collective-permute-start(f32[8,2048]{1,0:T(8,128)S(1)} %get-tuple-element.44), channel_id=1, source_target_pairs={{1,0},{2,1},{3,2},{4,3},{5,4},{6,5},{7,6},{8,7},{9,8},{10,9},{11,1... | collective-permute-start | bytes 196616 | tf_op jit(solution)/shard_map/ppermute | solution.py:20
  112.9 0.0 copy-done.2
  112.9 11.9 %relax_layers_second.1 = (f32[3,8,32,2048]{3,2,1,0:T(8,128)}, f32[2,32,2048]{2,1,0:T(8,128)S(1)}) custom-call(s32[2]{0:T(128)S(1)} %pad_add_fusion.where_ref.refs_0_, f32[3,8,32,2048]{3,2,1,0:T(8,128)} %get-tuple-element.36.refs_1_, f32[8,32,2048]{2,1,0:T(8,128)S(1)} %copy-done.2, f32[3,8,2048]{2,1,0:T(8,128)S(1)} %get-tuple-element.37.refs_3_, ...), custom_call_target="tpu_custom_call" | custom-call | tf_op jit(solution)/shard_map/relax_layers_second/pallas_call | solution.py:407
  124.8 12.8 %collective-permute-done.7.before = f32[8,2048]{1,0:T(8,128)S(1)} collective-permute-done((f32[8,2048]{1,0:T(8,128)S(1)}, f32[8,2048]{1,0:T(8,128)S(1)}, u32[]{:S(2)}, u32[]{:S(2)}) %collective-permute-start.7) | collective-permute-done | bytes 65568 | tf_op jit(solution)/shard_map/ppermute | solution.py:20
  137.5 0.0 collective-permute-done.8.after
  137.5 0.0 collective-permute-done.5.low
  137.5 1.9 %collective-permute-done.6.high = f32[3,32,2048]{2,1,0:T(8,128)S(1)} collective-permute-done((f32[3,32,2048]{2,1,0:T(8,128)S(1)}, f32[3,32,2048]{2,1,0:T(8,128)S(1)}, u32[]{:S(2)}, u32[]{:S(2)}) %collective-permute-start.6) | collective-permute-done | bytes 786464 | tf_op jit(solution)/shard_map/ppermute | solution.py:20
  139.4 3.3 %finish_second.1 = f32[3,8,32,2048]{3,2,1,0:T(8,128)} custom-call(s32[2]{0:T(128)S(1)} %pad_add_fusion.where_ref.refs_0_, f32[3,8,32,2048]{3,2,1,0:T(8,128)} %get-tuple-element.39.sums, f32[8,32,2048]{2,1,0:T(8,128)} %s_here.3, f32[2,32,2048]{2,1,0:T(8,128)S(1)} %get-tuple-element.40.totals, ...), custom_call_target="tpu_custom_call", output_to_operand_aliasing={{}: (1, {})} | custom-call | tf_op jit(solution)/shard_map/finish_second/pallas_call | solution.py:524
  (1 shorter events, 0.0 us)
Async XLA Ops:
  0.0 1.6 %copy-start = (f32[8,32,2048]{2,1,0:T(8,128)S(1)}, f32[8,32,2048]{2,1,0:T(8,128)}, u32[]{:S(2)}) copy-start(f32[8,32,2048]{2,1,0:T(8,128)} %s_here.3) | copy-start | bytes 6291460
  1.6 11.0 %copy-start.1 = (f32[8,32,2048]{2,1,0:T(8,128)S(1)}, f32[8,32,2048]{2,1,0:T(8,128)}, u32[]{:S(2)}) copy-start(f32[8,32,2048]{2,1,0:T(8,128)} %s_here.3) | copy-start | bytes 6291460
  4.9 62.0 %copy-start.4 = (s32[512,128]{1,0:T(8,128)S(1)}, s32[512,128]{1,0:T(8,128)}, u32[]{:S(2)}) copy-start(s32[512,128]{1,0:T(8,128)} %list_ref.1) | copy-start | bytes 786436
  4.9 62.0 %copy-start.5 = (s32[512]{0:T(512)S(1)}, s32[512]{0:T(512)}, u32[]{:S(2)}) copy-start(s32[512]{0:T(512)} %owner_ref.1) | copy-start | bytes 6148
  4.9 62.0 %copy-start.6 = (s32[512]{0:T(512)S(1)}, s32[512]{0:T(512)}, u32[]{:S(2)}) copy-start(s32[512]{0:T(512)} %count_ref.1) | copy-start | bytes 6148
  4.9 12.2 %collective-permute-start.1 = (f32[8,8,2048]{2,1,0:T(8,128)}, f32[8,8,2048]{2,1,0:T(8,128)S(1)}, u32[]{:S(2)}, u32[]{:S(2)}) collective-permute-start(f32[8,8,2048]{2,1,0:T(8,128)} %get-tuple-element.28.refs_11_), channel_id=1, source_target_pairs={{0,1},{1,2},{2,3},{3,4},{4,5},{5,6},{6,7},{7,8},{8,9},{9,10},{10,1... | collective-permute-start | bytes 1572872 | tf_op jit(solution)/shard_map/ppermute | solution.py:20
  9.1 13.3 %collective-permute-start.2 = (f32[8,8,2048]{2,1,0:T(8,128)}, f32[8,8,2048]{2,1,0:T(8,128)S(1)}, u32[]{:S(2)}, u32[]{:S(2)}) collective-permute-start(f32[8,8,2048]{2,1,0:T(8,128)} %get-tuple-element.25.after_ref.refs_10_), channel_id=1, source_target_pairs={{1,0},{2,1},{3,2},{4,3},{5,4},{6,5},{7,6},{8,7},{9,8},{10,9},{11,1... | collective-permute-start | bytes 1572872 | tf_op jit(solution)/shard_map/ppermute | solution.py:20
  12.5 40.4 %copy-start.7 = (f32[32,128]{1,0:T(8,128)S(1)}, f32[32,128]{1,0:T(8,128)}, u32[]{:S(2)}) copy-start(f32[32,128]{1,0:T(8,128)} %archard.1) | copy-start | bytes 49156
  12.5 4.6 %collective-permute-start = (f32[32,128]{1,0:T(8,128)}, f32[32,128]{1,0:T(8,128)S(1)}, u32[]{:S(2)}, u32[]{:S(2)}) collective-permute-start(f32[32,128]{1,0:T(8,128)} %archard.1), channel_id=1, source_target_pairs={{0,2},{1,3},{2,0},{3,1},{4,6},{5,7},{6,4},{7,5},{8,10},{9,11},{10,... | collective-permute-start | bytes 49160 | tf_op jit(solution)/shard_map/ppermute | solution.py:104
  22.4 72.6 %collective-permute-start.3 = (f32[4,32,2048]{2,1,0:T(8,128)}, f32[4,32,2048]{2,1,0:T(8,128)}, u32[]{:S(2)}, u32[]{:S(2)}) collective-permute-start(f32[4,32,2048]{2,1,0:T(8,128)} %get-tuple-element.34), channel_id=1, source_target_pairs={{0,16},{16,32},{32,48},{48,64},{64,80},{80,96},{96,112},{1,17},{17... | collective-permute-start | bytes 3145736 | tf_op jit(solution)/shard_map/ppermute | solution.py:20
  50.8 44.2 %collective-permute-start.4 = (f32[4,32,2048]{2,1,0:T(8,128)}, f32[4,32,2048]{2,1,0:T(8,128)}, u32[]{:S(2)}, u32[]{:S(2)}) collective-permute-start(f32[4,32,2048]{2,1,0:T(8,128)} %get-tuple-element.35), channel_id=1, source_target_pairs={{16,0},{32,16},{48,32},{64,48},{80,64},{96,80},{112,96},{17,1},{33... | collective-permute-start | bytes 3145736 | tf_op jit(solution)/shard_map/ppermute | solution.py:20
  66.8 2.2 %copy-start.3 = (s32[1048576]{0:T(1024)S(1)}, s32[1048576]{0:T(1024)}, u32[]{:S(2)}) copy-start(s32[1048576]{0:T(1024)} %param.19) | copy-start | bytes 12582916
  95.0 17.9 %copy-start.2 = (f32[8,32,2048]{2,1,0:T(8,128)S(1)}, f32[8,32,2048]{2,1,0:T(8,128)}, u32[]{:S(2)}) copy-start(f32[8,32,2048]{2,1,0:T(8,128)} %s_here.3) | copy-start | bytes 6291460
  98.8 38.7 %collective-permute-start.5 = (f32[3,32,2048]{2,1,0:T(8,128)S(1)}, f32[3,32,2048]{2,1,0:T(8,128)S(1)}, u32[]{:S(2)}, u32[]{:S(2)}) collective-permute-start(f32[3,32,2048]{2,1,0:T(8,128)S(1)} %get-tuple-element.41), channel_id=1, source_target_pairs={{0,16},{16,32},{32,48},{48,64},{64,80},{80,96},{96,112},{1,17},{17... | collective-permute-start | bytes 2359304 | tf_op jit(solution)/shard_map/ppermute | solution.py:20
  104.4 35.0 %collective-permute-start.6 = (f32[3,32,2048]{2,1,0:T(8,128)S(1)}, f32[3,32,2048]{2,1,0:T(8,128)S(1)}, u32[]{:S(2)}, u32[]{:S(2)}) collective-permute-start(f32[3,32,2048]{2,1,0:T(8,128)S(1)} %get-tuple-element.42), channel_id=1, source_target_pairs={{16,0},{32,16},{48,32},{64,48},{80,64},{96,80},{112,96},{17,1},{33... | collective-permute-start | bytes 2359304 | tf_op jit(solution)/shard_map/ppermute | solution.py:20
  106.5 31.0 %collective-permute-start.7 = (f32[8,2048]{1,0:T(8,128)S(1)}, f32[8,2048]{1,0:T(8,128)S(1)}, u32[]{:S(2)}, u32[]{:S(2)}) collective-permute-start(f32[8,2048]{1,0:T(8,128)S(1)} %get-tuple-element.43), channel_id=1, source_target_pairs={{0,1},{1,2},{2,3},{3,4},{4,5},{5,6},{6,7},{7,8},{8,9},{9,10},{10,1... | collective-permute-start | bytes 196616 | tf_op jit(solution)/shard_map/ppermute | solution.py:20
  108.4 29.1 %collective-permute-start.8 = (f32[8,2048]{1,0:T(8,128)S(1)}, f32[8,2048]{1,0:T(8,128)S(1)}, u32[]{:S(2)}, u32[]{:S(2)}) collective-permute-start(f32[8,2048]{1,0:T(8,128)S(1)} %get-tuple-element.44), channel_id=1, source_target_pairs={{1,0},{2,1},{3,2},{4,3},{5,4},{6,5},{7,6},{8,7},{9,8},{10,9},{11,1... | collective-permute-start | bytes 196616 | tf_op jit(solution)/shard_map/ppermute | solution.py:20

commit v8 on v6

--- a/solution.py
+++ b/solution.py
@@ -113,18 +113,18 @@
 
 
 def paint_kernel(
-    shard_tiles, where_ref, owner_ref, count_ref, wear_ref, list_ref, table_ref, out_ref,
-    own_ref, side_ref, acc_ref, edge_ref,
+    shard_tiles, half, where_ref, owner_ref, count_ref, wear_ref, list_ref, table_ref,
+    *refs,
 ):
-    slots = wear_ref.shape[1]
-    ntile = wear_ref.shape[0]
+    out_ref, own_ref, side_ref, acc_ref, edge_ref = refs[-5:]
+    ntile, slots = list_ref.shape
     rows_table = table_ref.shape[0] // ntile
     tile_len = rows_table * 128
     width = out_ref.shape[1]
     rows = out_ref.shape[0] - 16
     me = where_ref[0]
     on_top = where_ref[1]
-    out_ref[...] = jnp.zeros_like(out_ref)
+    out_ref[...] = jnp.zeros_like(out_ref) if half == 0 else refs[0][...]
 
     @pl.when(on_top == 1)
     def _():
@@ -133,7 +133,8 @@
 
         def collect(i, carry):
             n_own, n_side = carry
-            offset = owner_ref[i] - me
+            same = ((i // (2 * shard_tiles)) ^ (me // 2)) & 1
+            offset = jnp.where(same == half, owner_ref[i] - me, 2)
             own_ref[n_own] = i
             side_ref[n_side] = i
             n_own = n_own + jnp.where(offset == 0, 1, 0)
@@ -164,8 +165,7 @@
                 jnp.where(table_row == (local >> 7), picked, 0), axis=0, keepdims=True
             )
             shard = i // shard_tiles
-            half = jnp.where((shard // 2) % 2 == (me // 2) % 2, 0, 1)
-            place = half * (ntile // shard_tiles // 2) + (shard // 4) * 2 + shard % 2
+            place = (shard // 4) * 2 + shard % 2
             at = place * shard_tiles + i % shard_tiles
             wear = jnp.where(lane < live, wear_ref[pl.ds(at, 1), :], 0.0)
             return i, cell, wear
@@ -216,26 +216,27 @@
         lax.fori_loop(0, (n_own + GROUP - 1) // GROUP, own_group, 0)
         lax.fori_loop(0, (n_side + GROUP - 1) // GROUP, side_group, 0)
         for j in range(8):
-            out_ref[8 : 8 + rows, j * block : (j + 1) * block] = acc_ref[
+            out_ref[8 : 8 + rows, j * block : (j + 1) * block] += acc_ref[
                 j * rows : (j + 1) * rows, :
             ]
         for j in range(edge_blocks):
-            out_ref[7:8, j * 128 : (j + 1) * 128] = edge_ref[j : j + 1, :]
-            out_ref[8 + rows : 9 + rows, j * 128 : (j + 1) * 128] = edge_ref[
+            out_ref[7:8, j * 128 : (j + 1) * 128] += edge_ref[j : j + 1, :]
+            out_ref[8 + rows : 9 + rows, j * 128 : (j + 1) * 128] += edge_ref[
                 edge_blocks + j : edge_blocks + j + 1, :
             ]
 
 
-def paint(position, owner, counts, wear, lists, table, rows, width, shard_tiles):
+def paint(position, owner, counts, wear, lists, table, rows, width, shard_tiles, base=None):
     ntile, slots = lists.shape
+    args = [wear, lists, table] + ([] if base is None else [base])
     whole = lambda shape: pl.BlockSpec(shape, lambda i, *_: (0,) * len(shape))
     return pl.pallas_call(
-        functools.partial(paint_kernel, shard_tiles),
+        functools.partial(paint_kernel, shard_tiles, 0 if base is None else 1),
         name="paint_band",
         grid_spec=pltpu.PrefetchScalarGridSpec(
             num_scalar_prefetch=3,
             grid=(1,),
-            in_specs=[whole(wear.shape), whole(lists.shape), whole(table.shape)],
+            in_specs=[whole(a.shape) for a in args],
             out_specs=whole((rows + 16, width)),
             scratch_shapes=[
                 pltpu.SMEM((ntile + 1,), jnp.int32),
@@ -246,7 +247,7 @@
         ),
         out_shape=jax.ShapeDtypeStruct((rows + 16, width), jnp.float32),
         compiler_params=pltpu.CompilerParams(vmem_limit_bytes=VMEM_LIMIT),
-    )(position, owner, counts, wear, lists, table)
+    )(position, owner, counts, *args)
 
 
 def relax_tile(load, beside, has_high, has_low):
@@ -256,17 +257,23 @@
         here = load(c, 0)
         centers[c] = here
         width = here.shape[1]
-        lane = lax.broadcasted_iota(jnp.int32, here.shape, 1)
+        lane = lax.broadcasted_iota(jnp.int32, (here.shape[0], 128), 1)
         yield load(c, 1)
         yield load(c, -1)
         yield from beside(c, here)
-        yield jnp.where(lane == width - 1, 0.0, pltpu.roll(here, width - 1, 1))
-        yield jnp.where(lane == 0, 0.0, pltpu.roll(here, 1, 1))
+        right = pltpu.roll(here, width - 1, 1)
+        end = jnp.where(lane == 127, 0.0, right[:, width - 128 :])
+        yield jnp.concatenate([right[:, : width - 128], end], axis=1)
+        left = pltpu.roll(here, 1, 1)
+        end = jnp.where(lane == 0, 0.0, left[:, :128])
+        yield jnp.concatenate([end, left[:, 128:]], axis=1)
 
     around = list(neighbours(3))
     weights = [centers[3] + s for s in around]
-    weights[0] = weights[0] * has_high
-    weights[1] = weights[1] * has_low
+    if has_high is not None:
+        weights[0] = weights[0] * has_high
+    if has_low is not None:
+        weights[1] = weights[1] * has_low
     total = weights[0]
     for w in weights[1:]:
         total = total + w
@@ -286,7 +293,7 @@
             here = here + jnp.where(layer == 0, surface[at : at + 1, :], 0.0)
         return here if side == 0 else pltpu.roll(here, 7 if side == 1 else 1, 0)
 
-    sums, total, _ = relax_tile(load, lambda c, here: (far[c], inside[c]), 1.0, 1.0)
+    sums, total, _ = relax_tile(load, lambda c, here: (far[c], inside[c]), None, None)
     inverse = 1.0 / total
     between = jnp.logical_and(layer > 0, layer < out.shape[1] - 1)
     kept = jnp.logical_and(between, s_near[0] > 0.0)
@@ -326,8 +333,8 @@
             relax_outside(out_after, after, s_after, far_after, own_last, surface,
                           8 + 8 * ntiles, row)
 
-    has_low = jnp.where(layer == 0, 0.0, 1.0)
-    has_high = jnp.where(layer == last, 0.0, 1.0)
+    has_low = None if first_sweep else jnp.where(layer == 0, 0.0, 1.0)
+    has_high = None if first_sweep else jnp.where(layer == last, 0.0, 1.0)
     scale = jnp.where(layer == 1, 1.0, 0.0)
     pinned = jnp.logical_and(layer == 0, where_ref[1] == 1)
 
@@ -454,7 +461,7 @@
             yield jnp.where(row == 7, below, pltpu.roll(tile, 7, 0))
             yield jnp.where(row == 0, above, pltpu.roll(tile, 1, 0))
 
-        parts, total, _ = relax_tile(load, beside, 1.0, 0.0)
+        parts, total, _ = relax_tile(load, beside, None, 0.0)
         for c in range(3):
             sums[c, 0, at, :] = parts[c]
         totals[0, at, :] = total
@@ -627,20 +634,27 @@
     row_first, row_last = pack_rows(displacement, stiffness)
     before, after = shift_both(row_last, row_first, "tan")
     wear = archard(wear_class, pressure, slip_speed, rate_table)
-    wear = gather_wear(wear)
+    own, other = gather_wear(wear)
+    table = node_cell.reshape(-1, 128)
+    tiles_here = wear_class.shape[0]
+    surface = paint(position, tile_owner, active_count, own, node_list, table,
+                    rows, width, tiles_here)
     sums, totals = face_sums(displacement, stiffness)
-    low, high, wear = lax.optimization_barrier((low, high, wear))
+    low, high, other, surface = lax.optimization_barrier((low, high, other, surface))
     face_first, face_last, edge_first, edge_last = finish_first(
         sums, stiffness, totals, low, high, before, after
     )
     low_2, high_2 = shift_both(face_last, face_first, "depth")
-    edge_before, edge_after = shift_both(edge_last, edge_first, "tan")
-    surface = paint(position, tile_owner, active_count, jnp.concatenate(wear), node_list,
-                    node_cell.reshape(-1, 128), rows, width, wear_class.shape[0])
+    surface = paint(position, tile_owner, active_count, other, node_list, table,
+                    rows, width, tiles_here, surface)
     first, before_2, after_2 = relax_layers(
         position, displacement, stiffness, before, after, before, after, surface,
         (face_first, face_last), (row_first, row_last),
     )
+    edge_first, edge_last, before_2 = lax.optimization_barrier(
+        (edge_first, edge_last, before_2)
+    )
+    edge_before, edge_after = shift_both(edge_last, edge_first, "tan")
     result, totals = relax_layers(
         position, first, stiffness, before_2, after_2, before, after
     )

time: 131 us -> 128 us (0.977)
  waiting for transfers between devices: 25.1 us -> 11.3 us
  Pallas kernels: 54 us -> 62.4 us
  local copies, waits for them, and re-layouts: 4.93 us -> 6.77 us
    ppermute x1, waiting for transfers between devices: 25.1 us -> 11.3 us  [gather_wear(): return (own, lax.ppermute(own, 'tan', [(i, i ^ 2) for i in range(size)]))]
    pallas_call x1 -> x2, Pallas kernels: 12.4 us -> 22.4 us  [paint(): pl.pallas_call(functools.partial(paint_kernel, shard_tiles, 0 if base is...]
    unnamed x16 -> x22, local copies, waits for them, and re-layouts: 4.93 us -> 6.77 us
  transfers between devices with their start and end apart: 9 -> 9, of which waited for: 1 -> 1; matrix products, arithmetic and copies ran while one was open for 0% -> 0% of each run, Pallas kernels for 34% -> 42%
where the time goes in v8:
time: 128 us; the launch traced here: 127 us
  Pallas kernels  62.4 us (49%)
  starting transfers between devices  28.5 us (22%)
  blocking collectives  17.9 us (14%)
  waiting for transfers between devices  11.3 us (9%)
  local copies, waits for them, and re-layouts  6.77 us (5%)
    ppermute x8, starting transfers between devices, shift_both(): return (lax.ppermute(last, axis, up), lax.ppermute(first, axis, down))  28.4 us
    pallas_call x2, Pallas kernels, relax_layers(): pl.pallas_call(functools.partial(layer_kernel, first_sweep), name='relax_...  23.8 us
    pallas_call x2, Pallas kernels, paint(): pl.pallas_call(functools.partial(paint_kernel, shard_tiles, 0 if base is...  22.4 us
    all_gather x1, blocking collectives, gather_wear(): lax.all_gather(wear, 'tan', axis=0, axis_index_groups=groups, tiled=True)  17.9 us
    ppermute x1, waiting for transfers between devices, gather_wear(): return (own, lax.ppermute(own, 'tan', [(i, i ^ 2) for i in range(size)]))  11.3 us
    unnamed x22, local copies, waits for them, and re-layouts  6.77 us
    pallas_call x1, Pallas kernels, finish_second(): pl.pallas_call(finish_second_kernel, name='finish_second', grid_spec=pltp...  3.33 us
    pallas_call x1, Pallas kernels, pack_rows(): pl.pallas_call(rows_kernel, name='pack_rows', grid=(1,), in_specs=[f_spec...  3.25 us
  transfers between devices with their start and end apart: 9, of which 1 were waited for; matrix products, arithmetic and copies ran while one was open for 0% of the time, Pallas kernels for 42%

profile of v8, /device:TPU:4, one launch (start us, length us, event | category | flops | bytes accessed | tf_op | source)
XLA Modules:
  0.0 127.1 jit_solution(2073100609763173464)
XLA Ops:
  0.0 0.0 copy-start
  0.0 1.6 %copy-done = f32[8,32,2048]{2,1,0:T(8,128)S(1)} copy-done((f32[8,32,2048]{2,1,0:T(8,128)S(1)}, f32[8,32,2048]{2,1,0:T(8,128)}, u32[]{:S(2)}) %copy-start) | copy-done | bytes 2097176
  1.6 2.8 %pack_faces.1 = (f32[4,32,2048]{2,1,0:T(8,128)}, f32[4,32,2048]{2,1,0:T(8,128)}) custom-call(f32[3,8,32,2048]{3,2,1,0:T(8,128)} %refs_1_.1, f32[8,32,2048]{2,1,0:T(8,128)S(1)} %copy-done), custom_call_target="tpu_custom_call" | custom-call | tf_op jit(solution)/shard_map/pack_faces/pallas_call | solution.py:87
  4.4 6.7 %collective-permute-start.2 = (f32[4,32,2048]{2,1,0:T(8,128)}, f32[4,32,2048]{2,1,0:T(8,128)}, u32[]{:S(2)}, u32[]{:S(2)}) collective-permute-start(f32[4,32,2048]{2,1,0:T(8,128)} %get-tuple-element.29), channel_id=1, source_target_pairs={{0,16},{16,32},{32,48},{48,64},{64,80},{80,96},{96,112},{1,17},{17... | collective-permute-start | bytes 3145736 | tf_op jit(solution)/shard_map/ppermute | solution.py:20
  11.1 1.4 %collective-permute-start.3 = (f32[4,32,2048]{2,1,0:T(8,128)}, f32[4,32,2048]{2,1,0:T(8,128)}, u32[]{:S(2)}, u32[]{:S(2)}) collective-permute-start(f32[4,32,2048]{2,1,0:T(8,128)} %get-tuple-element.30), channel_id=1, source_target_pairs={{16,0},{32,16},{48,32},{64,48},{80,64},{96,80},{112,96},{17,1},{33... | collective-permute-start | bytes 3145736 | tf_op jit(solution)/shard_map/ppermute | solution.py:20
  12.5 3.2 %pack_rows.1 = (f32[8,8,2048]{2,1,0:T(8,128)}, f32[8,8,2048]{2,1,0:T(8,128)}) custom-call(f32[3,8,32,2048]{3,2,1,0:T(8,128)} %refs_1_.1, f32[8,32,2048]{2,1,0:T(8,128)S(1)} %copy-done, f32[3,8,32,2048]{3,2,1,0:T(8,128)} %refs_1_.1, f32[8,32,2048]{2,1,0:T(8,128)S(1)} %copy-done), custom_call_target="tpu_custom_call" | custom-call | tf_op jit(solution)/shard_map/pack_rows/pallas_call | solution.py:60
  15.8 1.9 %collective-permute-start = (f32[8,8,2048]{2,1,0:T(8,128)}, f32[8,8,2048]{2,1,0:T(8,128)S(1)}, u32[]{:S(2)}, u32[]{:S(2)}) collective-permute-start(f32[8,8,2048]{2,1,0:T(8,128)} %get-tuple-element.27.refs_13_), channel_id=1, source_target_pairs={{0,1},{1,2},{2,3},{3,4},{4,5},{5,6},{6,7},{7,8},{8,9},{9,10},{10,1... | collective-permute-start | bytes 1572872 | tf_op jit(solution)/shard_map/ppermute | solution.py:20
  17.7 4.5 %collective-permute-start.1 = (f32[8,8,2048]{2,1,0:T(8,128)}, f32[8,8,2048]{2,1,0:T(8,128)S(1)}, u32[]{:S(2)}, u32[]{:S(2)}) collective-permute-start(f32[8,8,2048]{2,1,0:T(8,128)} %get-tuple-element.28.refs_12_), channel_id=1, source_target_pairs={{1,0},{2,1},{3,2},{4,3},{5,4},{6,5},{7,6},{8,7},{9,8},{10,9},{11,1... | collective-permute-start | bytes 1572872 | tf_op jit(solution)/shard_map/ppermute | solution.py:20
  22.2 1.4 %archard.1 = f32[32,128]{1,0:T(8,128)} custom-call(f32[8]{0:T(128)} %rates_ref.1, s32[32,128]{1,0:T(8,128)} %class_ref.1, f32[32,128]{1,0:T(8,128)} %contact_ref.1, f32[32,128]{1,0:T(8,128)} %sliding_ref.1), custom_call_target="tpu_custom_call" | custom-call | tf_op jit(solution)/shard_map/archard/pallas_call | solution.py:34
  23.7 17.9 %all_gather.3.wear_ref = f32[256,128]{1,0:T(8,128)S(1)} all-gather(f32[32,128]{1,0:T(8,128)} %archard.1), channel_id=1, replica_groups={{0,1,4,5,8,9,12,13},{2,3,6,7,10,11,14,15},{16,17,20,21,24,25,28,29},{18..., dimensions={0}, use_global_device_ids=true | all-gather | bytes 147456 | tf_op jit(solution)/shard_map/all_gather | solution.py:104
  41.6 0.0 collective-permute-start.4
  41.6 0.0 copy-done.1
  41.6 0.0 copy-start.9
  41.6 0.0 copy-start.10
  41.6 3.1 %face_sums.1 = (f32[3,2,32,2048]{3,2,1,0:T(8,128)S(1)}, f32[2,32,2048]{2,1,0:T(8,128)S(1)}) custom-call(f32[3,8,32,2048]{3,2,1,0:T(8,128)} %refs_1_.1, f32[3,8,32,2048]{3,2,1,0:T(8,128)} %refs_1_.1, f32[8,32,2048]{2,1,0:T(8,128)S(1)} %copy-done.1, f32[8,32,2048]{2,1,0:T(8,128)S(1)} %copy-done.1), custom_call_target="tpu_custom_call" | custom-call | tf_op jit(solution)/shard_map/face_sums/pallas_call | solution.py:477
  44.7 0.0 copy-start.5
  44.8 1.1 copy-done.5
  45.9 0.8 copy-done.7
  46.7 0.1 pad_add_fusion.where_ref.refs_0_
  46.8 0.0 copy-done.6
  46.8 0.0 copy-done.9
  46.8 0.0 copy-done.10
  46.8 2.2 %copy-done.3 = s32[1048576]{0:T(1024)S(1)} copy-done((s32[1048576]{0:T(1024)S(1)}, s32[1048576]{0:T(1024)}, u32[]{:S(2)}) %copy-start.3) | copy-done | bytes 4194328
  49.0 10.6 %paint_band.2.refs_0_ = f32[48,2048]{1,0:T(8,128)S(1)} custom-call(s32[2]{0:T(128)S(1)} %pad_add_fusion.where_ref.refs_0_, s32[512]{0:T(512)S(1)} %copy-done.9, s32[512]{0:T(512)S(1)} %copy-done.10, f32[256,128]{1,0:T(8,128)S(1)} %all_gather.3.wear_ref, s32[512,128]{1,0:T(8,128)S(1)} %copy-done.6, s32[8192,128]{1,0:T(8,128)S(1)} %bitcast.3), custom_call_target="tpu_custom_call" | custom-call | tf_op jit(solution)/shard_map/paint_band/pallas_call | solution.py:233
  59.5 0.0 copy-start.4
  59.6 11.3 %collective-permute-done.4.wear_ref = f32[256,128]{1,0:T(8,128)} collective-permute-done((f32[256,128]{1,0:T(8,128)S(1)}, f32[256,128]{1,0:T(8,128)}, u32[]{:S(2)}, u32[]{:S(2)}) %collective-permute-start.4) | collective-permute-done | bytes 131104 | tf_op jit(solution)/shard_map/ppermute | solution.py:105
  70.8 0.0 collective-permute-done.2.low.s_low
  70.9 0.0 collective-permute-done.3.high.s_high
  70.9 0.0 collective-permute-done.before.s_before.refs_3_.refs_5_.refs_10_
  70.9 0.0 collective-permute-done.1.after.s_after.refs_4_.refs_6_.refs_11_
  70.9 0.0 copy-start.8
  70.9 1.0 copy-done.8
  71.9 2.4 %finish_first.1 = (f32[3,32,2048]{2,1,0:T(8,128)S(1)}, f32[3,32,2048]{2,1,0:T(8,128)S(1)}, f32[8,2048]{1,0:T(8,128)S(1)}, f32[8,2048]{1,0:T(8,128)S(1)}) custom-call(f32[3,2,32,2048]{3,2,1,0:T(8,128)} %copy-done.5, f32[8,32,2048]{2,1,0:T(8,128)} %s_here.5, f32[2,32,2048]{2,1,0:T(8,128)S(1)} %copy-done.8, f32[4,32,2048]{2,1,0:T(8,128)} %collective-permute-done.2.low.s_low, ...), custom_call_target="tpu_custom_call" | custom-call | tf_op jit(solution)/shard_map/finish_first/pallas_call | solution.py:541
  74.3 1.3 %collective-permute-start.6 = (f32[3,32,2048]{2,1,0:T(8,128)S(1)}, f32[3,32,2048]{2,1,0:T(8,128)S(1)}, u32[]{:S(2)}, u32[]{:S(2)}) collective-permute-start(f32[3,32,2048]{2,1,0:T(8,128)S(1)} %get-tuple-element.37.refs_8_), channel_id=1, source_target_pairs={{16,0},{32,16},{48,32},{64,48},{80,64},{96,80},{112,96},{17,1},{33... | collective-permute-start | bytes 2359304 | tf_op jit(solution)/shard_map/ppermute | solution.py:20
  75.6 6.1 %collective-permute-start.5 = (f32[3,32,2048]{2,1,0:T(8,128)S(1)}, f32[3,32,2048]{2,1,0:T(8,128)S(1)}, u32[]{:S(2)}, u32[]{:S(2)}) collective-permute-start(f32[3,32,2048]{2,1,0:T(8,128)S(1)} %get-tuple-element.38.refs_9_), channel_id=1, source_target_pairs={{0,16},{16,32},{32,48},{48,64},{64,80},{80,96},{96,112},{1,17},{17... | collective-permute-start | bytes 2359304 | tf_op jit(solution)/shard_map/ppermute | solution.py:20
  81.7 0.0 copy-done.4
  81.7 11.8 %paint_band.3.refs_7_ = f32[48,2048]{1,0:T(8,128)S(1)} custom-call(s32[2]{0:T(128)S(1)} %pad_add_fusion.where_ref.refs_0_, s32[512]{0:T(512)S(1)} %copy-done.9, s32[512]{0:T(512)S(1)} %copy-done.10, f32[256,128]{1,0:T(8,128)} %collective-permute-done.4.wear_ref, s32[512,128]{1,0:T(8,128)S(1)} %copy-done.6, s32[8192,128]{1,0:T(8,128)S(1)} %bitcast.4, ...), custom_call_target="tpu_custom_call" | custom-call | tf_op jit(solution)/shard_map/paint_band/pallas_call | solution.py:233
  93.5 0.0 copy-start.2
  93.5 11.9 %relax_layers_first.1 = (f32[3,8,32,2048]{3,2,1,0:T(8,128)}, f32[3,8,2048]{2,1,0:T(8,128)S(1)}, f32[3,8,2048]{2,1,0:T(8,128)S(1)}) custom-call(s32[2]{0:T(128)S(1)} %pad_add_fusion.where_ref.refs_0_, f32[3,8,32,2048]{3,2,1,0:T(8,128)} %refs_1_.1, f32[8,32,2048]{2,1,0:T(8,128)} %s_here.5, ...), custom_call_target="tpu_custom_call" | custom-call | tf_op jit(solution)/shard_map/relax_layers_first/pallas_call | solution.py:429
  105.5 1.9 %collective-permute-start.7 = (f32[8,2048]{1,0:T(8,128)S(1)}, f32[8,2048]{1,0:T(8,128)S(1)}, u32[]{:S(2)}, u32[]{:S(2)}) collective-permute-start(f32[8,2048]{1,0:T(8,128)S(1)} %get-tuple-element.47), channel_id=1, source_target_pairs={{0,1},{1,2},{2,3},{3,4},{4,5},{5,6},{6,7},{7,8},{8,9},{9,10},{10,1... | collective-permute-start | bytes 196616 | tf_op jit(solution)/shard_map/ppermute | solution.py:20
  107.4 4.5 %collective-permute-start.8 = (f32[8,2048]{1,0:T(8,128)S(1)}, f32[8,2048]{1,0:T(8,128)S(1)}, u32[]{:S(2)}, u32[]{:S(2)}) collective-permute-start(f32[8,2048]{1,0:T(8,128)S(1)} %get-tuple-element.48), channel_id=1, source_target_pairs={{1,0},{2,1},{3,2},{4,3},{5,4},{6,5},{7,6},{8,7},{9,8},{10,9},{11,1... | collective-permute-start | bytes 196616 | tf_op jit(solution)/shard_map/ppermute | solution.py:20
  111.9 0.0 copy-done.2
  111.9 11.8 %relax_layers_second.1 = (f32[3,8,32,2048]{3,2,1,0:T(8,128)}, f32[2,32,2048]{2,1,0:T(8,128)S(1)}) custom-call(s32[2]{0:T(128)S(1)} %pad_add_fusion.where_ref.refs_0_, f32[3,8,32,2048]{3,2,1,0:T(8,128)} %get-tuple-element.39.refs_1_, f32[8,32,2048]{2,1,0:T(8,128)S(1)} %copy-done.2, f32[3,8,2048]{2,1,0:T(8,128)S(1)} %get-tuple-element.43.refs_3_, ...), custom_call_target="tpu_custom_call" | custom-call | tf_op jit(solution)/shard_map/relax_layers_second/pallas_call | solution.py:429
  123.8 0.0 collective-permute-done.7.before
  123.8 0.0 collective-permute-done.8.after
  123.8 0.0 collective-permute-done.6.high
  123.8 0.0 collective-permute-done.5.low
  123.8 3.3 %finish_second.1 = f32[3,8,32,2048]{3,2,1,0:T(8,128)} custom-call(s32[2]{0:T(128)S(1)} %pad_add_fusion.where_ref.refs_0_, f32[3,8,32,2048]{3,2,1,0:T(8,128)} %get-tuple-element.45.sums, f32[8,32,2048]{2,1,0:T(8,128)} %s_here.5, f32[2,32,2048]{2,1,0:T(8,128)S(1)} %get-tuple-element.46.totals, ...), custom_call_target="tpu_custom_call", output_to_operand_aliasing={{}: (1, {})} | custom-call | tf_op jit(solution)/shard_map/finish_second/pallas_call | solution.py:598
  (4 shorter events, 0.0 us)
Async XLA Ops:
  0.0 1.6 %copy-start = (f32[8,32,2048]{2,1,0:T(8,128)S(1)}, f32[8,32,2048]{2,1,0:T(8,128)}, u32[]{:S(2)}) copy-start(f32[8,32,2048]{2,1,0:T(8,128)} %s_here.5) | copy-start | bytes 6291460
  4.4 66.5 %collective-permute-start.2 = (f32[4,32,2048]{2,1,0:T(8,128)}, f32[4,32,2048]{2,1,0:T(8,128)}, u32[]{:S(2)}, u32[]{:S(2)}) collective-permute-start(f32[4,32,2048]{2,1,0:T(8,128)} %get-tuple-element.29), channel_id=1, source_target_pairs={{0,16},{16,32},{32,48},{48,64},{64,80},{80,96},{96,112},{1,17},{17... | collective-permute-start | bytes 3145736 | tf_op jit(solution)/shard_map/ppermute | solution.py:20
  11.1 30.5 %copy-start.1 = (f32[8,32,2048]{2,1,0:T(8,128)S(1)}, f32[8,32,2048]{2,1,0:T(8,128)}, u32[]{:S(2)}) copy-start(f32[8,32,2048]{2,1,0:T(8,128)} %s_here.5) | copy-start | bytes 6291460
  11.1 59.7 %collective-permute-start.3 = (f32[4,32,2048]{2,1,0:T(8,128)}, f32[4,32,2048]{2,1,0:T(8,128)}, u32[]{:S(2)}, u32[]{:S(2)}) collective-permute-start(f32[4,32,2048]{2,1,0:T(8,128)} %get-tuple-element.30), channel_id=1, source_target_pairs={{16,0},{32,16},{48,32},{64,48},{80,64},{96,80},{112,96},{17,1},{33... | collective-permute-start | bytes 3145736 | tf_op jit(solution)/shard_map/ppermute | solution.py:20
  15.8 55.1 %collective-permute-start = (f32[8,8,2048]{2,1,0:T(8,128)}, f32[8,8,2048]{2,1,0:T(8,128)S(1)}, u32[]{:S(2)}, u32[]{:S(2)}) collective-permute-start(f32[8,8,2048]{2,1,0:T(8,128)} %get-tuple-element.27.refs_13_), channel_id=1, source_target_pairs={{0,1},{1,2},{2,3},{3,4},{4,5},{5,6},{6,7},{7,8},{8,9},{9,10},{10,1... | collective-permute-start | bytes 1572872 | tf_op jit(solution)/shard_map/ppermute | solution.py:20
  17.7 53.2 %collective-permute-start.1 = (f32[8,8,2048]{2,1,0:T(8,128)}, f32[8,8,2048]{2,1,0:T(8,128)S(1)}, u32[]{:S(2)}, u32[]{:S(2)}) collective-permute-start(f32[8,8,2048]{2,1,0:T(8,128)} %get-tuple-element.28.refs_12_), channel_id=1, source_target_pairs={{1,0},{2,1},{3,2},{4,3},{5,4},{6,5},{7,6},{8,7},{9,8},{10,9},{11,1... | collective-permute-start | bytes 1572872 | tf_op jit(solution)/shard_map/ppermute | solution.py:20
  41.6 29.3 %collective-permute-start.4 = (f32[256,128]{1,0:T(8,128)S(1)}, f32[256,128]{1,0:T(8,128)}, u32[]{:S(2)}, u32[]{:S(2)}) collective-permute-start(f32[256,128]{1,0:T(8,128)S(1)} %all_gather.3.wear_ref), channel_id=1, source_target_pairs={{0,2},{1,3},{2,0},{3,1},{4,6},{5,7},{6,4},{7,5},{8,10},{9,11},{10,... | collective-permute-start | bytes 393224 | tf_op jit(solution)/shard_map/ppermute | solution.py:105
  41.6 5.2 %copy-start.6 = (s32[512,128]{1,0:T(8,128)S(1)}, s32[512,128]{1,0:T(8,128)}, u32[]{:S(2)}) copy-start(s32[512,128]{1,0:T(8,128)} %list_ref.3) | copy-start | bytes 786436
  41.6 5.2 %copy-start.9 = (s32[512]{0:T(512)S(1)}, s32[512]{0:T(512)}, u32[]{:S(2)}) copy-start(s32[512]{0:T(512)} %owner_ref.3) | copy-start | bytes 6148
  41.6 5.2 %copy-start.10 = (s32[512]{0:T(512)S(1)}, s32[512]{0:T(512)}, u32[]{:S(2)}) copy-start(s32[512]{0:T(512)} %count_ref.3) | copy-start | bytes 6148
  44.7 1.1 copy-start.5
  45.9 0.8 copy-start.7
  46.8 2.2 %copy-start.3 = (s32[1048576]{0:T(1024)S(1)}, s32[1048576]{0:T(1024)}, u32[]{:S(2)}) copy-start(s32[1048576]{0:T(1024)} %param.19) | copy-start | bytes 12582916
  59.5 22.2 %copy-start.4 = (s32[1048576]{0:T(1024)S(1)}, s32[1048576]{0:T(1024)}, u32[]{:S(2)}) copy-start(s32[1048576]{0:T(1024)} %param.19) | copy-start | bytes 12582916
  70.9 1.0 copy-start.8
  74.3 49.5 %collective-permute-start.6 = (f32[3,32,2048]{2,1,0:T(8,128)S(1)}, f32[3,32,2048]{2,1,0:T(8,128)S(1)}, u32[]{:S(2)}, u32[]{:S(2)}) collective-permute-start(f32[3,32,2048]{2,1,0:T(8,128)S(1)} %get-tuple-element.37.refs_8_), channel_id=1, source_target_pairs={{16,0},{32,16},{48,32},{64,48},{80,64},{96,80},{112,96},{17,1},{33... | collective-permute-start | bytes 2359304 | tf_op jit(solution)/shard_map/ppermute | solution.py:20
  75.6 48.2 %collective-permute-start.5 = (f32[3,32,2048]{2,1,0:T(8,128)S(1)}, f32[3,32,2048]{2,1,0:T(8,128)S(1)}, u32[]{:S(2)}, u32[]{:S(2)}) collective-permute-start(f32[3,32,2048]{2,1,0:T(8,128)S(1)} %get-tuple-element.38.refs_9_), channel_id=1, source_target_pairs={{0,16},{16,32},{32,48},{48,64},{64,80},{80,96},{96,112},{1,17},{17... | collective-permute-start | bytes 2359304 | tf_op jit(solution)/shard_map/ppermute | solution.py:20
  93.5 18.4 %copy-start.2 = (f32[8,32,2048]{2,1,0:T(8,128)S(1)}, f32[8,32,2048]{2,1,0:T(8,128)}, u32[]{:S(2)}) copy-start(f32[8,32,2048]{2,1,0:T(8,128)} %s_here.5) | copy-start | bytes 6291460
  105.5 18.3 %collective-permute-start.7 = (f32[8,2048]{1,0:T(8,128)S(1)}, f32[8,2048]{1,0:T(8,128)S(1)}, u32[]{:S(2)}, u32[]{:S(2)}) collective-permute-start(f32[8,2048]{1,0:T(8,128)S(1)} %get-tuple-element.47), channel_id=1, source_target_pairs={{0,1},{1,2},{2,3},{3,4},{4,5},{5,6},{6,7},{7,8},{8,9},{9,10},{10,1... | collective-permute-start | bytes 196616 | tf_op jit(solution)/shard_map/ppermute | solution.py:20
  107.4 16.4 %collective-permute-start.8 = (f32[8,2048]{1,0:T(8,128)S(1)}, f32[8,2048]{1,0:T(8,128)S(1)}, u32[]{:S(2)}, u32[]{:S(2)}) collective-permute-start(f32[8,2048]{1,0:T(8,128)S(1)} %get-tuple-element.48), channel_id=1, source_target_pairs={{1,0},{2,1},{3,2},{4,3},{5,4},{6,5},{7,6},{8,7},{9,8},{10,9},{11,1... | collective-permute-start | bytes 196616 | tf_op jit(solution)/shard_map/ppermute | solution.py:20

commit v9 on v8

--- a/solution.py
+++ b/solution.py
@@ -112,11 +112,46 @@
     return high, middle, rest - middle
 
 
+def collect_kernel(shard_tiles, where_ref, owner_ref, out_ref):
+    ntile = owner_ref.shape[0]
+    room = out_ref.shape[0] // 4
+    me = where_ref[0]
+    for k in range(4):
+        out_ref[(k + 1) * room - 1] = 0
+
+    @pl.when(where_ref[1] == 1)
+    def _():
+        def step(i, ends):
+            offset = owner_ref[i] - me
+            other = ((i // (2 * shard_tiles)) ^ (me // 2)) & 1
+            kind = jnp.where(offset == 0, 0, jnp.where(offset * offset == 1, 1, 8)) + 2 * other
+            for end in ends:
+                out_ref[end] = i
+            return tuple(end + jnp.where(kind == k, 1, 0) for k, end in enumerate(ends))
+
+        starts = tuple(jnp.int32(k * room) for k in range(4))
+        ends = lax.fori_loop(0, ntile, step, starts, unroll=8)
+        for k in range(4):
+            out_ref[(k + 1) * room - 1] = ends[k] - k * room
+
+
+def collect(position, owner, shard_tiles):
+    return pl.pallas_call(
+        functools.partial(collect_kernel, shard_tiles),
+        name="collect_tiles",
+        in_specs=[pl.BlockSpec(memory_space=pltpu.SMEM)] * 2,
+        out_specs=pl.BlockSpec(memory_space=pltpu.SMEM),
+        out_shape=jax.ShapeDtypeStruct((4 * (owner.shape[0] + 128),), jnp.int32),
+    )(position, owner)
+
+
 def paint_kernel(
-    shard_tiles, half, where_ref, owner_ref, count_ref, wear_ref, list_ref, table_ref,
+    shard_tiles, half, where_ref, owner_ref, count_ref, tiles_ref, wear_ref, list_ref,
+    table_ref,
     *refs,
 ):
-    out_ref, own_ref, side_ref, acc_ref, edge_ref = refs[-5:]
+    out_ref, acc_ref, edge_ref = refs[-3:]
+    room = tiles_ref.shape[0] // 4
     ntile, slots = list_ref.shape
     rows_table = table_ref.shape[0] // ntile
     tile_len = rows_table * 128
@@ -131,20 +166,8 @@
         acc_ref[...] = jnp.zeros_like(acc_ref)
         edge_ref[...] = jnp.zeros_like(edge_ref)
 
-        def collect(i, carry):
-            n_own, n_side = carry
-            same = ((i // (2 * shard_tiles)) ^ (me // 2)) & 1
-            offset = jnp.where(same == half, owner_ref[i] - me, 2)
-            own_ref[n_own] = i
-            side_ref[n_side] = i
-            n_own = n_own + jnp.where(offset == 0, 1, 0)
-            n_side = n_side + jnp.where(offset * offset == 1, 1, 0)
-            return n_own, n_side
-
-        n_own, n_side = lax.fori_loop(
-            0, ntile, collect, (jnp.int32(0), jnp.int32(0)), unroll=8
-        )
-
+        n_own = tiles_ref[(2 * half + 1) * room - 1]
+        n_side = tiles_ref[(2 * half + 2) * room - 1]
         lane = lax.broadcasted_iota(jnp.int32, (1, slots), 1)
         table_row = lax.broadcasted_iota(jnp.int32, (rows_table, slots), 0)
         block = width // 8
@@ -154,8 +177,8 @@
         edge_blocks = width // 128
         coarse_edge = lax.broadcasted_iota(jnp.int32, (2 * edge_blocks, slots), 0)
 
-        def entry(tiles_ref, position, total):
-            i = tiles_ref[jnp.minimum(position, total - 1)]
+        def entry(kind, position, total):
+            i = tiles_ref[(2 * half + kind) * room + jnp.minimum(position, total - 1)]
             live = jnp.where(position < total, count_ref[i], 0)
             local = list_ref[pl.ds(i, 1), :] - i * tile_len
             table = table_ref[pl.ds(pl.multiple_of(i * rows_table, 8), rows_table), :]
@@ -186,7 +209,7 @@
             parts = ([], [], [])
             hots = []
             for j in range(GROUP):
-                _, cell, wear = entry(own_ref, g * GROUP + j, n_own)
+                _, cell, wear = entry(0, g * GROUP + j, n_own)
                 col = cell % width
                 a_index = (col // block) * rows + cell // width
                 hots.append(one_hot(fine == col % block, 1.0))
@@ -200,7 +223,7 @@
             parts = ([], [], [])
             hots = []
             for j in range(GROUP):
-                i, cell, wear = entry(side_ref, g * GROUP + j, n_side)
+                i, cell, wear = entry(1, g * GROUP + j, n_side)
                 below = owner_ref[i] > me
                 col = cell % width
                 wanted = jnp.where(below, 0, rows - 1)
@@ -226,28 +249,25 @@
             ]
 
 
-def paint(position, owner, counts, wear, lists, table, rows, width, shard_tiles, base=None):
-    ntile, slots = lists.shape
+def paint(position, owner, counts, tiles, wear, lists, table, rows, width, shard_tiles, base=None):
     args = [wear, lists, table] + ([] if base is None else [base])
     whole = lambda shape: pl.BlockSpec(shape, lambda i, *_: (0,) * len(shape))
     return pl.pallas_call(
         functools.partial(paint_kernel, shard_tiles, 0 if base is None else 1),
         name="paint_band",
         grid_spec=pltpu.PrefetchScalarGridSpec(
-            num_scalar_prefetch=3,
+            num_scalar_prefetch=4,
             grid=(1,),
             in_specs=[whole(a.shape) for a in args],
             out_specs=whole((rows + 16, width)),
             scratch_shapes=[
-                pltpu.SMEM((ntile + 1,), jnp.int32),
-                pltpu.SMEM((ntile + 1,), jnp.int32),
                 pltpu.VMEM((rows * 8, width // 8), jnp.float32),
                 pltpu.VMEM((2 * width // 128, 128), jnp.float32),
             ],
         ),
         out_shape=jax.ShapeDtypeStruct((rows + 16, width), jnp.float32),
         compiler_params=pltpu.CompilerParams(vmem_limit_bytes=VMEM_LIMIT),
-    )(position, owner, counts, *args)
+    )(position, owner, counts, tiles, *args)
 
 
 def relax_tile(load, beside, has_high, has_low):
@@ -637,7 +657,8 @@
     own, other = gather_wear(wear)
     table = node_cell.reshape(-1, 128)
     tiles_here = wear_class.shape[0]
-    surface = paint(position, tile_owner, active_count, own, node_list, table,
+    tiles = collect(position, tile_owner, tiles_here)
+    surface = paint(position, tile_owner, active_count, tiles, own, node_list, table,
                     rows, width, tiles_here)
     sums, totals = face_sums(displacement, stiffness)
     low, high, other, surface = lax.optimization_barrier((low, high, other, surface))
@@ -645,7 +666,7 @@
         sums, stiffness, totals, low, high, before, after
     )
     low_2, high_2 = shift_both(face_last, face_first, "depth")
-    surface = paint(position, tile_owner, active_count, other, node_list, table,
+    surface = paint(position, tile_owner, active_count, tiles, other, node_list, table,
                     rows, width, tiles_here, surface)
     first, before_2, after_2 = relax_layers(
         position, displacement, stiffness, before, after, before, after, surface,

time: 128 us -> 123 us (0.961); the launches traced: 127 us -> 121 us
  waiting for transfers between devices: 11.3 us -> 7.1 us
  Pallas kernels: 62.4 us -> 58.2 us
  local copies, waits for them, and re-layouts: 6.77 us -> 8.1 us
    pallas_call x2, Pallas kernels: 22.4 us -> 9.14 us  [paint(): pl.pallas_call(functools.partial(paint_kernel, shard_tiles, 0 if base is...]
    pallas_call x0 -> x1, Pallas kernels: none -> 9.09 us  [collect(): pl.pallas_call(functools.partial(collect_kernel, shard_tiles), name='coll...]
    ppermute x1, waiting for transfers between devices: 11.3 us -> 7.08 us  [gather_wear(): return (own, lax.ppermute(own, 'tan', [(i, i ^ 2) for i in range(size)]))]
    unnamed x22 -> x30, local copies, waits for them, and re-layouts: 6.77 us -> 8.1 us
  transfers between devices with their start and end apart: 9 -> 9, of which waited for: 1 -> 1; matrix products, arithmetic and copies ran while one was open for 0% -> 0% of each run, Pallas kernels for 42% -> 41%
where the time goes in v9:
time: 123 us; the launch traced here: 121 us
  Pallas kernels  58.2 us (47%)
  starting transfers between devices  28.4 us (23%)
  blocking collectives  17.9 us (15%)
  local copies, waits for them, and re-layouts  8.1 us (7%)
  waiting for transfers between devices  7.1 us (6%)
    ppermute x8, starting transfers between devices, shift_both(): return (lax.ppermute(last, axis, up), lax.ppermute(first, axis, down))  28.4 us
    pallas_call x2, Pallas kernels, relax_layers(): pl.pallas_call(functools.partial(layer_kernel, first_sweep), name='relax_...  23.7 us
    all_gather x1, blocking collectives, gather_wear(): lax.all_gather(wear, 'tan', axis=0, axis_index_groups=groups, tiled=True)  17.9 us
    pallas_call x2, Pallas kernels, paint(): pl.pallas_call(functools.partial(paint_kernel, shard_tiles, 0 if base is...  9.14 us
    pallas_call x1, Pallas kernels, collect(): pl.pallas_call(functools.partial(collect_kernel, shard_tiles), name='coll...  9.09 us
    unnamed x30, local copies, waits for them, and re-layouts  8.1 us
    ppermute x1, waiting for transfers between devices, gather_wear(): return (own, lax.ppermute(own, 'tan', [(i, i ^ 2) for i in range(size)]))  7.08 us
    pallas_call x1, Pallas kernels, finish_second(): pl.pallas_call(finish_second_kernel, name='finish_second', grid_spec=pltp...  3.33 us
  transfers between devices with their start and end apart: 9, of which 1 were waited for; matrix products, arithmetic and copies ran while one was open for 0% of the time, Pallas kernels for 41%

profile of v9, /device:TPU:4, one launch (start us, length us, event | category | flops | bytes accessed | tf_op | source)
XLA Modules:
  0.0 120.6 jit_solution(18435649112547742830)
XLA Ops:
  0.0 1.6 %copy-done = f32[8,32,2048]{2,1,0:T(8,128)S(1)} copy-done((f32[8,32,2048]{2,1,0:T(8,128)S(1)}, f32[8,32,2048]{2,1,0:T(8,128)}, u32[]{:S(2)}) %copy-start) | copy-done | bytes 2097176
  1.6 2.8 %pack_faces.1 = (f32[4,32,2048]{2,1,0:T(8,128)}, f32[4,32,2048]{2,1,0:T(8,128)}) custom-call(f32[3,8,32,2048]{3,2,1,0:T(8,128)} %refs_1_.1, f32[8,32,2048]{2,1,0:T(8,128)S(1)} %copy-done), custom_call_target="tpu_custom_call" | custom-call | tf_op jit(solution)/shard_map/pack_faces/pallas_call | solution.py:87
  4.4 6.7 %collective-permute-start.2 = (f32[4,32,2048]{2,1,0:T(8,128)}, f32[4,32,2048]{2,1,0:T(8,128)}, u32[]{:S(2)}, u32[]{:S(2)}) collective-permute-start(f32[4,32,2048]{2,1,0:T(8,128)} %get-tuple-element.29), channel_id=1, source_target_pairs={{0,16},{16,32},{32,48},{48,64},{64,80},{80,96},{96,112},{1,17},{17... | collective-permute-start | bytes 3145736 | tf_op jit(solution)/shard_map/ppermute | solution.py:20
  11.1 1.4 %collective-permute-start.3 = (f32[4,32,2048]{2,1,0:T(8,128)}, f32[4,32,2048]{2,1,0:T(8,128)}, u32[]{:S(2)}, u32[]{:S(2)}) collective-permute-start(f32[4,32,2048]{2,1,0:T(8,128)} %get-tuple-element.30), channel_id=1, source_target_pairs={{16,0},{32,16},{48,32},{64,48},{80,64},{96,80},{112,96},{17,1},{33... | collective-permute-start | bytes 3145736 | tf_op jit(solution)/shard_map/ppermute | solution.py:20
  12.5 3.2 %pack_rows.1 = (f32[8,8,2048]{2,1,0:T(8,128)}, f32[8,8,2048]{2,1,0:T(8,128)}) custom-call(f32[3,8,32,2048]{3,2,1,0:T(8,128)} %refs_1_.1, f32[8,32,2048]{2,1,0:T(8,128)S(1)} %copy-done, f32[3,8,32,2048]{3,2,1,0:T(8,128)} %refs_1_.1, f32[8,32,2048]{2,1,0:T(8,128)S(1)} %copy-done), custom_call_target="tpu_custom_call" | custom-call | tf_op jit(solution)/shard_map/pack_rows/pallas_call | solution.py:60
  15.7 1.9 %collective-permute-start = (f32[8,8,2048]{2,1,0:T(8,128)}, f32[8,8,2048]{2,1,0:T(8,128)S(1)}, u32[]{:S(2)}, u32[]{:S(2)}) collective-permute-start(f32[8,8,2048]{2,1,0:T(8,128)} %get-tuple-element.27.refs_13_), channel_id=1, source_target_pairs={{0,1},{1,2},{2,3},{3,4},{4,5},{5,6},{6,7},{7,8},{8,9},{9,10},{10,1... | collective-permute-start | bytes 1572872 | tf_op jit(solution)/shard_map/ppermute | solution.py:20
  17.7 4.5 %collective-permute-start.1 = (f32[8,8,2048]{2,1,0:T(8,128)}, f32[8,8,2048]{2,1,0:T(8,128)S(1)}, u32[]{:S(2)}, u32[]{:S(2)}) collective-permute-start(f32[8,8,2048]{2,1,0:T(8,128)} %get-tuple-element.28.refs_12_), channel_id=1, source_target_pairs={{1,0},{2,1},{3,2},{4,3},{5,4},{6,5},{7,6},{8,7},{9,8},{10,9},{11,1... | collective-permute-start | bytes 1572872 | tf_op jit(solution)/shard_map/ppermute | solution.py:20
  22.2 1.4 %archard.1 = f32[32,128]{1,0:T(8,128)} custom-call(f32[8]{0:T(128)} %rates_ref.1, s32[32,128]{1,0:T(8,128)} %class_ref.1, f32[32,128]{1,0:T(8,128)} %contact_ref.1, f32[32,128]{1,0:T(8,128)} %sliding_ref.1), custom_call_target="tpu_custom_call" | custom-call | tf_op jit(solution)/shard_map/archard/pallas_call | solution.py:34
  23.6 17.9 %all_gather.3.wear_ref = f32[256,128]{1,0:T(8,128)S(1)} all-gather(f32[32,128]{1,0:T(8,128)} %archard.1), channel_id=1, replica_groups={{0,1,4,5,8,9,12,13},{2,3,6,7,10,11,14,15},{16,17,20,21,24,25,28,29},{18..., dimensions={0}, use_global_device_ids=true | all-gather | bytes 147456 | tf_op jit(solution)/shard_map/all_gather | solution.py:104
  41.5 0.0 collective-permute-start.4
  41.5 0.0 copy-start.11
  41.6 0.0 copy-start.14
  41.6 3.1 %face_sums.1 = (f32[3,2,32,2048]{3,2,1,0:T(8,128)S(1)}, f32[2,32,2048]{2,1,0:T(8,128)S(1)}) custom-call(f32[3,8,32,2048]{3,2,1,0:T(8,128)} %refs_1_.1, f32[3,8,32,2048]{3,2,1,0:T(8,128)} %refs_1_.1, f32[8,32,2048]{2,1,0:T(8,128)S(1)} %copy-done.1, f32[8,32,2048]{2,1,0:T(8,128)S(1)} %copy-done.1), custom_call_target="tpu_custom_call" | custom-call | tf_op jit(solution)/shard_map/face_sums/pallas_call | solution.py:497
  44.7 0.0 copy-start.5
  44.7 1.1 copy-done.5
  45.9 0.8 copy-done.7
  46.7 0.6 pad_add_fusion.where_ref.refs_0_
  47.2 9.1 %collect_tiles.1.tiles_ref = s32[2560]{0:T(1024)} custom-call(s32[2]{0:T(128)} %pad_add_fusion.where_ref.refs_0_, s32[512]{0:T(512)} %owner_ref.5), custom_call_target="tpu_custom_call" | custom-call | tf_op jit(solution)/shard_map/collect_tiles/pallas_call | solution.py:139
  56.3 0.0 copy-done.6
  56.4 0.0 copy-done.11
  56.4 0.0 copy-done.14
  56.4 0.0 copy-start.3
  56.4 2.2 %copy-done.3 = s32[1048576]{0:T(1024)S(1)} copy-done((s32[1048576]{0:T(1024)S(1)}, s32[1048576]{0:T(1024)}, u32[]{:S(2)}) %copy-start.3) | copy-done | bytes 4194328
  58.6 0.7 copy-done.9
  59.3 0.6 copy-done.12
  59.9 3.9 %paint_band.2.refs_0_ = f32[48,2048]{1,0:T(8,128)S(1)} custom-call(s32[2]{0:T(128)S(1)} %copy-done.12, s32[512]{0:T(512)S(1)} %copy-done.11, s32[512]{0:T(512)S(1)} %copy-done.14, s32[2560]{0:T(1024)S(1)} %copy-done.9, f32[256,128]{1,0:T(8,128)S(1)} %all_gather.3.wear_ref, s32[512,128]{1,0:T(8,128)S(1)} %copy-done.6, s32[8192,128]{1,0:T(8,128)S(1)} %bitcast.3), custom_call_target="tpu_custom_call" | custom-call | tf_op jit(solution)/shard_map/paint_band/pallas_call | solution.py:255
  63.8 0.0 copy-start.4
  63.8 7.1 %collective-permute-done.4.wear_ref = f32[256,128]{1,0:T(8,128)} collective-permute-done((f32[256,128]{1,0:T(8,128)S(1)}, f32[256,128]{1,0:T(8,128)}, u32[]{:S(2)}, u32[]{:S(2)}) %collective-permute-start.4) | collective-permute-done | bytes 131104 | tf_op jit(solution)/shard_map/ppermute | solution.py:105
  70.9 0.0 collective-permute-done.2.low.s_low
  70.9 0.0 collective-permute-done.3.high.s_high
  70.9 0.0 collective-permute-done.before.s_before.refs_3_.refs_5_.refs_10_
  70.9 0.0 collective-permute-done.1.after.s_after.refs_4_.refs_6_.refs_11_
  70.9 1.0 copy-done.8
  71.9 2.4 %finish_first.1 = (f32[3,32,2048]{2,1,0:T(8,128)S(1)}, f32[3,32,2048]{2,1,0:T(8,128)S(1)}, f32[8,2048]{1,0:T(8,128)S(1)}, f32[8,2048]{1,0:T(8,128)S(1)}) custom-call(f32[3,2,32,2048]{3,2,1,0:T(8,128)} %copy-done.5, f32[8,32,2048]{2,1,0:T(8,128)} %s_here.5, f32[2,32,2048]{2,1,0:T(8,128)S(1)} %copy-done.8, f32[4,32,2048]{2,1,0:T(8,128)} %collective-permute-done.2.low.s_low, ...), custom_call_target="tpu_custom_call" | custom-call | tf_op jit(solution)/shard_map/finish_first/pallas_call | solution.py:561
  74.3 1.3 %collective-permute-start.6 = (f32[3,32,2048]{2,1,0:T(8,128)S(1)}, f32[3,32,2048]{2,1,0:T(8,128)S(1)}, u32[]{:S(2)}, u32[]{:S(2)}) collective-permute-start(f32[3,32,2048]{2,1,0:T(8,128)S(1)} %get-tuple-element.37.refs_8_), channel_id=1, source_target_pairs={{16,0},{32,16},{48,32},{64,48},{80,64},{96,80},{112,96},{17,1},{33... | collective-permute-start | bytes 2359304 | tf_op jit(solution)/shard_map/ppermute | solution.py:20
  75.6 6.1 %collective-permute-start.5 = (f32[3,32,2048]{2,1,0:T(8,128)S(1)}, f32[3,32,2048]{2,1,0:T(8,128)S(1)}, u32[]{:S(2)}, u32[]{:S(2)}) collective-permute-start(f32[3,32,2048]{2,1,0:T(8,128)S(1)} %get-tuple-element.38.refs_9_), channel_id=1, source_target_pairs={{0,16},{16,32},{32,48},{48,64},{64,80},{80,96},{96,112},{1,17},{17... | collective-permute-start | bytes 2359304 | tf_op jit(solution)/shard_map/ppermute | solution.py:20
  81.7 0.0 copy-done.10
  81.7 5.3 %paint_band.3.refs_7_ = f32[48,2048]{1,0:T(8,128)S(1)} custom-call(s32[2]{0:T(128)S(1)} %copy-done.13, s32[512]{0:T(512)S(1)} %copy-done.11, s32[512]{0:T(512)S(1)} %copy-done.14, s32[2560]{0:T(1024)S(1)} %copy-done.10, f32[256,128]{1,0:T(8,128)} %collective-permute-done.4.wear_ref, s32[512,128]{1,0:T(8,128)S(1)} %copy-done.6, s32[8192,128]{1,0:T(8,128)S(1)} %bitcast.4, ...), custom_call_target="tpu_custom_call" | custom-call | tf_op jit(solution)/shard_map/paint_band/pallas_call | solution.py:255
  87.0 0.0 copy-start.2
  87.0 11.9 %relax_layers_first.1 = (f32[3,8,32,2048]{3,2,1,0:T(8,128)}, f32[3,8,2048]{2,1,0:T(8,128)S(1)}, f32[3,8,2048]{2,1,0:T(8,128)S(1)}) custom-call(s32[2]{0:T(128)S(1)} %copy-done.13, f32[3,8,32,2048]{3,2,1,0:T(8,128)} %refs_1_.1, f32[8,32,2048]{2,1,0:T(8,128)} %s_here.5, f32[8,8,2048]{2,1,0:T(8,128)S(1)} %collective-permute-done.before.s_before.refs_3_.refs_5_.refs_10_, ...), custom_call_target="tpu_custom_call" | custom-call | tf_op jit(solution)/shard_map/relax_layers_first/pallas_call | solution.py:449
  98.9 1.9 %collective-permute-start.7 = (f32[8,2048]{1,0:T(8,128)S(1)}, f32[8,2048]{1,0:T(8,128)S(1)}, u32[]{:S(2)}, u32[]{:S(2)}) collective-permute-start(f32[8,2048]{1,0:T(8,128)S(1)} %get-tuple-element.47), channel_id=1, source_target_pairs={{0,1},{1,2},{2,3},{3,4},{4,5},{5,6},{6,7},{7,8},{8,9},{9,10},{10,1... | collective-permute-start | bytes 196616 | tf_op jit(solution)/shard_map/ppermute | solution.py:20
  100.8 4.5 %collective-permute-start.8 = (f32[8,2048]{1,0:T(8,128)S(1)}, f32[8,2048]{1,0:T(8,128)S(1)}, u32[]{:S(2)}, u32[]{:S(2)}) collective-permute-start(f32[8,2048]{1,0:T(8,128)S(1)} %get-tuple-element.48), channel_id=1, source_target_pairs={{1,0},{2,1},{3,2},{4,3},{5,4},{6,5},{7,6},{8,7},{9,8},{10,9},{11,1... | collective-permute-start | bytes 196616 | tf_op jit(solution)/shard_map/ppermute | solution.py:20
  105.4 11.8 %relax_layers_second.1 = (f32[3,8,32,2048]{3,2,1,0:T(8,128)}, f32[2,32,2048]{2,1,0:T(8,128)S(1)}) custom-call(s32[2]{0:T(128)S(1)} %copy-done.13, f32[3,8,32,2048]{3,2,1,0:T(8,128)} %get-tuple-element.39.refs_1_, f32[8,32,2048]{2,1,0:T(8,128)S(1)} %copy-done.2, f32[3,8,2048]{2,1,0:T(8,128)S(1)} %get-tuple-element.43.refs_3_, ...), custom_call_target="tpu_custom_call" | custom-call | tf_op jit(solution)/shard_map/relax_layers_second/pallas_call | solution.py:449
  117.2 0.0 collective-permute-done.7.before
  117.2 0.0 collective-permute-done.8.after
  117.2 0.0 collective-permute-done.6.high
  117.2 0.0 collective-permute-done.5.low
  117.2 3.3 %finish_second.1 = f32[3,8,32,2048]{3,2,1,0:T(8,128)} custom-call(s32[2]{0:T(128)S(1)} %copy-done.13, f32[3,8,32,2048]{3,2,1,0:T(8,128)} %get-tuple-element.45.sums, f32[8,32,2048]{2,1,0:T(8,128)} %s_here.5, f32[2,32,2048]{2,1,0:T(8,128)S(1)} %get-tuple-element.46.totals, ...), custom_call_target="tpu_custom_call", output_to_operand_aliasing={{}: (1, {})} | custom-call | tf_op jit(solution)/shard_map/finish_second/pallas_call | solution.py:618
  (13 shorter events, 0.0 us)
Async XLA Ops:
  0.0 1.6 %copy-start = (f32[8,32,2048]{2,1,0:T(8,128)S(1)}, f32[8,32,2048]{2,1,0:T(8,128)}, u32[]{:S(2)}) copy-start(f32[8,32,2048]{2,1,0:T(8,128)} %s_here.5) | copy-start | bytes 6291460
  4.4 66.5 %collective-permute-start.2 = (f32[4,32,2048]{2,1,0:T(8,128)}, f32[4,32,2048]{2,1,0:T(8,128)}, u32[]{:S(2)}, u32[]{:S(2)}) collective-permute-start(f32[4,32,2048]{2,1,0:T(8,128)} %get-tuple-element.29), channel_id=1, source_target_pairs={{0,16},{16,32},{32,48},{48,64},{64,80},{80,96},{96,112},{1,17},{17... | collective-permute-start | bytes 3145736 | tf_op jit(solution)/shard_map/ppermute | solution.py:20
  11.1 30.4 %copy-start.1 = (f32[8,32,2048]{2,1,0:T(8,128)S(1)}, f32[8,32,2048]{2,1,0:T(8,128)}, u32[]{:S(2)}) copy-start(f32[8,32,2048]{2,1,0:T(8,128)} %s_here.5) | copy-start | bytes 6291460
  11.1 59.7 %collective-permute-start.3 = (f32[4,32,2048]{2,1,0:T(8,128)}, f32[4,32,2048]{2,1,0:T(8,128)}, u32[]{:S(2)}, u32[]{:S(2)}) collective-permute-start(f32[4,32,2048]{2,1,0:T(8,128)} %get-tuple-element.30), channel_id=1, source_target_pairs={{16,0},{32,16},{48,32},{64,48},{80,64},{96,80},{112,96},{17,1},{33... | collective-permute-start | bytes 3145736 | tf_op jit(solution)/shard_map/ppermute | solution.py:20
  15.7 55.1 %collective-permute-start = (f32[8,8,2048]{2,1,0:T(8,128)}, f32[8,8,2048]{2,1,0:T(8,128)S(1)}, u32[]{:S(2)}, u32[]{:S(2)}) collective-permute-start(f32[8,8,2048]{2,1,0:T(8,128)} %get-tuple-element.27.refs_13_), channel_id=1, source_target_pairs={{0,1},{1,2},{2,3},{3,4},{4,5},{5,6},{6,7},{7,8},{8,9},{9,10},{10,1... | collective-permute-start | bytes 1572872 | tf_op jit(solution)/shard_map/ppermute | solution.py:20
  17.7 53.2 %collective-permute-start.1 = (f32[8,8,2048]{2,1,0:T(8,128)}, f32[8,8,2048]{2,1,0:T(8,128)S(1)}, u32[]{:S(2)}, u32[]{:S(2)}) collective-permute-start(f32[8,8,2048]{2,1,0:T(8,128)} %get-tuple-element.28.refs_12_), channel_id=1, source_target_pairs={{1,0},{2,1},{3,2},{4,3},{5,4},{6,5},{7,6},{8,7},{9,8},{10,9},{11,1... | collective-permute-start | bytes 1572872 | tf_op jit(solution)/shard_map/ppermute | solution.py:20
  41.5 29.3 %collective-permute-start.4 = (f32[256,128]{1,0:T(8,128)S(1)}, f32[256,128]{1,0:T(8,128)}, u32[]{:S(2)}, u32[]{:S(2)}) collective-permute-start(f32[256,128]{1,0:T(8,128)S(1)} %all_gather.3.wear_ref), channel_id=1, source_target_pairs={{0,2},{1,3},{2,0},{3,1},{4,6},{5,7},{6,4},{7,5},{8,10},{9,11},{10,... | collective-permute-start | bytes 393224 | tf_op jit(solution)/shard_map/ppermute | solution.py:105
  41.5 14.8 %copy-start.6 = (s32[512,128]{1,0:T(8,128)S(1)}, s32[512,128]{1,0:T(8,128)}, u32[]{:S(2)}) copy-start(s32[512,128]{1,0:T(8,128)} %list_ref.3) | copy-start | bytes 786436
  41.5 14.8 %copy-start.11 = (s32[512]{0:T(512)S(1)}, s32[512]{0:T(512)}, u32[]{:S(2)}) copy-start(s32[512]{0:T(512)} %owner_ref.5) | copy-start | bytes 6148
  41.6 14.8 %copy-start.14 = (s32[512]{0:T(512)S(1)}, s32[512]{0:T(512)}, u32[]{:S(2)}) copy-start(s32[512]{0:T(512)} %count_ref.3) | copy-start | bytes 6148
  44.7 1.1 copy-start.5
  45.9 0.8 copy-start.7
  56.4 2.2 %copy-start.3 = (s32[1048576]{0:T(1024)S(1)}, s32[1048576]{0:T(1024)}, u32[]{:S(2)}) copy-start(s32[1048576]{0:T(1024)} %param.19) | copy-start | bytes 12582916
  58.6 0.7 copy-start.9
  59.3 0.6 copy-start.12
  59.9 21.8 %copy-start.10 = (s32[2560]{0:T(1024)S(1)}, s32[2560]{0:T(1024)}, u32[]{:S(2)}) copy-start(s32[2560]{0:T(1024)} %collect_tiles.1.tiles_ref) | copy-start | bytes 30724
  59.9 21.8 %copy-start.13 = (s32[2]{0:T(128)S(1)}, s32[2]{0:T(128)}, u32[]{:S(2)}) copy-start(s32[2]{0:T(128)} %pad_add_fusion.where_ref.refs_0_) | copy-start | bytes 28
  63.8 18.0 %copy-start.4 = (s32[1048576]{0:T(1024)S(1)}, s32[1048576]{0:T(1024)}, u32[]{:S(2)}) copy-start(s32[1048576]{0:T(1024)} %param.19) | copy-start | bytes 12582916
  70.9 1.0 copy-start.8
  74.3 42.9 %collective-permute-start.6 = (f32[3,32,2048]{2,1,0:T(8,128)S(1)}, f32[3,32,2048]{2,1,0:T(8,128)S(1)}, u32[]{:S(2)}, u32[]{:S(2)}) collective-permute-start(f32[3,32,2048]{2,1,0:T(8,128)S(1)} %get-tuple-element.37.refs_8_), channel_id=1, source_target_pairs={{16,0},{32,16},{48,32},{64,48},{80,64},{96,80},{112,96},{17,1},{33... | collective-permute-start | bytes 2359304 | tf_op jit(solution)/shard_map/ppermute | solution.py:20
  75.6 41.6 %collective-permute-start.5 = (f32[3,32,2048]{2,1,0:T(8,128)S(1)}, f32[3,32,2048]{2,1,0:T(8,128)S(1)}, u32[]{:S(2)}, u32[]{:S(2)}) collective-permute-start(f32[3,32,2048]{2,1,0:T(8,128)S(1)} %get-tuple-element.38.refs_9_), channel_id=1, source_target_pairs={{0,16},{16,32},{32,48},{48,64},{64,80},{80,96},{96,112},{1,17},{17... | collective-permute-start | bytes 2359304 | tf_op jit(solution)/shard_map/ppermute | solution.py:20
  87.0 18.4 %copy-start.2 = (f32[8,32,2048]{2,1,0:T(8,128)S(1)}, f32[8,32,2048]{2,1,0:T(8,128)}, u32[]{:S(2)}) copy-start(f32[8,32,2048]{2,1,0:T(8,128)} %s_here.5) | copy-start | bytes 6291460
  98.9 18.3 %collective-permute-start.7 = (f32[8,2048]{1,0:T(8,128)S(1)}, f32[8,2048]{1,0:T(8,128)S(1)}, u32[]{:S(2)}, u32[]{:S(2)}) collective-permute-start(f32[8,2048]{1,0:T(8,128)S(1)} %get-tuple-element.47), channel_id=1, source_target_pairs={{0,1},{1,2},{2,3},{3,4},{4,5},{5,6},{6,7},{7,8},{8,9},{9,10},{10,1... | collective-permute-start | bytes 196616 | tf_op jit(solution)/shard_map/ppermute | solution.py:20
  100.8 16.4 %collective-permute-start.8 = (f32[8,2048]{1,0:T(8,128)S(1)}, f32[8,2048]{1,0:T(8,128)S(1)}, u32[]{:S(2)}, u32[]{:S(2)}) collective-permute-start(f32[8,2048]{1,0:T(8,128)S(1)} %get-tuple-element.48), channel_id=1, source_target_pairs={{1,0},{2,1},{3,2},{4,3},{5,4},{6,5},{7,6},{8,7},{9,8},{10,9},{11,1... | collective-permute-start | bytes 196616 | tf_op jit(solution)/shard_map/ppermute | solution.py:20

commit v10 on v9

--- a/solution.py
+++ b/solution.py
@@ -68,32 +68,32 @@
     )(field, stiffness, field, stiffness)
 
 
-def faces_kernel(field_ref, stiff_ref, first_ref, last_ref):
-    step = pl.program_id(0)
-
-    def put(to):
-        to[0:3] = field_ref[:, 0]
-        to[3:4] = stiff_ref[...]
-
-    pl.when(step == 0)(lambda: put(last_ref))
-    pl.when(step == 1)(lambda: put(first_ref))
+def faces_kernel(field_ref, stiff_ref, first_ref, last_ref, sems):
+    layers = field_ref.shape[1]
+    copies = []
+    for k, (to, layer) in enumerate(((last_ref, layers - 1), (first_ref, 0))):
+        copies.append(pltpu.make_async_copy(
+            field_ref.at[:, layer], to.at[pl.ds(0, 3)], sems.at[2 * k]))
+        copies.append(pltpu.make_async_copy(
+            stiff_ref.at[pl.ds(layer, 1)], to.at[pl.ds(3, 1)], sems.at[2 * k + 1]))
+    for copy in copies:
+        copy.start()
+    for copy in copies:
+        copy.wait()
 
 
 def pack_faces(field, stiffness):
-    _, layers, rows, width = field.shape
+    _, _, rows, width = field.shape
     face = jax.ShapeDtypeStruct((4, rows, width), jnp.float32)
-    layer = lambda i: (1 - i) * (layers - 1)
-    whole = pl.BlockSpec((4, rows, width), lambda i: (0, 0, 0))
+    far = pl.BlockSpec(memory_space=pltpu.HBM)
+    near = pl.BlockSpec(memory_space=pltpu.VMEM)
     return pl.pallas_call(
         faces_kernel,
         name="pack_faces",
-        grid=(2,),
-        in_specs=[
-            pl.BlockSpec((3, 1, rows, width), lambda i: (0, layer(i), 0, 0)),
-            pl.BlockSpec((1, rows, width), lambda i: (layer(i), 0, 0)),
-        ],
-        out_specs=[whole, whole],
+        in_specs=[far, far],
+        out_specs=[near, near],
         out_shape=[face, face],
+        scratch_shapes=[pltpu.SemaphoreType.DMA((4,))],
         compiler_params=pltpu.CompilerParams(vmem_limit_bytes=VMEM_LIMIT),
     )(field, stiffness)
 
@@ -251,20 +251,16 @@
 
 def paint(position, owner, counts, tiles, wear, lists, table, rows, width, shard_tiles, base=None):
     args = [wear, lists, table] + ([] if base is None else [base])
-    whole = lambda shape: pl.BlockSpec(shape, lambda i, *_: (0,) * len(shape))
     return pl.pallas_call(
         functools.partial(paint_kernel, shard_tiles, 0 if base is None else 1),
         name="paint_band",
-        grid_spec=pltpu.PrefetchScalarGridSpec(
-            num_scalar_prefetch=4,
-            grid=(1,),
-            in_specs=[whole(a.shape) for a in args],
-            out_specs=whole((rows + 16, width)),
-            scratch_shapes=[
-                pltpu.VMEM((rows * 8, width // 8), jnp.float32),
-                pltpu.VMEM((2 * width // 128, 128), jnp.float32),
-            ],
-        ),
+        in_specs=[pl.BlockSpec(memory_space=pltpu.SMEM)] * 4
+        + [pl.BlockSpec(memory_space=pltpu.VMEM)] * len(args),
+        out_specs=pl.BlockSpec(memory_space=pltpu.VMEM),
+        scratch_shapes=[
+            pltpu.VMEM((rows * 8, width // 8), jnp.float32),
+            pltpu.VMEM((2 * width // 128, 128), jnp.float32),
+        ],
         out_shape=jax.ShapeDtypeStruct((rows + 16, width), jnp.float32),
         compiler_params=pltpu.CompilerParams(vmem_limit_bytes=VMEM_LIMIT),
     )(position, owner, counts, tiles, *args)

time: 123 us -> 121 us (0.984); the launches traced: 121 us -> 120 us
  no operation moved by 1% of the time
where the time goes in v10:
time: 121 us; the launch traced here: 120 us
  Pallas kernels  57.9 us (48%)
  starting transfers between devices  28.5 us (24%)
  blocking collectives  17.9 us (15%)
  local copies, waits for them, and re-layouts  8.1 us (7%)
  waiting for transfers between devices  6.61 us (5%)
    ppermute x8, starting transfers between devices, shift_both(): return (lax.ppermute(last, axis, up), lax.ppermute(first, axis, down))  28.4 us
    pallas_call x2, Pallas kernels, relax_layers(): pl.pallas_call(functools.partial(layer_kernel, first_sweep), name='relax_...  23.7 us
    all_gather x1, blocking collectives, gather_wear(): lax.all_gather(wear, 'tan', axis=0, axis_index_groups=groups, tiled=True)  17.9 us
    pallas_call x1, Pallas kernels, collect(): pl.pallas_call(functools.partial(collect_kernel, shard_tiles), name='coll...  9.09 us
    pallas_call x2, Pallas kernels, paint(): pl.pallas_call(functools.partial(paint_kernel, shard_tiles, 0 if base is...  8.88 us
    unnamed x30, local copies, waits for them, and re-layouts  8.1 us
    ppermute x1, waiting for transfers between devices, gather_wear(): return (own, lax.ppermute(own, 'tan', [(i, i ^ 2) for i in range(size)]))  6.59 us
    pallas_call x1, Pallas kernels, finish_second(): pl.pallas_call(finish_second_kernel, name='finish_second', grid_spec=pltp...  3.33 us
  transfers between devices with their start and end apart: 9, of which 1 were waited for; matrix products, arithmetic and copies ran while one was open for 0% of the time, Pallas kernels for 41%

profile of v10, /device:TPU:4, one launch (start us, length us, event | category | flops | bytes accessed | tf_op | source)
XLA Modules:
  0.0 119.8 jit_solution(4050288235402898777)
XLA Ops:
  0.0 1.6 %copy-done = f32[8,32,2048]{2,1,0:T(8,128)S(1)} copy-done((f32[8,32,2048]{2,1,0:T(8,128)S(1)}, f32[8,32,2048]{2,1,0:T(8,128)}, u32[]{:S(2)}) %copy-start) | copy-done | bytes 2097176
  1.6 2.7 %pack_faces.1 = (f32[4,32,2048]{2,1,0:T(8,128)}, f32[4,32,2048]{2,1,0:T(8,128)}) custom-call(f32[3,8,32,2048]{3,2,1,0:T(8,128)} %refs_1_.1, f32[8,32,2048]{2,1,0:T(8,128)S(1)} %copy-done), custom_call_target="tpu_custom_call" | custom-call | tf_op jit(solution)/shard_map/pack_faces/pallas_call | solution.py:90
  4.3 6.7 %collective-permute-start.2 = (f32[4,32,2048]{2,1,0:T(8,128)}, f32[4,32,2048]{2,1,0:T(8,128)}, u32[]{:S(2)}, u32[]{:S(2)}) collective-permute-start(f32[4,32,2048]{2,1,0:T(8,128)} %get-tuple-element.29), channel_id=1, source_target_pairs={{0,16},{16,32},{32,48},{48,64},{64,80},{80,96},{96,112},{1,17},{17... | collective-permute-start | bytes 3145736 | tf_op jit(solution)/shard_map/ppermute | solution.py:20
  11.1 1.4 %collective-permute-start.3 = (f32[4,32,2048]{2,1,0:T(8,128)}, f32[4,32,2048]{2,1,0:T(8,128)}, u32[]{:S(2)}, u32[]{:S(2)}) collective-permute-start(f32[4,32,2048]{2,1,0:T(8,128)} %get-tuple-element.30), channel_id=1, source_target_pairs={{16,0},{32,16},{48,32},{64,48},{80,64},{96,80},{112,96},{17,1},{33... | collective-permute-start | bytes 3145736 | tf_op jit(solution)/shard_map/ppermute | solution.py:20
  12.5 3.2 %pack_rows.1 = (f32[8,8,2048]{2,1,0:T(8,128)}, f32[8,8,2048]{2,1,0:T(8,128)}) custom-call(f32[3,8,32,2048]{3,2,1,0:T(8,128)} %refs_1_.1, f32[8,32,2048]{2,1,0:T(8,128)S(1)} %copy-done, f32[3,8,32,2048]{3,2,1,0:T(8,128)} %refs_1_.1, f32[8,32,2048]{2,1,0:T(8,128)S(1)} %copy-done), custom_call_target="tpu_custom_call" | custom-call | tf_op jit(solution)/shard_map/pack_rows/pallas_call | solution.py:60
  15.7 1.9 %collective-permute-start = (f32[8,8,2048]{2,1,0:T(8,128)}, f32[8,8,2048]{2,1,0:T(8,128)S(1)}, u32[]{:S(2)}, u32[]{:S(2)}) collective-permute-start(f32[8,8,2048]{2,1,0:T(8,128)} %get-tuple-element.27.refs_13_), channel_id=1, source_target_pairs={{0,1},{1,2},{2,3},{3,4},{4,5},{5,6},{6,7},{7,8},{8,9},{9,10},{10,1... | collective-permute-start | bytes 1572872 | tf_op jit(solution)/shard_map/ppermute | solution.py:20
  17.6 4.5 %collective-permute-start.1 = (f32[8,8,2048]{2,1,0:T(8,128)}, f32[8,8,2048]{2,1,0:T(8,128)S(1)}, u32[]{:S(2)}, u32[]{:S(2)}) collective-permute-start(f32[8,8,2048]{2,1,0:T(8,128)} %get-tuple-element.28.refs_12_), channel_id=1, source_target_pairs={{1,0},{2,1},{3,2},{4,3},{5,4},{6,5},{7,6},{8,7},{9,8},{10,9},{11,1... | collective-permute-start | bytes 1572872 | tf_op jit(solution)/shard_map/ppermute | solution.py:20
  22.2 1.4 %archard.1 = f32[32,128]{1,0:T(8,128)} custom-call(f32[8]{0:T(128)} %rates_ref.1, s32[32,128]{1,0:T(8,128)} %class_ref.1, f32[32,128]{1,0:T(8,128)} %contact_ref.1, f32[32,128]{1,0:T(8,128)} %sliding_ref.1), custom_call_target="tpu_custom_call" | custom-call | tf_op jit(solution)/shard_map/archard/pallas_call | solution.py:34
  23.6 17.9 %all_gather.3.wear_ref = f32[256,128]{1,0:T(8,128)S(1)} all-gather(f32[32,128]{1,0:T(8,128)} %archard.1), channel_id=1, replica_groups={{0,1,4,5,8,9,12,13},{2,3,6,7,10,11,14,15},{16,17,20,21,24,25,28,29},{18..., dimensions={0}, use_global_device_ids=true | all-gather | bytes 147456 | tf_op jit(solution)/shard_map/all_gather | solution.py:104
  41.5 0.0 collective-permute-start.4
  41.5 0.0 copy-done.1
  41.5 0.0 copy-start.11
  41.5 0.0 copy-start.14
  41.6 3.1 %face_sums.1 = (f32[3,2,32,2048]{3,2,1,0:T(8,128)S(1)}, f32[2,32,2048]{2,1,0:T(8,128)S(1)}) custom-call(f32[3,8,32,2048]{3,2,1,0:T(8,128)} %refs_1_.1, f32[3,8,32,2048]{3,2,1,0:T(8,128)} %refs_1_.1, f32[8,32,2048]{2,1,0:T(8,128)S(1)} %copy-done.1, f32[8,32,2048]{2,1,0:T(8,128)S(1)} %copy-done.1), custom_call_target="tpu_custom_call" | custom-call | tf_op jit(solution)/shard_map/face_sums/pallas_call | solution.py:493
  44.7 0.0 copy-start.5
  44.7 1.1 copy-done.5
  45.8 0.8 copy-done.7
  46.7 0.6 pad_add_fusion.where_ref.refs_0_
  47.2 9.1 %collect_tiles.1.tiles_ref = s32[2560]{0:T(1024)} custom-call(s32[2]{0:T(128)} %pad_add_fusion.where_ref.refs_0_, s32[512]{0:T(512)} %owner_ref.5), custom_call_target="tpu_custom_call" | custom-call | tf_op jit(solution)/shard_map/collect_tiles/pallas_call | solution.py:139
  56.3 0.0 copy-done.6
  56.3 0.0 copy-done.11
  56.4 0.0 copy-done.14
  56.4 0.0 copy-start.3
  56.4 2.2 %copy-done.3 = s32[1048576]{0:T(1024)S(1)} copy-done((s32[1048576]{0:T(1024)S(1)}, s32[1048576]{0:T(1024)}, u32[]{:S(2)}) %copy-start.3) | copy-done | bytes 4194328
  58.6 0.7 copy-done.9
  59.3 0.6 copy-done.12
  59.9 4.4 %paint_band.2.refs_0_ = f32[48,2048]{1,0:T(8,128)S(1)} custom-call(s32[2]{0:T(128)S(1)} %copy-done.12, s32[512]{0:T(512)S(1)} %copy-done.11, s32[512]{0:T(512)S(1)} %copy-done.14, s32[2560]{0:T(1024)S(1)} %copy-done.9, f32[256,128]{1,0:T(8,128)S(1)} %all_gather.3.wear_ref, s32[512,128]{1,0:T(8,128)S(1)} %copy-done.6, s32[8192,128]{1,0:T(8,128)S(1)} %bitcast.3), custom_call_target="tpu_custom_call" | custom-call | tf_op jit(solution)/shard_map/paint_band/pallas_call | solution.py:254
  64.2 0.0 copy-start.4
  64.3 6.6 %collective-permute-done.4.wear_ref = f32[256,128]{1,0:T(8,128)} collective-permute-done((f32[256,128]{1,0:T(8,128)S(1)}, f32[256,128]{1,0:T(8,128)}, u32[]{:S(2)}, u32[]{:S(2)}) %collective-permute-start.4) | collective-permute-done | bytes 131104 | tf_op jit(solution)/shard_map/ppermute | solution.py:105
  70.8 0.0 collective-permute-done.2.low.s_low
  70.8 0.0 collective-permute-done.3.high.s_high
  70.8 0.0 collective-permute-done.before.s_before.refs_3_.refs_5_.refs_10_
  70.9 0.0 collective-permute-done.1.after.s_after.refs_4_.refs_6_.refs_11_
  70.9 1.0 copy-done.8
  71.9 2.4 %finish_first.1 = (f32[3,32,2048]{2,1,0:T(8,128)S(1)}, f32[3,32,2048]{2,1,0:T(8,128)S(1)}, f32[8,2048]{1,0:T(8,128)S(1)}, f32[8,2048]{1,0:T(8,128)S(1)}) custom-call(f32[3,2,32,2048]{3,2,1,0:T(8,128)} %copy-done.5, f32[8,32,2048]{2,1,0:T(8,128)} %s_here.5, f32[2,32,2048]{2,1,0:T(8,128)S(1)} %copy-done.8, f32[4,32,2048]{2,1,0:T(8,128)} %collective-permute-done.2.low.s_low, ...), custom_call_target="tpu_custom_call" | custom-call | tf_op jit(solution)/shard_map/finish_first/pallas_call | solution.py:557
  74.3 1.3 %collective-permute-start.6 = (f32[3,32,2048]{2,1,0:T(8,128)S(1)}, f32[3,32,2048]{2,1,0:T(8,128)S(1)}, u32[]{:S(2)}, u32[]{:S(2)}) collective-permute-start(f32[3,32,2048]{2,1,0:T(8,128)S(1)} %get-tuple-element.37.refs_8_), channel_id=1, source_target_pairs={{16,0},{32,16},{48,32},{64,48},{80,64},{96,80},{112,96},{17,1},{33... | collective-permute-start | bytes 2359304 | tf_op jit(solution)/shard_map/ppermute | solution.py:20
  75.6 6.1 %collective-permute-start.5 = (f32[3,32,2048]{2,1,0:T(8,128)S(1)}, f32[3,32,2048]{2,1,0:T(8,128)S(1)}, u32[]{:S(2)}, u32[]{:S(2)}) collective-permute-start(f32[3,32,2048]{2,1,0:T(8,128)S(1)} %get-tuple-element.38.refs_9_), channel_id=1, source_target_pairs={{0,16},{16,32},{32,48},{48,64},{64,80},{80,96},{96,112},{1,17},{17... | collective-permute-start | bytes 2359304 | tf_op jit(solution)/shard_map/ppermute | solution.py:20
  81.7 4.5 %paint_band.3.refs_7_ = f32[48,2048]{1,0:T(8,128)S(1)} custom-call(s32[2]{0:T(128)S(1)} %copy-done.13, s32[512]{0:T(512)S(1)} %copy-done.11, s32[512]{0:T(512)S(1)} %copy-done.14, s32[2560]{0:T(1024)S(1)} %copy-done.10, f32[256,128]{1,0:T(8,128)} %collective-permute-done.4.wear_ref, s32[512,128]{1,0:T(8,128)S(1)} %copy-done.6, s32[8192,128]{1,0:T(8,128)S(1)} %bitcast.4, ...), custom_call_target="tpu_custom_call" | custom-call | tf_op jit(solution)/shard_map/paint_band/pallas_call | solution.py:254
  86.3 0.0 copy-start.2
  86.3 11.9 %relax_layers_first.1 = (f32[3,8,32,2048]{3,2,1,0:T(8,128)}, f32[3,8,2048]{2,1,0:T(8,128)S(1)}, f32[3,8,2048]{2,1,0:T(8,128)S(1)}) custom-call(s32[2]{0:T(128)S(1)} %copy-done.13, f32[3,8,32,2048]{3,2,1,0:T(8,128)} %refs_1_.1, f32[8,32,2048]{2,1,0:T(8,128)} %s_here.5, f32[8,8,2048]{2,1,0:T(8,128)S(1)} %collective-permute-done.before.s_before.refs_3_.refs_5_.refs_10_, ...), custom_call_target="tpu_custom_call" | custom-call | tf_op jit(solution)/shard_map/relax_layers_first/pallas_call | solution.py:445
  98.1 1.9 %collective-permute-start.7 = (f32[8,2048]{1,0:T(8,128)S(1)}, f32[8,2048]{1,0:T(8,128)S(1)}, u32[]{:S(2)}, u32[]{:S(2)}) collective-permute-start(f32[8,2048]{1,0:T(8,128)S(1)} %get-tuple-element.47), channel_id=1, source_target_pairs={{0,1},{1,2},{2,3},{3,4},{4,5},{5,6},{6,7},{7,8},{8,9},{9,10},{10,1... | collective-permute-start | bytes 196616 | tf_op jit(solution)/shard_map/ppermute | solution.py:20
  100.1 4.5 %collective-permute-start.8 = (f32[8,2048]{1,0:T(8,128)S(1)}, f32[8,2048]{1,0:T(8,128)S(1)}, u32[]{:S(2)}, u32[]{:S(2)}) collective-permute-start(f32[8,2048]{1,0:T(8,128)S(1)} %get-tuple-element.48), channel_id=1, source_target_pairs={{1,0},{2,1},{3,2},{4,3},{5,4},{6,5},{7,6},{8,7},{9,8},{10,9},{11,1... | collective-permute-start | bytes 196616 | tf_op jit(solution)/shard_map/ppermute | solution.py:20
  104.6 11.8 %relax_layers_second.1 = (f32[3,8,32,2048]{3,2,1,0:T(8,128)}, f32[2,32,2048]{2,1,0:T(8,128)S(1)}) custom-call(s32[2]{0:T(128)S(1)} %copy-done.13, f32[3,8,32,2048]{3,2,1,0:T(8,128)} %get-tuple-element.39.refs_1_, f32[8,32,2048]{2,1,0:T(8,128)S(1)} %copy-done.2, f32[3,8,2048]{2,1,0:T(8,128)S(1)} %get-tuple-element.43.refs_3_, ...), custom_call_target="tpu_custom_call" | custom-call | tf_op jit(solution)/shard_map/relax_layers_second/pallas_call | solution.py:445
  116.5 0.0 collective-permute-done.7.before
  116.5 0.0 collective-permute-done.8.after
  116.5 0.0 collective-permute-done.6.high
  116.5 0.0 collective-permute-done.5.low
  116.5 3.3 %finish_second.1 = f32[3,8,32,2048]{3,2,1,0:T(8,128)} custom-call(s32[2]{0:T(128)S(1)} %copy-done.13, f32[3,8,32,2048]{3,2,1,0:T(8,128)} %get-tuple-element.45.sums, f32[8,32,2048]{2,1,0:T(8,128)} %s_here.5, f32[2,32,2048]{2,1,0:T(8,128)S(1)} %get-tuple-element.46.totals, ...), custom_call_target="tpu_custom_call", output_to_operand_aliasing={{}: (1, {})} | custom-call | tf_op jit(solution)/shard_map/finish_second/pallas_call | solution.py:614
  (13 shorter events, 0.0 us)
Async XLA Ops:
  0.0 1.6 %copy-start = (f32[8,32,2048]{2,1,0:T(8,128)S(1)}, f32[8,32,2048]{2,1,0:T(8,128)}, u32[]{:S(2)}) copy-start(f32[8,32,2048]{2,1,0:T(8,128)} %s_here.5) | copy-start | bytes 6291460
  4.3 66.5 %collective-permute-start.2 = (f32[4,32,2048]{2,1,0:T(8,128)}, f32[4,32,2048]{2,1,0:T(8,128)}, u32[]{:S(2)}, u32[]{:S(2)}) collective-permute-start(f32[4,32,2048]{2,1,0:T(8,128)} %get-tuple-element.29), channel_id=1, source_target_pairs={{0,16},{16,32},{32,48},{48,64},{64,80},{80,96},{96,112},{1,17},{17... | collective-permute-start | bytes 3145736 | tf_op jit(solution)/shard_map/ppermute | solution.py:20
  11.1 30.4 %copy-start.1 = (f32[8,32,2048]{2,1,0:T(8,128)S(1)}, f32[8,32,2048]{2,1,0:T(8,128)}, u32[]{:S(2)}) copy-start(f32[8,32,2048]{2,1,0:T(8,128)} %s_here.5) | copy-start | bytes 6291460
  11.1 59.7 %collective-permute-start.3 = (f32[4,32,2048]{2,1,0:T(8,128)}, f32[4,32,2048]{2,1,0:T(8,128)}, u32[]{:S(2)}, u32[]{:S(2)}) collective-permute-start(f32[4,32,2048]{2,1,0:T(8,128)} %get-tuple-element.30), channel_id=1, source_target_pairs={{16,0},{32,16},{48,32},{64,48},{80,64},{96,80},{112,96},{17,1},{33... | collective-permute-start | bytes 3145736 | tf_op jit(solution)/shard_map/ppermute | solution.py:20
  15.7 55.1 %collective-permute-start = (f32[8,8,2048]{2,1,0:T(8,128)}, f32[8,8,2048]{2,1,0:T(8,128)S(1)}, u32[]{:S(2)}, u32[]{:S(2)}) collective-permute-start(f32[8,8,2048]{2,1,0:T(8,128)} %get-tuple-element.27.refs_13_), channel_id=1, source_target_pairs={{0,1},{1,2},{2,3},{3,4},{4,5},{5,6},{6,7},{7,8},{8,9},{9,10},{10,1... | collective-permute-start | bytes 1572872 | tf_op jit(solution)/shard_map/ppermute | solution.py:20
  17.6 53.2 %collective-permute-start.1 = (f32[8,8,2048]{2,1,0:T(8,128)}, f32[8,8,2048]{2,1,0:T(8,128)S(1)}, u32[]{:S(2)}, u32[]{:S(2)}) collective-permute-start(f32[8,8,2048]{2,1,0:T(8,128)} %get-tuple-element.28.refs_12_), channel_id=1, source_target_pairs={{1,0},{2,1},{3,2},{4,3},{5,4},{6,5},{7,6},{8,7},{9,8},{10,9},{11,1... | collective-permute-start | bytes 1572872 | tf_op jit(solution)/shard_map/ppermute | solution.py:20
  41.5 29.3 %collective-permute-start.4 = (f32[256,128]{1,0:T(8,128)S(1)}, f32[256,128]{1,0:T(8,128)}, u32[]{:S(2)}, u32[]{:S(2)}) collective-permute-start(f32[256,128]{1,0:T(8,128)S(1)} %all_gather.3.wear_ref), channel_id=1, source_target_pairs={{0,2},{1,3},{2,0},{3,1},{4,6},{5,7},{6,4},{7,5},{8,10},{9,11},{10,... | collective-permute-start | bytes 393224 | tf_op jit(solution)/shard_map/ppermute | solution.py:105
  41.5 14.8 %copy-start.6 = (s32[512,128]{1,0:T(8,128)S(1)}, s32[512,128]{1,0:T(8,128)}, u32[]{:S(2)}) copy-start(s32[512,128]{1,0:T(8,128)} %list_ref.3) | copy-start | bytes 786436
  41.5 14.8 %copy-start.11 = (s32[512]{0:T(512)S(1)}, s32[512]{0:T(512)}, u32[]{:S(2)}) copy-start(s32[512]{0:T(512)} %owner_ref.5) | copy-start | bytes 6148
  41.5 14.8 %copy-start.14 = (s32[512]{0:T(512)S(1)}, s32[512]{0:T(512)}, u32[]{:S(2)}) copy-start(s32[512]{0:T(512)} %count_ref.3) | copy-start | bytes 6148
  44.7 1.1 copy-start.5
  45.8 0.8 copy-start.7
  56.4 2.2 %copy-start.3 = (s32[1048576]{0:T(1024)S(1)}, s32[1048576]{0:T(1024)}, u32[]{:S(2)}) copy-start(s32[1048576]{0:T(1024)} %param.19) | copy-start | bytes 12582916
  58.6 0.7 copy-start.9
  59.3 0.6 copy-start.12
  59.9 21.8 %copy-start.10 = (s32[2560]{0:T(1024)S(1)}, s32[2560]{0:T(1024)}, u32[]{:S(2)}) copy-start(s32[2560]{0:T(1024)} %collect_tiles.1.tiles_ref) | copy-start | bytes 30724
  59.9 21.8 %copy-start.13 = (s32[2]{0:T(128)S(1)}, s32[2]{0:T(128)}, u32[]{:S(2)}) copy-start(s32[2]{0:T(128)} %pad_add_fusion.where_ref.refs_0_) | copy-start | bytes 28
  64.2 17.5 %copy-start.4 = (s32[1048576]{0:T(1024)S(1)}, s32[1048576]{0:T(1024)}, u32[]{:S(2)}) copy-start(s32[1048576]{0:T(1024)} %param.19) | copy-start | bytes 12582916
  70.9 1.0 copy-start.8
  74.3 42.2 %collective-permute-start.6 = (f32[3,32,2048]{2,1,0:T(8,128)S(1)}, f32[3,32,2048]{2,1,0:T(8,128)S(1)}, u32[]{:S(2)}, u32[]{:S(2)}) collective-permute-start(f32[3,32,2048]{2,1,0:T(8,128)S(1)} %get-tuple-element.37.refs_8_), channel_id=1, source_target_pairs={{16,0},{32,16},{48,32},{64,48},{80,64},{96,80},{112,96},{17,1},{33... | collective-permute-start | bytes 2359304 | tf_op jit(solution)/shard_map/ppermute | solution.py:20
  75.6 40.9 %collective-permute-start.5 = (f32[3,32,2048]{2,1,0:T(8,128)S(1)}, f32[3,32,2048]{2,1,0:T(8,128)S(1)}, u32[]{:S(2)}, u32[]{:S(2)}) collective-permute-start(f32[3,32,2048]{2,1,0:T(8,128)S(1)} %get-tuple-element.38.refs_9_), channel_id=1, source_target_pairs={{0,16},{16,32},{32,48},{48,64},{64,80},{80,96},{96,112},{1,17},{17... | collective-permute-start | bytes 2359304 | tf_op jit(solution)/shard_map/ppermute | solution.py:20
  86.3 18.4 %copy-start.2 = (f32[8,32,2048]{2,1,0:T(8,128)S(1)}, f32[8,32,2048]{2,1,0:T(8,128)}, u32[]{:S(2)}) copy-start(f32[8,32,2048]{2,1,0:T(8,128)} %s_here.5) | copy-start | bytes 6291460
  98.1 18.3 %collective-permute-start.7 = (f32[8,2048]{1,0:T(8,128)S(1)}, f32[8,2048]{1,0:T(8,128)S(1)}, u32[]{:S(2)}, u32[]{:S(2)}) collective-permute-start(f32[8,2048]{1,0:T(8,128)S(1)} %get-tuple-element.47), channel_id=1, source_target_pairs={{0,1},{1,2},{2,3},{3,4},{4,5},{5,6},{6,7},{7,8},{8,9},{9,10},{10,1... | collective-permute-start | bytes 196616 | tf_op jit(solution)/shard_map/ppermute | solution.py:20
  100.1 16.4 %collective-permute-start.8 = (f32[8,2048]{1,0:T(8,128)S(1)}, f32[8,2048]{1,0:T(8,128)S(1)}, u32[]{:S(2)}, u32[]{:S(2)}) collective-permute-start(f32[8,2048]{1,0:T(8,128)S(1)} %get-tuple-element.48), channel_id=1, source_target_pairs={{1,0},{2,1},{3,2},{4,3},{5,4},{6,5},{7,6},{8,7},{9,8},{10,9},{11,1... | collective-permute-start | bytes 196616 | tf_op jit(solution)/shard_map/ppermute | solution.py:20

commit v11 on v10

--- a/solution.py
+++ b/solution.py
@@ -112,37 +112,20 @@
     return high, middle, rest - middle
 
 
-def collect_kernel(shard_tiles, where_ref, owner_ref, out_ref):
-    ntile = owner_ref.shape[0]
-    room = out_ref.shape[0] // 4
-    me = where_ref[0]
-    for k in range(4):
-        out_ref[(k + 1) * room - 1] = 0
-
-    @pl.when(where_ref[1] == 1)
-    def _():
-        def step(i, ends):
-            offset = owner_ref[i] - me
-            other = ((i // (2 * shard_tiles)) ^ (me // 2)) & 1
-            kind = jnp.where(offset == 0, 0, jnp.where(offset * offset == 1, 1, 8)) + 2 * other
-            for end in ends:
-                out_ref[end] = i
-            return tuple(end + jnp.where(kind == k, 1, 0) for k, end in enumerate(ends))
-
-        starts = tuple(jnp.int32(k * room) for k in range(4))
-        ends = lax.fori_loop(0, ntile, step, starts, unroll=8)
-        for k in range(4):
-            out_ref[(k + 1) * room - 1] = ends[k] - k * room
-
-
 def collect(position, owner, shard_tiles):
-    return pl.pallas_call(
-        functools.partial(collect_kernel, shard_tiles),
-        name="collect_tiles",
-        in_specs=[pl.BlockSpec(memory_space=pltpu.SMEM)] * 2,
-        out_specs=pl.BlockSpec(memory_space=pltpu.SMEM),
-        out_shape=jax.ShapeDtypeStruct((4 * (owner.shape[0] + 128),), jnp.int32),
-    )(position, owner)
+    tile = jnp.arange(owner.shape[0], dtype=jnp.int32)
+    offset = owner - position[0]
+    other = ((tile // (2 * shard_tiles)) ^ (position[0] // 2)) & 1
+    kind = jnp.where(offset == 0, 0, jnp.where(offset * offset == 1, 1, 8)) + 2 * other
+    mine = kind[None, :] == jnp.arange(4, dtype=jnp.int32)[:, None]
+    ahead = jnp.logical_and(tile[None, None, :] < tile[None, :, None], mine[:, None, :])
+    place = jnp.where(mine, jnp.sum(jnp.where(ahead, 1, 0), axis=-1), -1)
+    lists = jnp.sum(
+        jnp.where(place[:, None, :] == tile[None, :, None], tile[None, None, :], 0), axis=-1
+    )
+    counts = jnp.sum(jnp.where(mine, 1, 0), axis=-1, keepdims=True)
+    counts = jnp.broadcast_to(counts, (4, 128))
+    return jnp.concatenate([lists, counts], axis=1).astype(jnp.int32).reshape(-1)
 
 
 def paint_kernel(

time: 121 us -> 133 us (1.099)
  waiting for transfers between devices: 6.61 us -> 27.9 us
  blocking collectives: 17.9 us -> 11.7 us
  Pallas kernels: 57.9 us -> 51.9 us
  starting transfers between devices: 28.5 us -> 30.6 us
  other arithmetic: 0.58 us -> 2.17 us
  local copies, waits for them, and re-layouts: 8.1 us -> 6.53 us
    ppermute x8, waiting for transfers between devices: 0.02 us -> 27.9 us  [shift_both(): return (lax.ppermute(last, axis, up), lax.ppermute(first, axis, down))]
    pallas_call x1 -> x0, Pallas kernels: 9.09 us -> none  [collect(): pl.pallas_call(functools.partial(collect_kernel, shard_tiles), name='coll...]
    ppermute x1, waiting for transfers between devices: 6.59 us -> 0.01 us  [gather_wear(): return (own, lax.ppermute(own, 'tan', [(i, i ^ 2) for i in range(size)]))]
    all_gather x1, blocking collectives: 17.9 us -> 11.7 us  [gather_wear(): lax.all_gather(wear, 'tan', axis=0, axis_index_groups=groups, tiled=True)]
    unnamed x30 -> x22, local copies, waits for them, and re-layouts: 8.1 us -> 5.75 us
    pallas_call x2, Pallas kernels: 8.88 us -> 10.9 us  [paint(): pl.pallas_call(functools.partial(paint_kernel, shard_tiles, 0 if base is...]
    ppermute x1, starting transfers between devices: 0.01 us -> 1.92 us  [gather_wear(): return (own, lax.ppermute(own, 'tan', [(i, i ^ 2) for i in range(size)]))]
    reduce_sum x0 -> x3, other arithmetic: none -> 1.4 us  [the longest x1 0.73 us: collect(): place = jnp.where(mine, jnp.sum(jnp.where(ahead, 1, 0), axis=-1), -1)]
  transfers between devices with their start and end apart: 9 -> 9, of which waited for: 1 -> 1; matrix products, arithmetic and copies ran while one was open for 0% -> 2% of each run, Pallas kernels for 41% -> 34%
where the time goes in v11:
time: 133 us; the launch traced here: 131 us
  Pallas kernels  51.9 us (39%)
  starting transfers between devices  30.6 us (23%)
  waiting for transfers between devices  27.9 us (21%)
  blocking collectives  11.7 us (9%)
  local copies, waits for them, and re-layouts  6.53 us (5%)
  other arithmetic  2.17 us (2%)
    ppermute x8, starting transfers between devices, shift_both(): return (lax.ppermute(last, axis, up), lax.ppermute(first, axis, down))  28.6 us
    ppermute x8, waiting for transfers between devices, shift_both(): return (lax.ppermute(last, axis, up), lax.ppermute(first, axis, down))  27.9 us
    pallas_call x2, Pallas kernels, relax_layers(): pl.pallas_call(functools.partial(layer_kernel, first_sweep), name='relax_...  24.6 us
    all_gather x1, blocking collectives, gather_wear(): lax.all_gather(wear, 'tan', axis=0, axis_index_groups=groups, tiled=True)  11.7 us
    pallas_call x2, Pallas kernels, paint(): pl.pallas_call(functools.partial(paint_kernel, shard_tiles, 0 if base is...  10.9 us
    unnamed x22, local copies, waits for them, and re-layouts  5.75 us
    pallas_call x1, Pallas kernels, finish_second(): pl.pallas_call(finish_second_kernel, name='finish_second', grid_spec=pltp...  3.34 us
    pallas_call x1, Pallas kernels, pack_rows(): pl.pallas_call(rows_kernel, name='pack_rows', grid=(1,), in_specs=[f_spec...  3.21 us
  transfers between devices with their start and end apart: 9, of which 1 were waited for; matrix products, arithmetic and copies ran while one was open for 2% of the time, Pallas kernels for 34%

profile of v11, /device:TPU:4, one launch (start us, length us, event | category | flops | bytes accessed | tf_op | source)
XLA Modules:
  0.0 131.0 jit_solution(2058778338432072231)
XLA Ops:
  0.0 1.4 %archard.1 = f32[32,128]{1,0:T(8,128)} custom-call(f32[8]{0:T(128)} %rates_ref.1, s32[32,128]{1,0:T(8,128)} %class_ref.1, f32[32,128]{1,0:T(8,128)} %contact_ref.1, f32[32,128]{1,0:T(8,128)} %sliding_ref.1), custom_call_target="tpu_custom_call" | custom-call | tf_op jit(solution)/shard_map/archard/pallas_call | solution.py:34
  1.4 11.7 %all_gather.3.wear_ref = f32[256,128]{1,0:T(8,128)S(1)} all-gather(f32[32,128]{1,0:T(8,128)} %archard.1), channel_id=1, replica_groups={{0,1,4,5,8,9,12,13},{2,3,6,7,10,11,14,15},{16,17,20,21,24,25,28,29},{18..., dimensions={0}, use_global_device_ids=true | all-gather | bytes 147456 | tf_op jit(solution)/shard_map/all_gather | solution.py:104
  13.2 1.9 %collective-permute-start.4 = (f32[256,128]{1,0:T(8,128)S(1)}, f32[256,128]{1,0:T(8,128)}, u32[]{:S(2)}, u32[]{:S(2)}) collective-permute-start(f32[256,128]{1,0:T(8,128)S(1)} %all_gather.3.wear_ref), channel_id=1, source_target_pairs={{0,2},{1,3},{2,0},{3,1},{4,6},{5,7},{6,4},{7,5},{8,10},{9,11},{10,... | collective-permute-start | bytes 393224 | tf_op jit(solution)/shard_map/ppermute | solution.py:105
  15.1 1.6 %copy-done = f32[8,32,2048]{2,1,0:T(8,128)S(1)} copy-done((f32[8,32,2048]{2,1,0:T(8,128)S(1)}, f32[8,32,2048]{2,1,0:T(8,128)}, u32[]{:S(2)}) %copy-start) | copy-done | bytes 2097176
  16.7 3.2 %pack_rows.1 = (f32[8,8,2048]{2,1,0:T(8,128)}, f32[8,8,2048]{2,1,0:T(8,128)}) custom-call(f32[3,8,32,2048]{3,2,1,0:T(8,128)} %refs_1_.1, f32[8,32,2048]{2,1,0:T(8,128)S(1)} %copy-done, f32[3,8,32,2048]{3,2,1,0:T(8,128)} %refs_1_.1, f32[8,32,2048]{2,1,0:T(8,128)S(1)} %copy-done), custom_call_target="tpu_custom_call" | custom-call | tf_op jit(solution)/shard_map/pack_rows/pallas_call | solution.py:60
  19.9 2.0 %collective-permute-start = (f32[8,8,2048]{2,1,0:T(8,128)}, f32[8,8,2048]{2,1,0:T(8,128)S(1)}, u32[]{:S(2)}, u32[]{:S(2)}) collective-permute-start(f32[8,8,2048]{2,1,0:T(8,128)} %get-tuple-element.27.refs_13_), channel_id=1, source_target_pairs={{0,1},{1,2},{2,3},{3,4},{4,5},{5,6},{6,7},{7,8},{8,9},{9,10},{10,1... | collective-permute-start | bytes 1572872 | tf_op jit(solution)/shard_map/ppermute | solution.py:20
  21.8 0.0 copy-start.9
  21.9 0.0 copy-start.1
  21.9 4.6 %collective-permute-start.1 = (f32[8,8,2048]{2,1,0:T(8,128)}, f32[8,8,2048]{2,1,0:T(8,128)S(1)}, u32[]{:S(2)}, u32[]{:S(2)}) collective-permute-start(f32[8,8,2048]{2,1,0:T(8,128)} %get-tuple-element.28.refs_12_), channel_id=1, source_target_pairs={{1,0},{2,1},{3,2},{4,3},{5,4},{6,5},{7,6},{8,7},{9,8},{10,9},{11,1... | collective-permute-start | bytes 1572872 | tf_op jit(solution)/shard_map/ppermute | solution.py:20
  26.5 2.8 %pack_faces.1 = (f32[4,32,2048]{2,1,0:T(8,128)}, f32[4,32,2048]{2,1,0:T(8,128)}) custom-call(f32[3,8,32,2048]{3,2,1,0:T(8,128)} %refs_1_.1, f32[8,32,2048]{2,1,0:T(8,128)S(1)} %copy-done), custom_call_target="tpu_custom_call" | custom-call | tf_op jit(solution)/shard_map/pack_faces/pallas_call | solution.py:90
  29.3 6.5 %collective-permute-start.2 = (f32[4,32,2048]{2,1,0:T(8,128)}, f32[4,32,2048]{2,1,0:T(8,128)}, u32[]{:S(2)}, u32[]{:S(2)}) collective-permute-start(f32[4,32,2048]{2,1,0:T(8,128)} %get-tuple-element.29), channel_id=1, source_target_pairs={{0,16},{16,32},{32,48},{48,64},{64,80},{80,96},{96,112},{1,17},{17... | collective-permute-start | bytes 3145736 | tf_op jit(solution)/shard_map/ppermute | solution.py:20
  35.7 1.3 collective-permute-start.3
  37.1 0.1 select_reduce_fusion.2
  37.2 0.1 iota_compare_fusion.1
  37.3 0.7 select_reduce_fusion.1
  38.0 0.6 select_reduce_fusion
  38.6 0.1 broadcast_in_dim.59
  38.6 0.6 pad_add_fusion
  39.2 3.1 %face_sums.1 = (f32[3,2,32,2048]{3,2,1,0:T(8,128)S(1)}, f32[2,32,2048]{2,1,0:T(8,128)S(1)}) custom-call(f32[3,8,32,2048]{3,2,1,0:T(8,128)} %refs_1_.1, f32[3,8,32,2048]{3,2,1,0:T(8,128)} %refs_1_.1, f32[8,32,2048]{2,1,0:T(8,128)S(1)} %copy-done.1, f32[8,32,2048]{2,1,0:T(8,128)S(1)} %copy-done.1), custom_call_target="tpu_custom_call" | custom-call | tf_op jit(solution)/shard_map/face_sums/pallas_call | solution.py:476
  42.4 0.0 copy-start.5
  42.4 1.1 copy-done.5
  43.5 0.8 copy-done.7
  44.3 0.7 reshape.55.tiles_ref
  45.0 0.1 pad_add_fusion.1.where_ref.refs_0_
  45.1 0.0 copy-done.10
  45.1 2.2 %copy-done.3 = s32[1048576]{0:T(1024)S(1)} copy-done((s32[1048576]{0:T(1024)S(1)}, s32[1048576]{0:T(1024)}, u32[]{:S(2)}) %copy-start.3) | copy-done | bytes 4194328
  47.3 5.1 %paint_band.2.refs_0_ = f32[48,2048]{1,0:T(8,128)S(1)} custom-call(s32[2]{0:T(128)S(1)} %pad_add_fusion.1.where_ref.refs_0_, s32[512]{0:T(512)S(1)} %copy-done.9, s32[512]{0:T(512)S(1)} %copy-done.10, s32[2560]{0:T(1024)S(1)} %reshape.55.tiles_ref, f32[256,128]{1,0:T(8,128)S(1)} %all_gather.3.wear_ref, s32[512,128]{1,0:T(8,128)S(1)} %copy-done.6, ...), custom_call_target="tpu_custom_call" | custom-call | tf_op jit(solution)/shard_map/paint_band/pallas_call | solution.py:237
  52.4 0.0 collective-permute-done.4.wear_ref
  52.4 27.8 %collective-permute-done.2.low.s_low = f32[4,32,2048]{2,1,0:T(8,128)} collective-permute-done((f32[4,32,2048]{2,1,0:T(8,128)}, f32[4,32,2048]{2,1,0:T(8,128)}, u32[]{:S(2)}, u32[]{:S(2)}) %collective-permute-start.2) | collective-permute-done | bytes 1048608 | tf_op jit(solution)/shard_map/ppermute | solution.py:20
  80.3 0.0 collective-permute-done.3.high.s_high
  80.3 0.0 collective-permute-done.before.s_before.refs_3_.refs_5_.refs_10_
  80.3 0.0 collective-permute-done.1.after.s_after.refs_4_.refs_6_.refs_11_
  80.3 0.0 copy-done.8
  80.3 0.0 copy-start.4
  80.3 2.6 %finish_first.1 = (f32[3,32,2048]{2,1,0:T(8,128)S(1)}, f32[3,32,2048]{2,1,0:T(8,128)S(1)}, f32[8,2048]{1,0:T(8,128)S(1)}, f32[8,2048]{1,0:T(8,128)S(1)}) custom-call(f32[3,2,32,2048]{3,2,1,0:T(8,128)} %copy-done.5, f32[8,32,2048]{2,1,0:T(8,128)} %s_here.5, f32[2,32,2048]{2,1,0:T(8,128)S(1)} %copy-done.8, f32[4,32,2048]{2,1,0:T(8,128)} %collective-permute-done.2.low.s_low, ...), custom_call_target="tpu_custom_call" | custom-call | tf_op jit(solution)/shard_map/finish_first/pallas_call | solution.py:540
  82.9 1.3 collective-permute-start.6
  84.2 6.6 %collective-permute-start.5 = (f32[3,32,2048]{2,1,0:T(8,128)S(1)}, f32[3,32,2048]{2,1,0:T(8,128)S(1)}, u32[]{:S(2)}, u32[]{:S(2)}) collective-permute-start(f32[3,32,2048]{2,1,0:T(8,128)S(1)} %get-tuple-element.38.refs_9_), channel_id=1, source_target_pairs={{0,16},{16,32},{32,48},{48,64},{64,80},{80,96},{96,112},{1,17},{17... | collective-permute-start | bytes 2359304 | tf_op jit(solution)/shard_map/ppermute | solution.py:20
  90.8 5.8 %paint_band.3.refs_7_ = f32[48,2048]{1,0:T(8,128)S(1)} custom-call(s32[2]{0:T(128)S(1)} %pad_add_fusion.1.where_ref.refs_0_, s32[512]{0:T(512)S(1)} %copy-done.9, s32[512]{0:T(512)S(1)} %copy-done.10, s32[2560]{0:T(1024)S(1)} %reshape.55.tiles_ref, f32[256,128]{1,0:T(8,128)} %collective-permute-done.4.wear_ref, s32[512,128]{1,0:T(8,128)S(1)} %copy-done.6, ...), custom_call_target="tpu_custom_call" | custom-call | tf_op jit(solution)/shard_map/paint_band/pallas_call | solution.py:237
  96.6 0.0 copy-start.2
  96.6 12.3 %relax_layers_first.1 = (f32[3,8,32,2048]{3,2,1,0:T(8,128)}, f32[3,8,2048]{2,1,0:T(8,128)S(1)}, f32[3,8,2048]{2,1,0:T(8,128)S(1)}) custom-call(s32[2]{0:T(128)S(1)} %pad_add_fusion.1.where_ref.refs_0_, f32[3,8,32,2048]{3,2,1,0:T(8,128)} %refs_1_.1, f32[8,32,2048]{2,1,0:T(8,128)} %s_here.5, ...), custom_call_target="tpu_custom_call" | custom-call | tf_op jit(solution)/shard_map/relax_layers_first/pallas_call | solution.py:428
  108.9 1.9 %collective-permute-start.7 = (f32[8,2048]{1,0:T(8,128)S(1)}, f32[8,2048]{1,0:T(8,128)S(1)}, u32[]{:S(2)}, u32[]{:S(2)}) collective-permute-start(f32[8,2048]{1,0:T(8,128)S(1)} %get-tuple-element.47), channel_id=1, source_target_pairs={{0,1},{1,2},{2,3},{3,4},{4,5},{5,6},{6,7},{7,8},{8,9},{9,10},{10,1... | collective-permute-start | bytes 196616 | tf_op jit(solution)/shard_map/ppermute | solution.py:20
  110.8 4.5 %collective-permute-start.8 = (f32[8,2048]{1,0:T(8,128)S(1)}, f32[8,2048]{1,0:T(8,128)S(1)}, u32[]{:S(2)}, u32[]{:S(2)}) collective-permute-start(f32[8,2048]{1,0:T(8,128)S(1)} %get-tuple-element.48), channel_id=1, source_target_pairs={{1,0},{2,1},{3,2},{4,3},{5,4},{6,5},{7,6},{8,7},{9,8},{10,9},{11,1... | collective-permute-start | bytes 196616 | tf_op jit(solution)/shard_map/ppermute | solution.py:20
  115.3 12.3 %relax_layers_second.1 = (f32[3,8,32,2048]{3,2,1,0:T(8,128)}, f32[2,32,2048]{2,1,0:T(8,128)S(1)}) custom-call(s32[2]{0:T(128)S(1)} %pad_add_fusion.1.where_ref.refs_0_, f32[3,8,32,2048]{3,2,1,0:T(8,128)} %get-tuple-element.39.refs_1_, f32[8,32,2048]{2,1,0:T(8,128)S(1)} %copy-done.2, f32[3,8,2048]{2,1,0:T(8,128)S(1)} %get-tuple-element.43.refs_3_, ...), custom_call_target="tpu_custom_call" | custom-call | tf_op jit(solution)/shard_map/relax_layers_second/pallas_call | solution.py:428
  127.6 0.0 collective-permute-done.7.before
  127.6 0.0 collective-permute-done.8.after
  127.6 0.0 collective-permute-done.6.high
  127.6 0.0 collective-permute-done.5.low
  127.6 3.3 %finish_second.1 = f32[3,8,32,2048]{3,2,1,0:T(8,128)} custom-call(s32[2]{0:T(128)S(1)} %pad_add_fusion.1.where_ref.refs_0_, f32[3,8,32,2048]{3,2,1,0:T(8,128)} %get-tuple-element.45.sums, f32[8,32,2048]{2,1,0:T(8,128)} %s_here.5, f32[2,32,2048]{2,1,0:T(8,128)S(1)} %get-tuple-element.46.totals, ...), custom_call_target="tpu_custom_call", output_to_operand_aliasing={{}: (1, {})} | custom-call | tf_op jit(solution)/shard_map/finish_second/pallas_call | solution.py:597
  (13 shorter events, 0.0 us)
Async XLA Ops:
  13.2 39.3 %collective-permute-start.4 = (f32[256,128]{1,0:T(8,128)S(1)}, f32[256,128]{1,0:T(8,128)}, u32[]{:S(2)}, u32[]{:S(2)}) collective-permute-start(f32[256,128]{1,0:T(8,128)S(1)} %all_gather.3.wear_ref), channel_id=1, source_target_pairs={{0,2},{1,3},{2,0},{3,1},{4,6},{5,7},{6,4},{7,5},{8,10},{9,11},{10,... | collective-permute-start | bytes 393224 | tf_op jit(solution)/shard_map/ppermute | solution.py:105
  15.1 1.6 %copy-start = (f32[8,32,2048]{2,1,0:T(8,128)S(1)}, f32[8,32,2048]{2,1,0:T(8,128)}, u32[]{:S(2)}) copy-start(f32[8,32,2048]{2,1,0:T(8,128)} %s_here.5) | copy-start | bytes 6291460
  19.9 60.4 %collective-permute-start = (f32[8,8,2048]{2,1,0:T(8,128)}, f32[8,8,2048]{2,1,0:T(8,128)S(1)}, u32[]{:S(2)}, u32[]{:S(2)}) collective-permute-start(f32[8,8,2048]{2,1,0:T(8,128)} %get-tuple-element.27.refs_13_), channel_id=1, source_target_pairs={{0,1},{1,2},{2,3},{3,4},{4,5},{5,6},{6,7},{7,8},{8,9},{9,10},{10,1... | collective-permute-start | bytes 1572872 | tf_op jit(solution)/shard_map/ppermute | solution.py:20
  21.8 15.2 %copy-start.9 = (s32[512]{0:T(512)S(1)}, s32[512]{0:T(512)}, u32[]{:S(2)}) copy-start(s32[512]{0:T(512)} %owner_ref.3) | copy-start | bytes 6148
  21.9 17.4 %copy-start.1 = (f32[8,32,2048]{2,1,0:T(8,128)S(1)}, f32[8,32,2048]{2,1,0:T(8,128)}, u32[]{:S(2)}) copy-start(f32[8,32,2048]{2,1,0:T(8,128)} %s_here.5) | copy-start | bytes 6291460
  21.9 58.4 %collective-permute-start.1 = (f32[8,8,2048]{2,1,0:T(8,128)}, f32[8,8,2048]{2,1,0:T(8,128)S(1)}, u32[]{:S(2)}, u32[]{:S(2)}) collective-permute-start(f32[8,8,2048]{2,1,0:T(8,128)} %get-tuple-element.28.refs_12_), channel_id=1, source_target_pairs={{1,0},{2,1},{3,2},{4,3},{5,4},{6,5},{7,6},{8,7},{9,8},{10,9},{11,1... | collective-permute-start | bytes 1572872 | tf_op jit(solution)/shard_map/ppermute | solution.py:20
  29.3 51.0 %collective-permute-start.2 = (f32[4,32,2048]{2,1,0:T(8,128)}, f32[4,32,2048]{2,1,0:T(8,128)}, u32[]{:S(2)}, u32[]{:S(2)}) collective-permute-start(f32[4,32,2048]{2,1,0:T(8,128)} %get-tuple-element.29), channel_id=1, source_target_pairs={{0,16},{16,32},{32,48},{48,64},{64,80},{80,96},{96,112},{1,17},{17... | collective-permute-start | bytes 3145736 | tf_op jit(solution)/shard_map/ppermute | solution.py:20
  35.7 44.5 %collective-permute-start.3 = (f32[4,32,2048]{2,1,0:T(8,128)}, f32[4,32,2048]{2,1,0:T(8,128)}, u32[]{:S(2)}, u32[]{:S(2)}) collective-permute-start(f32[4,32,2048]{2,1,0:T(8,128)} %get-tuple-element.30), channel_id=1, source_target_pairs={{16,0},{32,16},{48,32},{64,48},{80,64},{96,80},{112,96},{17,1},{33... | collective-permute-start | bytes 3145736 | tf_op jit(solution)/shard_map/ppermute | solution.py:20
  39.2 5.9 %copy-start.6 = (s32[512,128]{1,0:T(8,128)S(1)}, s32[512,128]{1,0:T(8,128)}, u32[]{:S(2)}) copy-start(s32[512,128]{1,0:T(8,128)} %list_ref.3) | copy-start | bytes 786436
  39.2 5.9 %copy-start.10 = (s32[512]{0:T(512)S(1)}, s32[512]{0:T(512)}, u32[]{:S(2)}) copy-start(s32[512]{0:T(512)} %count_ref.3) | copy-start | bytes 6148
  42.4 1.1 copy-start.5
  43.5 0.8 copy-start.7
  45.1 2.2 %copy-start.3 = (s32[1048576]{0:T(1024)S(1)}, s32[1048576]{0:T(1024)}, u32[]{:S(2)}) copy-start(s32[1048576]{0:T(1024)} %param.19) | copy-start | bytes 12582916
  47.3 33.0 %copy-start.8 = (f32[2,32,2048]{2,1,0:T(8,128)S(1)}, f32[2,32,2048]{2,1,0:T(8,128)}, u32[]{:S(2)}) copy-start(f32[2,32,2048]{2,1,0:T(8,128)} %copy-done.7) | copy-start | bytes 1572868
  80.3 10.5 %copy-start.4 = (s32[1048576]{0:T(1024)S(1)}, s32[1048576]{0:T(1024)}, u32[]{:S(2)}) copy-start(s32[1048576]{0:T(1024)} %param.19) | copy-start | bytes 12582916
  82.9 44.7 %collective-permute-start.6 = (f32[3,32,2048]{2,1,0:T(8,128)S(1)}, f32[3,32,2048]{2,1,0:T(8,128)S(1)}, u32[]{:S(2)}, u32[]{:S(2)}) collective-permute-start(f32[3,32,2048]{2,1,0:T(8,128)S(1)} %get-tuple-element.37.refs_8_), channel_id=1, source_target_pairs={{16,0},{32,16},{48,32},{64,48},{80,64},{96,80},{112,96},{17,1},{33... | collective-permute-start | bytes 2359304 | tf_op jit(solution)/shard_map/ppermute | solution.py:20
  84.2 43.4 %collective-permute-start.5 = (f32[3,32,2048]{2,1,0:T(8,128)S(1)}, f32[3,32,2048]{2,1,0:T(8,128)S(1)}, u32[]{:S(2)}, u32[]{:S(2)}) collective-permute-start(f32[3,32,2048]{2,1,0:T(8,128)S(1)} %get-tuple-element.38.refs_9_), channel_id=1, source_target_pairs={{0,16},{16,32},{32,48},{48,64},{64,80},{80,96},{96,112},{1,17},{17... | collective-permute-start | bytes 2359304 | tf_op jit(solution)/shard_map/ppermute | solution.py:20
  96.6 18.8 %copy-start.2 = (f32[8,32,2048]{2,1,0:T(8,128)S(1)}, f32[8,32,2048]{2,1,0:T(8,128)}, u32[]{:S(2)}) copy-start(f32[8,32,2048]{2,1,0:T(8,128)} %s_here.5) | copy-start | bytes 6291460
  108.9 18.7 %collective-permute-start.7 = (f32[8,2048]{1,0:T(8,128)S(1)}, f32[8,2048]{1,0:T(8,128)S(1)}, u32[]{:S(2)}, u32[]{:S(2)}) collective-permute-start(f32[8,2048]{1,0:T(8,128)S(1)} %get-tuple-element.47), channel_id=1, source_target_pairs={{0,1},{1,2},{2,3},{3,4},{4,5},{5,6},{6,7},{7,8},{8,9},{9,10},{10,1... | collective-permute-start | bytes 196616 | tf_op jit(solution)/shard_map/ppermute | solution.py:20
  110.8 16.8 %collective-permute-start.8 = (f32[8,2048]{1,0:T(8,128)S(1)}, f32[8,2048]{1,0:T(8,128)S(1)}, u32[]{:S(2)}, u32[]{:S(2)}) collective-permute-start(f32[8,2048]{1,0:T(8,128)S(1)} %get-tuple-element.48), channel_id=1, source_target_pairs={{1,0},{2,1},{3,2},{4,3},{5,4},{6,5},{7,6},{8,7},{9,8},{10,9},{11,1... | collective-permute-start | bytes 196616 | tf_op jit(solution)/shard_map/ppermute | solution.py:20
